TPU v7x, 32 devices: a whole 2x2x4 slice. The times are simulated.
32 devices in a mesh: chan: 2 (over x), srow: 4 (over y, core), scol: 4 (over z).
Axes of the slice: x: 2, y: 2, z: 4, core: 2. Of those that a mesh axis runs over, the one named last changes fastest.
Arguments:
- vis: bfloat16 [2, 2, 512, 512], P('chan', None, 'srow', 'scol'), may hold values from -4 to 4
- model: bfloat16 [2, 64, 2, 512, 512], P('chan', None, None, 'srow', 'scol'), may hold values from -1 to 1, as said below
- flags: int32 [2, 32, 32], P('chan', 'srow', 'scol'), may hold values 0 or 1
- gains: float32 [2, 64, 2, 512], P('chan', None, None, ('srow', 'scol')), may hold values from -3 to 3
- consensus: float32 [64, 1, 2, 512], P(None, None, None, ('srow', 'scol')), may hold values from -3 to 3
- dual: float32 [2, 64, 2, 512], P('chan', None, None, ('srow', 'scol')), may hold values from -2 to 2
- rho: float32 [8], replicated, may hold values from 0.5 to 8
- cluster: int32 [64], replicated, may hold values from 0 to 7
Outputs:
- gains_out: float32 [2, 64, 2, 512], P('chan', None, None, ('srow', 'scol'))
- consensus_out: float32 [64, 1, 2, 512], P(None, None, None, ('srow', 'scol'))
- dual_out: float32 [2, 64, 2, 512], P('chan', None, None, ('srow', 'scol'))
Inputs may be any that keep to these rules, and one draw needn't show every extreme that they name: `model`: entries of about 1 / sqrt(512) in size.
All inputs are finite; a program needn't handle non-finite values. No bound on the sum of `flags` on one device may be relied on, other than what follows from the above.
Results may differ from a plain program's by a relative error of at most 0.0003.
Values sent between devices are 32-bit elements; how exact they have to be, the bound alone decides.
No kernel may reach another device: no remote copies, remote signals or barrier semaphores. Data moves between devices by JAX's collectives and lax.ppermute only.
A program may use at most 64 MiB of HBM per device.

v0:
```python
import math

import jax
import jax.numpy as jnp
from jax import lax
from jax.sharding import PartitionSpec as P

STATIONS = 512
TILE = 16
ITERS = 4


EPS = 1e-05
STEP = 0.5


def basis_table(groups, order):
    xval = (jnp.arange(groups, dtype=jnp.float32) + 0.5) / groups
    columns = [
        math.comb(order - 1, b) * xval**b * (1.0 - xval) ** (order - 1 - b) for b in range(order)
    ]
    return jnp.stack(columns, axis=1)


def local_terms(vis_block, model_block, weight, g_row, g_col):
    m_real = model_block[:, 0].astype(jnp.float32)
    m_imag = model_block[:, 1].astype(jnp.float32)
    c_real = g_col[:, 0][:, None, :]
    c_imag = g_col[:, 1][:, None, :]
    z_real = m_real * c_real + m_imag * c_imag
    z_imag = m_imag * c_real - m_real * c_imag
    r_real = g_row[:, 0][:, :, None]
    r_imag = g_row[:, 1][:, :, None]
    pred_real = jnp.sum(r_real * z_real - r_imag * z_imag, axis=0)
    pred_imag = jnp.sum(r_real * z_imag + r_imag * z_real, axis=0)
    res_real = vis_block[0].astype(jnp.float32) - pred_real
    res_imag = vis_block[1].astype(jnp.float32) - pred_imag
    w_real = weight * res_real
    w_imag = weight * res_imag
    power = jnp.sum(w_real * res_real + w_imag * res_imag)
    a_term = jnp.sum(weight[None] * (z_real * z_real + z_imag * z_imag), axis=-1)
    cross_real = jnp.sum(z_real * w_real[None] + z_imag * w_imag[None], axis=-1)
    cross_imag = jnp.sum(z_real * w_imag[None] - z_imag * w_real[None], axis=-1)
    return (power, a_term, jnp.stack([cross_real, cross_imag], axis=-2))


def solve(cross, a_term, g_now, target, rho_eff):
    denom = a_term + rho_eff[:, None]
    fresh = (cross + a_term[..., None, :] * g_now + rho_eff[:, None, None] * target) / denom[
        ..., None, :
    ]
    return g_now + STEP * (fresh - g_now)


def gram_solve(table, rhs):
    gram = jnp.dot(table.T, table, precision=lax.Precision.HIGHEST)
    factor = jnp.linalg.cholesky(gram)
    order = rhs.shape[1]
    flat = jnp.moveaxis(rhs, 1, 0).reshape(order, -1)
    sol = jax.scipy.linalg.cho_solve((factor, True), flat)
    return jnp.moveaxis(sol.reshape((order, rhs.shape[0]) + rhs.shape[2:]), 0, 1)


def sweep_terms(vis_block, model_block, weight, g_row, own_gains, rho_dir, groups):
    g_col = lax.all_gather(own_gains, "srow", axis=2, tiled=True)
    power, a_term, cross = local_terms(vis_block, model_block, weight, g_row, g_col)
    total = lax.psum(power, ("chan", "srow", "scol"))
    rho_eff = rho_dir * (total / (groups * STATIONS * STATIONS) + EPS)
    return (a_term, cross, rho_eff)


def shards(vis, model, flags, gains, consensus, dual, rho, cluster):
    groups = lax.axis_size("chan")
    order = consensus.shape[1]
    table = basis_table(groups, order)
    brow = lax.dynamic_index_in_dim(table, lax.axis_index("chan"), 0, keepdims=False)
    matches = cluster[:, None] == jnp.arange(rho.shape[0], dtype=jnp.int32)[None, :]
    rho_dir = jnp.sum(jnp.where(matches, rho[None, :], 0.0), axis=1)
    fl = flags[0].astype(jnp.float32)
    weight = jnp.repeat(jnp.repeat(fl, TILE, axis=0), TILE, axis=1)
    vis_block = vis[0]
    model_block = model[0]
    dual_own = dual[0]
    target = jnp.einsum("b,kbcp->kcp", brow, consensus, precision=lax.Precision.HIGHEST) - dual_own
    g = gains[0]
    for step in range(ITERS):
        g_row = lax.all_gather(g, "scol", axis=2, tiled=True)
        a_term, cross, rho_eff = sweep_terms(
            vis_block, model_block, weight, g_row, g, rho_dir, groups
        )
        a_own, cross_own = (
            lax.psum_scatter(a_term[:, None, :], "scol", scatter_dimension=2, tiled=True),
            lax.psum_scatter(cross, "scol", scatter_dimension=2, tiled=True),
        )
        g = solve(cross_own, a_own[:, 0, :], g, target, rho_eff)
    local = brow[None, :, None, None] * (g + dual_own)[:, None, :, :]
    sums = lax.psum(local, "chan")
    coeffs = gram_solve(table, sums)
    dual_new = (
        dual_own + g - jnp.einsum("b,kbcp->kcp", brow, coeffs, precision=lax.Precision.HIGHEST)
    )
    return (g[None], coeffs, dual_new[None])


def solution(mesh):
    placed = (
        P("chan", None, "srow", "scol"),
        P("chan", None, None, "srow", "scol"),
        P("chan", "srow", "scol"),
        P("chan", None, None, ("srow", "scol")),
        P(None, None, None, ("srow", "scol")),
        P("chan", None, None, ("srow", "scol")),
        P(),
        P(),
    )
    return jax.shard_map(
        shards,
        mesh=mesh,
        in_specs=placed,
        out_specs=(
            P("chan", None, None, ("srow", "scol")),
            P(None, None, None, ("srow", "scol")),
            P("chan", None, None, ("srow", "scol")),
        ),
        check_vma=False,
    )
```

profile of v0, /device:TPU:0, one launch (start us, length us, event | category | flops | bytes accessed | tf_op | source)
XLA Modules:
  0.0 436.5 jit_solution(12146551925661814514)
XLA Ops:
  7.2 15.3 %all-gather.1 = f32[1,64,2,128]{1,3,2,0:T(8,128)S(1)} all-gather(f32[1,64,2,32]{1,3,2,0:T(8,128)} %param.11), channel_id=3, replica_groups=mesh['chan'=2,'srow'=4,'scol'=4] {'scol'}, dimensions={3}, use_global_device_ids=true | all-gather | bytes 81920 | tf_op jit(solution)/shard_map/all_gather | solution.py:87
  22.5 5.6 %all-gather = f32[1,64,2,128]{1,3,2,0:T(8,128)S(1)} all-gather(f32[1,64,2,32]{1,3,2,0:T(8,128)} %param.11), channel_id=2, replica_groups=mesh['chan'=2,'srow'=4,'scol'=4] {'srow'}, dimensions={3}, use_global_device_ids=true | all-gather | bytes 81920 | tf_op jit(solution)/shard_map/all_gather | solution.py:65
  29.6 6.2 %subtract_reduce_fusion.7 = (f32[128,128]{1,0:T(8,128)S(1)}, f32[128,128]{1,0:T(8,128)S(1)}) fusion(f32[64,128]{1,0:T(8,128)S(1)} %copy.125, f32[64,128]{1,0:T(8,128)S(1)} %copy.124, f32[64,128]{1,0:T(8,128)S(1)} %copy.122, f32[64,128]{1,0:T(8,128)S(1)} %copy.121, bf16[64,2,128,128]{3,2,1,0:T(8,128)(2,1)} %bitcast.195), kind=kLoop, calls=%fused_computation.43 | loop fusion | flops 16744448 | bytes 4456448 | tf_op jit(solution)/shard_map/reduce_sum | solution.py:34
  36.4 4.1 add_reduce_fusion.6
  41.4 0.8 copy.128
  44.0 41.0 %psum.35 = f32[]{:T(128)} all-reduce(f32[]{:T(128)} %get-tuple-element.47), channel_id=1, replica_groups=mesh['chan'=2,'srow'=4,'scol'=4] {'chan','srow','scol'}, use_global_device_ids=true, to_apply=%region_9.10 | all-reduce | flops 1 | bytes 8 | tf_op jit(solution)/shard_map/psum | solution.py:67
  87.9 9.0 %all-reduce.9.cloned.1.call-done = f32[64,2,128]{0,1,2:T(2,128)} async-done(((f32[64,2,128]{0,1,2:T(2,128)}), f32[64,2,128]{0,1,2:T(2,128)}) %all-reduce.9.cloned.1.call-update) | async-done | bytes 65552
  96.9 0.9 bitcast_add_fusion.1
  97.8 13.5 %all_gather.27 = f32[64,2,128]{0,1,2:T(2,128)S(1)} all-gather(f32[64,2,32]{0,1,2:T(2,128)S(1)} %get-tuple-element.45), channel_id=1, replica_groups=mesh['chan'=2,'srow'=4,'scol'=4] {'scol'}, dimensions={2}, use_global_device_ids=true | all-gather | bytes 81920 | tf_op jit(solution)/shard_map/all_gather | solution.py:87
  111.3 5.4 %all_gather.26 = f32[64,2,128]{0,1,2:T(2,128)S(1)} all-gather(f32[64,2,32]{0,1,2:T(2,128)S(1)} %get-tuple-element.45), channel_id=1, replica_groups=mesh['chan'=2,'srow'=4,'scol'=4] {'srow'}, dimensions={2}, use_global_device_ids=true | all-gather | bytes 81920 | tf_op jit(solution)/shard_map/all_gather | solution.py:65
  117.3 6.2 %subtract_reduce_fusion.5 = (f32[128,128]{1,0:T(8,128)S(1)}, f32[128,128]{1,0:T(8,128)S(1)}) fusion(f32[64,128]{1,0:T(8,128)S(1)} %copy.136, f32[64,128]{1,0:T(8,128)S(1)} %copy.135, f32[64,128]{1,0:T(8,128)S(1)} %copy.134, f32[64,128]{1,0:T(8,128)S(1)} %copy.133, bf16[64,2,128,128]{3,2,1,0:T(8,128)(2,1)} %bitcast.196), kind=kLoop, calls=%fused_computation.38 | loop fusion | flops 16744448 | bytes 4456448 | tf_op jit(solution)/shard_map/reduce_sum | solution.py:34
  124.1 4.1 add_reduce_fusion.4
  129.0 39.0 %psum.36 = f32[]{:T(128)} all-reduce(f32[]{:T(128)} %get-tuple-element.42), channel_id=1, replica_groups=mesh['chan'=2,'srow'=4,'scol'=4] {'chan','srow','scol'}, use_global_device_ids=true, to_apply=%region_18.19 | all-reduce | flops 1 | bytes 8 | tf_op jit(solution)/shard_map/psum | solution.py:67
  168.7 0.8 copy.139
  170.3 33.9 %all-reduce.11.cloned.1.call-done = f32[64,2,128]{0,1,2:T(2,128)} async-done(((f32[64,2,128]{0,1,2:T(2,128)}), f32[64,2,128]{0,1,2:T(2,128)}) %all-reduce.11.cloned.1.call-update) | async-done | bytes 65552
  204.2 0.8 multiply_add_fusion.2
  205.0 13.5 %all_gather.29 = f32[64,2,128]{0,1,2:T(2,128)S(1)} all-gather(f32[64,2,32]{0,1,2:T(2,128)S(1)} %multiply_add_fusion.2), channel_id=1, replica_groups=mesh['chan'=2,'srow'=4,'scol'=4] {'scol'}, dimensions={2}, use_global_device_ids=true | all-gather | bytes 81920 | tf_op jit(solution)/shard_map/all_gather | solution.py:87
  218.5 5.6 %all_gather.28 = f32[64,2,128]{0,1,2:T(2,128)S(1)} all-gather(f32[64,2,32]{0,1,2:T(2,128)S(1)} %multiply_add_fusion.2), channel_id=1, replica_groups=mesh['chan'=2,'srow'=4,'scol'=4] {'srow'}, dimensions={2}, use_global_device_ids=true | all-gather | bytes 81920 | tf_op jit(solution)/shard_map/all_gather | solution.py:65
  224.7 6.2 %subtract_reduce_fusion.3 = (f32[128,128]{1,0:T(8,128)S(1)}, f32[128,128]{1,0:T(8,128)S(1)}) fusion(f32[64,128]{1,0:T(8,128)S(1)} %copy.144, f32[64,128]{1,0:T(8,128)S(1)} %copy.143, f32[64,128]{1,0:T(8,128)S(1)} %copy.142, f32[64,128]{1,0:T(8,128)S(1)} %copy.141, bf16[64,2,128,128]{3,2,1,0:T(8,128)(2,1)} %bitcast.197), kind=kLoop, calls=%fused_computation.33 | loop fusion | flops 16744448 | bytes 4456448 | tf_op jit(solution)/shard_map/reduce_sum | solution.py:34
  231.5 4.1 add_reduce_fusion.2
  236.4 38.9 %psum.37 = f32[]{:T(128)} all-reduce(f32[]{:T(128)} %get-tuple-element.39), channel_id=1, replica_groups=mesh['chan'=2,'srow'=4,'scol'=4] {'chan','srow','scol'}, use_global_device_ids=true, to_apply=%region_27.28 | all-reduce | flops 1 | bytes 8 | tf_op jit(solution)/shard_map/psum | solution.py:67
  276.0 0.8 copy.147
  277.6 33.9 %all-reduce.13.cloned.1.call-done = f32[64,2,128]{0,1,2:T(2,128)} async-done(((f32[64,2,128]{0,1,2:T(2,128)}), f32[64,2,128]{0,1,2:T(2,128)}) %all-reduce.13.cloned.1.call-update) | async-done | bytes 65552
  311.5 0.8 multiply_add_fusion.1
  312.3 13.6 %all_gather.31 = f32[64,2,128]{0,1,2:T(2,128)S(1)} all-gather(f32[64,2,32]{0,1,2:T(2,128)S(1)} %multiply_add_fusion.1), channel_id=1, replica_groups=mesh['chan'=2,'srow'=4,'scol'=4] {'scol'}, dimensions={2}, use_global_device_ids=true | all-gather | bytes 81920 | tf_op jit(solution)/shard_map/all_gather | solution.py:87
  325.9 5.4 %all_gather.30 = f32[64,2,128]{0,1,2:T(2,128)S(1)} all-gather(f32[64,2,32]{0,1,2:T(2,128)S(1)} %multiply_add_fusion.1), channel_id=1, replica_groups=mesh['chan'=2,'srow'=4,'scol'=4] {'srow'}, dimensions={2}, use_global_device_ids=true | all-gather | bytes 81920 | tf_op jit(solution)/shard_map/all_gather | solution.py:65
  331.8 6.2 %subtract_reduce_fusion.1 = (f32[128,128]{1,0:T(8,128)S(1)}, f32[128,128]{1,0:T(8,128)S(1)}) fusion(f32[64,128]{1,0:T(8,128)S(1)} %copy.152, f32[64,128]{1,0:T(8,128)S(1)} %copy.151, f32[64,128]{1,0:T(8,128)S(1)} %copy.150, f32[64,128]{1,0:T(8,128)S(1)} %copy.149, bf16[64,2,128,128]{3,2,1,0:T(8,128)(2,1)} %bitcast.198), kind=kLoop, calls=%fused_computation.28 | loop fusion | flops 16744448 | bytes 4456448 | tf_op jit(solution)/shard_map/reduce_sum | solution.py:34
  338.6 4.1 add_reduce_fusion
  343.6 38.9 %psum.38 = f32[]{:T(128)} all-reduce(f32[]{:T(128)} %get-tuple-element.36), channel_id=1, replica_groups=mesh['chan'=2,'srow'=4,'scol'=4] {'chan','srow','scol'}, use_global_device_ids=true, to_apply=%region_36.37 | all-reduce | flops 1 | bytes 8 | tf_op jit(solution)/shard_map/psum | solution.py:67
  384.7 33.9 %all-reduce.15.cloned.1.call-done = f32[64,2,128]{0,1,2:T(2,128)} async-done(((f32[64,2,128]{0,1,2:T(2,128)}), f32[64,2,128]{0,1,2:T(2,128)}) %all-reduce.15.cloned.1.call-update) | async-done | bytes 65552
  418.6 0.8 fusion.21
  420.1 8.3 %psum.39 = f32[64,1,2,32]{0,2,3,1:T(2,128)S(1)} all-reduce(f32[64,1,2,32]{0,2,3,1:T(2,128)S(1)} %get-tuple-element.34), channel_id=1, replica_groups=mesh['chan'=2,'srow'=4,'scol'=4] {'chan'}, use_global_device_ids=true, to_apply=%region_37.38 | all-reduce | flops 4096 | bytes 32768 | tf_op jit(solution)/shard_map/psum | solution.py:97
  (100 shorter events, 15.8 us)
Async XLA Ops:
  7.2 28.6 %copy-start.4 = (bf16[1,2,128,128]{3,2,1,0:T(8,128)(2,1)S(1)}, bf16[1,2,128,128]{3,2,1,0:T(8,128)(2,1)}, u32[]{:S(2)}) copy-start(bf16[1,2,128,128]{3,2,1,0:T(8,128)(2,1)} %param.8) | copy-start | bytes 196612
  7.2 80.0 %reduce-scatter.5.cloned.1.call-start = ((), (), s32[]{:S(2)}) async-start(), calls=%async_computation.4 | async-start | bytes 81920 | tf_op jit(solution)/shard_map/reduce_scatter | solution.py:92
  29.5 6.9 %copy-start = (bf16[1,64,2,128,128]{4,3,2,1,0:T(8,128)(2,1)S(1)}, bf16[1,64,2,128,128]{4,3,2,1,0:T(8,128)(2,1)}, u32[]{:S(2)}) copy-start(bf16[1,64,2,128,128]{4,3,2,1,0:T(8,128)(2,1)} %param.9) | copy-start | bytes 12582916
  29.5 13.3 %copy-start.10 = (u32[32]{0:T(128)S(1)}, u32[32]{0:T(128)}, u32[]{:S(2)}) copy-start(u32[32]{0:T(128)} %constant.53) | copy-start | bytes 388
  29.5 56.8 %copy-start.8 = (f32[8]{0:T(128)S(1)}, f32[8]{0:T(128)}, u32[]{:S(2)}) copy-start(f32[8]{0:T(128)} %param.14) | copy-start | bytes 100
  29.5 56.8 %copy-start.9 = (s32[64]{0:T(128)S(1)}, s32[64]{0:T(128)}, u32[]{:S(2)}) copy-start(s32[64]{0:T(128)} %param.15) | copy-start | bytes 772
  29.6 67.4 %copy-start.5 = (f32[1,64,2,32]{1,3,2,0:T(8,128)S(1)}, f32[1,64,2,32]{1,3,2,0:T(8,128)}, u32[]{:S(2)}) copy-start(f32[1,64,2,32]{1,3,2,0:T(8,128)} %param.11) | copy-start | bytes 49156
  29.6 67.4 %copy-start.6 = (f32[1,64,2,32]{1,3,2,0:T(8,128)S(1)}, f32[1,64,2,32]{1,3,2,0:T(8,128)}, u32[]{:S(2)}) copy-start(f32[1,64,2,32]{1,3,2,0:T(8,128)} %param.13) | copy-start | bytes 49156
  29.6 67.3 %copy-start.7 = (f32[64,1,2,32]{0,3,2,1:T(8,128)S(1)}, f32[64,1,2,32]{0,3,2,1:T(8,128)}, u32[]{:S(2)}) copy-start(f32[64,1,2,32]{0,3,2,1:T(8,128)} %param.12) | copy-start | bytes 49156
  41.3 55.6 %all-reduce.9.cloned.1.call-start = ((), (), s32[]{:S(2)}) async-start(), calls=%async_computation.8 | async-start | bytes 262144
  42.1 127.4 %reduce-scatter.7.cloned.1.call-start = ((), (), s32[]{:S(2)}) async-start(), calls=%async_computation.5 | async-start | bytes 81920 | tf_op jit(solution)/shard_map/reduce_scatter | solution.py:92
  117.3 6.8 %copy-start.1 = (bf16[1,64,2,128,128]{4,3,2,1,0:T(8,128)(2,1)S(1)}, bf16[1,64,2,128,128]{4,3,2,1,0:T(8,128)(2,1)}, u32[]{:S(2)}) copy-start(bf16[1,64,2,128,128]{4,3,2,1,0:T(8,128)(2,1)} %param.9) | copy-start | bytes 12582916
  129.0 75.2 %all-reduce.11.cloned.1.call-start = ((), (), s32[]{:S(2)}) async-start(), calls=%async_computation.9 | async-start | bytes 262144
  169.5 107.4 %reduce-scatter.9.cloned.1.call-start = ((), (), s32[]{:S(2)}) async-start(), calls=%async_computation.6 | async-start | bytes 81920 | tf_op jit(solution)/shard_map/reduce_scatter | solution.py:92
  224.6 6.8 %copy-start.2 = (bf16[1,64,2,128,128]{4,3,2,1,0:T(8,128)(2,1)S(1)}, bf16[1,64,2,128,128]{4,3,2,1,0:T(8,128)(2,1)}, u32[]{:S(2)}) copy-start(bf16[1,64,2,128,128]{4,3,2,1,0:T(8,128)(2,1)} %param.9) | copy-start | bytes 12582916
  236.4 75.1 %all-reduce.13.cloned.1.call-start = ((), (), s32[]{:S(2)}) async-start(), calls=%async_computation.10 | async-start | bytes 262144
  276.8 107.2 %reduce-scatter.11.cloned.1.call-start = ((), (), s32[]{:S(2)}) async-start(), calls=%async_computation.7 | async-start | bytes 81920 | tf_op jit(solution)/shard_map/reduce_scatter | solution.py:92
  331.8 6.8 %copy-start.3 = (bf16[1,64,2,128,128]{4,3,2,1,0:T(8,128)(2,1)S(1)}, bf16[1,64,2,128,128]{4,3,2,1,0:T(8,128)(2,1)}, u32[]{:S(2)}) copy-start(bf16[1,64,2,128,128]{4,3,2,1,0:T(8,128)(2,1)} %param.9) | copy-start | bytes 12582916
  343.5 75.1 %all-reduce.15.cloned.1.call-start = ((), (), s32[]{:S(2)}) async-start(), calls=%async_computation.11 | async-start | bytes 262144
Sparse Core Ops, SparseCore 0:
  41.4 20.3 reduce-scatter.4
  64.2 32.6 all-reduce.8
  129.1 18.5 reduce-scatter.6
  169.6 34.5 all-reduce.10
  236.5 18.5 reduce-scatter.8
  276.9 34.5 all-reduce.12
  343.6 18.5 reduce-scatter.10
  384.1 34.5 all-reduce.14
where the time goes:
time: 438 us; the launch traced here: 437 us
  blocking collectives  244 us (56%)
  waiting for transfers between devices  111 us (25%)
  other arithmetic  51.5 us (12%)
  between operations  19.1 us (4%)
  local copies, waits for them, and re-layouts  10.6 us (2%)
    psum x4, blocking collectives, sweep_terms(): total = lax.psum(power, ('chan', 'srow', 'scol'))  158 us
    unnamed x12, waiting for transfers between devices  111 us
    all_gather x4, blocking collectives, shards(): g_row = lax.all_gather(g, 'scol', axis=2, tiled=True)  55.9 us
    reduce_sum x4, other arithmetic, local_terms(): pred_real = jnp.sum(r_real * z_real - r_imag * z_imag, axis=0)  24.7 us
    all_gather x4, blocking collectives, sweep_terms(): g_col = lax.all_gather(own_gains, 'srow', axis=2, tiled=True)  22 us
    reduce_sum x4, other arithmetic, local_terms(): cross_real = jnp.sum(z_real * w_real[None] + z_imag * w_imag[None], axis=-1)  16.5 us
  transfers between devices with their start and end apart: 8, of which 4 were waited for; matrix products, arithmetic and copies ran while one was open for 2% of the time, Pallas kernels for 0%

commit v1 on v0

v1 whole, which is shorter than its diff:
```python
import functools
import math

import jax
import jax.numpy as jnp
from jax import lax
from jax.experimental import pallas as pl
from jax.experimental.pallas import tpu as pltpu
from jax.sharding import PartitionSpec as P

STATIONS = 512
TILE = 16
ITERS = 4

EPS = 1e-05
STEP = 0.5

VMEM_LIMIT = 40 << 20


def basis_table(groups, order):
    xval = (jnp.arange(groups, dtype=jnp.float32) + 0.5) / groups
    columns = [
        math.comb(order - 1, b) * xval**b * (1.0 - xval) ** (order - 1 - b) for b in range(order)
    ]
    return jnp.stack(columns, axis=1)


def gram_solve(table, rhs):
    gram = jnp.dot(table.T, table, precision=lax.Precision.HIGHEST)
    factor = jnp.linalg.cholesky(gram)
    order = rhs.shape[1]
    flat = jnp.moveaxis(rhs, 1, 0).reshape(order, -1)
    sol = jax.scipy.linalg.cho_solve((factor, True), flat)
    return jnp.moveaxis(sol.reshape((order, rhs.shape[0]) + rhs.shape[2:]), 0, 1)


def lane_block(shape, span):
    return lax.broadcasted_iota(jnp.int32, shape, 1) // span


def pack_plane(plane, block, span):
    dirs, lanes = plane.shape
    parts = lanes // span
    rows = dirs // parts
    where = lane_block((rows, lanes), span)
    packed = None
    for q in range(parts):
        piece = plane[q * rows : (q + 1) * rows]
        shift = lax.rem((q - block) * span + lanes, lanes)
        piece = pltpu.roll(piece, shift, 1)
        packed = piece if packed is None else jnp.where(where == q, piece, packed)
    return packed


def unpack_planes(pieces, blocks, span):
    rows, lanes = pieces[0].shape
    parts = lanes // span
    where = lane_block((rows, lanes), span)
    out = []
    for q in range(parts):
        plane = None
        for piece, block in zip(pieces, blocks):
            shift = lax.rem((block - q) * span + lanes, lanes)
            moved = pltpu.roll(piece, shift, 1)
            plane = moved if plane is None else jnp.where(where == block, moved, plane)
        out.append(plane)
    return jnp.concatenate(out, axis=0)


def solve(a, cr, ci, gr, gi, tr, ti, rho_eff):
    denom = a + rho_eff
    fresh_r = (cr + a * gr + rho_eff * tr) / denom
    fresh_i = (ci + a * gi + rho_eff * ti) / denom
    return gr + STEP * (fresh_r - gr), gi + STEP * (fresh_i - gi)


def prepare_kernel(model_ref, vis_ref, weight_ref, mt_ref, vt_ref):
    weight = weight_ref[...]
    for k in range(model_ref.shape[0]):
        for p in range(2):
            block = model_ref[k, p].astype(jnp.float32)
            mt_ref[k, p] = (block.T * weight).astype(jnp.bfloat16)

    @pl.when(pl.program_id(0) == 0)
    def _():
        for p in range(2):
            vt_ref[p] = vis_ref[p].astype(jnp.float32).T * weight


def prepare(model, vis, weight_t):
    dirs, _, rows, cols = model.shape
    step = 8
    return pl.pallas_call(
        prepare_kernel,
        grid=(dirs // step,),
        in_specs=[
            pl.BlockSpec((step, 2, rows, cols), lambda n: (n, 0, 0, 0)),
            pl.BlockSpec((2, rows, cols), lambda n: (0, 0, 0)),
            pl.BlockSpec((cols, rows), lambda n: (0, 0)),
        ],
        out_specs=[
            pl.BlockSpec((step, 2, cols, rows), lambda n: (n, 0, 0, 0)),
            pl.BlockSpec((2, cols, rows), lambda n: (0, 0, 0)),
        ],
        out_shape=[
            jax.ShapeDtypeStruct((dirs, 2, cols, rows), jnp.bfloat16),
            jax.ShapeDtypeStruct((2, cols, rows), jnp.float32),
        ],
        name="prepare",
    )(model, vis, weight_t)


def local_terms(mt_ref, vt_ref, grow_ref, gcol_ref, out_ref, z_ref, r_ref, ct_ref):
    dirs, _, cols, rows = mt_ref.shape
    ct_ref[...] = gcol_ref[...].T
    chunk = 16

    def predict(n, carry):
        c0 = pl.multiple_of(n * chunk, chunk)
        here = pl.ds(c0, chunk)
        ctile = ct_ref[here, :]
        acc_r = vt_ref[0, here, :]
        acc_i = vt_ref[1, here, :]
        for k in range(dirs):
            mr = mt_ref[k, 0, here, :].astype(jnp.float32)
            mi = mt_ref[k, 1, here, :].astype(jnp.float32)
            cr = jnp.broadcast_to(ctile[:, k : k + 1], (chunk, rows))
            ci = jnp.broadcast_to(ctile[:, dirs + k : dirs + k + 1], (chunk, rows))
            zr = mr * cr + mi * ci
            zi = mi * cr - mr * ci
            z_ref[k, 0, here, :] = zr
            z_ref[k, 1, here, :] = zi
            gr = grow_ref[k : k + 1, :]
            gi = grow_ref[dirs + k : dirs + k + 1, :]
            acc_r = acc_r - (gr * zr - gi * zi)
            acc_i = acc_i - (gr * zi + gi * zr)
        r_ref[0, here, :] = acc_r
        r_ref[1, here, :] = acc_i
        sq = acc_r * acc_r + acc_i * acc_i
        return carry + sq[:8] + sq[8:]

    power = lax.fori_loop(0, cols // chunk, predict, jnp.zeros((8, rows), jnp.float32))
    out_ref[3 * dirs : 3 * dirs + 8, :] = power

    group = 8

    def terms(n, carry):
        k0 = pl.multiple_of(n * group, group)
        for half in range(2):
            sums = [[None] * 3 for _ in range(group // 2)]
            for c in range(0, cols, 8):
                rr = r_ref[0, c : c + 8, :]
                ri = r_ref[1, c : c + 8, :]
                for kk in range(group // 2):
                    k = k0 + half * (group // 2) + kk
                    zr = z_ref[k, 0, c : c + 8, :]
                    zi = z_ref[k, 1, c : c + 8, :]
                    new = (zr * zr + zi * zi, zr * rr + zi * ri, zr * ri - zi * rr)
                    for s in range(3):
                        old = sums[kk][s]
                        sums[kk][s] = new[s] if old is None else old + new[s]
            for s in range(3):
                block = jnp.concatenate(
                    [jnp.sum(sums[kk][s], axis=0, keepdims=True) for kk in range(group // 2)], axis=0
                )
                out_ref[pl.ds(s * dirs + k0 + half * (group // 2), group // 2), :] = block
        return carry

    lax.fori_loop(0, dirs // group, terms, 0)


def first_kernel(ids_ref, *refs, ns, nz, span):
    rows_in = refs[:nz]
    cols_in = refs[nz : nz + ns]
    mt_ref, vt_ref = refs[nz + ns : nz + ns + 2]
    out_ref, grow_ref, gcol_ref, trow_ref, tcol_ref = refs[nz + ns + 2 : nz + ns + 7]
    scratch = refs[nz + ns + 7 :]
    dirs = mt_ref.shape[0]
    i, j = ids_ref[0], ids_ref[1]
    depth = dirs * span // mt_ref.shape[3]
    for pieces, g_ref, t_ref, me in ((rows_in, grow_ref, trow_ref, j), (cols_in, gcol_ref, tcol_ref, i)):
        blocks = [jnp.bitwise_xor(me, n) for n in range(len(pieces))]
        for q in range(4):
            plane = unpack_planes([p[q * depth : (q + 1) * depth, :] for p in pieces], blocks, span)
            dst = g_ref if q < 2 else t_ref
            at = (q % 2) * dirs
            dst[at : at + dirs, :] = plane
    local_terms(mt_ref, vt_ref, grow_ref, gcol_ref, out_ref, *scratch)


def sweep_kernel(ids_ref, *refs, ns, span, scale):
    pieces = refs[:ns]
    sum_ref, growin_ref, gcolin_ref, trow_ref, tcol_ref, rho_ref, mt_ref, vt_ref = refs[ns : ns + 8]
    out_ref, grow_ref, gcol_ref = refs[ns + 8 : ns + 11]
    scratch = refs[ns + 11 :]
    dirs = mt_ref.shape[0]
    i = ids_ref[0]
    depth = dirs * span // mt_ref.shape[3]
    power = pieces[0][3 * depth :, :]
    for p in pieces[1:]:
        power = power + p[3 * depth :, :]
    rho_eff = rho_ref[...] * (jnp.sum(power) * scale + EPS)
    re, im = slice(0, dirs), slice(dirs, 2 * dirs)
    grow_ref[re, :], grow_ref[im, :] = solve(
        sum_ref[0:dirs, :],
        sum_ref[dirs : 2 * dirs, :],
        sum_ref[2 * dirs : 3 * dirs, :],
        growin_ref[re, :],
        growin_ref[im, :],
        trow_ref[re, :],
        trow_ref[im, :],
        rho_eff,
    )
    blocks = [jnp.bitwise_xor(i, n) for n in range(ns)]
    a, cr, ci = [
        unpack_planes([p[q * depth : (q + 1) * depth, :] for p in pieces], blocks, span)
        for q in range(3)
    ]
    gcol_ref[re, :], gcol_ref[im, :] = solve(
        a, cr, ci, gcolin_ref[re, :], gcolin_ref[im, :], tcol_ref[re, :], tcol_ref[im, :], rho_eff
    )
    local_terms(mt_ref, vt_ref, grow_ref, gcol_ref, out_ref, *scratch)


def combine_kernel(ids_ref, *refs, nz, extra, span):
    parts = refs[:nz]
    powers = refs[nz : nz + extra]
    sum_ref, own_ref = refs[nz + extra :]
    dirs = sum_ref.shape[0] // 3
    j = ids_ref[1]
    depth = dirs * span // sum_ref.shape[1]
    for q in range(3):
        at = slice(q * dirs, (q + 1) * dirs)
        total = parts[0][at, :]
        for p in parts[1:]:
            total = total + p[at, :]
        sum_ref[at, :] = total
        own_ref[q * depth : (q + 1) * depth, :] = pack_plane(total, j, span)
    power = parts[0][3 * dirs :, :]
    for p in parts[1:]:
        power = power + p[3 * dirs :, :]
    for p in powers:
        power = power + p[...]
    own_ref[3 * depth :, :] = power


def final_kernel(*refs, ns, scale):
    pieces = refs[:ns]
    g_ref, t_ref, rho_ref, out_ref = refs[ns:]
    depth = rho_ref.shape[0]
    power = pieces[0][3 * depth :, :]
    for p in pieces[1:]:
        power = power + p[3 * depth :, :]
    rho_eff = rho_ref[...] * (jnp.sum(power) * scale + EPS)
    own = pieces[0]
    out_ref[0:depth, :], out_ref[depth : 2 * depth, :] = solve(
        own[0:depth, :],
        own[depth : 2 * depth, :],
        own[2 * depth : 3 * depth, :],
        g_ref[0:depth, :],
        g_ref[depth : 2 * depth, :],
        t_ref[0:depth, :],
        t_ref[depth : 2 * depth, :],
        rho_eff,
    )


SMEM = pl.BlockSpec(memory_space=pltpu.SMEM)
VMEM = pl.BlockSpec(memory_space=pltpu.VMEM)


def f32(*shape):
    return jax.ShapeDtypeStruct(shape, jnp.float32)


def call(kernel, name, ids, args, outs, scratch=()):
    lead = [] if ids is None else [ids]
    return pl.pallas_call(
        kernel,
        in_specs=[SMEM] * len(lead) + [VMEM] * len(args),
        out_specs=[VMEM] * len(outs),
        out_shape=outs,
        scratch_shapes=scratch,
        compiler_params=pltpu.CompilerParams(vmem_limit_bytes=VMEM_LIMIT),
        name=name,
    )(*lead, *args)


def swap(x, axis, n):
    size = lax.axis_size(axis)
    return lax.ppermute(x, axis, [(m, m ^ n) for m in range(size)])


def to_packed(x, lanes):
    dirs, _, span = x.shape
    parts = lanes // span
    x = x.reshape(parts, dirs // parts, 2, span)
    return x.transpose(2, 1, 0, 3).reshape(2 * dirs // parts, lanes)


def from_packed(x, span):
    rows, lanes = x.shape
    parts = lanes // span
    x = x.reshape(2, rows // 2, parts, span)
    return x.transpose(2, 1, 0, 3).reshape(parts * rows // 2, 2, span)


def shards(vis, model, flags, gains, consensus, dual, rho, cluster):
    groups = lax.axis_size("chan")
    ns = lax.axis_size("srow")
    nz = lax.axis_size("scol")
    order = consensus.shape[1]
    dirs = gains.shape[1]
    span = gains.shape[3]
    rows, cols = vis.shape[2:]
    i, j, f = lax.axis_index("srow"), lax.axis_index("scol"), lax.axis_index("chan")
    ids = jnp.stack([i, j]).astype(jnp.int32)

    table = basis_table(groups, order)
    brow = lax.dynamic_index_in_dim(table, f, 0, keepdims=False)
    dual_own = dual[0]
    target = jnp.einsum("b,kbcp->kcp", brow, consensus, precision=lax.Precision.HIGHEST) - dual_own
    start = jnp.concatenate([to_packed(gains[0], rows), to_packed(target, rows)], axis=0)

    row_parts = [start] + [swap(start, "scol", n) for n in range(1, nz)]
    col_parts = [start] + [swap(start, "srow", n) for n in range(1, ns)]

    matches = cluster[:, None] == jnp.arange(rho.shape[0], dtype=jnp.int32)[None, :]
    rho_dir = jnp.sum(jnp.where(matches, rho[None, :], 0.0), axis=1)
    rho_rows = jnp.broadcast_to(rho_dir[:, None], (dirs, rows))
    parts = rows // span
    rho_packed = jnp.repeat(rho_dir.reshape(parts, dirs // parts).T, span, axis=1)
    fl = flags[0].astype(jnp.float32).T
    weight_t = jnp.repeat(jnp.repeat(fl, TILE, axis=0), TILE, axis=1)
    mt, vt = prepare(model[0], vis[0], weight_t)

    scratch = [
        pltpu.VMEM((dirs, 2, cols, rows), jnp.float32),
        pltpu.VMEM((2, cols, rows), jnp.float32),
        pltpu.VMEM((cols, 2 * dirs), jnp.float32),
    ]
    scale = 1.0 / (groups * STATIONS * STATIONS)
    depth = dirs * span // rows
    plane = f32(2 * dirs, rows)
    partial, grow, gcol, trow, tcol = call(
        functools.partial(first_kernel, ns=ns, nz=nz, span=span),
        "first",
        ids,
        row_parts + col_parts + [mt, vt],
        [f32(3 * dirs + 8, rows), plane, plane, plane, plane],
        scratch,
    )
    g_packed, t_packed = start[: 2 * depth], start[2 * depth :]
    for step in range(ITERS):
        swaps = [partial] + [swap(partial, "scol", n) for n in range(1, nz)]
        power = partial[3 * dirs :]
        if groups == 2:
            both = ("chan", "scol")
            powers = [swap(power, both, nz + n) for n in range(nz)]
        else:
            powers = [lax.psum(power, ("chan", "scol")) - sum(s[3 * dirs :] for s in swaps)]
        sums, own = call(
            functools.partial(combine_kernel, nz=nz, extra=len(powers), span=span),
            "combine",
            ids,
            swaps + powers,
            [f32(3 * dirs, rows), f32(3 * depth + 8, rows)],
        )
        pieces = [own] + [swap(own, "srow", n) for n in range(1, ns)]
        if step < ITERS - 1:
            partial, grow_new, gcol_new = call(
                functools.partial(sweep_kernel, ns=ns, span=span, scale=scale),
                "sweep",
                ids,
                pieces + [sums, grow, gcol, trow, tcol, rho_rows, mt, vt],
                [f32(3 * dirs + 8, rows), plane, plane],
                scratch,
            )
            grow, gcol = grow_new, gcol_new
        own_g = call(
            functools.partial(final_kernel, ns=ns, scale=scale),
            "own",
            None,
            pieces + [g_packed, t_packed, rho_packed],
            [f32(2 * depth, rows)],
        )[0]
        g_packed = own_g
    g = from_packed(g_packed, span)
    local = brow[None, :, None, None] * (g + dual_own)[:, None, :, :]
    if groups == 2:
        sums = local + swap(local, "chan", 1)
    else:
        sums = lax.psum(local, "chan")
    coeffs = gram_solve(table, sums)
    dual_new = (
        dual_own + g - jnp.einsum("b,kbcp->kcp", brow, coeffs, precision=lax.Precision.HIGHEST)
    )
    return (g[None], coeffs, dual_new[None])


def solution(mesh):
    placed = (
        P("chan", None, "srow", "scol"),
        P("chan", None, None, "srow", "scol"),
        P("chan", "srow", "scol"),
        P("chan", None, None, ("srow", "scol")),
        P(None, None, None, ("srow", "scol")),
        P("chan", None, None, ("srow", "scol")),
        P(),
        P(),
    )
    return jax.shard_map(
        shards,
        mesh=mesh,
        in_specs=placed,
        out_specs=(
            P("chan", None, None, ("srow", "scol")),
            P(None, None, None, ("srow", "scol")),
            P("chan", None, None, ("srow", "scol")),
        ),
        check_vma=False,
    )
```

time: 438 us -> 147 us (0.34)
  blocking collectives: 244 us -> 0 us
  waiting for transfers between devices: 111 us -> 36.3 us
  starting transfers between devices: 0.33 us -> 58.4 us
  other arithmetic: 51.5 us -> 1.5 us
  Pallas kernels: 0 us -> 38.7 us
  between operations: 19.1 us -> 2.29 us
    psum x5 -> x0, blocking collectives: 166 us -> none  [the longest x4 158 us: sweep_terms(): total = lax.psum(power, ('chan', 'srow', 'scol'))]
    unnamed x12 -> x0, waiting for transfers between devices: 111 us -> none
    all_gather x8 -> x0, blocking collectives: 77.9 us -> none  [the longest x4 55.9 us: shards(): g_row = lax.all_gather(g, 'scol', axis=2, tiled=True)]
    ppermute x0 -> x47, starting transfers between devices: none -> 58.4 us  [swap(): return lax.ppermute(x, axis, [(m, m ^ n) for m in range(size)])]
    reduce_sum x12 -> x0, other arithmetic: 43.7 us -> none  [the longest x4 24.7 us: local_terms(): pred_real = jnp.sum(r_real * z_real - r_imag * z_imag, axis=0)]
    pallas_call x0 -> x13, Pallas kernels: none -> 38.7 us  [the longest x12 31.3 us: call(): pl.pallas_call(kernel, in_specs=[SMEM] * len(lead) + [VMEM] * len(args),...]
    ppermute x0 -> x47, waiting for transfers between devices: none -> 36.3 us  [swap(): return lax.ppermute(x, axis, [(m, m ^ n) for m in range(size)])]
    add x7 -> x1, other arithmetic: 5.4 us -> 0.01 us  [shards(): local = brow[None, :, None, None] * (g + dual_own)[:, None, :, :]]
  transfers between devices with their start and end apart: 8 -> 47, of which waited for: 4 -> 24; matrix products, arithmetic and copies ran while one was open for 2% -> 2% of each run, Pallas kernels for 0% -> 5%
where the time goes in v1:
time: 147 us
  starting transfers between devices  58.4 us (40%)
  Pallas kernels  38.7 us (26%)
  waiting for transfers between devices  36.3 us (25%)
  local copies, waits for them, and re-layouts  9.33 us (6%)
  between operations  2.29 us (2%)
  other arithmetic  1.5 us (1%)
    ppermute x47, starting transfers between devices, swap(): return lax.ppermute(x, axis, [(m, m ^ n) for m in range(size)])  58.4 us
    ppermute x47, waiting for transfers between devices, swap(): return lax.ppermute(x, axis, [(m, m ^ n) for m in range(size)])  36.3 us
    pallas_call x12, Pallas kernels, call(): pl.pallas_call(kernel, in_specs=[SMEM] * len(lead) + [VMEM] * len(args),...  31.3 us
    unnamed x17, local copies, waits for them, and re-layouts  7.69 us
    pallas_call x1, Pallas kernels, prepare(): pl.pallas_call(prepare_kernel, grid=(dirs // step,), in_specs=[pl.BlockSp...  7.46 us
  transfers between devices with their start and end apart: 47, of which 24 were waited for; matrix products, arithmetic and copies ran while one was open for 2% of the time, Pallas kernels for 5%

profile of v1, /device:TPU:0, one launch (start us, length us, event | category | flops | bytes accessed | tf_op | source)
XLA Modules:
  0.0 146.6 jit_solution(12996391598181808620)
XLA Ops:
  3.5 3.1 %collective-permute-start = (f32[64,128]{1,0:T(8,128)S(1)}, f32[64,128]{1,0:T(8,128)S(1)}, u32[]{:S(2)}, u32[]{:S(2)}) collective-permute-start(f32[64,128]{1,0:T(8,128)S(1)} %constant_dynamic-update-slice_fusion.refs_0_.refs_4_), channel_id=1, source_target_pairs={{0,1},{1,0},{2,3},{3,2},{4,5},{5,4},{6,7},{7,6},{8,9},{9,8},{10,11... | collective-permute-start | bytes 98312 | tf_op jit(solution)/shard_map/ppermute | solution.py:292
  6.6 2.6 %collective-permute-start.1 = (f32[64,128]{1,0:T(8,128)S(1)}, f32[64,128]{1,0:T(8,128)S(1)}, u32[]{:S(2)}, u32[]{:S(2)}) collective-permute-start(f32[64,128]{1,0:T(8,128)S(1)} %constant_dynamic-update-slice_fusion.refs_0_.refs_4_), channel_id=1, source_target_pairs={{0,2},{1,3},{2,0},{3,1},{4,6},{5,7},{6,4},{7,5},{8,10},{9,11},{10,... | collective-permute-start | bytes 98312 | tf_op jit(solution)/shard_map/ppermute | solution.py:292
  9.1 1.7 %collective-permute-start.4 = (f32[64,128]{1,0:T(8,128)S(1)}, f32[64,128]{1,0:T(8,128)S(1)}, u32[]{:S(2)}, u32[]{:S(2)}) collective-permute-start(f32[64,128]{1,0:T(8,128)S(1)} %constant_dynamic-update-slice_fusion.refs_0_.refs_4_), channel_id=1, source_target_pairs={{0,8},{4,12},{8,0},{12,4},{1,9},{5,13},{9,1},{13,5},{2,10},{6,14},... | collective-permute-start | bytes 98312 | tf_op jit(solution)/shard_map/ppermute | solution.py:292
  12.7 7.5 %prepare.1 = (bf16[64,2,128,128]{3,2,1,0:T(8,128)(2,1)}, f32[2,128,128]{2,1,0:T(8,128)}) custom-call(bf16[64,2,128,128]{3,2,1,0:T(8,128)(2,1)} %bitcast.41, bf16[2,128,128]{2,1,0:T(8,128)(2,1)} %bitcast.47, f32[128,128]{1,0:T(8,128)} %copy.35.weight_ref), custom_call_target="tpu_custom_call" | custom-call | tf_op jit(solution)/shard_map/prepare/pallas_call | solution.py:94
  20.2 2.2 %copy-done = bf16[64,2,128,128]{3,2,1,0:T(8,128)(2,1)S(1)} copy-done((bf16[64,2,128,128]{3,2,1,0:T(8,128)(2,1)S(1)}, bf16[64,2,128,128]{3,2,1,0:T(8,128)(2,1)}, u32[]{:S(2)}) %copy-start) | copy-done | bytes 4194328
  23.3 6.9 %first.1 = (f32[200,128]{1,0:T(8,128)S(1)}, f32[128,128]{1,0:T(8,128)S(1)}, f32[128,128]{1,0:T(8,128)S(1)}, f32[128,128]{1,0:T(8,128)S(1)}, f32[128,128]{1,0:T(8,128)S(1)}) custom-call(s32[2]{0:T(128)S(1)} %pad_add_fusion.ids_ref, f32[64,128]{1,0:T(8,128)S(1)} %constant_dynamic-update-slice_fusion.refs_0_.refs_4_, ...), custom_call_target="tpu_custom_call" | custom-call | tf_op jit(solution)/shard_map/first/pallas_call | solution.py:279
  31.1 3.5 %collective-permute-start.7 = (f32[200,128]{1,0:T(8,128)S(1)}, f32[200,128]{1,0:T(8,128)S(1)}, u32[]{:S(2)}, u32[]{:S(2)}) collective-permute-start(f32[200,128]{1,0:T(8,128)S(1)} %get-tuple-element.26.refs_0_), channel_id=1, source_target_pairs={{0,2},{1,3},{2,0},{3,1},{4,6},{5,7},{6,4},{7,5},{8,10},{9,11},{10,... | collective-permute-start | bytes 307208 | tf_op jit(solution)/shard_map/ppermute | solution.py:292
  34.6 1.5 %collective-permute-start.10 = (f32[8,128]{1,0:T(8,128)S(1)}, f32[8,128]{1,0:T(8,128)S(1)}, u32[]{:S(2)}, u32[]{:S(2)}) collective-permute-start(f32[8,128]{1,0:T(8,128)S(1)} %slice.18), channel_id=1, source_target_pairs={{0,17},{1,16},{2,19},{3,18},{16,1},{17,0},{18,3},{19,2},{4,21},{5,... | collective-permute-start | bytes 12296 | tf_op jit(solution)/shard_map/ppermute | solution.py:292
  36.1 3.8 %collective-permute-start.11 = (f32[8,128]{1,0:T(8,128)S(1)}, f32[8,128]{1,0:T(8,128)S(1)}, u32[]{:S(2)}, u32[]{:S(2)}) collective-permute-start(f32[8,128]{1,0:T(8,128)S(1)} %slice.18), channel_id=1, source_target_pairs={{0,18},{1,19},{2,16},{3,17},{16,2},{17,3},{18,0},{19,1},{4,22},{5,... | collective-permute-start | bytes 12296 | tf_op jit(solution)/shard_map/ppermute | solution.py:292
  39.9 4.4 %collective-permute-start.12 = (f32[8,128]{1,0:T(8,128)S(1)}, f32[8,128]{1,0:T(8,128)S(1)}, u32[]{:S(2)}, u32[]{:S(2)}) collective-permute-start(f32[8,128]{1,0:T(8,128)S(1)} %slice.18), channel_id=1, source_target_pairs={{0,19},{1,18},{2,17},{3,16},{16,3},{17,2},{18,1},{19,0},{4,23},{5,... | collective-permute-start | bytes 12296 | tf_op jit(solution)/shard_map/ppermute | solution.py:292
  46.2 2.8 %collective-permute-done.9.refs_4_ = f32[8,128]{1,0:T(8,128)S(1)} collective-permute-done((f32[8,128]{1,0:T(8,128)S(1)}, f32[8,128]{1,0:T(8,128)S(1)}, u32[]{:S(2)}, u32[]{:S(2)}) %collective-permute-start.9) | collective-permute-done | bytes 4128 | tf_op jit(solution)/shard_map/ppermute | solution.py:292
  49.8 1.6 %collective-permute-start.14 = (f32[56,128]{1,0:T(8,128)S(1)}, f32[56,128]{1,0:T(8,128)S(1)}, u32[]{:S(2)}, u32[]{:S(2)}) collective-permute-start(f32[56,128]{1,0:T(8,128)S(1)} %get-tuple-element.27.refs_0_), channel_id=1, source_target_pairs={{0,8},{4,12},{8,0},{12,4},{1,9},{5,13},{9,1},{13,5},{2,10},{6,14},... | collective-permute-start | bytes 86024 | tf_op jit(solution)/shard_map/ppermute | solution.py:292
  51.7 2.0 %collective-permute-done.14.refs_2_ = f32[56,128]{1,0:T(8,128)S(1)} collective-permute-done((f32[56,128]{1,0:T(8,128)S(1)}, f32[56,128]{1,0:T(8,128)S(1)}, u32[]{:S(2)}, u32[]{:S(2)}) %collective-permute-start.14) | collective-permute-done | bytes 28704 | tf_op jit(solution)/shard_map/ppermute | solution.py:292
  54.7 6.8 %sweep.3 = (f32[200,128]{1,0:T(8,128)S(1)}, f32[128,128]{1,0:T(8,128)S(1)}, f32[128,128]{1,0:T(8,128)S(1)}) custom-call(s32[2]{0:T(128)S(1)} %pad_add_fusion.ids_ref, f32[56,128]{1,0:T(8,128)S(1)} %get-tuple-element.27.refs_0_, f32[56,128]{1,0:T(8,128)S(1)} %collective-permute-done.13.refs_1_, f32[56,128]{1,0:T(8,128)S(1)} %collective-permute-done.14.refs_2_, ...), custom_call_target="tpu_custom_call" | custom-call | tf_op jit(solution)/shard_map/sweep/pallas_call | solution.py:279
  61.6 3.0 %collective-permute-start.17 = (f32[200,128]{1,0:T(8,128)S(1)}, f32[200,128]{1,0:T(8,128)S(1)}, u32[]{:S(2)}, u32[]{:S(2)}) collective-permute-start(f32[200,128]{1,0:T(8,128)S(1)} %get-tuple-element.33.refs_0_), channel_id=1, source_target_pairs={{0,2},{1,3},{2,0},{3,1},{4,6},{5,7},{6,4},{7,5},{8,10},{9,11},{10,... | collective-permute-start | bytes 307208 | tf_op jit(solution)/shard_map/ppermute | solution.py:292
  66.7 2.9 %collective-permute-done.19.refs_4_ = f32[8,128]{1,0:T(8,128)S(1)} collective-permute-done((f32[8,128]{1,0:T(8,128)S(1)}, f32[8,128]{1,0:T(8,128)S(1)}, u32[]{:S(2)}, u32[]{:S(2)}) %collective-permute-start.19) | collective-permute-done | bytes 4128 | tf_op jit(solution)/shard_map/ppermute | solution.py:292
  71.4 3.1 %collective-permute-start.22 = (f32[8,128]{1,0:T(8,128)S(1)}, f32[8,128]{1,0:T(8,128)S(1)}, u32[]{:S(2)}, u32[]{:S(2)}) collective-permute-start(f32[8,128]{1,0:T(8,128)S(1)} %slice.19), channel_id=1, source_target_pairs={{0,19},{1,18},{2,17},{3,16},{16,3},{17,2},{18,1},{19,0},{4,23},{5,... | collective-permute-start | bytes 12296 | tf_op jit(solution)/shard_map/ppermute | solution.py:292
  75.0 2.7 %collective-permute-done.22.refs_7_ = f32[8,128]{1,0:T(8,128)S(1)} collective-permute-done((f32[8,128]{1,0:T(8,128)S(1)}, f32[8,128]{1,0:T(8,128)S(1)}, u32[]{:S(2)}, u32[]{:S(2)}) %collective-permute-start.22) | collective-permute-done | bytes 4128 | tf_op jit(solution)/shard_map/ppermute | solution.py:292
  80.3 2.1 %collective-permute-done.24.refs_2_ = f32[56,128]{1,0:T(8,128)S(1)} collective-permute-done((f32[56,128]{1,0:T(8,128)S(1)}, f32[56,128]{1,0:T(8,128)S(1)}, u32[]{:S(2)}, u32[]{:S(2)}) %collective-permute-start.24) | collective-permute-done | bytes 28704 | tf_op jit(solution)/shard_map/ppermute | solution.py:292
  82.7 6.8 %sweep.4 = (f32[200,128]{1,0:T(8,128)S(1)}, f32[128,128]{1,0:T(8,128)S(1)}, f32[128,128]{1,0:T(8,128)S(1)}) custom-call(s32[2]{0:T(128)S(1)} %pad_add_fusion.ids_ref, f32[56,128]{1,0:T(8,128)S(1)} %get-tuple-element.34.refs_0_, f32[56,128]{1,0:T(8,128)S(1)} %collective-permute-done.23.refs_1_, f32[56,128]{1,0:T(8,128)S(1)} %collective-permute-done.24.refs_2_, ...), custom_call_target="tpu_custom_call" | custom-call | tf_op jit(solution)/shard_map/sweep/pallas_call | solution.py:279
  89.6 2.9 %collective-permute-start.27 = (f32[200,128]{1,0:T(8,128)S(1)}, f32[200,128]{1,0:T(8,128)S(1)}, u32[]{:S(2)}, u32[]{:S(2)}) collective-permute-start(f32[200,128]{1,0:T(8,128)S(1)} %get-tuple-element.38.refs_0_), channel_id=1, source_target_pairs={{0,2},{1,3},{2,0},{3,1},{4,6},{5,7},{6,4},{7,5},{8,10},{9,11},{10,... | collective-permute-start | bytes 307208 | tf_op jit(solution)/shard_map/ppermute | solution.py:292
  95.4 2.1 %collective-permute-done.29.refs_4_ = f32[8,128]{1,0:T(8,128)S(1)} collective-permute-done((f32[8,128]{1,0:T(8,128)S(1)}, f32[8,128]{1,0:T(8,128)S(1)}, u32[]{:S(2)}, u32[]{:S(2)}) %collective-permute-start.29) | collective-permute-done | bytes 4128 | tf_op jit(solution)/shard_map/ppermute | solution.py:292
  97.5 1.6 %collective-permute-start.31 = (f32[8,128]{1,0:T(8,128)S(1)}, f32[8,128]{1,0:T(8,128)S(1)}, u32[]{:S(2)}, u32[]{:S(2)}) collective-permute-start(f32[8,128]{1,0:T(8,128)S(1)} %slice.20), channel_id=1, source_target_pairs={{0,18},{1,19},{2,16},{3,17},{16,2},{17,3},{18,0},{19,1},{4,22},{5,... | collective-permute-start | bytes 12296 | tf_op jit(solution)/shard_map/ppermute | solution.py:292
  100.1 2.2 %collective-permute-start.32 = (f32[8,128]{1,0:T(8,128)S(1)}, f32[8,128]{1,0:T(8,128)S(1)}, u32[]{:S(2)}, u32[]{:S(2)}) collective-permute-start(f32[8,128]{1,0:T(8,128)S(1)} %slice.20), channel_id=1, source_target_pairs={{0,19},{1,18},{2,17},{3,16},{16,3},{17,2},{18,1},{19,0},{4,23},{5,... | collective-permute-start | bytes 12296 | tf_op jit(solution)/shard_map/ppermute | solution.py:292
  103.2 3.2 %collective-permute-done.32.refs_7_ = f32[8,128]{1,0:T(8,128)S(1)} collective-permute-done((f32[8,128]{1,0:T(8,128)S(1)}, f32[8,128]{1,0:T(8,128)S(1)}, u32[]{:S(2)}, u32[]{:S(2)}) %collective-permute-start.32) | collective-permute-done | bytes 4128 | tf_op jit(solution)/shard_map/ppermute | solution.py:292
  109.1 2.1 %collective-permute-done.34.refs_2_ = f32[56,128]{1,0:T(8,128)S(1)} collective-permute-done((f32[56,128]{1,0:T(8,128)S(1)}, f32[56,128]{1,0:T(8,128)S(1)}, u32[]{:S(2)}, u32[]{:S(2)}) %collective-permute-start.34) | collective-permute-done | bytes 28704 | tf_op jit(solution)/shard_map/ppermute | solution.py:292
  111.7 7.2 %sweep.5 = (f32[200,128]{1,0:T(8,128)S(1)}, f32[128,128]{1,0:T(8,128)}, f32[128,128]{1,0:T(8,128)}) custom-call(s32[2]{0:T(128)S(1)} %pad_add_fusion.ids_ref, f32[56,128]{1,0:T(8,128)S(1)} %get-tuple-element.39.refs_0_, f32[56,128]{1,0:T(8,128)S(1)} %collective-permute-done.33.refs_1_, f32[56,128]{1,0:T(8,128)S(1)} %collective-permute-done.34.refs_2_, ...), custom_call_target="tpu_custom_call" | custom-call | tf_op jit(solution)/shard_map/sweep/pallas_call | solution.py:279
  118.9 2.7 %collective-permute-start.37 = (f32[200,128]{1,0:T(8,128)S(1)}, f32[200,128]{1,0:T(8,128)S(1)}, u32[]{:S(2)}, u32[]{:S(2)}) collective-permute-start(f32[200,128]{1,0:T(8,128)S(1)} %get-tuple-element.43.refs_0_), channel_id=1, source_target_pairs={{0,2},{1,3},{2,0},{3,1},{4,6},{5,7},{6,4},{7,5},{8,10},{9,11},{10,... | collective-permute-start | bytes 307208 | tf_op jit(solution)/shard_map/ppermute | solution.py:292
  121.6 1.7 %collective-permute-start.38 = (f32[200,128]{1,0:T(8,128)S(1)}, f32[200,128]{1,0:T(8,128)S(1)}, u32[]{:S(2)}, u32[]{:S(2)}) collective-permute-start(f32[200,128]{1,0:T(8,128)S(1)} %get-tuple-element.43.refs_0_), channel_id=1, source_target_pairs={{0,3},{1,2},{2,1},{3,0},{4,7},{5,6},{6,5},{7,4},{8,11},{9,10},{10,... | collective-permute-start | bytes 307208 | tf_op jit(solution)/shard_map/ppermute | solution.py:292
  124.0 2.9 %collective-permute-done.39.refs_4_ = f32[8,128]{1,0:T(8,128)S(1)} collective-permute-done((f32[8,128]{1,0:T(8,128)S(1)}, f32[8,128]{1,0:T(8,128)S(1)}, u32[]{:S(2)}, u32[]{:S(2)}) %collective-permute-start.39) | collective-permute-done | bytes 4128 | tf_op jit(solution)/shard_map/ppermute | solution.py:292
  128.9 2.6 %collective-permute-start.42 = (f32[8,128]{1,0:T(8,128)S(1)}, f32[8,128]{1,0:T(8,128)S(1)}, u32[]{:S(2)}, u32[]{:S(2)}) collective-permute-start(f32[8,128]{1,0:T(8,128)S(1)} %slice.21), channel_id=1, source_target_pairs={{0,19},{1,18},{2,17},{3,16},{16,3},{17,2},{18,1},{19,0},{4,23},{5,... | collective-permute-start | bytes 12296 | tf_op jit(solution)/shard_map/ppermute | solution.py:292
  132.3 2.9 %collective-permute-done.42.refs_7_ = f32[8,128]{1,0:T(8,128)S(1)} collective-permute-done((f32[8,128]{1,0:T(8,128)S(1)}, f32[8,128]{1,0:T(8,128)S(1)}, u32[]{:S(2)}, u32[]{:S(2)}) %collective-permute-start.42) | collective-permute-done | bytes 4128 | tf_op jit(solution)/shard_map/ppermute | solution.py:292
  (119 shorter events, 39.3 us)
Async XLA Ops:
  3.5 8.1 %collective-permute-start = (f32[64,128]{1,0:T(8,128)S(1)}, f32[64,128]{1,0:T(8,128)S(1)}, u32[]{:S(2)}, u32[]{:S(2)}) collective-permute-start(f32[64,128]{1,0:T(8,128)S(1)} %constant_dynamic-update-slice_fusion.refs_0_.refs_4_), channel_id=1, source_target_pairs={{0,1},{1,0},{2,3},{3,2},{4,5},{5,4},{6,7},{7,6},{8,9},{9,8},{10,11... | collective-permute-start | bytes 98312 | tf_op jit(solution)/shard_map/ppermute | solution.py:292
  6.6 13.6 %collective-permute-start.1 = (f32[64,128]{1,0:T(8,128)S(1)}, f32[64,128]{1,0:T(8,128)S(1)}, u32[]{:S(2)}, u32[]{:S(2)}) collective-permute-start(f32[64,128]{1,0:T(8,128)S(1)} %constant_dynamic-update-slice_fusion.refs_0_.refs_4_), channel_id=1, source_target_pairs={{0,2},{1,3},{2,0},{3,1},{4,6},{5,7},{6,4},{7,5},{8,10},{9,11},{10,... | collective-permute-start | bytes 98312 | tf_op jit(solution)/shard_map/ppermute | solution.py:292
  9.1 11.0 %collective-permute-start.2 = (f32[64,128]{1,0:T(8,128)S(1)}, f32[64,128]{1,0:T(8,128)S(1)}, u32[]{:S(2)}, u32[]{:S(2)}) collective-permute-start(f32[64,128]{1,0:T(8,128)S(1)} %constant_dynamic-update-slice_fusion.refs_0_.refs_4_), channel_id=1, source_target_pairs={{0,3},{1,2},{2,1},{3,0},{4,7},{5,6},{6,5},{7,4},{8,11},{9,10},{10,... | collective-permute-start | bytes 98312 | tf_op jit(solution)/shard_map/ppermute | solution.py:292
  9.1 11.0 %collective-permute-start.3 = (f32[64,128]{1,0:T(8,128)S(1)}, f32[64,128]{1,0:T(8,128)S(1)}, u32[]{:S(2)}, u32[]{:S(2)}) collective-permute-start(f32[64,128]{1,0:T(8,128)S(1)} %constant_dynamic-update-slice_fusion.refs_0_.refs_4_), channel_id=1, source_target_pairs={{0,4},{4,0},{8,12},{12,8},{1,5},{5,1},{9,13},{13,9},{2,6},{6,2},{1... | collective-permute-start | bytes 98312 | tf_op jit(solution)/shard_map/ppermute | solution.py:292
  9.1 11.0 %collective-permute-start.4 = (f32[64,128]{1,0:T(8,128)S(1)}, f32[64,128]{1,0:T(8,128)S(1)}, u32[]{:S(2)}, u32[]{:S(2)}) collective-permute-start(f32[64,128]{1,0:T(8,128)S(1)} %constant_dynamic-update-slice_fusion.refs_0_.refs_4_), channel_id=1, source_target_pairs={{0,8},{4,12},{8,0},{12,4},{1,9},{5,13},{9,1},{13,5},{2,10},{6,14},... | collective-permute-start | bytes 98312 | tf_op jit(solution)/shard_map/ppermute | solution.py:292
  11.6 8.6 %collective-permute-start.5 = (f32[64,128]{1,0:T(8,128)S(1)}, f32[64,128]{1,0:T(8,128)S(1)}, u32[]{:S(2)}, u32[]{:S(2)}) collective-permute-start(f32[64,128]{1,0:T(8,128)S(1)} %constant_dynamic-update-slice_fusion.refs_0_.refs_4_), channel_id=1, source_target_pairs={{0,12},{4,8},{8,4},{12,0},{1,13},{5,9},{9,5},{13,1},{2,14},{6,10},... | collective-permute-start | bytes 98312 | tf_op jit(solution)/shard_map/ppermute | solution.py:292
  30.2 18.9 %collective-permute-start.6 = (f32[200,128]{1,0:T(8,128)S(1)}, f32[200,128]{1,0:T(8,128)S(1)}, u32[]{:S(2)}, u32[]{:S(2)}) collective-permute-start(f32[200,128]{1,0:T(8,128)S(1)} %get-tuple-element.26.refs_0_), channel_id=1, source_target_pairs={{0,1},{1,0},{2,3},{3,2},{4,5},{5,4},{6,7},{7,6},{8,9},{9,8},{10,11... | collective-permute-start | bytes 307208 | tf_op jit(solution)/shard_map/ppermute | solution.py:292
  31.1 17.9 %collective-permute-start.7 = (f32[200,128]{1,0:T(8,128)S(1)}, f32[200,128]{1,0:T(8,128)S(1)}, u32[]{:S(2)}, u32[]{:S(2)}) collective-permute-start(f32[200,128]{1,0:T(8,128)S(1)} %get-tuple-element.26.refs_0_), channel_id=1, source_target_pairs={{0,2},{1,3},{2,0},{3,1},{4,6},{5,7},{6,4},{7,5},{8,10},{9,11},{10,... | collective-permute-start | bytes 307208 | tf_op jit(solution)/shard_map/ppermute | solution.py:292
  34.6 14.4 %collective-permute-start.8 = (f32[200,128]{1,0:T(8,128)S(1)}, f32[200,128]{1,0:T(8,128)S(1)}, u32[]{:S(2)}, u32[]{:S(2)}) collective-permute-start(f32[200,128]{1,0:T(8,128)S(1)} %get-tuple-element.26.refs_0_), channel_id=1, source_target_pairs={{0,3},{1,2},{2,1},{3,0},{4,7},{5,6},{6,5},{7,4},{8,11},{9,10},{10,... | collective-permute-start | bytes 307208 | tf_op jit(solution)/shard_map/ppermute | solution.py:292
  34.6 5.3 %collective-permute-start.10 = (f32[8,128]{1,0:T(8,128)S(1)}, f32[8,128]{1,0:T(8,128)S(1)}, u32[]{:S(2)}, u32[]{:S(2)}) collective-permute-start(f32[8,128]{1,0:T(8,128)S(1)} %slice.18), channel_id=1, source_target_pairs={{0,17},{1,16},{2,19},{3,18},{16,1},{17,0},{18,3},{19,2},{4,21},{5,... | collective-permute-start | bytes 12296 | tf_op jit(solution)/shard_map/ppermute | solution.py:292
  36.1 9.3 %collective-permute-start.11 = (f32[8,128]{1,0:T(8,128)S(1)}, f32[8,128]{1,0:T(8,128)S(1)}, u32[]{:S(2)}, u32[]{:S(2)}) collective-permute-start(f32[8,128]{1,0:T(8,128)S(1)} %slice.18), channel_id=1, source_target_pairs={{0,18},{1,19},{2,16},{3,17},{16,2},{17,3},{18,0},{19,1},{4,22},{5,... | collective-permute-start | bytes 12296 | tf_op jit(solution)/shard_map/ppermute | solution.py:292
  39.9 6.3 %collective-permute-start.12 = (f32[8,128]{1,0:T(8,128)S(1)}, f32[8,128]{1,0:T(8,128)S(1)}, u32[]{:S(2)}, u32[]{:S(2)}) collective-permute-start(f32[8,128]{1,0:T(8,128)S(1)} %slice.18), channel_id=1, source_target_pairs={{0,19},{1,18},{2,17},{3,16},{16,3},{17,2},{18,1},{19,0},{4,23},{5,... | collective-permute-start | bytes 12296 | tf_op jit(solution)/shard_map/ppermute | solution.py:292
  61.5 16.2 %collective-permute-start.16 = (f32[200,128]{1,0:T(8,128)S(1)}, f32[200,128]{1,0:T(8,128)S(1)}, u32[]{:S(2)}, u32[]{:S(2)}) collective-permute-start(f32[200,128]{1,0:T(8,128)S(1)} %get-tuple-element.33.refs_0_), channel_id=1, source_target_pairs={{0,1},{1,0},{2,3},{3,2},{4,5},{5,4},{6,7},{7,6},{8,9},{9,8},{10,11... | collective-permute-start | bytes 307208 | tf_op jit(solution)/shard_map/ppermute | solution.py:292
  61.6 16.1 %collective-permute-start.17 = (f32[200,128]{1,0:T(8,128)S(1)}, f32[200,128]{1,0:T(8,128)S(1)}, u32[]{:S(2)}, u32[]{:S(2)}) collective-permute-start(f32[200,128]{1,0:T(8,128)S(1)} %get-tuple-element.33.refs_0_), channel_id=1, source_target_pairs={{0,2},{1,3},{2,0},{3,1},{4,6},{5,7},{6,4},{7,5},{8,10},{9,11},{10,... | collective-permute-start | bytes 307208 | tf_op jit(solution)/shard_map/ppermute | solution.py:292
  64.6 13.1 %collective-permute-start.18 = (f32[200,128]{1,0:T(8,128)S(1)}, f32[200,128]{1,0:T(8,128)S(1)}, u32[]{:S(2)}, u32[]{:S(2)}) collective-permute-start(f32[200,128]{1,0:T(8,128)S(1)} %get-tuple-element.33.refs_0_), channel_id=1, source_target_pairs={{0,3},{1,2},{2,1},{3,0},{4,7},{5,6},{6,5},{7,4},{8,11},{9,10},{10,... | collective-permute-start | bytes 307208 | tf_op jit(solution)/shard_map/ppermute | solution.py:292
  66.5 4.9 %collective-permute-start.20 = (f32[8,128]{1,0:T(8,128)S(1)}, f32[8,128]{1,0:T(8,128)S(1)}, u32[]{:S(2)}, u32[]{:S(2)}) collective-permute-start(f32[8,128]{1,0:T(8,128)S(1)} %slice.19), channel_id=1, source_target_pairs={{0,17},{1,16},{2,19},{3,18},{16,1},{17,0},{18,3},{19,2},{4,21},{5,... | collective-permute-start | bytes 12296 | tf_op jit(solution)/shard_map/ppermute | solution.py:292
  69.6 5.4 %collective-permute-start.21 = (f32[8,128]{1,0:T(8,128)S(1)}, f32[8,128]{1,0:T(8,128)S(1)}, u32[]{:S(2)}, u32[]{:S(2)}) collective-permute-start(f32[8,128]{1,0:T(8,128)S(1)} %slice.19), channel_id=1, source_target_pairs={{0,18},{1,19},{2,16},{3,17},{16,2},{17,3},{18,0},{19,1},{4,22},{5,... | collective-permute-start | bytes 12296 | tf_op jit(solution)/shard_map/ppermute | solution.py:292
  71.4 6.3 %collective-permute-start.22 = (f32[8,128]{1,0:T(8,128)S(1)}, f32[8,128]{1,0:T(8,128)S(1)}, u32[]{:S(2)}, u32[]{:S(2)}) collective-permute-start(f32[8,128]{1,0:T(8,128)S(1)} %slice.19), channel_id=1, source_target_pairs={{0,19},{1,18},{2,17},{3,16},{16,3},{17,2},{18,1},{19,0},{4,23},{5,... | collective-permute-start | bytes 12296 | tf_op jit(solution)/shard_map/ppermute | solution.py:292
  78.5 4.0 %collective-permute-start.24 = (f32[56,128]{1,0:T(8,128)S(1)}, f32[56,128]{1,0:T(8,128)S(1)}, u32[]{:S(2)}, u32[]{:S(2)}) collective-permute-start(f32[56,128]{1,0:T(8,128)S(1)} %get-tuple-element.34.refs_0_), channel_id=1, source_target_pairs={{0,8},{4,12},{8,0},{12,4},{1,9},{5,13},{9,1},{13,5},{2,10},{6,14},... | collective-permute-start | bytes 86024 | tf_op jit(solution)/shard_map/ppermute | solution.py:292
  89.5 17.0 %collective-permute-start.26 = (f32[200,128]{1,0:T(8,128)S(1)}, f32[200,128]{1,0:T(8,128)S(1)}, u32[]{:S(2)}, u32[]{:S(2)}) collective-permute-start(f32[200,128]{1,0:T(8,128)S(1)} %get-tuple-element.38.refs_0_), channel_id=1, source_target_pairs={{0,1},{1,0},{2,3},{3,2},{4,5},{5,4},{6,7},{7,6},{8,9},{9,8},{10,11... | collective-permute-start | bytes 307208 | tf_op jit(solution)/shard_map/ppermute | solution.py:292
  89.6 16.9 %collective-permute-start.27 = (f32[200,128]{1,0:T(8,128)S(1)}, f32[200,128]{1,0:T(8,128)S(1)}, u32[]{:S(2)}, u32[]{:S(2)}) collective-permute-start(f32[200,128]{1,0:T(8,128)S(1)} %get-tuple-element.38.refs_0_), channel_id=1, source_target_pairs={{0,2},{1,3},{2,0},{3,1},{4,6},{5,7},{6,4},{7,5},{8,10},{9,11},{10,... | collective-permute-start | bytes 307208 | tf_op jit(solution)/shard_map/ppermute | solution.py:292
  92.5 14.0 %collective-permute-start.28 = (f32[200,128]{1,0:T(8,128)S(1)}, f32[200,128]{1,0:T(8,128)S(1)}, u32[]{:S(2)}, u32[]{:S(2)}) collective-permute-start(f32[200,128]{1,0:T(8,128)S(1)} %get-tuple-element.38.refs_0_), channel_id=1, source_target_pairs={{0,3},{1,2},{2,1},{3,0},{4,7},{5,6},{6,5},{7,4},{8,11},{9,10},{10,... | collective-permute-start | bytes 307208 | tf_op jit(solution)/shard_map/ppermute | solution.py:292
  95.4 4.7 %collective-permute-start.30 = (f32[8,128]{1,0:T(8,128)S(1)}, f32[8,128]{1,0:T(8,128)S(1)}, u32[]{:S(2)}, u32[]{:S(2)}) collective-permute-start(f32[8,128]{1,0:T(8,128)S(1)} %slice.20), channel_id=1, source_target_pairs={{0,17},{1,16},{2,19},{3,18},{16,1},{17,0},{18,3},{19,2},{4,21},{5,... | collective-permute-start | bytes 12296 | tf_op jit(solution)/shard_map/ppermute | solution.py:292
  97.5 5.7 %collective-permute-start.31 = (f32[8,128]{1,0:T(8,128)S(1)}, f32[8,128]{1,0:T(8,128)S(1)}, u32[]{:S(2)}, u32[]{:S(2)}) collective-permute-start(f32[8,128]{1,0:T(8,128)S(1)} %slice.20), channel_id=1, source_target_pairs={{0,18},{1,19},{2,16},{3,17},{16,2},{17,3},{18,0},{19,1},{4,22},{5,... | collective-permute-start | bytes 12296 | tf_op jit(solution)/shard_map/ppermute | solution.py:292
  100.1 6.3 %collective-permute-start.32 = (f32[8,128]{1,0:T(8,128)S(1)}, f32[8,128]{1,0:T(8,128)S(1)}, u32[]{:S(2)}, u32[]{:S(2)}) collective-permute-start(f32[8,128]{1,0:T(8,128)S(1)} %slice.20), channel_id=1, source_target_pairs={{0,19},{1,18},{2,17},{3,16},{16,3},{17,2},{18,1},{19,0},{4,23},{5,... | collective-permute-start | bytes 12296 | tf_op jit(solution)/shard_map/ppermute | solution.py:292
  118.9 16.3 %collective-permute-start.36 = (f32[200,128]{1,0:T(8,128)S(1)}, f32[200,128]{1,0:T(8,128)S(1)}, u32[]{:S(2)}, u32[]{:S(2)}) collective-permute-start(f32[200,128]{1,0:T(8,128)S(1)} %get-tuple-element.43.refs_0_), channel_id=1, source_target_pairs={{0,1},{1,0},{2,3},{3,2},{4,5},{5,4},{6,7},{7,6},{8,9},{9,8},{10,11... | collective-permute-start | bytes 307208 | tf_op jit(solution)/shard_map/ppermute | solution.py:292
  118.9 16.3 %collective-permute-start.37 = (f32[200,128]{1,0:T(8,128)S(1)}, f32[200,128]{1,0:T(8,128)S(1)}, u32[]{:S(2)}, u32[]{:S(2)}) collective-permute-start(f32[200,128]{1,0:T(8,128)S(1)} %get-tuple-element.43.refs_0_), channel_id=1, source_target_pairs={{0,2},{1,3},{2,0},{3,1},{4,6},{5,7},{6,4},{7,5},{8,10},{9,11},{10,... | collective-permute-start | bytes 307208 | tf_op jit(solution)/shard_map/ppermute | solution.py:292
  121.6 13.6 %collective-permute-start.38 = (f32[200,128]{1,0:T(8,128)S(1)}, f32[200,128]{1,0:T(8,128)S(1)}, u32[]{:S(2)}, u32[]{:S(2)}) collective-permute-start(f32[200,128]{1,0:T(8,128)S(1)} %get-tuple-element.43.refs_0_), channel_id=1, source_target_pairs={{0,3},{1,2},{2,1},{3,0},{4,7},{5,6},{6,5},{7,4},{8,11},{9,10},{10,... | collective-permute-start | bytes 307208 | tf_op jit(solution)/shard_map/ppermute | solution.py:292
  124.0 4.9 %collective-permute-start.40 = (f32[8,128]{1,0:T(8,128)S(1)}, f32[8,128]{1,0:T(8,128)S(1)}, u32[]{:S(2)}, u32[]{:S(2)}) collective-permute-start(f32[8,128]{1,0:T(8,128)S(1)} %slice.21), channel_id=1, source_target_pairs={{0,17},{1,16},{2,19},{3,18},{16,1},{17,0},{18,3},{19,2},{4,21},{5,... | collective-permute-start | bytes 12296 | tf_op jit(solution)/shard_map/ppermute | solution.py:292
  126.9 5.4 %collective-permute-start.41 = (f32[8,128]{1,0:T(8,128)S(1)}, f32[8,128]{1,0:T(8,128)S(1)}, u32[]{:S(2)}, u32[]{:S(2)}) collective-permute-start(f32[8,128]{1,0:T(8,128)S(1)} %slice.21), channel_id=1, source_target_pairs={{0,18},{1,19},{2,16},{3,17},{16,2},{17,3},{18,0},{19,1},{4,22},{5,... | collective-permute-start | bytes 12296 | tf_op jit(solution)/shard_map/ppermute | solution.py:292
  128.9 6.3 %collective-permute-start.42 = (f32[8,128]{1,0:T(8,128)S(1)}, f32[8,128]{1,0:T(8,128)S(1)}, u32[]{:S(2)}, u32[]{:S(2)}) collective-permute-start(f32[8,128]{1,0:T(8,128)S(1)} %slice.21), channel_id=1, source_target_pairs={{0,19},{1,18},{2,17},{3,16},{16,3},{17,2},{18,1},{19,0},{4,23},{5,... | collective-permute-start | bytes 12296 | tf_op jit(solution)/shard_map/ppermute | solution.py:292
  140.9 4.3 %collective-permute-start.46 = (f32[64,1,2,32]{3,0,2,1:T(8,128)S(1)}, f32[64,1,2,32]{3,0,2,1:T(8,128)S(1)}, u32[]{:S(2)}, u32[]{:S(2)}) collective-permute-start(f32[64,1,2,32]{3,0,2,1:T(8,128)S(1)} %bitcast_add_fusion.1), channel_id=1, source_target_pairs={{0,16},{16,0},{1,17},{17,1},{2,18},{18,2},{3,19},{19,3},{4,20},{20... | collective-permute-start | bytes 49160 | tf_op jit(solution)/shard_map/ppermute | solution.py:292
  (20 other events, 160.5 us)

commit v2 on v1

--- a/solution.py
+++ b/solution.py
@@ -15,7 +15,7 @@
 EPS = 1e-05
 STEP = 0.5
 
-VMEM_LIMIT = 40 << 20
+VMEM_LIMIT = 24 << 20
 
 
 def basis_table(groups, order):
@@ -111,14 +111,13 @@
     )(model, vis, weight_t)
 
 
-def local_terms(mt_ref, vt_ref, grow_ref, gcol_ref, out_ref, z_ref, r_ref, ct_ref):
+def residual(mt_ref, vt_ref, grow_ref, gcol_ref, z_ref, r_ref, p_ref, ct_ref):
     dirs, _, cols, rows = mt_ref.shape
     ct_ref[...] = gcol_ref[...].T
-    chunk = 16
+    chunk = 64
 
     def predict(n, carry):
-        c0 = pl.multiple_of(n * chunk, chunk)
-        here = pl.ds(c0, chunk)
+        here = pl.ds(pl.multiple_of(n * chunk, chunk), chunk)
         ctile = ct_ref[here, :]
         acc_r = vt_ref[0, here, :]
         acc_i = vt_ref[1, here, :]
@@ -138,44 +137,49 @@
         r_ref[0, here, :] = acc_r
         r_ref[1, here, :] = acc_i
         sq = acc_r * acc_r + acc_i * acc_i
-        return carry + sq[:8] + sq[8:]
-
-    power = lax.fori_loop(0, cols // chunk, predict, jnp.zeros((8, rows), jnp.float32))
-    out_ref[3 * dirs : 3 * dirs + 8, :] = power
-
+        for c in range(0, chunk, 8):
+            carry = carry + sq[c : c + 8]
+        return carry
+
+    p_ref[...] = lax.fori_loop(0, cols // chunk, predict, jnp.zeros(p_ref.shape, jnp.float32))
+
+
+def terms_kernel(z_ref, r_ref, out_ref):
+    dirs, _, cols, rows = z_ref.shape
     group = 8
+    part = 4
 
     def terms(n, carry):
         k0 = pl.multiple_of(n * group, group)
-        for half in range(2):
-            sums = [[None] * 3 for _ in range(group // 2)]
+        blocks = [[], [], []]
+        for half in range(0, group, part):
+            sums = [[None] * 3 for _ in range(part)]
             for c in range(0, cols, 8):
                 rr = r_ref[0, c : c + 8, :]
                 ri = r_ref[1, c : c + 8, :]
-                for kk in range(group // 2):
-                    k = k0 + half * (group // 2) + kk
-                    zr = z_ref[k, 0, c : c + 8, :]
-                    zi = z_ref[k, 1, c : c + 8, :]
+                for kk in range(part):
+                    zr = z_ref[k0 + half + kk, 0, c : c + 8, :]
+                    zi = z_ref[k0 + half + kk, 1, c : c + 8, :]
                     new = (zr * zr + zi * zi, zr * rr + zi * ri, zr * ri - zi * rr)
                     for s in range(3):
                         old = sums[kk][s]
                         sums[kk][s] = new[s] if old is None else old + new[s]
             for s in range(3):
-                block = jnp.concatenate(
-                    [jnp.sum(sums[kk][s], axis=0, keepdims=True) for kk in range(group // 2)], axis=0
-                )
-                out_ref[pl.ds(s * dirs + k0 + half * (group // 2), group // 2), :] = block
+                blocks[s] += [jnp.sum(sums[kk][s], axis=0, keepdims=True) for kk in range(part)]
+        for s in range(3):
+            out_ref[pl.ds(s * dirs + k0, group), :] = jnp.concatenate(blocks[s], axis=0)
         return carry
 
     lax.fori_loop(0, dirs // group, terms, 0)
+    out_ref[3 * dirs :, :] = jnp.zeros((8, rows), jnp.float32)
 
 
 def first_kernel(ids_ref, *refs, ns, nz, span):
     rows_in = refs[:nz]
     cols_in = refs[nz : nz + ns]
     mt_ref, vt_ref = refs[nz + ns : nz + ns + 2]
-    out_ref, grow_ref, gcol_ref, trow_ref, tcol_ref = refs[nz + ns + 2 : nz + ns + 7]
-    scratch = refs[nz + ns + 7 :]
+    outs = refs[nz + ns + 2 : nz + ns + 5]
+    grow_ref, gcol_ref, trow_ref, tcol_ref, ct_ref = refs[nz + ns + 5 :]
     dirs = mt_ref.shape[0]
     i, j = ids_ref[0], ids_ref[1]
     depth = dirs * span // mt_ref.shape[3]
@@ -186,14 +190,14 @@
             dst = g_ref if q < 2 else t_ref
             at = (q % 2) * dirs
             dst[at : at + dirs, :] = plane
-    local_terms(mt_ref, vt_ref, grow_ref, gcol_ref, out_ref, *scratch)
+    residual(mt_ref, vt_ref, grow_ref, gcol_ref, *outs, ct_ref)
 
 
 def sweep_kernel(ids_ref, *refs, ns, span, scale):
     pieces = refs[:ns]
     sum_ref, growin_ref, gcolin_ref, trow_ref, tcol_ref, rho_ref, mt_ref, vt_ref = refs[ns : ns + 8]
-    out_ref, grow_ref, gcol_ref = refs[ns + 8 : ns + 11]
-    scratch = refs[ns + 11 :]
+    outs = refs[ns + 8 : ns + 11]
+    grow_ref, gcol_ref, ct_ref = refs[ns + 11 :]
     dirs = mt_ref.shape[0]
     i = ids_ref[0]
     depth = dirs * span // mt_ref.shape[3]
@@ -220,13 +224,12 @@
     gcol_ref[re, :], gcol_ref[im, :] = solve(
         a, cr, ci, gcolin_ref[re, :], gcolin_ref[im, :], tcol_ref[re, :], tcol_ref[im, :], rho_eff
     )
-    local_terms(mt_ref, vt_ref, grow_ref, gcol_ref, out_ref, *scratch)
-
-
-def combine_kernel(ids_ref, *refs, nz, extra, span):
+    residual(mt_ref, vt_ref, grow_ref, gcol_ref, *outs, ct_ref)
+
+
+def combine_kernel(ids_ref, *refs, nz, span):
     parts = refs[:nz]
-    powers = refs[nz : nz + extra]
-    sum_ref, own_ref = refs[nz + extra :]
+    sum_ref, own_ref = refs[nz:]
     dirs = sum_ref.shape[0] // 3
     j = ids_ref[1]
     depth = dirs * span // sum_ref.shape[1]
@@ -240,8 +243,6 @@
     power = parts[0][3 * dirs :, :]
     for p in parts[1:]:
         power = power + p[3 * dirs :, :]
-    for p in powers:
-        power = power + p[...]
     own_ref[3 * depth :, :] = power
 
 
@@ -335,57 +336,52 @@
     weight_t = jnp.repeat(jnp.repeat(fl, TILE, axis=0), TILE, axis=1)
     mt, vt = prepare(model[0], vis[0], weight_t)
 
-    scratch = [
-        pltpu.VMEM((dirs, 2, cols, rows), jnp.float32),
-        pltpu.VMEM((2, cols, rows), jnp.float32),
-        pltpu.VMEM((cols, 2 * dirs), jnp.float32),
-    ]
+    scratch = [pltpu.VMEM((cols, 2 * dirs), jnp.float32)]
     scale = 1.0 / (groups * STATIONS * STATIONS)
     depth = dirs * span // rows
     plane = f32(2 * dirs, rows)
-    partial, grow, gcol, trow, tcol = call(
+    fields = [f32(dirs, 2, cols, rows), f32(2, cols, rows), f32(8, rows)]
+    z, r, power, grow, gcol, trow, tcol = call(
         functools.partial(first_kernel, ns=ns, nz=nz, span=span),
         "first",
         ids,
         row_parts + col_parts + [mt, vt],
-        [f32(3 * dirs + 8, rows), plane, plane, plane, plane],
+        fields + [plane, plane, plane, plane],
         scratch,
     )
     g_packed, t_packed = start[: 2 * depth], start[2 * depth :]
     for step in range(ITERS):
-        swaps = [partial] + [swap(partial, "scol", n) for n in range(1, nz)]
-        power = partial[3 * dirs :]
         if groups == 2:
-            both = ("chan", "scol")
-            powers = [swap(power, both, nz + n) for n in range(nz)]
+            power = power + swap(power, ("chan", "srow"), ns + 1)
         else:
-            powers = [lax.psum(power, ("chan", "scol")) - sum(s[3 * dirs :] for s in swaps)]
+            power = lax.psum(power, "chan")
+        partial = call(terms_kernel, "terms", None, [z, r], [f32(3 * dirs + 8, rows)])[0]
+        partial = lax.dynamic_update_slice(partial, power, (3 * dirs, 0))
         sums, own = call(
-            functools.partial(combine_kernel, nz=nz, extra=len(powers), span=span),
+            functools.partial(combine_kernel, nz=nz, span=span),
             "combine",
             ids,
-            swaps + powers,
+            [partial] + [swap(partial, "scol", n) for n in range(nz - 1, 0, -1)],
             [f32(3 * dirs, rows), f32(3 * depth + 8, rows)],
         )
         pieces = [own] + [swap(own, "srow", n) for n in range(1, ns)]
         if step < ITERS - 1:
-            partial, grow_new, gcol_new = call(
+            z, r, power, grow_new, gcol_new = call(
                 functools.partial(sweep_kernel, ns=ns, span=span, scale=scale),
                 "sweep",
                 ids,
                 pieces + [sums, grow, gcol, trow, tcol, rho_rows, mt, vt],
-                [f32(3 * dirs + 8, rows), plane, plane],
+                fields + [plane, plane],
                 scratch,
             )
             grow, gcol = grow_new, gcol_new
-        own_g = call(
+        g_packed = call(
             functools.partial(final_kernel, ns=ns, scale=scale),
             "own",
             None,
             pieces + [g_packed, t_packed, rho_packed],
             [f32(2 * depth, rows)],
         )[0]
-        g_packed = own_g
     g = from_packed(g_packed, span)
     local = brow[None, :, None, None] * (g + dual_own)[:, None, :, :]
     if groups == 2:

time: 147 us -> 126 us (0.86)
  starting transfers between devices: 58.4 us -> 38.1 us
  Pallas kernels: 38.7 us -> 34 us
  waiting for transfers between devices: 36.3 us -> 39.8 us
    ppermute x47 -> x35, starting transfers between devices: 58.4 us -> 38.1 us  [swap(): return lax.ppermute(x, axis, [(m, m ^ n) for m in range(size)])]
    pallas_call x12 -> x16, Pallas kernels: 31.3 us -> 26.6 us  [call(): pl.pallas_call(kernel, in_specs=[SMEM] * len(lead) + [VMEM] * len(args),...]
    ppermute x47 -> x35, waiting for transfers between devices: 36.3 us -> 39.8 us  [swap(): return lax.ppermute(x, axis, [(m, m ^ n) for m in range(size)])]
  transfers between devices with their start and end apart: 47 -> 35, of which waited for: 24 -> 20; matrix products, arithmetic and copies ran while one was open for 2% -> 3% of each run, Pallas kernels for 5% -> 13%
where the time goes in v2:
time: 126 us; the launch traced here: 125 us
  waiting for transfers between devices  39.8 us (32%)
  starting transfers between devices  38.1 us (30%)
  Pallas kernels  34 us (27%)
  local copies, waits for them, and re-layouts  9.31 us (7%)
  between operations  2.26 us (2%)
  other arithmetic  1.51 us (1%)
    ppermute x35, waiting for transfers between devices, swap(): return lax.ppermute(x, axis, [(m, m ^ n) for m in range(size)])  39.8 us
    ppermute x35, starting transfers between devices, swap(): return lax.ppermute(x, axis, [(m, m ^ n) for m in range(size)])  38.1 us
    pallas_call x16, Pallas kernels, call(): pl.pallas_call(kernel, in_specs=[SMEM] * len(lead) + [VMEM] * len(args),...  26.6 us
    unnamed x17, local copies, waits for them, and re-layouts  7.69 us
    pallas_call x1, Pallas kernels, prepare(): pl.pallas_call(prepare_kernel, grid=(dirs // step,), in_specs=[pl.BlockSp...  7.46 us
  transfers between devices with their start and end apart: 35, of which 20 were waited for; matrix products, arithmetic and copies ran while one was open for 3% of the time, Pallas kernels for 13%

profile of v2, /device:TPU:0, one launch (start us, length us, event | category | flops | bytes accessed | tf_op | source)
XLA Modules:
  0.0 125.0 jit_solution(1982087083839863120)
XLA Ops:
  3.5 3.1 %collective-permute-start = (f32[64,128]{1,0:T(8,128)S(1)}, f32[64,128]{1,0:T(8,128)S(1)}, u32[]{:S(2)}, u32[]{:S(2)}) collective-permute-start(f32[64,128]{1,0:T(8,128)S(1)} %constant_dynamic-update-slice_fusion.refs_0_.refs_4_), channel_id=1, source_target_pairs={{0,1},{1,0},{2,3},{3,2},{4,5},{5,4},{6,7},{7,6},{8,9},{9,8},{10,11... | collective-permute-start | bytes 98312 | tf_op jit(solution)/shard_map/ppermute | solution.py:293
  6.6 2.6 %collective-permute-start.1 = (f32[64,128]{1,0:T(8,128)S(1)}, f32[64,128]{1,0:T(8,128)S(1)}, u32[]{:S(2)}, u32[]{:S(2)}) collective-permute-start(f32[64,128]{1,0:T(8,128)S(1)} %constant_dynamic-update-slice_fusion.refs_0_.refs_4_), channel_id=1, source_target_pairs={{0,2},{1,3},{2,0},{3,1},{4,6},{5,7},{6,4},{7,5},{8,10},{9,11},{10,... | collective-permute-start | bytes 98312 | tf_op jit(solution)/shard_map/ppermute | solution.py:293
  9.1 1.7 %collective-permute-start.4 = (f32[64,128]{1,0:T(8,128)S(1)}, f32[64,128]{1,0:T(8,128)S(1)}, u32[]{:S(2)}, u32[]{:S(2)}) collective-permute-start(f32[64,128]{1,0:T(8,128)S(1)} %constant_dynamic-update-slice_fusion.refs_0_.refs_4_), channel_id=1, source_target_pairs={{0,8},{4,12},{8,0},{12,4},{1,9},{5,13},{9,1},{13,5},{2,10},{6,14},... | collective-permute-start | bytes 98312 | tf_op jit(solution)/shard_map/ppermute | solution.py:293
  12.7 7.5 %prepare.1 = (bf16[64,2,128,128]{3,2,1,0:T(8,128)(2,1)}, f32[2,128,128]{2,1,0:T(8,128)}) custom-call(bf16[64,2,128,128]{3,2,1,0:T(8,128)(2,1)} %bitcast.41, bf16[2,128,128]{2,1,0:T(8,128)(2,1)} %bitcast.47, f32[128,128]{1,0:T(8,128)} %copy.35.weight_ref), custom_call_target="tpu_custom_call" | custom-call | tf_op jit(solution)/shard_map/prepare/pallas_call | solution.py:94
  20.2 2.2 %copy-done = bf16[64,2,128,128]{3,2,1,0:T(8,128)(2,1)S(1)} copy-done((bf16[64,2,128,128]{3,2,1,0:T(8,128)(2,1)S(1)}, bf16[64,2,128,128]{3,2,1,0:T(8,128)(2,1)}, u32[]{:S(2)}) %copy-start) | copy-done | bytes 4194328
  23.3 3.7 %first.1 = (f32[64,2,128,128]{3,2,1,0:T(8,128)S(1)}, f32[2,128,128]{2,1,0:T(8,128)S(1)}, f32[8,128]{1,0:T(8,128)S(1)}, f32[128,128]{1,0:T(8,128)S(1)}, f32[128,1...) custom-call(s32[2]{0:T(128)S(1)} %pad_add_fusion.ids_ref, ...), custom_call_target="tpu_custom_call" | custom-call | tf_op jit(solution)/shard_map/first/pallas_call | solution.py:280
  27.0 1.7 %collective-permute-start.6 = (f32[8,128]{1,0:T(8,128)S(1)}, f32[8,128]{1,0:T(8,128)S(1)}, u32[]{:S(2)}, u32[]{:S(2)}) collective-permute-start(f32[8,128]{1,0:T(8,128)S(1)} %get-tuple-element.36), channel_id=1, source_target_pairs={{0,20},{4,16},{8,28},{12,24},{16,4},{20,0},{24,12},{28,8},{1,21},{... | collective-permute-start | bytes 12296 | tf_op jit(solution)/shard_map/ppermute | solution.py:293
  28.6 2.0 %terms.4 = f32[200,128]{1,0:T(8,128)S(1)} custom-call(f32[64,2,128,128]{3,2,1,0:T(8,128)S(1)} %get-tuple-element.34.z_ref, f32[2,128,128]{2,1,0:T(8,128)S(1)} %get-tuple-element.35.r_ref), custom_call_target="tpu_custom_call" | custom-call | tf_op jit(solution)/shard_map/terms/pallas_call | solution.py:280
  30.7 3.7 %collective-permute-start.7 = (f32[200,128]{1,0:T(8,128)S(1)}, f32[200,128]{1,0:T(8,128)S(1)}, u32[]{:S(2)}, u32[]{:S(2)}) collective-permute-start(f32[200,128]{1,0:T(8,128)S(1)} %add_dynamic-update-slice_fusion.3.refs_0_), channel_id=1, source_target_pairs={{0,3},{1,2},{2,1},{3,0},{4,7},{5,6},{6,5},{7,4},{8,11},{9,10},{10,... | collective-permute-start | bytes 307208 | tf_op jit(solution)/shard_map/ppermute | solution.py:293
  35.1 3.2 %collective-permute-done.7.refs_1_ = f32[200,128]{1,0:T(8,128)S(1)} collective-permute-done((f32[200,128]{1,0:T(8,128)S(1)}, f32[200,128]{1,0:T(8,128)S(1)}, u32[]{:S(2)}, u32[]{:S(2)}) %collective-permute-start.7) | collective-permute-done | bytes 102432 | tf_op jit(solution)/shard_map/ppermute | solution.py:293
  38.3 4.1 %collective-permute-done.8.refs_2_ = f32[200,128]{1,0:T(8,128)S(1)} collective-permute-done((f32[200,128]{1,0:T(8,128)S(1)}, f32[200,128]{1,0:T(8,128)S(1)}, u32[]{:S(2)}, u32[]{:S(2)}) %collective-permute-start.8) | collective-permute-done | bytes 102432 | tf_op jit(solution)/shard_map/ppermute | solution.py:293
  43.2 1.6 %collective-permute-start.11 = (f32[56,128]{1,0:T(8,128)S(1)}, f32[56,128]{1,0:T(8,128)S(1)}, u32[]{:S(2)}, u32[]{:S(2)}) collective-permute-start(f32[56,128]{1,0:T(8,128)S(1)} %get-tuple-element.37.refs_0_), channel_id=1, source_target_pairs={{0,8},{4,12},{8,0},{12,4},{1,9},{5,13},{9,1},{13,5},{2,10},{6,14},... | collective-permute-start | bytes 86024 | tf_op jit(solution)/shard_map/ppermute | solution.py:293
  45.1 2.0 %collective-permute-done.11.refs_2_ = f32[56,128]{1,0:T(8,128)S(1)} collective-permute-done((f32[56,128]{1,0:T(8,128)S(1)}, f32[56,128]{1,0:T(8,128)S(1)}, u32[]{:S(2)}, u32[]{:S(2)}) %collective-permute-start.11) | collective-permute-done | bytes 28704 | tf_op jit(solution)/shard_map/ppermute | solution.py:293
  48.1 3.6 %sweep.3 = (f32[64,2,128,128]{3,2,1,0:T(8,128)S(1)}, f32[2,128,128]{2,1,0:T(8,128)S(1)}, f32[8,128]{1,0:T(8,128)S(1)}, f32[128,128]{1,0:T(8,128)S(1)}, f32[128,128]{1,0:T(8,128)S(1)}) custom-call(s32[2]{0:T(128)S(1)} %pad_add_fusion.ids_ref, f32[56,128]{1,0:T(8,128)S(1)} %get-tuple-element.37.refs_0_, f32[56,128]{1,0:T(8,128)S(1)} %collective-permute-done.10.refs_1_, ...), custom_call_target="tpu_custom_call" | custom-call | tf_op jit(solution)/shard_map/sweep/pallas_call | solution.py:280
  52.7 2.0 %terms.5 = f32[200,128]{1,0:T(8,128)S(1)} custom-call(f32[64,2,128,128]{3,2,1,0:T(8,128)S(1)} %get-tuple-element.43.z_ref, f32[2,128,128]{2,1,0:T(8,128)S(1)} %get-tuple-element.44.r_ref), custom_call_target="tpu_custom_call" | custom-call | tf_op jit(solution)/shard_map/terms/pallas_call | solution.py:280
  54.8 2.5 %collective-permute-start.14 = (f32[200,128]{1,0:T(8,128)S(1)}, f32[200,128]{1,0:T(8,128)S(1)}, u32[]{:S(2)}, u32[]{:S(2)}) collective-permute-start(f32[200,128]{1,0:T(8,128)S(1)} %add_dynamic-update-slice_fusion.2.refs_0_), channel_id=1, source_target_pairs={{0,3},{1,2},{2,1},{3,0},{4,7},{5,6},{6,5},{7,4},{8,11},{9,10},{10,... | collective-permute-start | bytes 307208 | tf_op jit(solution)/shard_map/ppermute | solution.py:293
  57.6 1.6 %collective-permute-start.16 = (f32[200,128]{1,0:T(8,128)S(1)}, f32[200,128]{1,0:T(8,128)S(1)}, u32[]{:S(2)}, u32[]{:S(2)}) collective-permute-start(f32[200,128]{1,0:T(8,128)S(1)} %add_dynamic-update-slice_fusion.2.refs_0_), channel_id=1, source_target_pairs={{0,1},{1,0},{2,3},{3,2},{4,5},{5,4},{6,7},{7,6},{8,9},{9,8},{10,11... | collective-permute-start | bytes 307208 | tf_op jit(solution)/shard_map/ppermute | solution.py:293
  59.2 3.2 %collective-permute-done.14.refs_1_ = f32[200,128]{1,0:T(8,128)S(1)} collective-permute-done((f32[200,128]{1,0:T(8,128)S(1)}, f32[200,128]{1,0:T(8,128)S(1)}, u32[]{:S(2)}, u32[]{:S(2)}) %collective-permute-start.14) | collective-permute-done | bytes 102432 | tf_op jit(solution)/shard_map/ppermute | solution.py:293
  62.4 4.8 %collective-permute-done.15.refs_2_ = f32[200,128]{1,0:T(8,128)S(1)} collective-permute-done((f32[200,128]{1,0:T(8,128)S(1)}, f32[200,128]{1,0:T(8,128)S(1)}, u32[]{:S(2)}, u32[]{:S(2)}) %collective-permute-start.15) | collective-permute-done | bytes 102432 | tf_op jit(solution)/shard_map/ppermute | solution.py:293
  69.9 2.1 %collective-permute-done.18.refs_2_ = f32[56,128]{1,0:T(8,128)S(1)} collective-permute-done((f32[56,128]{1,0:T(8,128)S(1)}, f32[56,128]{1,0:T(8,128)S(1)}, u32[]{:S(2)}, u32[]{:S(2)}) %collective-permute-start.18) | collective-permute-done | bytes 28704 | tf_op jit(solution)/shard_map/ppermute | solution.py:293
  72.3 3.6 %sweep.4 = (f32[64,2,128,128]{3,2,1,0:T(8,128)S(1)}, f32[2,128,128]{2,1,0:T(8,128)S(1)}, f32[8,128]{1,0:T(8,128)S(1)}, f32[128,128]{1,0:T(8,128)S(1)}, f32[128,128]{1,0:T(8,128)S(1)}) custom-call(s32[2]{0:T(128)S(1)} %pad_add_fusion.ids_ref, f32[56,128]{1,0:T(8,128)S(1)} %get-tuple-element.46.refs_0_, f32[56,128]{1,0:T(8,128)S(1)} %collective-permute-done.17.refs_1_, ...), custom_call_target="tpu_custom_call" | custom-call | tf_op jit(solution)/shard_map/sweep/pallas_call | solution.py:280
  76.7 1.9 %terms.6 = f32[200,128]{1,0:T(8,128)S(1)} custom-call(f32[64,2,128,128]{3,2,1,0:T(8,128)S(1)} %get-tuple-element.50.z_ref, f32[2,128,128]{2,1,0:T(8,128)S(1)} %get-tuple-element.51.r_ref), custom_call_target="tpu_custom_call" | custom-call | tf_op jit(solution)/shard_map/terms/pallas_call | solution.py:280
  80.3 3.1 %collective-permute-start.23 = (f32[200,128]{1,0:T(8,128)S(1)}, f32[200,128]{1,0:T(8,128)S(1)}, u32[]{:S(2)}, u32[]{:S(2)}) collective-permute-start(f32[200,128]{1,0:T(8,128)S(1)} %add_dynamic-update-slice_fusion.1.refs_0_), channel_id=1, source_target_pairs={{0,1},{1,0},{2,3},{3,2},{4,5},{5,4},{6,7},{7,6},{8,9},{9,8},{10,11... | collective-permute-start | bytes 307208 | tf_op jit(solution)/shard_map/ppermute | solution.py:293
  83.3 3.2 %collective-permute-done.21.refs_1_ = f32[200,128]{1,0:T(8,128)S(1)} collective-permute-done((f32[200,128]{1,0:T(8,128)S(1)}, f32[200,128]{1,0:T(8,128)S(1)}, u32[]{:S(2)}, u32[]{:S(2)}) %collective-permute-start.21) | collective-permute-done | bytes 102432 | tf_op jit(solution)/shard_map/ppermute | solution.py:293
  86.6 3.5 %collective-permute-done.22.refs_2_ = f32[200,128]{1,0:T(8,128)S(1)} collective-permute-done((f32[200,128]{1,0:T(8,128)S(1)}, f32[200,128]{1,0:T(8,128)S(1)}, u32[]{:S(2)}, u32[]{:S(2)}) %collective-permute-start.22) | collective-permute-done | bytes 102432 | tf_op jit(solution)/shard_map/ppermute | solution.py:293
  92.6 2.1 %collective-permute-done.25.refs_2_ = f32[56,128]{1,0:T(8,128)S(1)} collective-permute-done((f32[56,128]{1,0:T(8,128)S(1)}, f32[56,128]{1,0:T(8,128)S(1)}, u32[]{:S(2)}, u32[]{:S(2)}) %collective-permute-start.25) | collective-permute-done | bytes 28704 | tf_op jit(solution)/shard_map/ppermute | solution.py:293
  95.3 4.1 %sweep.5 = (f32[64,2,128,128]{3,2,1,0:T(8,128)S(1)}, f32[2,128,128]{2,1,0:T(8,128)S(1)}, f32[8,128]{1,0:T(8,128)S(1)}, f32[128,128]{1,0:T(8,128)}, f32[128,128]{1,0:T(8,128)}) custom-call(s32[2]{0:T(128)S(1)} %pad_add_fusion.ids_ref, f32[56,128]{1,0:T(8,128)S(1)} %get-tuple-element.53.refs_0_, f32[56,128]{1,0:T(8,128)S(1)} %collective-permute-done.24.refs_1_, ...), custom_call_target="tpu_custom_call" | custom-call | tf_op jit(solution)/shard_map/sweep/pallas_call | solution.py:280
  100.2 2.0 %terms.7 = f32[200,128]{1,0:T(8,128)S(1)} custom-call(f32[64,2,128,128]{3,2,1,0:T(8,128)S(1)} %get-tuple-element.57.z_ref, f32[2,128,128]{2,1,0:T(8,128)S(1)} %get-tuple-element.58.r_ref), custom_call_target="tpu_custom_call" | custom-call | tf_op jit(solution)/shard_map/terms/pallas_call | solution.py:280
  102.5 1.3 %collective-permute-start.28 = (f32[200,128]{1,0:T(8,128)S(1)}, f32[200,128]{1,0:T(8,128)S(1)}, u32[]{:S(2)}, u32[]{:S(2)}) collective-permute-start(f32[200,128]{1,0:T(8,128)S(1)} %add_dynamic-update-slice_fusion.refs_0_), channel_id=1, source_target_pairs={{0,3},{1,2},{2,1},{3,0},{4,7},{5,6},{6,5},{7,4},{8,11},{9,10},{10,... | collective-permute-start | bytes 307208 | tf_op jit(solution)/shard_map/ppermute | solution.py:293
  103.8 3.1 %collective-permute-start.30 = (f32[200,128]{1,0:T(8,128)S(1)}, f32[200,128]{1,0:T(8,128)S(1)}, u32[]{:S(2)}, u32[]{:S(2)}) collective-permute-start(f32[200,128]{1,0:T(8,128)S(1)} %add_dynamic-update-slice_fusion.refs_0_), channel_id=1, source_target_pairs={{0,1},{1,0},{2,3},{3,2},{4,5},{5,4},{6,7},{7,6},{8,9},{9,8},{10,11... | collective-permute-start | bytes 307208 | tf_op jit(solution)/shard_map/ppermute | solution.py:293
  106.8 3.2 %collective-permute-done.28.refs_1_ = f32[200,128]{1,0:T(8,128)S(1)} collective-permute-done((f32[200,128]{1,0:T(8,128)S(1)}, f32[200,128]{1,0:T(8,128)S(1)}, u32[]{:S(2)}, u32[]{:S(2)}) %collective-permute-start.28) | collective-permute-done | bytes 102432 | tf_op jit(solution)/shard_map/ppermute | solution.py:293
  110.1 3.5 %collective-permute-done.29.refs_2_ = f32[200,128]{1,0:T(8,128)S(1)} collective-permute-done((f32[200,128]{1,0:T(8,128)S(1)}, f32[200,128]{1,0:T(8,128)S(1)}, u32[]{:S(2)}, u32[]{:S(2)}) %collective-permute-start.29) | collective-permute-done | bytes 102432 | tf_op jit(solution)/shard_map/ppermute | solution.py:293
  (99 shorter events, 29.3 us)
Async XLA Ops:
  3.5 8.1 %collective-permute-start = (f32[64,128]{1,0:T(8,128)S(1)}, f32[64,128]{1,0:T(8,128)S(1)}, u32[]{:S(2)}, u32[]{:S(2)}) collective-permute-start(f32[64,128]{1,0:T(8,128)S(1)} %constant_dynamic-update-slice_fusion.refs_0_.refs_4_), channel_id=1, source_target_pairs={{0,1},{1,0},{2,3},{3,2},{4,5},{5,4},{6,7},{7,6},{8,9},{9,8},{10,11... | collective-permute-start | bytes 98312 | tf_op jit(solution)/shard_map/ppermute | solution.py:293
  6.6 13.6 %collective-permute-start.1 = (f32[64,128]{1,0:T(8,128)S(1)}, f32[64,128]{1,0:T(8,128)S(1)}, u32[]{:S(2)}, u32[]{:S(2)}) collective-permute-start(f32[64,128]{1,0:T(8,128)S(1)} %constant_dynamic-update-slice_fusion.refs_0_.refs_4_), channel_id=1, source_target_pairs={{0,2},{1,3},{2,0},{3,1},{4,6},{5,7},{6,4},{7,5},{8,10},{9,11},{10,... | collective-permute-start | bytes 98312 | tf_op jit(solution)/shard_map/ppermute | solution.py:293
  9.1 11.0 %collective-permute-start.2 = (f32[64,128]{1,0:T(8,128)S(1)}, f32[64,128]{1,0:T(8,128)S(1)}, u32[]{:S(2)}, u32[]{:S(2)}) collective-permute-start(f32[64,128]{1,0:T(8,128)S(1)} %constant_dynamic-update-slice_fusion.refs_0_.refs_4_), channel_id=1, source_target_pairs={{0,3},{1,2},{2,1},{3,0},{4,7},{5,6},{6,5},{7,4},{8,11},{9,10},{10,... | collective-permute-start | bytes 98312 | tf_op jit(solution)/shard_map/ppermute | solution.py:293
  9.1 11.0 %collective-permute-start.3 = (f32[64,128]{1,0:T(8,128)S(1)}, f32[64,128]{1,0:T(8,128)S(1)}, u32[]{:S(2)}, u32[]{:S(2)}) collective-permute-start(f32[64,128]{1,0:T(8,128)S(1)} %constant_dynamic-update-slice_fusion.refs_0_.refs_4_), channel_id=1, source_target_pairs={{0,4},{4,0},{8,12},{12,8},{1,5},{5,1},{9,13},{13,9},{2,6},{6,2},{1... | collective-permute-start | bytes 98312 | tf_op jit(solution)/shard_map/ppermute | solution.py:293
  9.1 11.0 %collective-permute-start.4 = (f32[64,128]{1,0:T(8,128)S(1)}, f32[64,128]{1,0:T(8,128)S(1)}, u32[]{:S(2)}, u32[]{:S(2)}) collective-permute-start(f32[64,128]{1,0:T(8,128)S(1)} %constant_dynamic-update-slice_fusion.refs_0_.refs_4_), channel_id=1, source_target_pairs={{0,8},{4,12},{8,0},{12,4},{1,9},{5,13},{9,1},{13,5},{2,10},{6,14},... | collective-permute-start | bytes 98312 | tf_op jit(solution)/shard_map/ppermute | solution.py:293
  11.6 8.6 %collective-permute-start.5 = (f32[64,128]{1,0:T(8,128)S(1)}, f32[64,128]{1,0:T(8,128)S(1)}, u32[]{:S(2)}, u32[]{:S(2)}) collective-permute-start(f32[64,128]{1,0:T(8,128)S(1)} %constant_dynamic-update-slice_fusion.refs_0_.refs_4_), channel_id=1, source_target_pairs={{0,12},{4,8},{8,4},{12,0},{1,13},{5,9},{9,5},{13,1},{2,14},{6,10},... | collective-permute-start | bytes 98312 | tf_op jit(solution)/shard_map/ppermute | solution.py:293
  27.0 3.7 %collective-permute-start.6 = (f32[8,128]{1,0:T(8,128)S(1)}, f32[8,128]{1,0:T(8,128)S(1)}, u32[]{:S(2)}, u32[]{:S(2)}) collective-permute-start(f32[8,128]{1,0:T(8,128)S(1)} %get-tuple-element.36), channel_id=1, source_target_pairs={{0,20},{4,16},{8,28},{12,24},{16,4},{20,0},{24,12},{28,8},{1,21},{... | collective-permute-start | bytes 12296 | tf_op jit(solution)/shard_map/ppermute | solution.py:293
  30.7 7.7 %collective-permute-start.7 = (f32[200,128]{1,0:T(8,128)S(1)}, f32[200,128]{1,0:T(8,128)S(1)}, u32[]{:S(2)}, u32[]{:S(2)}) collective-permute-start(f32[200,128]{1,0:T(8,128)S(1)} %add_dynamic-update-slice_fusion.3.refs_0_), channel_id=1, source_target_pairs={{0,3},{1,2},{2,1},{3,0},{4,7},{5,6},{6,5},{7,4},{8,11},{9,10},{10,... | collective-permute-start | bytes 307208 | tf_op jit(solution)/shard_map/ppermute | solution.py:293
  34.3 8.1 %collective-permute-start.8 = (f32[200,128]{1,0:T(8,128)S(1)}, f32[200,128]{1,0:T(8,128)S(1)}, u32[]{:S(2)}, u32[]{:S(2)}) collective-permute-start(f32[200,128]{1,0:T(8,128)S(1)} %add_dynamic-update-slice_fusion.3.refs_0_), channel_id=1, source_target_pairs={{0,2},{1,3},{2,0},{3,1},{4,6},{5,7},{6,4},{7,5},{8,10},{9,11},{10,... | collective-permute-start | bytes 307208 | tf_op jit(solution)/shard_map/ppermute | solution.py:293
  34.3 8.1 %collective-permute-start.9 = (f32[200,128]{1,0:T(8,128)S(1)}, f32[200,128]{1,0:T(8,128)S(1)}, u32[]{:S(2)}, u32[]{:S(2)}) collective-permute-start(f32[200,128]{1,0:T(8,128)S(1)} %add_dynamic-update-slice_fusion.3.refs_0_), channel_id=1, source_target_pairs={{0,1},{1,0},{2,3},{3,2},{4,5},{5,4},{6,7},{7,6},{8,9},{9,8},{10,11... | collective-permute-start | bytes 307208 | tf_op jit(solution)/shard_map/ppermute | solution.py:293
  43.2 3.9 %collective-permute-start.11 = (f32[56,128]{1,0:T(8,128)S(1)}, f32[56,128]{1,0:T(8,128)S(1)}, u32[]{:S(2)}, u32[]{:S(2)}) collective-permute-start(f32[56,128]{1,0:T(8,128)S(1)} %get-tuple-element.37.refs_0_), channel_id=1, source_target_pairs={{0,8},{4,12},{8,0},{12,4},{1,9},{5,13},{9,1},{13,5},{2,10},{6,14},... | collective-permute-start | bytes 86024 | tf_op jit(solution)/shard_map/ppermute | solution.py:293
  44.8 3.3 %collective-permute-start.12 = (f32[56,128]{1,0:T(8,128)S(1)}, f32[56,128]{1,0:T(8,128)S(1)}, u32[]{:S(2)}, u32[]{:S(2)}) collective-permute-start(f32[56,128]{1,0:T(8,128)S(1)} %get-tuple-element.37.refs_0_), channel_id=1, source_target_pairs={{0,12},{4,8},{8,4},{12,0},{1,13},{5,9},{9,5},{13,1},{2,14},{6,10},... | collective-permute-start | bytes 86024 | tf_op jit(solution)/shard_map/ppermute | solution.py:293
  51.7 3.1 %collective-permute-start.13 = (f32[8,128]{1,0:T(8,128)S(1)}, f32[8,128]{1,0:T(8,128)S(1)}, u32[]{:S(2)}, u32[]{:S(2)}) collective-permute-start(f32[8,128]{1,0:T(8,128)S(1)} %get-tuple-element.45), channel_id=1, source_target_pairs={{0,20},{4,16},{8,28},{12,24},{16,4},{20,0},{24,12},{28,8},{1,21},{... | collective-permute-start | bytes 12296 | tf_op jit(solution)/shard_map/ppermute | solution.py:293
  54.8 7.6 %collective-permute-start.14 = (f32[200,128]{1,0:T(8,128)S(1)}, f32[200,128]{1,0:T(8,128)S(1)}, u32[]{:S(2)}, u32[]{:S(2)}) collective-permute-start(f32[200,128]{1,0:T(8,128)S(1)} %add_dynamic-update-slice_fusion.2.refs_0_), channel_id=1, source_target_pairs={{0,3},{1,2},{2,1},{3,0},{4,7},{5,6},{6,5},{7,4},{8,11},{9,10},{10,... | collective-permute-start | bytes 307208 | tf_op jit(solution)/shard_map/ppermute | solution.py:293
  57.3 10.0 %collective-permute-start.15 = (f32[200,128]{1,0:T(8,128)S(1)}, f32[200,128]{1,0:T(8,128)S(1)}, u32[]{:S(2)}, u32[]{:S(2)}) collective-permute-start(f32[200,128]{1,0:T(8,128)S(1)} %add_dynamic-update-slice_fusion.2.refs_0_), channel_id=1, source_target_pairs={{0,2},{1,3},{2,0},{3,1},{4,6},{5,7},{6,4},{7,5},{8,10},{9,11},{10,... | collective-permute-start | bytes 307208 | tf_op jit(solution)/shard_map/ppermute | solution.py:293
  57.6 9.6 %collective-permute-start.16 = (f32[200,128]{1,0:T(8,128)S(1)}, f32[200,128]{1,0:T(8,128)S(1)}, u32[]{:S(2)}, u32[]{:S(2)}) collective-permute-start(f32[200,128]{1,0:T(8,128)S(1)} %add_dynamic-update-slice_fusion.2.refs_0_), channel_id=1, source_target_pairs={{0,1},{1,0},{2,3},{3,2},{4,5},{5,4},{6,7},{7,6},{8,9},{9,8},{10,11... | collective-permute-start | bytes 307208 | tf_op jit(solution)/shard_map/ppermute | solution.py:293
  68.0 4.0 %collective-permute-start.18 = (f32[56,128]{1,0:T(8,128)S(1)}, f32[56,128]{1,0:T(8,128)S(1)}, u32[]{:S(2)}, u32[]{:S(2)}) collective-permute-start(f32[56,128]{1,0:T(8,128)S(1)} %get-tuple-element.46.refs_0_), channel_id=1, source_target_pairs={{0,8},{4,12},{8,0},{12,4},{1,9},{5,13},{9,1},{13,5},{2,10},{6,14},... | collective-permute-start | bytes 86024 | tf_op jit(solution)/shard_map/ppermute | solution.py:293
  68.9 3.4 %collective-permute-start.19 = (f32[56,128]{1,0:T(8,128)S(1)}, f32[56,128]{1,0:T(8,128)S(1)}, u32[]{:S(2)}, u32[]{:S(2)}) collective-permute-start(f32[56,128]{1,0:T(8,128)S(1)} %get-tuple-element.46.refs_0_), channel_id=1, source_target_pairs={{0,12},{4,8},{8,4},{12,0},{1,13},{5,9},{9,5},{13,1},{2,14},{6,10},... | collective-permute-start | bytes 86024 | tf_op jit(solution)/shard_map/ppermute | solution.py:293
  75.9 3.1 %collective-permute-start.20 = (f32[8,128]{1,0:T(8,128)S(1)}, f32[8,128]{1,0:T(8,128)S(1)}, u32[]{:S(2)}, u32[]{:S(2)}) collective-permute-start(f32[8,128]{1,0:T(8,128)S(1)} %get-tuple-element.52), channel_id=1, source_target_pairs={{0,20},{4,16},{8,28},{12,24},{16,4},{20,0},{24,12},{28,8},{1,21},{... | collective-permute-start | bytes 12296 | tf_op jit(solution)/shard_map/ppermute | solution.py:293
  79.0 7.6 %collective-permute-start.21 = (f32[200,128]{1,0:T(8,128)S(1)}, f32[200,128]{1,0:T(8,128)S(1)}, u32[]{:S(2)}, u32[]{:S(2)}) collective-permute-start(f32[200,128]{1,0:T(8,128)S(1)} %add_dynamic-update-slice_fusion.1.refs_0_), channel_id=1, source_target_pairs={{0,3},{1,2},{2,1},{3,0},{4,7},{5,6},{6,5},{7,4},{8,11},{9,10},{10,... | collective-permute-start | bytes 307208 | tf_op jit(solution)/shard_map/ppermute | solution.py:293
  80.3 9.8 %collective-permute-start.22 = (f32[200,128]{1,0:T(8,128)S(1)}, f32[200,128]{1,0:T(8,128)S(1)}, u32[]{:S(2)}, u32[]{:S(2)}) collective-permute-start(f32[200,128]{1,0:T(8,128)S(1)} %add_dynamic-update-slice_fusion.1.refs_0_), channel_id=1, source_target_pairs={{0,2},{1,3},{2,0},{3,1},{4,6},{5,7},{6,4},{7,5},{8,10},{9,11},{10,... | collective-permute-start | bytes 307208 | tf_op jit(solution)/shard_map/ppermute | solution.py:293
  80.3 9.8 %collective-permute-start.23 = (f32[200,128]{1,0:T(8,128)S(1)}, f32[200,128]{1,0:T(8,128)S(1)}, u32[]{:S(2)}, u32[]{:S(2)}) collective-permute-start(f32[200,128]{1,0:T(8,128)S(1)} %add_dynamic-update-slice_fusion.1.refs_0_), channel_id=1, source_target_pairs={{0,1},{1,0},{2,3},{3,2},{4,5},{5,4},{6,7},{7,6},{8,9},{9,8},{10,11... | collective-permute-start | bytes 307208 | tf_op jit(solution)/shard_map/ppermute | solution.py:293
  90.8 3.9 %collective-permute-start.25 = (f32[56,128]{1,0:T(8,128)S(1)}, f32[56,128]{1,0:T(8,128)S(1)}, u32[]{:S(2)}, u32[]{:S(2)}) collective-permute-start(f32[56,128]{1,0:T(8,128)S(1)} %get-tuple-element.53.refs_0_), channel_id=1, source_target_pairs={{0,8},{4,12},{8,0},{12,4},{1,9},{5,13},{9,1},{13,5},{2,10},{6,14},... | collective-permute-start | bytes 86024 | tf_op jit(solution)/shard_map/ppermute | solution.py:293
  92.0 3.3 %collective-permute-start.26 = (f32[56,128]{1,0:T(8,128)S(1)}, f32[56,128]{1,0:T(8,128)S(1)}, u32[]{:S(2)}, u32[]{:S(2)}) collective-permute-start(f32[56,128]{1,0:T(8,128)S(1)} %get-tuple-element.53.refs_0_), channel_id=1, source_target_pairs={{0,12},{4,8},{8,4},{12,0},{1,13},{5,9},{9,5},{13,1},{2,14},{6,10},... | collective-permute-start | bytes 86024 | tf_op jit(solution)/shard_map/ppermute | solution.py:293
  99.4 3.0 %collective-permute-start.27 = (f32[8,128]{1,0:T(8,128)S(1)}, f32[8,128]{1,0:T(8,128)S(1)}, u32[]{:S(2)}, u32[]{:S(2)}) collective-permute-start(f32[8,128]{1,0:T(8,128)S(1)} %get-tuple-element.59), channel_id=1, source_target_pairs={{0,20},{4,16},{8,28},{12,24},{16,4},{20,0},{24,12},{28,8},{1,21},{... | collective-permute-start | bytes 12296 | tf_op jit(solution)/shard_map/ppermute | solution.py:293
  102.5 7.6 %collective-permute-start.28 = (f32[200,128]{1,0:T(8,128)S(1)}, f32[200,128]{1,0:T(8,128)S(1)}, u32[]{:S(2)}, u32[]{:S(2)}) collective-permute-start(f32[200,128]{1,0:T(8,128)S(1)} %add_dynamic-update-slice_fusion.refs_0_), channel_id=1, source_target_pairs={{0,3},{1,2},{2,1},{3,0},{4,7},{5,6},{6,5},{7,4},{8,11},{9,10},{10,... | collective-permute-start | bytes 307208 | tf_op jit(solution)/shard_map/ppermute | solution.py:293
  103.8 9.8 %collective-permute-start.29 = (f32[200,128]{1,0:T(8,128)S(1)}, f32[200,128]{1,0:T(8,128)S(1)}, u32[]{:S(2)}, u32[]{:S(2)}) collective-permute-start(f32[200,128]{1,0:T(8,128)S(1)} %add_dynamic-update-slice_fusion.refs_0_), channel_id=1, source_target_pairs={{0,2},{1,3},{2,0},{3,1},{4,6},{5,7},{6,4},{7,5},{8,10},{9,11},{10,... | collective-permute-start | bytes 307208 | tf_op jit(solution)/shard_map/ppermute | solution.py:293
  103.8 9.8 %collective-permute-start.30 = (f32[200,128]{1,0:T(8,128)S(1)}, f32[200,128]{1,0:T(8,128)S(1)}, u32[]{:S(2)}, u32[]{:S(2)}) collective-permute-start(f32[200,128]{1,0:T(8,128)S(1)} %add_dynamic-update-slice_fusion.refs_0_), channel_id=1, source_target_pairs={{0,1},{1,0},{2,3},{3,2},{4,5},{5,4},{6,7},{7,6},{8,9},{9,8},{10,11... | collective-permute-start | bytes 307208 | tf_op jit(solution)/shard_map/ppermute | solution.py:293
  114.8 2.6 %collective-permute-start.31 = (f32[56,128]{1,0:T(8,128)S(1)}, f32[56,128]{1,0:T(8,128)S(1)}, u32[]{:S(2)}, u32[]{:S(2)}) collective-permute-start(f32[56,128]{1,0:T(8,128)S(1)} %get-tuple-element.60.refs_0_), channel_id=1, source_target_pairs={{0,4},{4,0},{8,12},{12,8},{1,5},{5,1},{9,13},{13,9},{2,6},{6,2},{1... | collective-permute-start | bytes 86024 | tf_op jit(solution)/shard_map/ppermute | solution.py:293
  114.8 3.9 %collective-permute-start.32 = (f32[56,128]{1,0:T(8,128)S(1)}, f32[56,128]{1,0:T(8,128)S(1)}, u32[]{:S(2)}, u32[]{:S(2)}) collective-permute-start(f32[56,128]{1,0:T(8,128)S(1)} %get-tuple-element.60.refs_0_), channel_id=1, source_target_pairs={{0,8},{4,12},{8,0},{12,4},{1,9},{5,13},{9,1},{13,5},{2,10},{6,14},... | collective-permute-start | bytes 86024 | tf_op jit(solution)/shard_map/ppermute | solution.py:293
  115.7 3.3 %collective-permute-start.33 = (f32[56,128]{1,0:T(8,128)S(1)}, f32[56,128]{1,0:T(8,128)S(1)}, u32[]{:S(2)}, u32[]{:S(2)}) collective-permute-start(f32[56,128]{1,0:T(8,128)S(1)} %get-tuple-element.60.refs_0_), channel_id=1, source_target_pairs={{0,12},{4,8},{8,4},{12,0},{1,13},{5,9},{9,5},{13,1},{2,14},{6,10},... | collective-permute-start | bytes 86024 | tf_op jit(solution)/shard_map/ppermute | solution.py:293
  119.3 4.3 %collective-permute-start.34 = (f32[64,1,2,32]{3,0,2,1:T(8,128)S(1)}, f32[64,1,2,32]{3,0,2,1:T(8,128)S(1)}, u32[]{:S(2)}, u32[]{:S(2)}) collective-permute-start(f32[64,1,2,32]{3,0,2,1:T(8,128)S(1)} %bitcast_add_fusion.1), channel_id=1, source_target_pairs={{0,16},{16,0},{1,17},{17,1},{2,18},{18,2},{3,19},{19,3},{4,20},{20... | collective-permute-start | bytes 49160 | tf_op jit(solution)/shard_map/ppermute | solution.py:293
  (8 other events, 98.7 us)

commit v3 on v2

--- a/solution.py
+++ b/solution.py
@@ -75,40 +75,59 @@
     return gr + STEP * (fresh_r - gr), gi + STEP * (fresh_i - gi)
 
 
-def prepare_kernel(model_ref, vis_ref, weight_ref, mt_ref, vt_ref):
-    weight = weight_ref[...]
-    for k in range(model_ref.shape[0]):
-        for p in range(2):
-            block = model_ref[k, p].astype(jnp.float32)
-            mt_ref[k, p] = (block.T * weight).astype(jnp.bfloat16)
-
-    @pl.when(pl.program_id(0) == 0)
-    def _():
-        for p in range(2):
-            vt_ref[p] = vis_ref[p].astype(jnp.float32).T * weight
-
-
-def prepare(model, vis, weight_t):
-    dirs, _, rows, cols = model.shape
-    step = 8
-    return pl.pallas_call(
-        prepare_kernel,
-        grid=(dirs // step,),
-        in_specs=[
-            pl.BlockSpec((step, 2, rows, cols), lambda n: (n, 0, 0, 0)),
-            pl.BlockSpec((2, rows, cols), lambda n: (0, 0, 0)),
-            pl.BlockSpec((cols, rows), lambda n: (0, 0)),
-        ],
-        out_specs=[
-            pl.BlockSpec((step, 2, cols, rows), lambda n: (n, 0, 0, 0)),
-            pl.BlockSpec((2, cols, rows), lambda n: (0, 0, 0)),
-        ],
-        out_shape=[
-            jax.ShapeDtypeStruct((dirs, 2, cols, rows), jnp.bfloat16),
-            jax.ShapeDtypeStruct((2, cols, rows), jnp.float32),
-        ],
-        name="prepare",
-    )(model, vis, weight_t)
+def pack_kernel(brow_ref, gains_ref, consensus_ref, dual_ref, start_ref, dual_out_ref):
+    span, dirs = gains_ref.shape[1:]
+    lanes = start_ref.shape[1]
+    depth = dirs * span // lanes
+    rows = []
+    for p in range(2):
+        target = brow_ref[0] * consensus_ref[0, p]
+        for b in range(1, consensus_ref.shape[0]):
+            target = target + brow_ref[b] * consensus_ref[b, p]
+        rows.append(target - dual_ref[p])
+    for fields, out_ref in (
+        ([gains_ref[0], gains_ref[1]] + rows, start_ref),
+        ([dual_ref[0], dual_ref[1]], dual_out_ref),
+    ):
+        plane = to_plane(fields, lanes)[:dirs]
+        for n in range(len(fields)):
+            out_ref[n * depth : (n + 1) * depth, :] = pack_plane(plane, n, span)
+
+
+def to_plane(fields, lanes):
+    x = jnp.concatenate(fields, axis=0)
+    if x.shape[0] < lanes:
+        x = jnp.concatenate([x, jnp.zeros((lanes - x.shape[0], x.shape[1]), x.dtype)], axis=0)
+    if x.shape[1] < lanes:
+        x = jnp.concatenate([x, jnp.zeros((lanes, lanes - x.shape[1]), x.dtype)], axis=1)
+    return x.T
+
+
+def prepare_kernel(rho_ref, cluster_ref, flags_ref, model_ref, vis_ref, *outs):
+    mt_ref, vt_ref, rho_rows_ref, rho_packed_ref = outs
+    dirs, _, rows, cols = model_ref.shape
+    where = lax.broadcasted_iota(jnp.int32, (1, rows), 1) // TILE
+    bands = []
+    for b in range(cols // TILE):
+        band = jnp.zeros((1, rows), jnp.float32)
+        for r in range(rows // TILE):
+            band = jnp.where(where == r, flags_ref[r, b].astype(jnp.float32), band)
+        bands.append(jnp.broadcast_to(band, (TILE, rows)))
+    weight = jnp.concatenate(bands, axis=0)
+    weight_bf16 = weight.astype(jnp.bfloat16)
+    for p in range(2):
+        vt_ref[p] = vis_ref[p].astype(jnp.float32).T * weight
+    for k in range(dirs):
+        rho_rows_ref[k : k + 1, :] = jnp.full((1, rows), rho_ref[cluster_ref[k]], jnp.float32)
+    rho_packed_ref[...] = pack_plane(rho_rows_ref[...], 0, rows * rho_packed_ref.shape[0] // dirs)
+
+    def turn(n, carry):
+        for k in range(4):
+            for p in range(2):
+                mt_ref[4 * n + k, p] = model_ref[4 * n + k, p].T * weight_bf16
+        return carry
+
+    lax.fori_loop(0, dirs // 4, turn, 0)
 
 
 def residual(mt_ref, vt_ref, grow_ref, gcol_ref, z_ref, r_ref, p_ref, ct_ref):
@@ -174,6 +193,19 @@
     out_ref[3 * dirs :, :] = jnp.zeros((8, rows), jnp.float32)
 
 
+def last_terms_kernel(ids_ref, z_ref, r_ref, *refs, span):
+    outs, all_ref = refs[:-1], refs[-1]
+    dirs, _, cols, rows = z_ref.shape
+    depth = dirs * span // rows
+    terms_kernel(z_ref, r_ref, all_ref)
+    for n, out_ref in enumerate(outs):
+        block = jnp.bitwise_xor(ids_ref[1], n)
+        for q in range(3):
+            plane = all_ref[q * dirs : (q + 1) * dirs, :]
+            out_ref[q * depth : (q + 1) * depth, :] = pack_plane(plane, block, span)
+        out_ref[3 * depth :, :] = jnp.zeros((8, rows), jnp.float32)
+
+
 def first_kernel(ids_ref, *refs, ns, nz, span):
     rows_in = refs[:nz]
     cols_in = refs[nz : nz + ns]
@@ -246,25 +278,62 @@
     own_ref[3 * depth :, :] = power
 
 
-def final_kernel(*refs, ns, scale):
-    pieces = refs[:ns]
-    g_ref, t_ref, rho_ref, out_ref = refs[ns:]
-    depth = rho_ref.shape[0]
-    power = pieces[0][3 * depth :, :]
-    for p in pieces[1:]:
-        power = power + p[3 * depth :, :]
+def last_combine_kernel(ids_ref, *refs, nz, span):
+    parts = refs[:nz]
+    g_ref, t_ref, d_ref, power_ref, mail_ref = refs[nz:]
+    dirs = g_ref.shape[0] // 2
+    depth = dirs * span // g_ref.shape[1]
+    j = ids_ref[1]
+    total = parts[0][...]
+    for p in parts[1:]:
+        total = total + p[...]
+    mail_ref[: 3 * depth, :] = total[: 3 * depth]
+    power_ref[...] = total[3 * depth :]
+    for n, ref in enumerate((g_ref, t_ref)):
+        for p in range(2):
+            at = (3 + 2 * n + p) * depth
+            plane = ref[p * dirs : (p + 1) * dirs, :]
+            mail_ref[at : at + depth, :] = pack_plane(plane, j, span)
+    mail_ref[7 * depth :, :] = d_ref[...]
+
+
+def final_kernel(ids_ref, scal_ref, *refs, ns, scale, pair, span):
+    powers = refs[:ns]
+    mails = refs[ns : ns + 1 + pair]
+    rho_ref = refs[ns + 1 + pair]
+    outs = refs[ns + 2 + pair :]
+    depth, lanes = rho_ref.shape
+    dirs = depth * lanes // span
+    power = powers[0][...]
+    for p in powers[1:]:
+        power = power + p[...]
     rho_eff = rho_ref[...] * (jnp.sum(power) * scale + EPS)
-    own = pieces[0]
-    out_ref[0:depth, :], out_ref[depth : 2 * depth, :] = solve(
-        own[0:depth, :],
-        own[depth : 2 * depth, :],
-        own[2 * depth : 3 * depth, :],
-        g_ref[0:depth, :],
-        g_ref[depth : 2 * depth, :],
-        t_ref[0:depth, :],
-        t_ref[depth : 2 * depth, :],
-        rho_eff,
-    )
+    news = []
+    for mail in mails:
+        a, cr, ci, gr, gi, tr, ti = [mail[q * depth : (q + 1) * depth, :] for q in range(7)]
+        news.append(solve(a, cr, ci, gr, gi, tr, ti, rho_eff))
+    fields = list(news[0])
+    if pair:
+        duals = [[m[q * depth : (q + 1) * depth, :] for q in (7, 8)] for m in mails]
+        first = ids_ref[2] == 0
+        coeffs, new_duals = [], []
+        for p in range(2):
+            own, other = [news[n][p] + duals[n][p] for n in range(2)]
+            low, high = jnp.where(first, own, other), jnp.where(first, other, own)
+            total = scal_ref[0] * low + scal_ref[1] * high
+            coeffs.append(total / scal_ref[2] / scal_ref[2])
+            brow = jnp.where(first, scal_ref[0], scal_ref[1])
+            new_duals.append(duals[0][p] + news[0][p] - brow * coeffs[p])
+        fields += coeffs + new_duals
+    parts = lanes // span
+    for at in range(0, len(fields), parts):
+        group = fields[at : at + parts]
+        plane = unpack_planes(group, list(range(len(group))), span)
+        plane = jnp.concatenate([plane, jnp.zeros((lanes - dirs, lanes), jnp.float32)], axis=0)
+        turned = plane.T
+        for n in range(len(group)):
+            out_ref = outs[(at + n) // 2]
+            out_ref[(at + n) % 2] = turned[n * span : (n + 1) * span, :dirs]
 
 
 SMEM = pl.BlockSpec(memory_space=pltpu.SMEM)
@@ -275,8 +344,7 @@
     return jax.ShapeDtypeStruct(shape, jnp.float32)
 
 
-def call(kernel, name, ids, args, outs, scratch=()):
-    lead = [] if ids is None else [ids]
+def call(kernel, name, lead, args, outs, scratch=()):
     return pl.pallas_call(
         kernel,
         in_specs=[SMEM] * len(lead) + [VMEM] * len(args),
@@ -293,20 +361,6 @@
     return lax.ppermute(x, axis, [(m, m ^ n) for m in range(size)])
 
 
-def to_packed(x, lanes):
-    dirs, _, span = x.shape
-    parts = lanes // span
-    x = x.reshape(parts, dirs // parts, 2, span)
-    return x.transpose(2, 1, 0, 3).reshape(2 * dirs // parts, lanes)
-
-
-def from_packed(x, span):
-    rows, lanes = x.shape
-    parts = lanes // span
-    x = x.reshape(2, rows // 2, parts, span)
-    return x.transpose(2, 1, 0, 3).reshape(parts * rows // 2, 2, span)
-
-
 def shards(vis, model, flags, gains, consensus, dual, rho, cluster):
     groups = lax.axis_size("chan")
     ns = lax.axis_size("srow")
@@ -315,80 +369,115 @@
     dirs = gains.shape[1]
     span = gains.shape[3]
     rows, cols = vis.shape[2:]
+    depth = dirs * span // rows
     i, j, f = lax.axis_index("srow"), lax.axis_index("scol"), lax.axis_index("chan")
-    ids = jnp.stack([i, j]).astype(jnp.int32)
+    ids = jnp.stack([i, j, f]).astype(jnp.int32)
+    pair = groups == 2 and order == 1
 
     table = basis_table(groups, order)
     brow = lax.dynamic_index_in_dim(table, f, 0, keepdims=False)
-    dual_own = dual[0]
-    target = jnp.einsum("b,kbcp->kcp", brow, consensus, precision=lax.Precision.HIGHEST) - dual_own
-    start = jnp.concatenate([to_packed(gains[0], rows), to_packed(target, rows)], axis=0)
-
+    start, dual_packed = call(
+        pack_kernel,
+        "pack",
+        [brow],
+        [
+            gains[0].transpose(1, 2, 0),
+            consensus.transpose(1, 2, 3, 0),
+            dual[0].transpose(1, 2, 0),
+        ],
+        [f32(4 * depth, rows), f32(2 * depth, rows)],
+    )
     row_parts = [start] + [swap(start, "scol", n) for n in range(1, nz)]
     col_parts = [start] + [swap(start, "srow", n) for n in range(1, ns)]
-
-    matches = cluster[:, None] == jnp.arange(rho.shape[0], dtype=jnp.int32)[None, :]
-    rho_dir = jnp.sum(jnp.where(matches, rho[None, :], 0.0), axis=1)
-    rho_rows = jnp.broadcast_to(rho_dir[:, None], (dirs, rows))
-    parts = rows // span
-    rho_packed = jnp.repeat(rho_dir.reshape(parts, dirs // parts).T, span, axis=1)
-    fl = flags[0].astype(jnp.float32).T
-    weight_t = jnp.repeat(jnp.repeat(fl, TILE, axis=0), TILE, axis=1)
-    mt, vt = prepare(model[0], vis[0], weight_t)
+    mt, vt, rho_rows, rho_packed = call(
+        prepare_kernel,
+        "prepare",
+        [rho, cluster, flags[0]],
+        [model[0], vis[0]],
+        [
+            jax.ShapeDtypeStruct((dirs, 2, cols, rows), jnp.bfloat16),
+            f32(2, cols, rows),
+            f32(dirs, rows),
+            f32(depth, rows),
+        ],
+    )
 
     scratch = [pltpu.VMEM((cols, 2 * dirs), jnp.float32)]
     scale = 1.0 / (groups * STATIONS * STATIONS)
-    depth = dirs * span // rows
     plane = f32(2 * dirs, rows)
     fields = [f32(dirs, 2, cols, rows), f32(2, cols, rows), f32(8, rows)]
     z, r, power, grow, gcol, trow, tcol = call(
         functools.partial(first_kernel, ns=ns, nz=nz, span=span),
         "first",
-        ids,
+        [ids],
         row_parts + col_parts + [mt, vt],
         fields + [plane, plane, plane, plane],
         scratch,
     )
-    g_packed, t_packed = start[: 2 * depth], start[2 * depth :]
     for step in range(ITERS):
+        last = step == ITERS - 1
         if groups == 2:
             power = power + swap(power, ("chan", "srow"), ns + 1)
         else:
             power = lax.psum(power, "chan")
-        partial = call(terms_kernel, "terms", None, [z, r], [f32(3 * dirs + 8, rows)])[0]
+        if last:
+            break
+        partial = call(terms_kernel, "terms", [], [z, r], [f32(3 * dirs + 8, rows)])[0]
         partial = lax.dynamic_update_slice(partial, power, (3 * dirs, 0))
+        order_z = sorted(range(1, nz), key=lambda n: (n > 2, -n))
         sums, own = call(
             functools.partial(combine_kernel, nz=nz, span=span),
             "combine",
-            ids,
-            [partial] + [swap(partial, "scol", n) for n in range(nz - 1, 0, -1)],
+            [ids],
+            [partial] + [swap(partial, "scol", n) for n in order_z],
             [f32(3 * dirs, rows), f32(3 * depth + 8, rows)],
         )
         pieces = [own] + [swap(own, "srow", n) for n in range(1, ns)]
-        if step < ITERS - 1:
-            z, r, power, grow_new, gcol_new = call(
-                functools.partial(sweep_kernel, ns=ns, span=span, scale=scale),
-                "sweep",
-                ids,
-                pieces + [sums, grow, gcol, trow, tcol, rho_rows, mt, vt],
-                fields + [plane, plane],
-                scratch,
-            )
-            grow, gcol = grow_new, gcol_new
-        g_packed = call(
-            functools.partial(final_kernel, ns=ns, scale=scale),
-            "own",
-            None,
-            pieces + [g_packed, t_packed, rho_packed],
-            [f32(2 * depth, rows)],
-        )[0]
-    g = from_packed(g_packed, span)
+        z, r, power, grow, gcol = call(
+            functools.partial(sweep_kernel, ns=ns, span=span, scale=scale),
+            "sweep",
+            [ids],
+            pieces + [sums, grow, gcol, trow, tcol, rho_rows, mt, vt],
+            fields + [plane, plane],
+            scratch,
+        )
+
+    parts = call(
+        functools.partial(last_terms_kernel, span=span),
+        "terms",
+        [ids],
+        [z, r],
+        [f32(3 * depth + 8, rows)] * nz,
+        [pltpu.VMEM((3 * dirs + 8, rows), jnp.float32)],
+    )
+    parts = [lax.dynamic_update_slice(part, power, (3 * depth, 0)) for part in parts]
+    power, mail = call(
+        functools.partial(last_combine_kernel, nz=nz, span=span),
+        "combine",
+        [ids],
+        [parts[0]] + [swap(parts[n], "scol", n) for n in range(1, nz)] + [grow, trow, dual_packed],
+        [f32(8, rows), f32(9 * depth, rows)],
+    )
+    powers = [power] + [swap(power, "srow", n) for n in range(1, ns)]
+    mails = [mail] + ([swap(mail, "chan", 1)] if pair else [])
+    gram = jnp.dot(table.T, table, precision=lax.Precision.HIGHEST)
+    factor = jnp.linalg.cholesky(gram)
+    scal = jnp.concatenate([table[:, 0], factor[:1, 0]])
+    outs = call(
+        functools.partial(final_kernel, ns=ns, scale=scale, pair=int(pair), span=span),
+        "final",
+        [ids, scal],
+        powers + mails + [rho_packed],
+        [f32(2, span, dirs)] * (3 if pair else 1),
+    )
+    outs = [x.transpose(2, 0, 1) for x in outs]
+    if pair:
+        g, coeffs, dual_new = outs
+        return (g[None], coeffs[:, None], dual_new[None])
+    g = outs[0]
+    dual_own = dual[0]
     local = brow[None, :, None, None] * (g + dual_own)[:, None, :, :]
-    if groups == 2:
-        sums = local + swap(local, "chan", 1)
-    else:
-        sums = lax.psum(local, "chan")
-    coeffs = gram_solve(table, sums)
+    coeffs = gram_solve(table, lax.psum(local, "chan"))
     dual_new = (
         dual_own + g - jnp.einsum("b,kbcp->kcp", brow, coeffs, precision=lax.Precision.HIGHEST)
     )

time: 126 us -> 112 us (0.89)
  waiting for transfers between devices: 39.8 us -> 33.4 us
  Pallas kernels: 34 us -> 30.2 us
  local copies, waits for them, and re-layouts: 9.31 us -> 7.37 us
    pallas_call x1 -> x0, Pallas kernels: 7.46 us -> none  [prepare(): pl.pallas_call(prepare_kernel, grid=(dirs // step,), in_specs=[pl.BlockSp...]
    ppermute x35, waiting for transfers between devices: 39.8 us -> 33.4 us  [swap(): return lax.ppermute(x, axis, [(m, m ^ n) for m in range(size)])]
    pallas_call x16 -> x15, Pallas kernels: 26.6 us -> 30.2 us  [call(): pl.pallas_call(kernel, in_specs=[SMEM] * len(lead) + [VMEM] * len(args),...]
    unnamed x17 -> x16, local copies, waits for them, and re-layouts: 7.69 us -> 7.29 us
  transfers between devices with their start and end apart: 35 -> 35, of which waited for: 20 -> 17; matrix products, arithmetic and copies ran while one was open for 3% -> 1% of each run, Pallas kernels for 13% -> 10%
where the time goes in v3:
time: 112 us
  starting transfers between devices  38.2 us (34%)
  waiting for transfers between devices  33.4 us (30%)
  Pallas kernels  30.2 us (27%)
  local copies, waits for them, and re-layouts  7.37 us (7%)
  between operations  2.22 us (2%)
    ppermute x35, starting transfers between devices, swap(): return lax.ppermute(x, axis, [(m, m ^ n) for m in range(size)])  38.2 us
    ppermute x35, waiting for transfers between devices, swap(): return lax.ppermute(x, axis, [(m, m ^ n) for m in range(size)])  33.4 us
    pallas_call x15, Pallas kernels, call(): pl.pallas_call(kernel, in_specs=[SMEM] * len(lead) + [VMEM] * len(args),...  30.2 us
    unnamed x16, local copies, waits for them, and re-layouts  7.29 us
  transfers between devices with their start and end apart: 35, of which 17 were waited for; matrix products, arithmetic and copies ran while one was open for 1% of the time, Pallas kernels for 10%

profile of v3, /device:TPU:0, one launch (start us, length us, event | category | flops | bytes accessed | tf_op | source)
XLA Modules:
  0.0 112.0 jit_solution(11050943245750063159)
XLA Ops:
  3.1 3.1 %collective-permute-start = (f32[64,128]{1,0:T(8,128)S(1)}, f32[64,128]{1,0:T(8,128)S(1)}, u32[]{:S(2)}, u32[]{:S(2)}) collective-permute-start(f32[64,128]{1,0:T(8,128)S(1)} %get-tuple-element.45.refs_0_.refs_4_), channel_id=1, source_target_pairs={{0,1},{1,0},{2,3},{3,2},{4,5},{5,4},{6,7},{7,6},{8,9},{9,8},{10,11... | collective-permute-start | bytes 98312 | tf_op jit(solution)/shard_map/ppermute | solution.py:361
  6.2 2.6 %collective-permute-start.1 = (f32[64,128]{1,0:T(8,128)S(1)}, f32[64,128]{1,0:T(8,128)S(1)}, u32[]{:S(2)}, u32[]{:S(2)}) collective-permute-start(f32[64,128]{1,0:T(8,128)S(1)} %get-tuple-element.45.refs_0_.refs_4_), channel_id=1, source_target_pairs={{0,2},{1,3},{2,0},{3,1},{4,6},{5,7},{6,4},{7,5},{8,10},{9,11},{10,... | collective-permute-start | bytes 98312 | tf_op jit(solution)/shard_map/ppermute | solution.py:361
  8.8 1.7 %collective-permute-start.4 = (f32[64,128]{1,0:T(8,128)S(1)}, f32[64,128]{1,0:T(8,128)S(1)}, u32[]{:S(2)}, u32[]{:S(2)}) collective-permute-start(f32[64,128]{1,0:T(8,128)S(1)} %get-tuple-element.45.refs_0_.refs_4_), channel_id=1, source_target_pairs={{0,8},{4,12},{8,0},{12,4},{1,9},{5,13},{9,1},{13,5},{2,10},{6,14},... | collective-permute-start | bytes 98312 | tf_op jit(solution)/shard_map/ppermute | solution.py:361
  10.7 2.2 %copy-done = bf16[1,64,2,128,128]{4,3,2,1,0:T(8,128)(2,1)S(1)} copy-done((bf16[1,64,2,128,128]{4,3,2,1,0:T(8,128)(2,1)S(1)}, bf16[1,64,2,128,128]{4,3,2,1,0:T(8,128)(2,1)}, u32[]{:S(2)}) %copy-start) | copy-done | bytes 4194328
  15.8 2.7 %prepare.1 = (bf16[64,2,128,128]{3,2,1,0:T(8,128)(2,1)S(1)}, f32[2,128,128]{2,1,0:T(8,128)S(1)}, f32[64,128]{1,0:T(8,128)S(1)}, f32[16,128]{1,0:T(8,128)S(1)}) custom-call(f32[8]{0:T(128)S(1)} %copy-done.6, s32[64]{0:T(128)S(1)} %copy-done.7, s32[8,8]{1,0:T(8,128)S(1)} %bitcast.29, bf16[64,2,128,128]{3,2,1,0:T(8,128)(2,1)S(1)} %bitcast.24, ...), custom_call_target="tpu_custom_call" | custom-call | tf_op jit(solution)/shard_map/prepare/pallas_call | solution.py:348
  18.5 3.7 %first.1 = (f32[64,2,128,128]{3,2,1,0:T(8,128)S(1)}, f32[2,128,128]{2,1,0:T(8,128)S(1)}, f32[8,128]{1,0:T(8,128)S(1)}, f32[128,128]{1,0:T(8,128)S(1)}, f32[128,1...) custom-call(s32[3]{0:T(128)S(1)} %pad_add_fusion.ids_ref, ...), custom_call_target="tpu_custom_call" | custom-call | tf_op jit(solution)/shard_map/first/pallas_call | solution.py:348
  22.3 1.6 %collective-permute-start.6 = (f32[8,128]{1,0:T(8,128)S(1)}, f32[8,128]{1,0:T(8,128)S(1)}, u32[]{:S(2)}, u32[]{:S(2)}) collective-permute-start(f32[8,128]{1,0:T(8,128)S(1)} %get-tuple-element.50), channel_id=1, source_target_pairs={{0,20},{4,16},{8,28},{12,24},{16,4},{20,0},{24,12},{28,8},{1,21},{... | collective-permute-start | bytes 12296 | tf_op jit(solution)/shard_map/ppermute | solution.py:361
  23.9 2.0 %terms.4 = f32[200,128]{1,0:T(8,128)S(1)} custom-call(f32[64,2,128,128]{3,2,1,0:T(8,128)S(1)} %get-tuple-element.48.z_ref, f32[2,128,128]{2,1,0:T(8,128)S(1)} %get-tuple-element.49.r_ref), custom_call_target="tpu_custom_call" | custom-call | tf_op jit(solution)/shard_map/terms/pallas_call | solution.py:348
  25.9 1.8 %collective-permute-start.7 = (f32[200,128]{1,0:T(8,128)S(1)}, f32[200,128]{1,0:T(8,128)S(1)}, u32[]{:S(2)}, u32[]{:S(2)}) collective-permute-start(f32[200,128]{1,0:T(8,128)S(1)} %add_dynamic-update-slice_fusion.2.refs_0_), channel_id=1, source_target_pairs={{0,2},{1,3},{2,0},{3,1},{4,6},{5,7},{6,4},{7,5},{8,10},{9,11},{10,... | collective-permute-start | bytes 307208 | tf_op jit(solution)/shard_map/ppermute | solution.py:361
  27.7 2.5 %collective-permute-start.8 = (f32[200,128]{1,0:T(8,128)S(1)}, f32[200,128]{1,0:T(8,128)S(1)}, u32[]{:S(2)}, u32[]{:S(2)}) collective-permute-start(f32[200,128]{1,0:T(8,128)S(1)} %add_dynamic-update-slice_fusion.2.refs_0_), channel_id=1, source_target_pairs={{0,1},{1,0},{2,3},{3,2},{4,5},{5,4},{6,7},{7,6},{8,9},{9,8},{10,11... | collective-permute-start | bytes 307208 | tf_op jit(solution)/shard_map/ppermute | solution.py:361
  30.4 4.5 %collective-permute-done.7.refs_1_ = f32[200,128]{1,0:T(8,128)S(1)} collective-permute-done((f32[200,128]{1,0:T(8,128)S(1)}, f32[200,128]{1,0:T(8,128)S(1)}, u32[]{:S(2)}, u32[]{:S(2)}) %collective-permute-start.7) | collective-permute-done | bytes 102432 | tf_op jit(solution)/shard_map/ppermute | solution.py:361
  34.9 2.5 %collective-permute-done.9.refs_3_ = f32[200,128]{1,0:T(8,128)S(1)} collective-permute-done((f32[200,128]{1,0:T(8,128)S(1)}, f32[200,128]{1,0:T(8,128)S(1)}, u32[]{:S(2)}, u32[]{:S(2)}) %collective-permute-start.9) | collective-permute-done | bytes 102432 | tf_op jit(solution)/shard_map/ppermute | solution.py:361
  38.2 1.6 %collective-permute-start.11 = (f32[56,128]{1,0:T(8,128)S(1)}, f32[56,128]{1,0:T(8,128)S(1)}, u32[]{:S(2)}, u32[]{:S(2)}) collective-permute-start(f32[56,128]{1,0:T(8,128)S(1)} %get-tuple-element.51.refs_0_), channel_id=1, source_target_pairs={{0,8},{4,12},{8,0},{12,4},{1,9},{5,13},{9,1},{13,5},{2,10},{6,14},... | collective-permute-start | bytes 86024 | tf_op jit(solution)/shard_map/ppermute | solution.py:361
  40.0 2.1 %collective-permute-done.11.refs_2_ = f32[56,128]{1,0:T(8,128)S(1)} collective-permute-done((f32[56,128]{1,0:T(8,128)S(1)}, f32[56,128]{1,0:T(8,128)S(1)}, u32[]{:S(2)}, u32[]{:S(2)}) %collective-permute-start.11) | collective-permute-done | bytes 28704 | tf_op jit(solution)/shard_map/ppermute | solution.py:361
  43.0 3.6 %sweep.3 = (f32[64,2,128,128]{3,2,1,0:T(8,128)S(1)}, f32[2,128,128]{2,1,0:T(8,128)S(1)}, f32[8,128]{1,0:T(8,128)S(1)}, f32[128,128]{1,0:T(8,128)S(1)}, f32[128,128]{1,0:T(8,128)S(1)}) custom-call(s32[3]{0:T(128)S(1)} %pad_add_fusion.ids_ref, f32[56,128]{1,0:T(8,128)S(1)} %get-tuple-element.51.refs_0_, f32[56,128]{1,0:T(8,128)S(1)} %collective-permute-done.10.refs_1_, ...), custom_call_target="tpu_custom_call" | custom-call | tf_op jit(solution)/shard_map/sweep/pallas_call | solution.py:348
  47.6 2.0 %terms.5 = f32[200,128]{1,0:T(8,128)S(1)} custom-call(f32[64,2,128,128]{3,2,1,0:T(8,128)S(1)} %get-tuple-element.58.z_ref, f32[2,128,128]{2,1,0:T(8,128)S(1)} %get-tuple-element.59.r_ref), custom_call_target="tpu_custom_call" | custom-call | tf_op jit(solution)/shard_map/terms/pallas_call | solution.py:348
  49.7 2.8 %collective-permute-start.14 = (f32[200,128]{1,0:T(8,128)S(1)}, f32[200,128]{1,0:T(8,128)S(1)}, u32[]{:S(2)}, u32[]{:S(2)}) collective-permute-start(f32[200,128]{1,0:T(8,128)S(1)} %add_dynamic-update-slice_fusion.1.refs_0_), channel_id=1, source_target_pairs={{0,2},{1,3},{2,0},{3,1},{4,6},{5,7},{6,4},{7,5},{8,10},{9,11},{10,... | collective-permute-start | bytes 307208 | tf_op jit(solution)/shard_map/ppermute | solution.py:361
  52.5 1.6 %collective-permute-start.16 = (f32[200,128]{1,0:T(8,128)S(1)}, f32[200,128]{1,0:T(8,128)S(1)}, u32[]{:S(2)}, u32[]{:S(2)}) collective-permute-start(f32[200,128]{1,0:T(8,128)S(1)} %add_dynamic-update-slice_fusion.1.refs_0_), channel_id=1, source_target_pairs={{0,3},{1,2},{2,1},{3,0},{4,7},{5,6},{6,5},{7,4},{8,11},{9,10},{10,... | collective-permute-start | bytes 307208 | tf_op jit(solution)/shard_map/ppermute | solution.py:361
  54.1 4.5 %collective-permute-done.14.refs_1_ = f32[200,128]{1,0:T(8,128)S(1)} collective-permute-done((f32[200,128]{1,0:T(8,128)S(1)}, f32[200,128]{1,0:T(8,128)S(1)}, u32[]{:S(2)}, u32[]{:S(2)}) %collective-permute-start.14) | collective-permute-done | bytes 102432 | tf_op jit(solution)/shard_map/ppermute | solution.py:361
  58.7 2.6 %collective-permute-done.16.refs_3_ = f32[200,128]{1,0:T(8,128)S(1)} collective-permute-done((f32[200,128]{1,0:T(8,128)S(1)}, f32[200,128]{1,0:T(8,128)S(1)}, u32[]{:S(2)}, u32[]{:S(2)}) %collective-permute-start.16) | collective-permute-done | bytes 102432 | tf_op jit(solution)/shard_map/ppermute | solution.py:361
  63.9 2.1 %collective-permute-done.18.refs_2_ = f32[56,128]{1,0:T(8,128)S(1)} collective-permute-done((f32[56,128]{1,0:T(8,128)S(1)}, f32[56,128]{1,0:T(8,128)S(1)}, u32[]{:S(2)}, u32[]{:S(2)}) %collective-permute-start.18) | collective-permute-done | bytes 28704 | tf_op jit(solution)/shard_map/ppermute | solution.py:361
  66.3 3.6 %sweep.4 = (f32[64,2,128,128]{3,2,1,0:T(8,128)S(1)}, f32[2,128,128]{2,1,0:T(8,128)S(1)}, f32[8,128]{1,0:T(8,128)S(1)}, f32[128,128]{1,0:T(8,128)S(1)}, f32[128,128]{1,0:T(8,128)S(1)}) custom-call(s32[3]{0:T(128)S(1)} %pad_add_fusion.ids_ref, f32[56,128]{1,0:T(8,128)S(1)} %get-tuple-element.61.refs_0_, f32[56,128]{1,0:T(8,128)S(1)} %collective-permute-done.17.refs_1_, ...), custom_call_target="tpu_custom_call" | custom-call | tf_op jit(solution)/shard_map/sweep/pallas_call | solution.py:348
  70.7 2.0 %terms.6 = f32[200,128]{1,0:T(8,128)S(1)} custom-call(f32[64,2,128,128]{3,2,1,0:T(8,128)S(1)} %get-tuple-element.65.z_ref, f32[2,128,128]{2,1,0:T(8,128)S(1)} %get-tuple-element.66.r_ref), custom_call_target="tpu_custom_call" | custom-call | tf_op jit(solution)/shard_map/terms/pallas_call | solution.py:348
  73.7 2.4 %collective-permute-start.22 = (f32[200,128]{1,0:T(8,128)S(1)}, f32[200,128]{1,0:T(8,128)S(1)}, u32[]{:S(2)}, u32[]{:S(2)}) collective-permute-start(f32[200,128]{1,0:T(8,128)S(1)} %add_dynamic-update-slice_fusion.refs_0_), channel_id=1, source_target_pairs={{0,1},{1,0},{2,3},{3,2},{4,5},{5,4},{6,7},{7,6},{8,9},{9,8},{10,11... | collective-permute-start | bytes 307208 | tf_op jit(solution)/shard_map/ppermute | solution.py:361
  77.4 4.7 %collective-permute-done.21.refs_1_ = f32[200,128]{1,0:T(8,128)S(1)} collective-permute-done((f32[200,128]{1,0:T(8,128)S(1)}, f32[200,128]{1,0:T(8,128)S(1)}, u32[]{:S(2)}, u32[]{:S(2)}) %collective-permute-start.21) | collective-permute-done | bytes 102432 | tf_op jit(solution)/shard_map/ppermute | solution.py:361
  82.1 2.5 %collective-permute-done.23.refs_3_ = f32[200,128]{1,0:T(8,128)S(1)} collective-permute-done((f32[200,128]{1,0:T(8,128)S(1)}, f32[200,128]{1,0:T(8,128)S(1)}, u32[]{:S(2)}, u32[]{:S(2)}) %collective-permute-start.23) | collective-permute-done | bytes 102432 | tf_op jit(solution)/shard_map/ppermute | solution.py:361
  87.2 2.1 %collective-permute-done.25.refs_2_ = f32[56,128]{1,0:T(8,128)S(1)} collective-permute-done((f32[56,128]{1,0:T(8,128)S(1)}, f32[56,128]{1,0:T(8,128)S(1)}, u32[]{:S(2)}, u32[]{:S(2)}) %collective-permute-start.25) | collective-permute-done | bytes 28704 | tf_op jit(solution)/shard_map/ppermute | solution.py:361
  89.8 3.6 %sweep.5 = (f32[64,2,128,128]{3,2,1,0:T(8,128)S(1)}, f32[2,128,128]{2,1,0:T(8,128)S(1)}, f32[8,128]{1,0:T(8,128)S(1)}, f32[128,128]{1,0:T(8,128)S(1)}, f32[128,128]{1,0:T(8,128)}) custom-call(s32[3]{0:T(128)S(1)} %pad_add_fusion.ids_ref, f32[56,128]{1,0:T(8,128)S(1)} %get-tuple-element.68.refs_0_, f32[56,128]{1,0:T(8,128)S(1)} %collective-permute-done.24.refs_1_, ...), custom_call_target="tpu_custom_call" | custom-call | tf_op jit(solution)/shard_map/sweep/pallas_call | solution.py:348
  94.2 2.7 %terms.7 = (f32[56,128]{1,0:T(8,128)S(1)}, f32[56,128]{1,0:T(8,128)S(1)}, f32[56,128]{1,0:T(8,128)S(1)}, f32[56,128]{1,0:T(8,128)S(1)}) custom-call(s32[3]{0:T(128)S(1)} %pad_add_fusion.ids_ref, f32[64,2,128,128]{3,2,1,0:T(8,128)S(1)} %get-tuple-element.72.z_ref, f32[2,128,128]{2,1,0:T(8,128)S(1)} %get-tuple-element.73.r_ref), custom_call_target="tpu_custom_call" | custom-call | tf_op jit(solution)/shard_map/terms/pallas_call | solution.py:348
  97.0 1.5 %collective-permute-start.28 = (f32[56,128]{1,0:T(8,128)S(1)}, f32[56,128]{1,0:T(8,128)S(1)}, u32[]{:S(2)}, u32[]{:S(2)}) collective-permute-start(f32[56,128]{1,0:T(8,128)S(1)} %get-tuple-element.90), channel_id=1, source_target_pairs={{0,1},{1,0},{2,3},{3,2},{4,5},{5,4},{6,7},{7,6},{8,9},{9,8},{10,11... | collective-permute-start | bytes 86024 | tf_op jit(solution)/shard_map/ppermute | solution.py:361
  99.2 2.2 %collective-permute-start.30 = (f32[56,128]{1,0:T(8,128)S(1)}, f32[56,128]{1,0:T(8,128)S(1)}, u32[]{:S(2)}, u32[]{:S(2)}) collective-permute-start(f32[56,128]{1,0:T(8,128)S(1)} %get-tuple-element.87), channel_id=1, source_target_pairs={{0,3},{1,2},{2,1},{3,0},{4,7},{5,6},{6,5},{7,4},{8,11},{9,10},{10,... | collective-permute-start | bytes 86024 | tf_op jit(solution)/shard_map/ppermute | solution.py:361
  101.4 2.5 %collective-permute-done.29.refs_2_ = f32[56,128]{1,0:T(8,128)S(1)} collective-permute-done((f32[56,128]{1,0:T(8,128)S(1)}, f32[56,128]{1,0:T(8,128)S(1)}, u32[]{:S(2)}, u32[]{:S(2)}) %collective-permute-start.29) | collective-permute-done | bytes 28704 | tf_op jit(solution)/shard_map/ppermute | solution.py:361
  (77 shorter events, 26.1 us)
Async XLA Ops:
  3.1 7.4 %collective-permute-start = (f32[64,128]{1,0:T(8,128)S(1)}, f32[64,128]{1,0:T(8,128)S(1)}, u32[]{:S(2)}, u32[]{:S(2)}) collective-permute-start(f32[64,128]{1,0:T(8,128)S(1)} %get-tuple-element.45.refs_0_.refs_4_), channel_id=1, source_target_pairs={{0,1},{1,0},{2,3},{3,2},{4,5},{5,4},{6,7},{7,6},{8,9},{9,8},{10,11... | collective-permute-start | bytes 98312 | tf_op jit(solution)/shard_map/ppermute | solution.py:361
  6.2 12.3 %collective-permute-start.1 = (f32[64,128]{1,0:T(8,128)S(1)}, f32[64,128]{1,0:T(8,128)S(1)}, u32[]{:S(2)}, u32[]{:S(2)}) collective-permute-start(f32[64,128]{1,0:T(8,128)S(1)} %get-tuple-element.45.refs_0_.refs_4_), channel_id=1, source_target_pairs={{0,2},{1,3},{2,0},{3,1},{4,6},{5,7},{6,4},{7,5},{8,10},{9,11},{10,... | collective-permute-start | bytes 98312 | tf_op jit(solution)/shard_map/ppermute | solution.py:361
  8.8 9.7 %collective-permute-start.2 = (f32[64,128]{1,0:T(8,128)S(1)}, f32[64,128]{1,0:T(8,128)S(1)}, u32[]{:S(2)}, u32[]{:S(2)}) collective-permute-start(f32[64,128]{1,0:T(8,128)S(1)} %get-tuple-element.45.refs_0_.refs_4_), channel_id=1, source_target_pairs={{0,3},{1,2},{2,1},{3,0},{4,7},{5,6},{6,5},{7,4},{8,11},{9,10},{10,... | collective-permute-start | bytes 98312 | tf_op jit(solution)/shard_map/ppermute | solution.py:361
  8.8 9.7 %collective-permute-start.3 = (f32[64,128]{1,0:T(8,128)S(1)}, f32[64,128]{1,0:T(8,128)S(1)}, u32[]{:S(2)}, u32[]{:S(2)}) collective-permute-start(f32[64,128]{1,0:T(8,128)S(1)} %get-tuple-element.45.refs_0_.refs_4_), channel_id=1, source_target_pairs={{0,4},{4,0},{8,12},{12,8},{1,5},{5,1},{9,13},{13,9},{2,6},{6,2},{1... | collective-permute-start | bytes 98312 | tf_op jit(solution)/shard_map/ppermute | solution.py:361
  8.8 9.7 %collective-permute-start.4 = (f32[64,128]{1,0:T(8,128)S(1)}, f32[64,128]{1,0:T(8,128)S(1)}, u32[]{:S(2)}, u32[]{:S(2)}) collective-permute-start(f32[64,128]{1,0:T(8,128)S(1)} %get-tuple-element.45.refs_0_.refs_4_), channel_id=1, source_target_pairs={{0,8},{4,12},{8,0},{12,4},{1,9},{5,13},{9,1},{13,5},{2,10},{6,14},... | collective-permute-start | bytes 98312 | tf_op jit(solution)/shard_map/ppermute | solution.py:361
  10.5 8.0 %collective-permute-start.5 = (f32[64,128]{1,0:T(8,128)S(1)}, f32[64,128]{1,0:T(8,128)S(1)}, u32[]{:S(2)}, u32[]{:S(2)}) collective-permute-start(f32[64,128]{1,0:T(8,128)S(1)} %get-tuple-element.45.refs_0_.refs_4_), channel_id=1, source_target_pairs={{0,12},{4,8},{8,4},{12,0},{1,13},{5,9},{9,5},{13,1},{2,14},{6,10},... | collective-permute-start | bytes 98312 | tf_op jit(solution)/shard_map/ppermute | solution.py:361
  22.3 3.7 %collective-permute-start.6 = (f32[8,128]{1,0:T(8,128)S(1)}, f32[8,128]{1,0:T(8,128)S(1)}, u32[]{:S(2)}, u32[]{:S(2)}) collective-permute-start(f32[8,128]{1,0:T(8,128)S(1)} %get-tuple-element.50), channel_id=1, source_target_pairs={{0,20},{4,16},{8,28},{12,24},{16,4},{20,0},{24,12},{28,8},{1,21},{... | collective-permute-start | bytes 12296 | tf_op jit(solution)/shard_map/ppermute | solution.py:361
  25.9 9.0 %collective-permute-start.7 = (f32[200,128]{1,0:T(8,128)S(1)}, f32[200,128]{1,0:T(8,128)S(1)}, u32[]{:S(2)}, u32[]{:S(2)}) collective-permute-start(f32[200,128]{1,0:T(8,128)S(1)} %add_dynamic-update-slice_fusion.2.refs_0_), channel_id=1, source_target_pairs={{0,2},{1,3},{2,0},{3,1},{4,6},{5,7},{6,4},{7,5},{8,10},{9,11},{10,... | collective-permute-start | bytes 307208 | tf_op jit(solution)/shard_map/ppermute | solution.py:361
  27.7 7.2 %collective-permute-start.8 = (f32[200,128]{1,0:T(8,128)S(1)}, f32[200,128]{1,0:T(8,128)S(1)}, u32[]{:S(2)}, u32[]{:S(2)}) collective-permute-start(f32[200,128]{1,0:T(8,128)S(1)} %add_dynamic-update-slice_fusion.2.refs_0_), channel_id=1, source_target_pairs={{0,1},{1,0},{2,3},{3,2},{4,5},{5,4},{6,7},{7,6},{8,9},{9,8},{10,11... | collective-permute-start | bytes 307208 | tf_op jit(solution)/shard_map/ppermute | solution.py:361
  30.2 7.2 %collective-permute-start.9 = (f32[200,128]{1,0:T(8,128)S(1)}, f32[200,128]{1,0:T(8,128)S(1)}, u32[]{:S(2)}, u32[]{:S(2)}) collective-permute-start(f32[200,128]{1,0:T(8,128)S(1)} %add_dynamic-update-slice_fusion.2.refs_0_), channel_id=1, source_target_pairs={{0,3},{1,2},{2,1},{3,0},{4,7},{5,6},{6,5},{7,4},{8,11},{9,10},{10,... | collective-permute-start | bytes 307208 | tf_op jit(solution)/shard_map/ppermute | solution.py:361
  38.2 3.9 %collective-permute-start.11 = (f32[56,128]{1,0:T(8,128)S(1)}, f32[56,128]{1,0:T(8,128)S(1)}, u32[]{:S(2)}, u32[]{:S(2)}) collective-permute-start(f32[56,128]{1,0:T(8,128)S(1)} %get-tuple-element.51.refs_0_), channel_id=1, source_target_pairs={{0,8},{4,12},{8,0},{12,4},{1,9},{5,13},{9,1},{13,5},{2,10},{6,14},... | collective-permute-start | bytes 86024 | tf_op jit(solution)/shard_map/ppermute | solution.py:361
  39.7 3.3 %collective-permute-start.12 = (f32[56,128]{1,0:T(8,128)S(1)}, f32[56,128]{1,0:T(8,128)S(1)}, u32[]{:S(2)}, u32[]{:S(2)}) collective-permute-start(f32[56,128]{1,0:T(8,128)S(1)} %get-tuple-element.51.refs_0_), channel_id=1, source_target_pairs={{0,12},{4,8},{8,4},{12,0},{1,13},{5,9},{9,5},{13,1},{2,14},{6,10},... | collective-permute-start | bytes 86024 | tf_op jit(solution)/shard_map/ppermute | solution.py:361
  46.6 3.1 %collective-permute-start.13 = (f32[8,128]{1,0:T(8,128)S(1)}, f32[8,128]{1,0:T(8,128)S(1)}, u32[]{:S(2)}, u32[]{:S(2)}) collective-permute-start(f32[8,128]{1,0:T(8,128)S(1)} %get-tuple-element.60), channel_id=1, source_target_pairs={{0,20},{4,16},{8,28},{12,24},{16,4},{20,0},{24,12},{28,8},{1,21},{... | collective-permute-start | bytes 12296 | tf_op jit(solution)/shard_map/ppermute | solution.py:361
  49.7 8.9 %collective-permute-start.14 = (f32[200,128]{1,0:T(8,128)S(1)}, f32[200,128]{1,0:T(8,128)S(1)}, u32[]{:S(2)}, u32[]{:S(2)}) collective-permute-start(f32[200,128]{1,0:T(8,128)S(1)} %add_dynamic-update-slice_fusion.1.refs_0_), channel_id=1, source_target_pairs={{0,2},{1,3},{2,0},{3,1},{4,6},{5,7},{6,4},{7,5},{8,10},{9,11},{10,... | collective-permute-start | bytes 307208 | tf_op jit(solution)/shard_map/ppermute | solution.py:361
  52.5 6.1 %collective-permute-start.15 = (f32[200,128]{1,0:T(8,128)S(1)}, f32[200,128]{1,0:T(8,128)S(1)}, u32[]{:S(2)}, u32[]{:S(2)}) collective-permute-start(f32[200,128]{1,0:T(8,128)S(1)} %add_dynamic-update-slice_fusion.1.refs_0_), channel_id=1, source_target_pairs={{0,1},{1,0},{2,3},{3,2},{4,5},{5,4},{6,7},{7,6},{8,9},{9,8},{10,11... | collective-permute-start | bytes 307208 | tf_op jit(solution)/shard_map/ppermute | solution.py:361
  52.5 8.8 %collective-permute-start.16 = (f32[200,128]{1,0:T(8,128)S(1)}, f32[200,128]{1,0:T(8,128)S(1)}, u32[]{:S(2)}, u32[]{:S(2)}) collective-permute-start(f32[200,128]{1,0:T(8,128)S(1)} %add_dynamic-update-slice_fusion.1.refs_0_), channel_id=1, source_target_pairs={{0,3},{1,2},{2,1},{3,0},{4,7},{5,6},{6,5},{7,4},{8,11},{9,10},{10,... | collective-permute-start | bytes 307208 | tf_op jit(solution)/shard_map/ppermute | solution.py:361
  62.0 4.0 %collective-permute-start.18 = (f32[56,128]{1,0:T(8,128)S(1)}, f32[56,128]{1,0:T(8,128)S(1)}, u32[]{:S(2)}, u32[]{:S(2)}) collective-permute-start(f32[56,128]{1,0:T(8,128)S(1)} %get-tuple-element.61.refs_0_), channel_id=1, source_target_pairs={{0,8},{4,12},{8,0},{12,4},{1,9},{5,13},{9,1},{13,5},{2,10},{6,14},... | collective-permute-start | bytes 86024 | tf_op jit(solution)/shard_map/ppermute | solution.py:361
  62.9 3.4 %collective-permute-start.19 = (f32[56,128]{1,0:T(8,128)S(1)}, f32[56,128]{1,0:T(8,128)S(1)}, u32[]{:S(2)}, u32[]{:S(2)}) collective-permute-start(f32[56,128]{1,0:T(8,128)S(1)} %get-tuple-element.61.refs_0_), channel_id=1, source_target_pairs={{0,12},{4,8},{8,4},{12,0},{1,13},{5,9},{9,5},{13,1},{2,14},{6,10},... | collective-permute-start | bytes 86024 | tf_op jit(solution)/shard_map/ppermute | solution.py:361
  69.9 3.1 %collective-permute-start.20 = (f32[8,128]{1,0:T(8,128)S(1)}, f32[8,128]{1,0:T(8,128)S(1)}, u32[]{:S(2)}, u32[]{:S(2)}) collective-permute-start(f32[8,128]{1,0:T(8,128)S(1)} %get-tuple-element.67), channel_id=1, source_target_pairs={{0,20},{4,16},{8,28},{12,24},{16,4},{20,0},{24,12},{28,8},{1,21},{... | collective-permute-start | bytes 12296 | tf_op jit(solution)/shard_map/ppermute | solution.py:361
  73.0 9.1 %collective-permute-start.21 = (f32[200,128]{1,0:T(8,128)S(1)}, f32[200,128]{1,0:T(8,128)S(1)}, u32[]{:S(2)}, u32[]{:S(2)}) collective-permute-start(f32[200,128]{1,0:T(8,128)S(1)} %add_dynamic-update-slice_fusion.refs_0_), channel_id=1, source_target_pairs={{0,2},{1,3},{2,0},{3,1},{4,6},{5,7},{6,4},{7,5},{8,10},{9,11},{10,... | collective-permute-start | bytes 307208 | tf_op jit(solution)/shard_map/ppermute | solution.py:361
  73.7 8.4 %collective-permute-start.22 = (f32[200,128]{1,0:T(8,128)S(1)}, f32[200,128]{1,0:T(8,128)S(1)}, u32[]{:S(2)}, u32[]{:S(2)}) collective-permute-start(f32[200,128]{1,0:T(8,128)S(1)} %add_dynamic-update-slice_fusion.refs_0_), channel_id=1, source_target_pairs={{0,1},{1,0},{2,3},{3,2},{4,5},{5,4},{6,7},{7,6},{8,9},{9,8},{10,11... | collective-permute-start | bytes 307208 | tf_op jit(solution)/shard_map/ppermute | solution.py:361
  76.1 8.4 %collective-permute-start.23 = (f32[200,128]{1,0:T(8,128)S(1)}, f32[200,128]{1,0:T(8,128)S(1)}, u32[]{:S(2)}, u32[]{:S(2)}) collective-permute-start(f32[200,128]{1,0:T(8,128)S(1)} %add_dynamic-update-slice_fusion.refs_0_), channel_id=1, source_target_pairs={{0,3},{1,2},{2,1},{3,0},{4,7},{5,6},{6,5},{7,4},{8,11},{9,10},{10,... | collective-permute-start | bytes 307208 | tf_op jit(solution)/shard_map/ppermute | solution.py:361
  85.3 3.9 %collective-permute-start.25 = (f32[56,128]{1,0:T(8,128)S(1)}, f32[56,128]{1,0:T(8,128)S(1)}, u32[]{:S(2)}, u32[]{:S(2)}) collective-permute-start(f32[56,128]{1,0:T(8,128)S(1)} %get-tuple-element.68.refs_0_), channel_id=1, source_target_pairs={{0,8},{4,12},{8,0},{12,4},{1,9},{5,13},{9,1},{13,5},{2,10},{6,14},... | collective-permute-start | bytes 86024 | tf_op jit(solution)/shard_map/ppermute | solution.py:361
  86.5 3.3 %collective-permute-start.26 = (f32[56,128]{1,0:T(8,128)S(1)}, f32[56,128]{1,0:T(8,128)S(1)}, u32[]{:S(2)}, u32[]{:S(2)}) collective-permute-start(f32[56,128]{1,0:T(8,128)S(1)} %get-tuple-element.68.refs_0_), channel_id=1, source_target_pairs={{0,12},{4,8},{8,4},{12,0},{1,13},{5,9},{9,5},{13,1},{2,14},{6,10},... | collective-permute-start | bytes 86024 | tf_op jit(solution)/shard_map/ppermute | solution.py:361
  93.3 3.6 %collective-permute-start.27 = (f32[8,128]{1,0:T(8,128)S(1)}, f32[8,128]{1,0:T(8,128)S(1)}, u32[]{:S(2)}, u32[]{:S(2)}) collective-permute-start(f32[8,128]{1,0:T(8,128)S(1)} %get-tuple-element.75), channel_id=1, source_target_pairs={{0,20},{4,16},{8,28},{12,24},{16,4},{20,0},{24,12},{28,8},{1,21},{... | collective-permute-start | bytes 12296 | tf_op jit(solution)/shard_map/ppermute | solution.py:361
  97.0 4.5 %collective-permute-start.28 = (f32[56,128]{1,0:T(8,128)S(1)}, f32[56,128]{1,0:T(8,128)S(1)}, u32[]{:S(2)}, u32[]{:S(2)}) collective-permute-start(f32[56,128]{1,0:T(8,128)S(1)} %get-tuple-element.90), channel_id=1, source_target_pairs={{0,1},{1,0},{2,3},{3,2},{4,5},{5,4},{6,7},{7,6},{8,9},{9,8},{10,11... | collective-permute-start | bytes 86024 | tf_op jit(solution)/shard_map/ppermute | solution.py:361
  98.5 5.4 %collective-permute-start.29 = (f32[56,128]{1,0:T(8,128)S(1)}, f32[56,128]{1,0:T(8,128)S(1)}, u32[]{:S(2)}, u32[]{:S(2)}) collective-permute-start(f32[56,128]{1,0:T(8,128)S(1)} %get-tuple-element.89), channel_id=1, source_target_pairs={{0,2},{1,3},{2,0},{3,1},{4,6},{5,7},{6,4},{7,5},{8,10},{9,11},{10,... | collective-permute-start | bytes 86024 | tf_op jit(solution)/shard_map/ppermute | solution.py:361
  99.2 5.7 %collective-permute-start.30 = (f32[56,128]{1,0:T(8,128)S(1)}, f32[56,128]{1,0:T(8,128)S(1)}, u32[]{:S(2)}, u32[]{:S(2)}) collective-permute-start(f32[56,128]{1,0:T(8,128)S(1)} %get-tuple-element.87), channel_id=1, source_target_pairs={{0,3},{1,2},{2,1},{3,0},{4,7},{5,6},{6,5},{7,4},{8,11},{9,10},{10,... | collective-permute-start | bytes 86024 | tf_op jit(solution)/shard_map/ppermute | solution.py:361
  105.5 5.0 %collective-permute-start.34 = (f32[144,128]{1,0:T(8,128)S(1)}, f32[144,128]{1,0:T(8,128)S(1)}, u32[]{:S(2)}, u32[]{:S(2)}) collective-permute-start(f32[144,128]{1,0:T(8,128)S(1)} %get-tuple-element.82.refs_4_), channel_id=1, source_target_pairs={{0,16},{16,0},{1,17},{17,1},{2,18},{18,2},{3,19},{19,3},{4,20},{20... | collective-permute-start | bytes 221192 | tf_op jit(solution)/shard_map/ppermute | solution.py:361
  106.6 3.9 %collective-permute-start.31 = (f32[8,128]{1,0:T(8,128)S(1)}, f32[8,128]{1,0:T(8,128)S(1)}, u32[]{:S(2)}, u32[]{:S(2)}) collective-permute-start(f32[8,128]{1,0:T(8,128)S(1)} %get-tuple-element.81.refs_0_), channel_id=1, source_target_pairs={{0,4},{4,0},{8,12},{12,8},{1,5},{5,1},{9,13},{13,9},{2,6},{6,2},{1... | collective-permute-start | bytes 12296 | tf_op jit(solution)/shard_map/ppermute | solution.py:361
  106.6 3.9 %collective-permute-start.32 = (f32[8,128]{1,0:T(8,128)S(1)}, f32[8,128]{1,0:T(8,128)S(1)}, u32[]{:S(2)}, u32[]{:S(2)}) collective-permute-start(f32[8,128]{1,0:T(8,128)S(1)} %get-tuple-element.81.refs_0_), channel_id=1, source_target_pairs={{0,8},{4,12},{8,0},{12,4},{1,9},{5,13},{9,1},{13,5},{2,10},{6,14},... | collective-permute-start | bytes 12296 | tf_op jit(solution)/shard_map/ppermute | solution.py:361
  107.5 3.0 %collective-permute-start.33 = (f32[8,128]{1,0:T(8,128)S(1)}, f32[8,128]{1,0:T(8,128)S(1)}, u32[]{:S(2)}, u32[]{:S(2)}) collective-permute-start(f32[8,128]{1,0:T(8,128)S(1)} %get-tuple-element.81.refs_0_), channel_id=1, source_target_pairs={{0,12},{4,8},{8,4},{12,0},{1,13},{5,9},{9,5},{13,1},{2,14},{6,10},... | collective-permute-start | bytes 12296 | tf_op jit(solution)/shard_map/ppermute | solution.py:361
  (11 other events, 13.1 us)

commit v4 on v3

--- a/solution.py
+++ b/solution.py
@@ -3,6 +3,7 @@
 
 import jax
 import jax.numpy as jnp
+import numpy as np
 from jax import lax
 from jax.experimental import pallas as pl
 from jax.experimental.pallas import tpu as pltpu
@@ -24,6 +25,14 @@
         math.comb(order - 1, b) * xval**b * (1.0 - xval) ** (order - 1 - b) for b in range(order)
     ]
     return jnp.stack(columns, axis=1)
+
+
+def pair_scalars(pair):
+    if not pair:
+        return None
+    xval = (np.arange(2, dtype=np.float32) + np.float32(0.5)) / np.float32(2)
+    column = xval**0 * (np.float32(1.0) - xval) ** 0
+    return float(column[0]), float(column[1]), float(np.sqrt(np.sum(column * column)))
 
 
 def gram_solve(table, rhs):
@@ -75,7 +84,21 @@
     return gr + STEP * (fresh_r - gr), gi + STEP * (fresh_i - gi)
 
 
-def pack_kernel(brow_ref, gains_ref, consensus_ref, dual_ref, start_ref, dual_out_ref):
+def fetch(sources, targets, sems):
+    copies = [
+        pltpu.make_async_copy(src, dst, sems.at[n])
+        for n, (src, dst) in enumerate(zip(sources, targets))
+    ]
+    for copy in copies:
+        copy.start()
+    return copies
+
+
+def pack_kernel(brow_ref, *refs):
+    start_ref, dual_out_ref = refs[3:5]
+    gains_ref, consensus_ref, dual_ref = refs[5:8]
+    for copy in fetch(refs[:3], refs[5:8], refs[8]):
+        copy.wait()
     span, dirs = gains_ref.shape[1:]
     lanes = start_ref.shape[1]
     depth = dirs * span // lanes
@@ -103,9 +126,21 @@
     return x.T
 
 
-def prepare_kernel(rho_ref, cluster_ref, flags_ref, model_ref, vis_ref, *outs):
-    mt_ref, vt_ref, rho_rows_ref, rho_packed_ref = outs
+def prepare_kernel(*refs):
+    ins = refs[:5]
+    mt_ref, vt_ref, rho_rows_ref, rho_packed_ref = refs[5:9]
+    rho_ref, cluster_ref, flags_ref, model_ref, vis_ref, sems = refs[9:]
     dirs, _, rows, cols = model_ref.shape
+    pieces = 8
+    size = dirs // pieces
+    small = fetch(ins[:3] + ins[4:], [rho_ref, cluster_ref, flags_ref, vis_ref], sems)
+    large = fetch(
+        [ins[3].at[pl.ds(n * size, size)] for n in range(pieces)],
+        [model_ref.at[pl.ds(n * size, size)] for n in range(pieces)],
+        sems.at[pl.ds(4, pieces)],
+    )
+    for copy in small:
+        copy.wait()
     where = lax.broadcasted_iota(jnp.int32, (1, rows), 1) // TILE
     bands = []
     for b in range(cols // TILE):
@@ -120,14 +155,17 @@
     for k in range(dirs):
         rho_rows_ref[k : k + 1, :] = jnp.full((1, rows), rho_ref[cluster_ref[k]], jnp.float32)
     rho_packed_ref[...] = pack_plane(rho_rows_ref[...], 0, rows * rho_packed_ref.shape[0] // dirs)
-
-    def turn(n, carry):
-        for k in range(4):
-            for p in range(2):
-                mt_ref[4 * n + k, p] = model_ref[4 * n + k, p].T * weight_bf16
-        return carry
-
-    lax.fori_loop(0, dirs // 4, turn, 0)
+    for n in range(pieces):
+        large[n].wait()
+
+        def turn(m, carry):
+            for k in range(4):
+                for p in range(2):
+                    at = n * size + 4 * m + k
+                    mt_ref[at, p] = model_ref[at, p].T * weight_bf16
+            return carry
+
+        lax.fori_loop(0, size // 4, turn, 0)
 
 
 def residual(mt_ref, vt_ref, grow_ref, gcol_ref, z_ref, r_ref, p_ref, ct_ref):
@@ -297,7 +335,7 @@
     mail_ref[7 * depth :, :] = d_ref[...]
 
 
-def final_kernel(ids_ref, scal_ref, *refs, ns, scale, pair, span):
+def final_kernel(ids_ref, *refs, ns, scale, pair, span, scal):
     powers = refs[:ns]
     mails = refs[ns : ns + 1 + pair]
     rho_ref = refs[ns + 1 + pair]
@@ -320,9 +358,9 @@
         for p in range(2):
             own, other = [news[n][p] + duals[n][p] for n in range(2)]
             low, high = jnp.where(first, own, other), jnp.where(first, other, own)
-            total = scal_ref[0] * low + scal_ref[1] * high
-            coeffs.append(total / scal_ref[2] / scal_ref[2])
-            brow = jnp.where(first, scal_ref[0], scal_ref[1])
+            total = scal[0] * low + scal[1] * high
+            coeffs.append(total / scal[2] / scal[2])
+            brow = jnp.where(first, scal[0], scal[1])
             new_duals.append(duals[0][p] + news[0][p] - brow * coeffs[p])
         fields += coeffs + new_duals
     parts = lanes // span
@@ -338,16 +376,19 @@
 
 SMEM = pl.BlockSpec(memory_space=pltpu.SMEM)
 VMEM = pl.BlockSpec(memory_space=pltpu.VMEM)
+HBM = pl.BlockSpec(memory_space=pltpu.HBM)
 
 
 def f32(*shape):
     return jax.ShapeDtypeStruct(shape, jnp.float32)
 
 
-def call(kernel, name, lead, args, outs, scratch=()):
+def call(kernel, name, lead, args, outs, scratch=(), place=VMEM):
+    if place is HBM:
+        args = [pltpu.with_memory_space_constraint(x, pltpu.HBM) for x in args]
     return pl.pallas_call(
         kernel,
-        in_specs=[SMEM] * len(lead) + [VMEM] * len(args),
+        in_specs=[SMEM] * len(lead) + [place] * len(args),
         out_specs=[VMEM] * len(outs),
         out_shape=outs,
         scratch_shapes=scratch,
@@ -376,30 +417,37 @@
 
     table = basis_table(groups, order)
     brow = lax.dynamic_index_in_dim(table, f, 0, keepdims=False)
+    own_in = [
+        gains[0].transpose(1, 2, 0),
+        consensus.transpose(1, 2, 3, 0),
+        dual[0].transpose(1, 2, 0),
+    ]
     start, dual_packed = call(
         pack_kernel,
         "pack",
         [brow],
-        [
-            gains[0].transpose(1, 2, 0),
-            consensus.transpose(1, 2, 3, 0),
-            dual[0].transpose(1, 2, 0),
-        ],
+        own_in,
         [f32(4 * depth, rows), f32(2 * depth, rows)],
+        [pltpu.VMEM(x.shape, jnp.float32) for x in own_in] + [pltpu.SemaphoreType.DMA((3,))],
+        HBM,
     )
     row_parts = [start] + [swap(start, "scol", n) for n in range(1, nz)]
     col_parts = [start] + [swap(start, "srow", n) for n in range(1, ns)]
+    field_in = [rho, cluster, flags[0], model[0], vis[0]]
     mt, vt, rho_rows, rho_packed = call(
         prepare_kernel,
         "prepare",
-        [rho, cluster, flags[0]],
-        [model[0], vis[0]],
+        [],
+        field_in,
         [
             jax.ShapeDtypeStruct((dirs, 2, cols, rows), jnp.bfloat16),
             f32(2, cols, rows),
             f32(dirs, rows),
             f32(depth, rows),
         ],
+        [(pltpu.SMEM if n < 3 else pltpu.VMEM)(x.shape, x.dtype) for n, x in enumerate(field_in)]
+        + [pltpu.SemaphoreType.DMA((12,))],
+        HBM,
     )
 
     scratch = [pltpu.VMEM((cols, 2 * dirs), jnp.float32)]
@@ -460,13 +508,12 @@
     )
     powers = [power] + [swap(power, "srow", n) for n in range(1, ns)]
     mails = [mail] + ([swap(mail, "chan", 1)] if pair else [])
-    gram = jnp.dot(table.T, table, precision=lax.Precision.HIGHEST)
-    factor = jnp.linalg.cholesky(gram)
-    scal = jnp.concatenate([table[:, 0], factor[:1, 0]])
     outs = call(
-        functools.partial(final_kernel, ns=ns, scale=scale, pair=int(pair), span=span),
+        functools.partial(
+            final_kernel, ns=ns, scale=scale, pair=int(pair), span=span, scal=pair_scalars(pair)
+        ),
         "final",
-        [ids, scal],
+        [ids],
         powers + mails + [rho_packed],
         [f32(2, span, dirs)] * (3 if pair else 1),
     )

time: 112 us -> 107 us (0.955)
  local copies, waits for them, and re-layouts: 7.37 us -> 0.01 us
  waiting for transfers between devices: 33.4 us -> 39.9 us
  starting transfers between devices: 38.2 us -> 34.5 us
  between operations: 2.22 us -> 0.8 us
  Pallas kernels: 30.2 us -> 31.5 us
    unnamed x16 -> x0, local copies, waits for them, and re-layouts: 7.29 us -> none
    ppermute x35, waiting for transfers between devices: 33.4 us -> 39.9 us  [swap(): return lax.ppermute(x, axis, [(m, m ^ n) for m in range(size)])]
    ppermute x35, starting transfers between devices: 38.2 us -> 34.5 us  [swap(): return lax.ppermute(x, axis, [(m, m ^ n) for m in range(size)])]
    pallas_call x15, Pallas kernels: 30.2 us -> 31.5 us  [call(): pl.pallas_call(kernel, in_specs=[SMEM] * len(lead) + [place] * len(args),...]
  transfers between devices with their start and end apart: 35 -> 35, of which waited for: 17 -> 25; matrix products, arithmetic and copies ran while one was open for 1% -> 0% of each run, Pallas kernels for 10% -> 11%
where the time goes in v4:
time: 107 us
  waiting for transfers between devices  39.9 us (37%)
  starting transfers between devices  34.5 us (32%)
  Pallas kernels  31.5 us (29%)
    ppermute x35, waiting for transfers between devices, swap(): return lax.ppermute(x, axis, [(m, m ^ n) for m in range(size)])  39.9 us
    ppermute x35, starting transfers between devices, swap(): return lax.ppermute(x, axis, [(m, m ^ n) for m in range(size)])  34.5 us
    pallas_call x15, Pallas kernels, call(): pl.pallas_call(kernel, in_specs=[SMEM] * len(lead) + [place] * len(args),...  31.5 us
  transfers between devices with their start and end apart: 35, of which 25 were waited for; matrix products, arithmetic and copies ran while one was open for 0% of the time, Pallas kernels for 11%

profile of v4, /device:TPU:0, one launch (start us, length us, event | category | flops | bytes accessed | tf_op | source)
XLA Modules:
  0.0 106.8 jit_solution(16859444116314292751)
XLA Ops:
  1.6 2.5 %collective-permute-start.5 = (f32[64,128]{1,0:T(8,128)S(1)}, f32[64,128]{1,0:T(8,128)S(1)}, u32[]{:S(2)}, u32[]{:S(2)}) collective-permute-start(f32[64,128]{1,0:T(8,128)S(1)} %get-tuple-element.45.refs_0_.refs_4_), channel_id=1, source_target_pairs={{0,12},{4,8},{8,4},{12,0},{1,13},{5,9},{9,5},{13,1},{2,14},{6,10},... | collective-permute-start | bytes 98312 | tf_op jit(solution)/shard_map/ppermute | solution.py:402
  4.8 3.8 %collective-permute-start.2 = (f32[64,128]{1,0:T(8,128)S(1)}, f32[64,128]{1,0:T(8,128)S(1)}, u32[]{:S(2)}, u32[]{:S(2)}) collective-permute-start(f32[64,128]{1,0:T(8,128)S(1)} %get-tuple-element.45.refs_0_.refs_4_), channel_id=1, source_target_pairs={{0,3},{1,2},{2,1},{3,0},{4,7},{5,6},{6,5},{7,4},{8,11},{9,10},{10,... | collective-permute-start | bytes 98312 | tf_op jit(solution)/shard_map/ppermute | solution.py:402
  9.3 3.2 %prepare.1 = (bf16[64,2,128,128]{3,2,1,0:T(8,128)(2,1)S(1)}, f32[2,128,128]{2,1,0:T(8,128)S(1)}, f32[64,128]{1,0:T(8,128)S(1)}, f32[16,128]{1,0:T(8,128)S(1)}) custom-call(f32[8]{0:T(128)} %refs_0_.1, s32[64]{0:T(128)} %refs_1_.1, s32[8,8]{1,0:T(8,128)} %bitcast.27, bf16[64,2,128,128]{3,2,1,0:T(8,128)(2,1)} %bitcast.22, bf16[2,128,128]{2,1,0:T(8,128)(2,1)} %bitcast.23), custom_call_target="tpu_custom_call" | custom-call | tf_op jit(solution)/shard_map/prepare/pallas_call | solution.py:389
  13.4 3.7 %first.1 = (f32[64,2,128,128]{3,2,1,0:T(8,128)S(1)}, f32[2,128,128]{2,1,0:T(8,128)S(1)}, f32[8,128]{1,0:T(8,128)S(1)}, f32[128,128]{1,0:T(8,128)S(1)}, f32[128,1...) custom-call(s32[3]{0:T(128)S(1)} %pad_add_fusion.ids_ref, ...), custom_call_target="tpu_custom_call" | custom-call | tf_op jit(solution)/shard_map/first/pallas_call | solution.py:389
  17.6 2.0 %terms.4 = f32[200,128]{1,0:T(8,128)S(1)} custom-call(f32[64,2,128,128]{3,2,1,0:T(8,128)S(1)} %get-tuple-element.48.z_ref, f32[2,128,128]{2,1,0:T(8,128)S(1)} %get-tuple-element.49.r_ref), custom_call_target="tpu_custom_call" | custom-call | tf_op jit(solution)/shard_map/terms/pallas_call | solution.py:389
  20.2 2.9 %collective-permute-start.9 = (f32[200,128]{1,0:T(8,128)S(1)}, f32[200,128]{1,0:T(8,128)S(1)}, u32[]{:S(2)}, u32[]{:S(2)}) collective-permute-start(f32[200,128]{1,0:T(8,128)S(1)} %add_dynamic-update-slice_fusion.2.refs_0_), channel_id=1, source_target_pairs={{0,3},{1,2},{2,1},{3,0},{4,7},{5,6},{6,5},{7,4},{8,11},{9,10},{10,... | collective-permute-start | bytes 307208 | tf_op jit(solution)/shard_map/ppermute | solution.py:402
  23.1 1.5 %collective-permute-start.7 = (f32[200,128]{1,0:T(8,128)S(1)}, f32[200,128]{1,0:T(8,128)S(1)}, u32[]{:S(2)}, u32[]{:S(2)}) collective-permute-start(f32[200,128]{1,0:T(8,128)S(1)} %add_dynamic-update-slice_fusion.2.refs_0_), channel_id=1, source_target_pairs={{0,2},{1,3},{2,0},{3,1},{4,6},{5,7},{6,4},{7,5},{8,10},{9,11},{10,... | collective-permute-start | bytes 307208 | tf_op jit(solution)/shard_map/ppermute | solution.py:402
  24.7 3.2 %collective-permute-done.9.refs_3_ = f32[200,128]{1,0:T(8,128)S(1)} collective-permute-done((f32[200,128]{1,0:T(8,128)S(1)}, f32[200,128]{1,0:T(8,128)S(1)}, u32[]{:S(2)}, u32[]{:S(2)}) %collective-permute-start.9) | collective-permute-done | bytes 102432 | tf_op jit(solution)/shard_map/ppermute | solution.py:402
  27.8 3.6 %collective-permute-done.8.refs_2_ = f32[200,128]{1,0:T(8,128)S(1)} collective-permute-done((f32[200,128]{1,0:T(8,128)S(1)}, f32[200,128]{1,0:T(8,128)S(1)}, u32[]{:S(2)}, u32[]{:S(2)}) %collective-permute-start.8) | collective-permute-done | bytes 102432 | tf_op jit(solution)/shard_map/ppermute | solution.py:402
  33.2 1.3 %collective-permute-start.12 = (f32[56,128]{1,0:T(8,128)S(1)}, f32[56,128]{1,0:T(8,128)S(1)}, u32[]{:S(2)}, u32[]{:S(2)}) collective-permute-start(f32[56,128]{1,0:T(8,128)S(1)} %get-tuple-element.51.refs_0_), channel_id=1, source_target_pairs={{0,12},{4,8},{8,4},{12,0},{1,13},{5,9},{9,5},{13,1},{2,14},{6,10},... | collective-permute-start | bytes 86024 | tf_op jit(solution)/shard_map/ppermute | solution.py:402
  35.2 1.4 %collective-permute-done.12.refs_3_ = f32[56,128]{1,0:T(8,128)S(1)} collective-permute-done((f32[56,128]{1,0:T(8,128)S(1)}, f32[56,128]{1,0:T(8,128)S(1)}, u32[]{:S(2)}, u32[]{:S(2)}) %collective-permute-start.12) | collective-permute-done | bytes 28704 | tf_op jit(solution)/shard_map/ppermute | solution.py:402
  36.6 1.8 %collective-permute-done.11.refs_2_ = f32[56,128]{1,0:T(8,128)S(1)} collective-permute-done((f32[56,128]{1,0:T(8,128)S(1)}, f32[56,128]{1,0:T(8,128)S(1)}, u32[]{:S(2)}, u32[]{:S(2)}) %collective-permute-start.11) | collective-permute-done | bytes 28704 | tf_op jit(solution)/shard_map/ppermute | solution.py:402
  38.4 3.6 %sweep.3 = (f32[64,2,128,128]{3,2,1,0:T(8,128)S(1)}, f32[2,128,128]{2,1,0:T(8,128)S(1)}, f32[8,128]{1,0:T(8,128)S(1)}, f32[128,128]{1,0:T(8,128)S(1)}, f32[128,128]{1,0:T(8,128)S(1)}) custom-call(s32[3]{0:T(128)S(1)} %pad_add_fusion.ids_ref, f32[56,128]{1,0:T(8,128)S(1)} %get-tuple-element.51.refs_0_, f32[56,128]{1,0:T(8,128)S(1)} %collective-permute-done.10.refs_1_, ...), custom_call_target="tpu_custom_call" | custom-call | tf_op jit(solution)/shard_map/sweep/pallas_call | solution.py:389
  42.1 2.0 %terms.5 = f32[200,128]{1,0:T(8,128)S(1)} custom-call(f32[64,2,128,128]{3,2,1,0:T(8,128)S(1)} %get-tuple-element.58.z_ref, f32[2,128,128]{2,1,0:T(8,128)S(1)} %get-tuple-element.59.r_ref), custom_call_target="tpu_custom_call" | custom-call | tf_op jit(solution)/shard_map/terms/pallas_call | solution.py:389
  45.1 1.8 %collective-permute-start.16 = (f32[200,128]{1,0:T(8,128)S(1)}, f32[200,128]{1,0:T(8,128)S(1)}, u32[]{:S(2)}, u32[]{:S(2)}) collective-permute-start(f32[200,128]{1,0:T(8,128)S(1)} %add_dynamic-update-slice_fusion.1.refs_0_), channel_id=1, source_target_pairs={{0,3},{1,2},{2,1},{3,0},{4,7},{5,6},{6,5},{7,4},{8,11},{9,10},{10,... | collective-permute-start | bytes 307208 | tf_op jit(solution)/shard_map/ppermute | solution.py:402
  46.9 2.6 %collective-permute-start.14 = (f32[200,128]{1,0:T(8,128)S(1)}, f32[200,128]{1,0:T(8,128)S(1)}, u32[]{:S(2)}, u32[]{:S(2)}) collective-permute-start(f32[200,128]{1,0:T(8,128)S(1)} %add_dynamic-update-slice_fusion.1.refs_0_), channel_id=1, source_target_pairs={{0,2},{1,3},{2,0},{3,1},{4,6},{5,7},{6,4},{7,5},{8,10},{9,11},{10,... | collective-permute-start | bytes 307208 | tf_op jit(solution)/shard_map/ppermute | solution.py:402
  49.5 3.2 %collective-permute-done.16.refs_3_ = f32[200,128]{1,0:T(8,128)S(1)} collective-permute-done((f32[200,128]{1,0:T(8,128)S(1)}, f32[200,128]{1,0:T(8,128)S(1)}, u32[]{:S(2)}, u32[]{:S(2)}) %collective-permute-start.16) | collective-permute-done | bytes 102432 | tf_op jit(solution)/shard_map/ppermute | solution.py:402
  52.7 2.5 %collective-permute-done.15.refs_2_ = f32[200,128]{1,0:T(8,128)S(1)} collective-permute-done((f32[200,128]{1,0:T(8,128)S(1)}, f32[200,128]{1,0:T(8,128)S(1)}, u32[]{:S(2)}, u32[]{:S(2)}) %collective-permute-start.15) | collective-permute-done | bytes 102432 | tf_op jit(solution)/shard_map/ppermute | solution.py:402
  58.6 1.7 %collective-permute-done.19.refs_3_ = f32[56,128]{1,0:T(8,128)S(1)} collective-permute-done((f32[56,128]{1,0:T(8,128)S(1)}, f32[56,128]{1,0:T(8,128)S(1)}, u32[]{:S(2)}, u32[]{:S(2)}) %collective-permute-start.19) | collective-permute-done | bytes 28704 | tf_op jit(solution)/shard_map/ppermute | solution.py:402
  61.1 3.6 %sweep.4 = (f32[64,2,128,128]{3,2,1,0:T(8,128)S(1)}, f32[2,128,128]{2,1,0:T(8,128)S(1)}, f32[8,128]{1,0:T(8,128)S(1)}, f32[128,128]{1,0:T(8,128)S(1)}, f32[128,128]{1,0:T(8,128)S(1)}) custom-call(s32[3]{0:T(128)S(1)} %pad_add_fusion.ids_ref, f32[56,128]{1,0:T(8,128)S(1)} %get-tuple-element.61.refs_0_, f32[56,128]{1,0:T(8,128)S(1)} %collective-permute-done.17.refs_1_, ...), custom_call_target="tpu_custom_call" | custom-call | tf_op jit(solution)/shard_map/sweep/pallas_call | solution.py:389
  64.9 2.0 %terms.6 = f32[200,128]{1,0:T(8,128)S(1)} custom-call(f32[64,2,128,128]{3,2,1,0:T(8,128)S(1)} %get-tuple-element.65.z_ref, f32[2,128,128]{2,1,0:T(8,128)S(1)} %get-tuple-element.66.r_ref), custom_call_target="tpu_custom_call" | custom-call | tf_op jit(solution)/shard_map/terms/pallas_call | solution.py:389
  67.8 2.5 %collective-permute-start.23 = (f32[200,128]{1,0:T(8,128)S(1)}, f32[200,128]{1,0:T(8,128)S(1)}, u32[]{:S(2)}, u32[]{:S(2)}) collective-permute-start(f32[200,128]{1,0:T(8,128)S(1)} %add_dynamic-update-slice_fusion.refs_0_), channel_id=1, source_target_pairs={{0,3},{1,2},{2,1},{3,0},{4,7},{5,6},{6,5},{7,4},{8,11},{9,10},{10,... | collective-permute-start | bytes 307208 | tf_op jit(solution)/shard_map/ppermute | solution.py:402
  70.3 1.9 %collective-permute-start.21 = (f32[200,128]{1,0:T(8,128)S(1)}, f32[200,128]{1,0:T(8,128)S(1)}, u32[]{:S(2)}, u32[]{:S(2)}) collective-permute-start(f32[200,128]{1,0:T(8,128)S(1)} %add_dynamic-update-slice_fusion.refs_0_), channel_id=1, source_target_pairs={{0,2},{1,3},{2,0},{3,1},{4,6},{5,7},{6,4},{7,5},{8,10},{9,11},{10,... | collective-permute-start | bytes 307208 | tf_op jit(solution)/shard_map/ppermute | solution.py:402
  72.2 3.2 %collective-permute-done.23.refs_3_ = f32[200,128]{1,0:T(8,128)S(1)} collective-permute-done((f32[200,128]{1,0:T(8,128)S(1)}, f32[200,128]{1,0:T(8,128)S(1)}, u32[]{:S(2)}, u32[]{:S(2)}) %collective-permute-start.23) | collective-permute-done | bytes 102432 | tf_op jit(solution)/shard_map/ppermute | solution.py:402
  75.3 3.5 %collective-permute-done.22.refs_2_ = f32[200,128]{1,0:T(8,128)S(1)} collective-permute-done((f32[200,128]{1,0:T(8,128)S(1)}, f32[200,128]{1,0:T(8,128)S(1)}, u32[]{:S(2)}, u32[]{:S(2)}) %collective-permute-start.22) | collective-permute-done | bytes 102432 | tf_op jit(solution)/shard_map/ppermute | solution.py:402
  82.1 1.7 %collective-permute-done.26.refs_3_ = f32[56,128]{1,0:T(8,128)S(1)} collective-permute-done((f32[56,128]{1,0:T(8,128)S(1)}, f32[56,128]{1,0:T(8,128)S(1)}, u32[]{:S(2)}, u32[]{:S(2)}) %collective-permute-start.26) | collective-permute-done | bytes 28704 | tf_op jit(solution)/shard_map/ppermute | solution.py:402
  84.8 3.6 %sweep.5 = (f32[64,2,128,128]{3,2,1,0:T(8,128)S(1)}, f32[2,128,128]{2,1,0:T(8,128)S(1)}, f32[8,128]{1,0:T(8,128)S(1)}, f32[128,128]{1,0:T(8,128)S(1)}, f32[128,128]{1,0:T(8,128)}) custom-call(s32[3]{0:T(128)S(1)} %pad_add_fusion.ids_ref, f32[56,128]{1,0:T(8,128)S(1)} %get-tuple-element.68.refs_0_, f32[56,128]{1,0:T(8,128)S(1)} %collective-permute-done.24.refs_1_, ...), custom_call_target="tpu_custom_call" | custom-call | tf_op jit(solution)/shard_map/sweep/pallas_call | solution.py:389
  88.8 2.7 %terms.7 = (f32[56,128]{1,0:T(8,128)S(1)}, f32[56,128]{1,0:T(8,128)S(1)}, f32[56,128]{1,0:T(8,128)S(1)}, f32[56,128]{1,0:T(8,128)S(1)}) custom-call(s32[3]{0:T(128)S(1)} %pad_add_fusion.ids_ref, f32[64,2,128,128]{3,2,1,0:T(8,128)S(1)} %get-tuple-element.72.z_ref, f32[2,128,128]{2,1,0:T(8,128)S(1)} %get-tuple-element.73.r_ref), custom_call_target="tpu_custom_call" | custom-call | tf_op jit(solution)/shard_map/terms/pallas_call | solution.py:389
  92.7 1.8 %collective-permute-start.28 = (f32[56,128]{1,0:T(8,128)S(1)}, f32[56,128]{1,0:T(8,128)S(1)}, u32[]{:S(2)}, u32[]{:S(2)}) collective-permute-start(f32[56,128]{1,0:T(8,128)S(1)} %get-tuple-element.90), channel_id=1, source_target_pairs={{0,1},{1,0},{2,3},{3,2},{4,5},{5,4},{6,7},{7,6},{8,9},{9,8},{10,11... | collective-permute-start | bytes 86024 | tf_op jit(solution)/shard_map/ppermute | solution.py:402
  94.6 1.4 %collective-permute-start.30 = (f32[56,128]{1,0:T(8,128)S(1)}, f32[56,128]{1,0:T(8,128)S(1)}, u32[]{:S(2)}, u32[]{:S(2)}) collective-permute-start(f32[56,128]{1,0:T(8,128)S(1)} %get-tuple-element.87), channel_id=1, source_target_pairs={{0,3},{1,2},{2,1},{3,0},{4,7},{5,6},{6,5},{7,4},{8,11},{9,10},{10,... | collective-permute-start | bytes 86024 | tf_op jit(solution)/shard_map/ppermute | solution.py:402
  96.9 3.3 %collective-permute-done.30.refs_3_ = f32[56,128]{1,0:T(8,128)S(1)} collective-permute-done((f32[56,128]{1,0:T(8,128)S(1)}, f32[56,128]{1,0:T(8,128)S(1)}, u32[]{:S(2)}, u32[]{:S(2)}) %collective-permute-start.30) | collective-permute-done | bytes 28704 | tf_op jit(solution)/shard_map/ppermute | solution.py:402
  105.3 1.5 %final.1 = (f32[2,32,64]{2,1,0:T(8,128)}, f32[2,32,64]{2,1,0:T(8,128)}, f32[2,32,64]{2,1,0:T(8,128)}) custom-call(s32[3]{0:T(128)S(1)} %pad_add_fusion.ids_ref, f32[8,128]{1,0:T(8,128)S(1)} %get-tuple-element.81.refs_0_, f32[8,128]{1,0:T(8,128)S(1)} %collective-permute-done.31.refs_1_, f32[8,128]{1,0:T(8,128)S(1)} %collective-permute-done.32.refs_2_, ...), custom_call_target="tpu_custom_call" | custom-call | tf_op jit(solution)/shard_map/final/pallas_call | solution.py:389
  (59 shorter events, 25.0 us)
Async XLA Ops:
  1.6 7.0 %collective-permute-start.5 = (f32[64,128]{1,0:T(8,128)S(1)}, f32[64,128]{1,0:T(8,128)S(1)}, u32[]{:S(2)}, u32[]{:S(2)}) collective-permute-start(f32[64,128]{1,0:T(8,128)S(1)} %get-tuple-element.45.refs_0_.refs_4_), channel_id=1, source_target_pairs={{0,12},{4,8},{8,4},{12,0},{1,13},{5,9},{9,5},{13,1},{2,14},{6,10},... | collective-permute-start | bytes 98312 | tf_op jit(solution)/shard_map/ppermute | solution.py:402
  4.1 8.3 %collective-permute-start.4 = (f32[64,128]{1,0:T(8,128)S(1)}, f32[64,128]{1,0:T(8,128)S(1)}, u32[]{:S(2)}, u32[]{:S(2)}) collective-permute-start(f32[64,128]{1,0:T(8,128)S(1)} %get-tuple-element.45.refs_0_.refs_4_), channel_id=1, source_target_pairs={{0,8},{4,12},{8,0},{12,4},{1,9},{5,13},{9,1},{13,5},{2,10},{6,14},... | collective-permute-start | bytes 98312 | tf_op jit(solution)/shard_map/ppermute | solution.py:402
  4.7 7.7 %collective-permute-start.3 = (f32[64,128]{1,0:T(8,128)S(1)}, f32[64,128]{1,0:T(8,128)S(1)}, u32[]{:S(2)}, u32[]{:S(2)}) collective-permute-start(f32[64,128]{1,0:T(8,128)S(1)} %get-tuple-element.45.refs_0_.refs_4_), channel_id=1, source_target_pairs={{0,4},{4,0},{8,12},{12,8},{1,5},{5,1},{9,13},{13,9},{2,6},{6,2},{1... | collective-permute-start | bytes 98312 | tf_op jit(solution)/shard_map/ppermute | solution.py:402
  4.8 7.7 %collective-permute-start.2 = (f32[64,128]{1,0:T(8,128)S(1)}, f32[64,128]{1,0:T(8,128)S(1)}, u32[]{:S(2)}, u32[]{:S(2)}) collective-permute-start(f32[64,128]{1,0:T(8,128)S(1)} %get-tuple-element.45.refs_0_.refs_4_), channel_id=1, source_target_pairs={{0,3},{1,2},{2,1},{3,0},{4,7},{5,6},{6,5},{7,4},{8,11},{9,10},{10,... | collective-permute-start | bytes 98312 | tf_op jit(solution)/shard_map/ppermute | solution.py:402
  8.6 4.8 %collective-permute-start.1 = (f32[64,128]{1,0:T(8,128)S(1)}, f32[64,128]{1,0:T(8,128)S(1)}, u32[]{:S(2)}, u32[]{:S(2)}) collective-permute-start(f32[64,128]{1,0:T(8,128)S(1)} %get-tuple-element.45.refs_0_.refs_4_), channel_id=1, source_target_pairs={{0,2},{1,3},{2,0},{3,1},{4,6},{5,7},{6,4},{7,5},{8,10},{9,11},{10,... | collective-permute-start | bytes 98312 | tf_op jit(solution)/shard_map/ppermute | solution.py:402
  8.6 4.8 %collective-permute-start = (f32[64,128]{1,0:T(8,128)S(1)}, f32[64,128]{1,0:T(8,128)S(1)}, u32[]{:S(2)}, u32[]{:S(2)}) collective-permute-start(f32[64,128]{1,0:T(8,128)S(1)} %get-tuple-element.45.refs_0_.refs_4_), channel_id=1, source_target_pairs={{0,1},{1,0},{2,3},{3,2},{4,5},{5,4},{6,7},{7,6},{8,9},{9,8},{10,11... | collective-permute-start | bytes 98312 | tf_op jit(solution)/shard_map/ppermute | solution.py:402
  17.1 3.1 %collective-permute-start.6 = (f32[8,128]{1,0:T(8,128)S(1)}, f32[8,128]{1,0:T(8,128)S(1)}, u32[]{:S(2)}, u32[]{:S(2)}) collective-permute-start(f32[8,128]{1,0:T(8,128)S(1)} %get-tuple-element.50), channel_id=1, source_target_pairs={{0,20},{4,16},{8,28},{12,24},{16,4},{20,0},{24,12},{28,8},{1,21},{... | collective-permute-start | bytes 12296 | tf_op jit(solution)/shard_map/ppermute | solution.py:402
  20.2 7.6 %collective-permute-start.9 = (f32[200,128]{1,0:T(8,128)S(1)}, f32[200,128]{1,0:T(8,128)S(1)}, u32[]{:S(2)}, u32[]{:S(2)}) collective-permute-start(f32[200,128]{1,0:T(8,128)S(1)} %add_dynamic-update-slice_fusion.2.refs_0_), channel_id=1, source_target_pairs={{0,3},{1,2},{2,1},{3,0},{4,7},{5,6},{6,5},{7,4},{8,11},{9,10},{10,... | collective-permute-start | bytes 307208 | tf_op jit(solution)/shard_map/ppermute | solution.py:402
  23.1 8.3 %collective-permute-start.8 = (f32[200,128]{1,0:T(8,128)S(1)}, f32[200,128]{1,0:T(8,128)S(1)}, u32[]{:S(2)}, u32[]{:S(2)}) collective-permute-start(f32[200,128]{1,0:T(8,128)S(1)} %add_dynamic-update-slice_fusion.2.refs_0_), channel_id=1, source_target_pairs={{0,1},{1,0},{2,3},{3,2},{4,5},{5,4},{6,7},{7,6},{8,9},{9,8},{10,11... | collective-permute-start | bytes 307208 | tf_op jit(solution)/shard_map/ppermute | solution.py:402
  23.1 9.4 %collective-permute-start.7 = (f32[200,128]{1,0:T(8,128)S(1)}, f32[200,128]{1,0:T(8,128)S(1)}, u32[]{:S(2)}, u32[]{:S(2)}) collective-permute-start(f32[200,128]{1,0:T(8,128)S(1)} %add_dynamic-update-slice_fusion.2.refs_0_), channel_id=1, source_target_pairs={{0,2},{1,3},{2,0},{3,1},{4,6},{5,7},{6,4},{7,5},{8,10},{9,11},{10,... | collective-permute-start | bytes 307208 | tf_op jit(solution)/shard_map/ppermute | solution.py:402
  33.2 3.4 %collective-permute-start.12 = (f32[56,128]{1,0:T(8,128)S(1)}, f32[56,128]{1,0:T(8,128)S(1)}, u32[]{:S(2)}, u32[]{:S(2)}) collective-permute-start(f32[56,128]{1,0:T(8,128)S(1)} %get-tuple-element.51.refs_0_), channel_id=1, source_target_pairs={{0,12},{4,8},{8,4},{12,0},{1,13},{5,9},{9,5},{13,1},{2,14},{6,10},... | collective-permute-start | bytes 86024 | tf_op jit(solution)/shard_map/ppermute | solution.py:402
  34.5 3.9 %collective-permute-start.11 = (f32[56,128]{1,0:T(8,128)S(1)}, f32[56,128]{1,0:T(8,128)S(1)}, u32[]{:S(2)}, u32[]{:S(2)}) collective-permute-start(f32[56,128]{1,0:T(8,128)S(1)} %get-tuple-element.51.refs_0_), channel_id=1, source_target_pairs={{0,8},{4,12},{8,0},{12,4},{1,9},{5,13},{9,1},{13,5},{2,10},{6,14},... | collective-permute-start | bytes 86024 | tf_op jit(solution)/shard_map/ppermute | solution.py:402
  35.0 3.4 %collective-permute-start.10 = (f32[56,128]{1,0:T(8,128)S(1)}, f32[56,128]{1,0:T(8,128)S(1)}, u32[]{:S(2)}, u32[]{:S(2)}) collective-permute-start(f32[56,128]{1,0:T(8,128)S(1)} %get-tuple-element.51.refs_0_), channel_id=1, source_target_pairs={{0,4},{4,0},{8,12},{12,8},{1,5},{5,1},{9,13},{13,9},{2,6},{6,2},{1... | collective-permute-start | bytes 86024 | tf_op jit(solution)/shard_map/ppermute | solution.py:402
  42.0 3.1 %collective-permute-start.13 = (f32[8,128]{1,0:T(8,128)S(1)}, f32[8,128]{1,0:T(8,128)S(1)}, u32[]{:S(2)}, u32[]{:S(2)}) collective-permute-start(f32[8,128]{1,0:T(8,128)S(1)} %get-tuple-element.60), channel_id=1, source_target_pairs={{0,20},{4,16},{8,28},{12,24},{16,4},{20,0},{24,12},{28,8},{1,21},{... | collective-permute-start | bytes 12296 | tf_op jit(solution)/shard_map/ppermute | solution.py:402
  45.1 7.6 %collective-permute-start.16 = (f32[200,128]{1,0:T(8,128)S(1)}, f32[200,128]{1,0:T(8,128)S(1)}, u32[]{:S(2)}, u32[]{:S(2)}) collective-permute-start(f32[200,128]{1,0:T(8,128)S(1)} %add_dynamic-update-slice_fusion.1.refs_0_), channel_id=1, source_target_pairs={{0,3},{1,2},{2,1},{3,0},{4,7},{5,6},{6,5},{7,4},{8,11},{9,10},{10,... | collective-permute-start | bytes 307208 | tf_op jit(solution)/shard_map/ppermute | solution.py:402
  46.9 8.3 %collective-permute-start.15 = (f32[200,128]{1,0:T(8,128)S(1)}, f32[200,128]{1,0:T(8,128)S(1)}, u32[]{:S(2)}, u32[]{:S(2)}) collective-permute-start(f32[200,128]{1,0:T(8,128)S(1)} %add_dynamic-update-slice_fusion.1.refs_0_), channel_id=1, source_target_pairs={{0,1},{1,0},{2,3},{3,2},{4,5},{5,4},{6,7},{7,6},{8,9},{9,8},{10,11... | collective-permute-start | bytes 307208 | tf_op jit(solution)/shard_map/ppermute | solution.py:402
  46.9 9.1 %collective-permute-start.14 = (f32[200,128]{1,0:T(8,128)S(1)}, f32[200,128]{1,0:T(8,128)S(1)}, u32[]{:S(2)}, u32[]{:S(2)}) collective-permute-start(f32[200,128]{1,0:T(8,128)S(1)} %add_dynamic-update-slice_fusion.1.refs_0_), channel_id=1, source_target_pairs={{0,2},{1,3},{2,0},{3,1},{4,6},{5,7},{6,4},{7,5},{8,10},{9,11},{10,... | collective-permute-start | bytes 307208 | tf_op jit(solution)/shard_map/ppermute | solution.py:402
  56.7 3.6 %collective-permute-start.19 = (f32[56,128]{1,0:T(8,128)S(1)}, f32[56,128]{1,0:T(8,128)S(1)}, u32[]{:S(2)}, u32[]{:S(2)}) collective-permute-start(f32[56,128]{1,0:T(8,128)S(1)} %get-tuple-element.61.refs_0_), channel_id=1, source_target_pairs={{0,12},{4,8},{8,4},{12,0},{1,13},{5,9},{9,5},{13,1},{2,14},{6,10},... | collective-permute-start | bytes 86024 | tf_op jit(solution)/shard_map/ppermute | solution.py:402
  57.2 3.9 %collective-permute-start.18 = (f32[56,128]{1,0:T(8,128)S(1)}, f32[56,128]{1,0:T(8,128)S(1)}, u32[]{:S(2)}, u32[]{:S(2)}) collective-permute-start(f32[56,128]{1,0:T(8,128)S(1)} %get-tuple-element.61.refs_0_), channel_id=1, source_target_pairs={{0,8},{4,12},{8,0},{12,4},{1,9},{5,13},{9,1},{13,5},{2,10},{6,14},... | collective-permute-start | bytes 86024 | tf_op jit(solution)/shard_map/ppermute | solution.py:402
  64.7 3.1 %collective-permute-start.20 = (f32[8,128]{1,0:T(8,128)S(1)}, f32[8,128]{1,0:T(8,128)S(1)}, u32[]{:S(2)}, u32[]{:S(2)}) collective-permute-start(f32[8,128]{1,0:T(8,128)S(1)} %get-tuple-element.67), channel_id=1, source_target_pairs={{0,20},{4,16},{8,28},{12,24},{16,4},{20,0},{24,12},{28,8},{1,21},{... | collective-permute-start | bytes 12296 | tf_op jit(solution)/shard_map/ppermute | solution.py:402
  67.8 7.5 %collective-permute-start.23 = (f32[200,128]{1,0:T(8,128)S(1)}, f32[200,128]{1,0:T(8,128)S(1)}, u32[]{:S(2)}, u32[]{:S(2)}) collective-permute-start(f32[200,128]{1,0:T(8,128)S(1)} %add_dynamic-update-slice_fusion.refs_0_), channel_id=1, source_target_pairs={{0,3},{1,2},{2,1},{3,0},{4,7},{5,6},{6,5},{7,4},{8,11},{9,10},{10,... | collective-permute-start | bytes 307208 | tf_op jit(solution)/shard_map/ppermute | solution.py:402
  70.3 8.6 %collective-permute-start.22 = (f32[200,128]{1,0:T(8,128)S(1)}, f32[200,128]{1,0:T(8,128)S(1)}, u32[]{:S(2)}, u32[]{:S(2)}) collective-permute-start(f32[200,128]{1,0:T(8,128)S(1)} %add_dynamic-update-slice_fusion.refs_0_), channel_id=1, source_target_pairs={{0,1},{1,0},{2,3},{3,2},{4,5},{5,4},{6,7},{7,6},{8,9},{9,8},{10,11... | collective-permute-start | bytes 307208 | tf_op jit(solution)/shard_map/ppermute | solution.py:402
  70.3 9.2 %collective-permute-start.21 = (f32[200,128]{1,0:T(8,128)S(1)}, f32[200,128]{1,0:T(8,128)S(1)}, u32[]{:S(2)}, u32[]{:S(2)}) collective-permute-start(f32[200,128]{1,0:T(8,128)S(1)} %add_dynamic-update-slice_fusion.refs_0_), channel_id=1, source_target_pairs={{0,2},{1,3},{2,0},{3,1},{4,6},{5,7},{6,4},{7,5},{8,10},{9,11},{10,... | collective-permute-start | bytes 307208 | tf_op jit(solution)/shard_map/ppermute | solution.py:402
  80.2 3.7 %collective-permute-start.26 = (f32[56,128]{1,0:T(8,128)S(1)}, f32[56,128]{1,0:T(8,128)S(1)}, u32[]{:S(2)}, u32[]{:S(2)}) collective-permute-start(f32[56,128]{1,0:T(8,128)S(1)} %get-tuple-element.68.refs_0_), channel_id=1, source_target_pairs={{0,12},{4,8},{8,4},{12,0},{1,13},{5,9},{9,5},{13,1},{2,14},{6,10},... | collective-permute-start | bytes 86024 | tf_op jit(solution)/shard_map/ppermute | solution.py:402
  81.0 3.9 %collective-permute-start.25 = (f32[56,128]{1,0:T(8,128)S(1)}, f32[56,128]{1,0:T(8,128)S(1)}, u32[]{:S(2)}, u32[]{:S(2)}) collective-permute-start(f32[56,128]{1,0:T(8,128)S(1)} %get-tuple-element.68.refs_0_), channel_id=1, source_target_pairs={{0,8},{4,12},{8,0},{12,4},{1,9},{5,13},{9,1},{13,5},{2,10},{6,14},... | collective-permute-start | bytes 86024 | tf_op jit(solution)/shard_map/ppermute | solution.py:402
  81.7 3.1 %collective-permute-start.24 = (f32[56,128]{1,0:T(8,128)S(1)}, f32[56,128]{1,0:T(8,128)S(1)}, u32[]{:S(2)}, u32[]{:S(2)}) collective-permute-start(f32[56,128]{1,0:T(8,128)S(1)} %get-tuple-element.68.refs_0_), channel_id=1, source_target_pairs={{0,4},{4,0},{8,12},{12,8},{1,5},{5,1},{9,13},{13,9},{2,6},{6,2},{1... | collective-permute-start | bytes 86024 | tf_op jit(solution)/shard_map/ppermute | solution.py:402
  88.4 3.1 %collective-permute-start.27 = (f32[8,128]{1,0:T(8,128)S(1)}, f32[8,128]{1,0:T(8,128)S(1)}, u32[]{:S(2)}, u32[]{:S(2)}) collective-permute-start(f32[8,128]{1,0:T(8,128)S(1)} %get-tuple-element.75), channel_id=1, source_target_pairs={{0,20},{4,16},{8,28},{12,24},{16,4},{20,0},{24,12},{28,8},{1,21},{... | collective-permute-start | bytes 12296 | tf_op jit(solution)/shard_map/ppermute | solution.py:402
  91.5 5.1 %collective-permute-start.29 = (f32[56,128]{1,0:T(8,128)S(1)}, f32[56,128]{1,0:T(8,128)S(1)}, u32[]{:S(2)}, u32[]{:S(2)}) collective-permute-start(f32[56,128]{1,0:T(8,128)S(1)} %get-tuple-element.89), channel_id=1, source_target_pairs={{0,2},{1,3},{2,0},{3,1},{4,6},{5,7},{6,4},{7,5},{8,10},{9,11},{10,... | collective-permute-start | bytes 86024 | tf_op jit(solution)/shard_map/ppermute | solution.py:402
  92.7 4.2 %collective-permute-start.28 = (f32[56,128]{1,0:T(8,128)S(1)}, f32[56,128]{1,0:T(8,128)S(1)}, u32[]{:S(2)}, u32[]{:S(2)}) collective-permute-start(f32[56,128]{1,0:T(8,128)S(1)} %get-tuple-element.90), channel_id=1, source_target_pairs={{0,1},{1,0},{2,3},{3,2},{4,5},{5,4},{6,7},{7,6},{8,9},{9,8},{10,11... | collective-permute-start | bytes 86024 | tf_op jit(solution)/shard_map/ppermute | solution.py:402
  94.6 5.7 %collective-permute-start.30 = (f32[56,128]{1,0:T(8,128)S(1)}, f32[56,128]{1,0:T(8,128)S(1)}, u32[]{:S(2)}, u32[]{:S(2)}) collective-permute-start(f32[56,128]{1,0:T(8,128)S(1)} %get-tuple-element.87), channel_id=1, source_target_pairs={{0,3},{1,2},{2,1},{3,0},{4,7},{5,6},{6,5},{7,4},{8,11},{9,10},{10,... | collective-permute-start | bytes 86024 | tf_op jit(solution)/shard_map/ppermute | solution.py:402
  100.9 4.4 %collective-permute-start.34 = (f32[144,128]{1,0:T(8,128)S(1)}, f32[144,128]{1,0:T(8,128)S(1)}, u32[]{:S(2)}, u32[]{:S(2)}) collective-permute-start(f32[144,128]{1,0:T(8,128)S(1)} %get-tuple-element.82.refs_4_), channel_id=1, source_target_pairs={{0,16},{16,0},{1,17},{17,1},{2,18},{18,2},{3,19},{19,3},{4,20},{20... | collective-permute-start | bytes 221192 | tf_op jit(solution)/shard_map/ppermute | solution.py:402
  101.5 3.6 %collective-permute-start.32 = (f32[8,128]{1,0:T(8,128)S(1)}, f32[8,128]{1,0:T(8,128)S(1)}, u32[]{:S(2)}, u32[]{:S(2)}) collective-permute-start(f32[8,128]{1,0:T(8,128)S(1)} %get-tuple-element.81.refs_0_), channel_id=1, source_target_pairs={{0,8},{4,12},{8,0},{12,4},{1,9},{5,13},{9,1},{13,5},{2,10},{6,14},... | collective-permute-start | bytes 12296 | tf_op jit(solution)/shard_map/ppermute | solution.py:402
  (3 other events, 8.5 us)

commit v5 on v4

--- a/solution.py
+++ b/solution.py
@@ -201,7 +201,7 @@
     p_ref[...] = lax.fori_loop(0, cols // chunk, predict, jnp.zeros(p_ref.shape, jnp.float32))
 
 
-def terms_kernel(z_ref, r_ref, out_ref):
+def normal_terms(z_ref, r_ref, out_ref):
     dirs, _, cols, rows = z_ref.shape
     group = 8
     part = 4
@@ -228,14 +228,53 @@
         return carry
 
     lax.fori_loop(0, dirs // group, terms, 0)
-    out_ref[3 * dirs :, :] = jnp.zeros((8, rows), jnp.float32)
+
+
+def own_parity(shape, span, j):
+    return lax.rem(lane_block(shape, span), 2) == lax.rem(j, 2)
+
+
+def terms_kernel(ids_ref, z_ref, r_ref, same_ref, other_ref, all_ref, *, span):
+    dirs, _, cols, rows = z_ref.shape
+    half = dirs // 2
+    normal_terms(z_ref, r_ref, all_ref)
+    mine = own_parity((half, rows), span, ids_ref[1])
+    for q in range(3):
+        low = all_ref[q * dirs : q * dirs + half, :]
+        high = pltpu.roll(all_ref[q * dirs + half : (q + 1) * dirs, :], span, 1)
+        same_ref[q * half : (q + 1) * half, :] = jnp.where(mine, low, high)
+        other_ref[q * half : (q + 1) * half, :] = jnp.where(mine, high, low)
+    for ref in (same_ref, other_ref):
+        ref[3 * half :, :] = jnp.zeros((8, rows), jnp.float32)
+
+
+def unfold(same, other, span, j):
+    mine = own_parity(same.shape, span, j)
+    low = jnp.where(mine, same, other)
+    high = pltpu.roll(jnp.where(mine, other, same), same.shape[1] - span, 1)
+    return jnp.concatenate([low, high], axis=0)
+
+
+def pack_folded(piece, j, span):
+    half, lanes = piece.shape
+    parts = lanes // span
+    depth = 2 * half // parts
+    where = lane_block((depth, lanes), span)
+    packed = None
+    for q in range(parts):
+        block = j + q * depth // half
+        at = q * depth % half
+        shift = lax.rem((q - block) * span + 2 * lanes, lanes)
+        moved = pltpu.roll(piece[at : at + depth], shift, 1)
+        packed = moved if packed is None else jnp.where(where == q, moved, packed)
+    return packed
 
 
 def last_terms_kernel(ids_ref, z_ref, r_ref, *refs, span):
     outs, all_ref = refs[:-1], refs[-1]
     dirs, _, cols, rows = z_ref.shape
     depth = dirs * span // rows
-    terms_kernel(z_ref, r_ref, all_ref)
+    normal_terms(z_ref, r_ref, all_ref)
     for n, out_ref in enumerate(outs):
         block = jnp.bitwise_xor(ids_ref[1], n)
         for q in range(3):
@@ -265,9 +304,10 @@
 
 def sweep_kernel(ids_ref, *refs, ns, span, scale):
     pieces = refs[:ns]
-    sum_ref, growin_ref, gcolin_ref, trow_ref, tcol_ref, rho_ref, mt_ref, vt_ref = refs[ns : ns + 8]
-    outs = refs[ns + 8 : ns + 11]
-    grow_ref, gcol_ref, ct_ref = refs[ns + 11 :]
+    same_ref, other_ref, growin_ref, gcolin_ref, trow_ref, tcol_ref = refs[ns : ns + 6]
+    rho_ref, mt_ref, vt_ref = refs[ns + 6 : ns + 9]
+    outs = refs[ns + 9 : ns + 12]
+    grow_ref, gcol_ref, ct_ref = refs[ns + 12 :]
     dirs = mt_ref.shape[0]
     i = ids_ref[0]
     depth = dirs * span // mt_ref.shape[3]
@@ -276,15 +316,18 @@
         power = power + p[3 * depth :, :]
     rho_eff = rho_ref[...] * (jnp.sum(power) * scale + EPS)
     re, im = slice(0, dirs), slice(dirs, 2 * dirs)
+    half = dirs // 2
+    a, cr, ci = [
+        unfold(
+            same_ref[q * half : (q + 1) * half, :],
+            other_ref[q * half : (q + 1) * half, :],
+            span,
+            ids_ref[1],
+        )
+        for q in range(3)
+    ]
     grow_ref[re, :], grow_ref[im, :] = solve(
-        sum_ref[0:dirs, :],
-        sum_ref[dirs : 2 * dirs, :],
-        sum_ref[2 * dirs : 3 * dirs, :],
-        growin_ref[re, :],
-        growin_ref[im, :],
-        trow_ref[re, :],
-        trow_ref[im, :],
-        rho_eff,
+        a, cr, ci, growin_ref[re, :], growin_ref[im, :], trow_ref[re, :], trow_ref[im, :], rho_eff
     )
     blocks = [jnp.bitwise_xor(i, n) for n in range(ns)]
     a, cr, ci = [
@@ -299,21 +342,17 @@
 
 def combine_kernel(ids_ref, *refs, nz, span):
     parts = refs[:nz]
-    sum_ref, own_ref = refs[nz:]
-    dirs = sum_ref.shape[0] // 3
-    j = ids_ref[1]
-    depth = dirs * span // sum_ref.shape[1]
+    pair_ref, own_ref = refs[nz:]
+    half = pair_ref.shape[0] // 3
+    depth = 2 * half * span // pair_ref.shape[1]
+    total = parts[0][...]
+    for p in parts[1:]:
+        total = total + p[...]
+    pair_ref[...] = total[: 3 * half]
     for q in range(3):
-        at = slice(q * dirs, (q + 1) * dirs)
-        total = parts[0][at, :]
-        for p in parts[1:]:
-            total = total + p[at, :]
-        sum_ref[at, :] = total
-        own_ref[q * depth : (q + 1) * depth, :] = pack_plane(total, j, span)
-    power = parts[0][3 * dirs :, :]
-    for p in parts[1:]:
-        power = power + p[3 * dirs :, :]
-    own_ref[3 * depth :, :] = power
+        piece = total[q * half : (q + 1) * half]
+        own_ref[q * depth : (q + 1) * depth, :] = pack_folded(piece, ids_ref[1], span)
+    own_ref[3 * depth :, :] = total[3 * half :]
 
 
 def last_combine_kernel(ids_ref, *refs, nz, span):
@@ -470,22 +509,31 @@
             power = lax.psum(power, "chan")
         if last:
             break
-        partial = call(terms_kernel, "terms", [], [z, r], [f32(3 * dirs + 8, rows)])[0]
-        partial = lax.dynamic_update_slice(partial, power, (3 * dirs, 0))
-        order_z = sorted(range(1, nz), key=lambda n: (n > 2, -n))
-        sums, own = call(
+        half = 3 * dirs // 2
+        same, other = call(
+            functools.partial(terms_kernel, span=span),
+            "terms",
+            [ids],
+            [z, r],
+            [f32(half + 8, rows)] * 2,
+            [pltpu.VMEM((3 * dirs, rows), jnp.float32)],
+        )
+        same = lax.dynamic_update_slice(same, power, (half, 0))
+        other = lax.dynamic_update_slice(other, power, (half, 0))
+        pair_sums, own = call(
             functools.partial(combine_kernel, nz=nz, span=span),
             "combine",
             [ids],
-            [partial] + [swap(partial, "scol", n) for n in order_z],
-            [f32(3 * dirs, rows), f32(3 * depth + 8, rows)],
+            [same] + [swap(same if n % 2 == 0 else other, "scol", n) for n in range(1, nz)],
+            [f32(half, rows), f32(3 * depth + 8, rows)],
         )
+        other_sums = swap(pair_sums, "scol", 1)
         pieces = [own] + [swap(own, "srow", n) for n in range(1, ns)]
         z, r, power, grow, gcol = call(
             functools.partial(sweep_kernel, ns=ns, span=span, scale=scale),
             "sweep",
             [ids],
-            pieces + [sums, grow, gcol, trow, tcol, rho_rows, mt, vt],
+            pieces + [pair_sums, other_sums, grow, gcol, trow, tcol, rho_rows, mt, vt],
             fields + [plane, plane],
             scratch,
         )
@@ -496,7 +544,7 @@
         [ids],
         [z, r],
         [f32(3 * depth + 8, rows)] * nz,
-        [pltpu.VMEM((3 * dirs + 8, rows), jnp.float32)],
+        [pltpu.VMEM((3 * dirs, rows), jnp.float32)],
     )
     parts = [lax.dynamic_update_slice(part, power, (3 * depth, 0)) for part in parts]
     power, mail = call(

time: 107 us -> 100 us (0.935)
  waiting for transfers between devices: 39.9 us -> 25.7 us
  starting transfers between devices: 34.5 us -> 40.1 us
  Pallas kernels: 31.5 us -> 33.4 us
    ppermute x35 -> x38, waiting for transfers between devices: 39.9 us -> 25.7 us  [swap(): return lax.ppermute(x, axis, [(m, m ^ n) for m in range(size)])]
    ppermute x35 -> x38, starting transfers between devices: 34.5 us -> 40.1 us  [swap(): return lax.ppermute(x, axis, [(m, m ^ n) for m in range(size)])]
    pallas_call x15, Pallas kernels: 31.5 us -> 33.4 us  [call(): pl.pallas_call(kernel, in_specs=[SMEM] * len(lead) + [place] * len(args),...]
  transfers between devices with their start and end apart: 35 -> 38, of which waited for: 25 -> 21; matrix products, arithmetic and copies ran while one was open for 0% -> 0% of each run, Pallas kernels for 11% -> 14%
where the time goes in v5:
time: 100 us
  starting transfers between devices  40.1 us (40%)
  Pallas kernels  33.4 us (33%)
  waiting for transfers between devices  25.7 us (26%)
    ppermute x38, starting transfers between devices, swap(): return lax.ppermute(x, axis, [(m, m ^ n) for m in range(size)])  40.1 us
    pallas_call x15, Pallas kernels, call(): pl.pallas_call(kernel, in_specs=[SMEM] * len(lead) + [place] * len(args),...  33.4 us
    ppermute x38, waiting for transfers between devices, swap(): return lax.ppermute(x, axis, [(m, m ^ n) for m in range(size)])  25.7 us
  transfers between devices with their start and end apart: 38, of which 21 were waited for; matrix products, arithmetic and copies ran while one was open for 0% of the time, Pallas kernels for 14%

profile of v5, /device:TPU:0, one launch (start us, length us, event | category | flops | bytes accessed | tf_op | source)
XLA Modules:
  0.0 100.1 jit_solution(12248426844466066314)
XLA Ops:
  1.6 2.5 %collective-permute-start.5 = (f32[64,128]{1,0:T(8,128)S(1)}, f32[64,128]{1,0:T(8,128)S(1)}, u32[]{:S(2)}, u32[]{:S(2)}) collective-permute-start(f32[64,128]{1,0:T(8,128)S(1)} %get-tuple-element.51.refs_0_.refs_4_), channel_id=1, source_target_pairs={{0,12},{4,8},{8,4},{12,0},{1,13},{5,9},{9,5},{13,1},{2,14},{6,10},... | collective-permute-start | bytes 98312 | tf_op jit(solution)/shard_map/ppermute | solution.py:441
  4.8 3.8 %collective-permute-start.2 = (f32[64,128]{1,0:T(8,128)S(1)}, f32[64,128]{1,0:T(8,128)S(1)}, u32[]{:S(2)}, u32[]{:S(2)}) collective-permute-start(f32[64,128]{1,0:T(8,128)S(1)} %get-tuple-element.51.refs_0_.refs_4_), channel_id=1, source_target_pairs={{0,3},{1,2},{2,1},{3,0},{4,7},{5,6},{6,5},{7,4},{8,11},{9,10},{10,... | collective-permute-start | bytes 98312 | tf_op jit(solution)/shard_map/ppermute | solution.py:441
  9.3 3.2 %prepare.1 = (bf16[64,2,128,128]{3,2,1,0:T(8,128)(2,1)S(1)}, f32[2,128,128]{2,1,0:T(8,128)S(1)}, f32[64,128]{1,0:T(8,128)S(1)}, f32[16,128]{1,0:T(8,128)S(1)}) custom-call(f32[8]{0:T(128)} %refs_0_.1, s32[64]{0:T(128)} %refs_1_.1, s32[8,8]{1,0:T(8,128)} %bitcast.27, bf16[64,2,128,128]{3,2,1,0:T(8,128)(2,1)} %bitcast.22, bf16[2,128,128]{2,1,0:T(8,128)(2,1)} %bitcast.23), custom_call_target="tpu_custom_call" | custom-call | tf_op jit(solution)/shard_map/prepare/pallas_call | solution.py:428
  13.4 3.7 %first.1 = (f32[64,2,128,128]{3,2,1,0:T(8,128)S(1)}, f32[2,128,128]{2,1,0:T(8,128)S(1)}, f32[8,128]{1,0:T(8,128)S(1)}, f32[128,128]{1,0:T(8,128)S(1)}, f32[128,1...) custom-call(s32[3]{0:T(128)S(1)} %pad_add_fusion.ids_ref, ...), custom_call_target="tpu_custom_call" | custom-call | tf_op jit(solution)/shard_map/first/pallas_call | solution.py:428
  17.6 2.6 %terms.4 = (f32[104,128]{1,0:T(8,128)S(1)}, f32[104,128]{1,0:T(8,128)S(1)}) custom-call(s32[3]{0:T(128)S(1)} %pad_add_fusion.ids_ref, f32[64,2,128,128]{3,2,1,0:T(8,128)S(1)} %get-tuple-element.54.z_ref, f32[2,128,128]{2,1,0:T(8,128)S(1)} %get-tuple-element.55.r_ref), custom_call_target="tpu_custom_call" | custom-call | tf_op jit(solution)/shard_map/terms/pallas_call | solution.py:428
  20.2 3.1 %collective-permute-start.9 = (f32[104,128]{1,0:T(8,128)S(1)}, f32[104,128]{1,0:T(8,128)S(1)}, u32[]{:S(2)}, u32[]{:S(2)}) collective-permute-start(f32[104,128]{1,0:T(8,128)S(1)} %get-tuple-element.105), channel_id=1, source_target_pairs={{0,3},{1,2},{2,1},{3,0},{4,7},{5,6},{6,5},{7,4},{8,11},{9,10},{10,... | collective-permute-start | bytes 159752 | tf_op jit(solution)/shard_map/ppermute | solution.py:441
  23.3 1.3 %collective-permute-start.8 = (f32[104,128]{1,0:T(8,128)S(1)}, f32[104,128]{1,0:T(8,128)S(1)}, u32[]{:S(2)}, u32[]{:S(2)}) collective-permute-start(f32[104,128]{1,0:T(8,128)S(1)} %get-tuple-element.106.refs_0_), channel_id=1, source_target_pairs={{0,2},{1,3},{2,0},{3,1},{4,6},{5,7},{6,4},{7,5},{8,10},{9,11},{10,... | collective-permute-start | bytes 159752 | tf_op jit(solution)/shard_map/ppermute | solution.py:441
  24.7 1.8 %collective-permute-done.9.refs_3_ = f32[104,128]{1,0:T(8,128)S(1)} collective-permute-done((f32[104,128]{1,0:T(8,128)S(1)}, f32[104,128]{1,0:T(8,128)S(1)}, u32[]{:S(2)}, u32[]{:S(2)}) %collective-permute-start.9) | collective-permute-done | bytes 53280 | tf_op jit(solution)/shard_map/ppermute | solution.py:441
  26.5 2.7 %collective-permute-done.7.refs_1_ = f32[104,128]{1,0:T(8,128)S(1)} collective-permute-done((f32[104,128]{1,0:T(8,128)S(1)}, f32[104,128]{1,0:T(8,128)S(1)}, u32[]{:S(2)}, u32[]{:S(2)}) %collective-permute-start.7) | collective-permute-done | bytes 53280 | tf_op jit(solution)/shard_map/ppermute | solution.py:441
  29.9 1.4 %collective-permute-start.13 = (f32[96,128]{1,0:T(8,128)S(1)}, f32[96,128]{1,0:T(8,128)S(1)}, u32[]{:S(2)}, u32[]{:S(2)}) collective-permute-start(f32[96,128]{1,0:T(8,128)S(1)} %get-tuple-element.60.refs_4_), channel_id=1, source_target_pairs={{0,1},{1,0},{2,3},{3,2},{4,5},{5,4},{6,7},{7,6},{8,9},{9,8},{10,11... | collective-permute-start | bytes 147464 | tf_op jit(solution)/shard_map/ppermute | solution.py:441
  33.1 1.7 %collective-permute-done.12.refs_3_ = f32[56,128]{1,0:T(8,128)S(1)} collective-permute-done((f32[56,128]{1,0:T(8,128)S(1)}, f32[56,128]{1,0:T(8,128)S(1)}, u32[]{:S(2)}, u32[]{:S(2)}) %collective-permute-start.12) | collective-permute-done | bytes 28704 | tf_op jit(solution)/shard_map/ppermute | solution.py:441
  34.8 1.3 %collective-permute-done.11.refs_2_ = f32[56,128]{1,0:T(8,128)S(1)} collective-permute-done((f32[56,128]{1,0:T(8,128)S(1)}, f32[56,128]{1,0:T(8,128)S(1)}, u32[]{:S(2)}, u32[]{:S(2)}) %collective-permute-start.11) | collective-permute-done | bytes 28704 | tf_op jit(solution)/shard_map/ppermute | solution.py:441
  36.1 3.6 %sweep.3 = (f32[64,2,128,128]{3,2,1,0:T(8,128)S(1)}, f32[2,128,128]{2,1,0:T(8,128)S(1)}, f32[8,128]{1,0:T(8,128)S(1)}, f32[128,128]{1,0:T(8,128)S(1)}, f32[128,128]{1,0:T(8,128)S(1)}) custom-call(s32[3]{0:T(128)S(1)} %pad_add_fusion.ids_ref, f32[56,128]{1,0:T(8,128)S(1)} %get-tuple-element.59.refs_0_, f32[56,128]{1,0:T(8,128)S(1)} %collective-permute-done.10.refs_1_, ...), custom_call_target="tpu_custom_call" | custom-call | tf_op jit(solution)/shard_map/sweep/pallas_call | solution.py:428
  40.0 2.6 %terms.5 = (f32[104,128]{1,0:T(8,128)S(1)}, f32[104,128]{1,0:T(8,128)S(1)}) custom-call(s32[3]{0:T(128)S(1)} %pad_add_fusion.ids_ref, f32[64,2,128,128]{3,2,1,0:T(8,128)S(1)} %get-tuple-element.66.z_ref, f32[2,128,128]{2,1,0:T(8,128)S(1)} %get-tuple-element.67.r_ref), custom_call_target="tpu_custom_call" | custom-call | tf_op jit(solution)/shard_map/terms/pallas_call | solution.py:428
  42.8 1.8 %collective-permute-start.17 = (f32[104,128]{1,0:T(8,128)S(1)}, f32[104,128]{1,0:T(8,128)S(1)}, u32[]{:S(2)}, u32[]{:S(2)}) collective-permute-start(f32[104,128]{1,0:T(8,128)S(1)} %get-tuple-element.103), channel_id=1, source_target_pairs={{0,3},{1,2},{2,1},{3,0},{4,7},{5,6},{6,5},{7,4},{8,11},{9,10},{10,... | collective-permute-start | bytes 159752 | tf_op jit(solution)/shard_map/ppermute | solution.py:441
  45.1 2.1 %collective-permute-start.16 = (f32[104,128]{1,0:T(8,128)S(1)}, f32[104,128]{1,0:T(8,128)S(1)}, u32[]{:S(2)}, u32[]{:S(2)}) collective-permute-start(f32[104,128]{1,0:T(8,128)S(1)} %get-tuple-element.104.refs_0_), channel_id=1, source_target_pairs={{0,2},{1,3},{2,0},{3,1},{4,6},{5,7},{6,4},{7,5},{8,10},{9,11},{10,... | collective-permute-start | bytes 159752 | tf_op jit(solution)/shard_map/ppermute | solution.py:441
  47.2 1.9 %collective-permute-done.17.refs_3_ = f32[104,128]{1,0:T(8,128)S(1)} collective-permute-done((f32[104,128]{1,0:T(8,128)S(1)}, f32[104,128]{1,0:T(8,128)S(1)}, u32[]{:S(2)}, u32[]{:S(2)}) %collective-permute-start.17) | collective-permute-done | bytes 53280 | tf_op jit(solution)/shard_map/ppermute | solution.py:441
  54.3 1.4 %collective-permute-done.20.refs_3_ = f32[56,128]{1,0:T(8,128)S(1)} collective-permute-done((f32[56,128]{1,0:T(8,128)S(1)}, f32[56,128]{1,0:T(8,128)S(1)}, u32[]{:S(2)}, u32[]{:S(2)}) %collective-permute-start.20) | collective-permute-done | bytes 28704 | tf_op jit(solution)/shard_map/ppermute | solution.py:441
  56.4 3.6 %sweep.4 = (f32[64,2,128,128]{3,2,1,0:T(8,128)S(1)}, f32[2,128,128]{2,1,0:T(8,128)S(1)}, f32[8,128]{1,0:T(8,128)S(1)}, f32[128,128]{1,0:T(8,128)S(1)}, f32[128,128]{1,0:T(8,128)S(1)}) custom-call(s32[3]{0:T(128)S(1)} %pad_add_fusion.ids_ref, f32[56,128]{1,0:T(8,128)S(1)} %get-tuple-element.71.refs_0_, f32[56,128]{1,0:T(8,128)S(1)} %collective-permute-done.18.refs_1_, ...), custom_call_target="tpu_custom_call" | custom-call | tf_op jit(solution)/shard_map/sweep/pallas_call | solution.py:428
  61.3 2.6 %terms.6 = (f32[104,128]{1,0:T(8,128)S(1)}, f32[104,128]{1,0:T(8,128)S(1)}) custom-call(s32[3]{0:T(128)S(1)} %pad_add_fusion.ids_ref, f32[64,2,128,128]{3,2,1,0:T(8,128)S(1)} %get-tuple-element.75.z_ref, f32[2,128,128]{2,1,0:T(8,128)S(1)} %get-tuple-element.76.r_ref), custom_call_target="tpu_custom_call" | custom-call | tf_op jit(solution)/shard_map/terms/pallas_call | solution.py:428
  63.9 1.7 %collective-permute-start.25 = (f32[104,128]{1,0:T(8,128)S(1)}, f32[104,128]{1,0:T(8,128)S(1)}, u32[]{:S(2)}, u32[]{:S(2)}) collective-permute-start(f32[104,128]{1,0:T(8,128)S(1)} %get-tuple-element.101), channel_id=1, source_target_pairs={{0,3},{1,2},{2,1},{3,0},{4,7},{5,6},{6,5},{7,4},{8,11},{9,10},{10,... | collective-permute-start | bytes 159752 | tf_op jit(solution)/shard_map/ppermute | solution.py:441
  66.4 2.0 %collective-permute-start.24 = (f32[104,128]{1,0:T(8,128)S(1)}, f32[104,128]{1,0:T(8,128)S(1)}, u32[]{:S(2)}, u32[]{:S(2)}) collective-permute-start(f32[104,128]{1,0:T(8,128)S(1)} %get-tuple-element.102.refs_0_), channel_id=1, source_target_pairs={{0,2},{1,3},{2,0},{3,1},{4,6},{5,7},{6,4},{7,5},{8,10},{9,11},{10,... | collective-permute-start | bytes 159752 | tf_op jit(solution)/shard_map/ppermute | solution.py:441
  68.4 2.1 %collective-permute-done.25.refs_3_ = f32[104,128]{1,0:T(8,128)S(1)} collective-permute-done((f32[104,128]{1,0:T(8,128)S(1)}, f32[104,128]{1,0:T(8,128)S(1)}, u32[]{:S(2)}, u32[]{:S(2)}) %collective-permute-start.25) | collective-permute-done | bytes 53280 | tf_op jit(solution)/shard_map/ppermute | solution.py:441
  70.5 1.3 %collective-permute-done.23.refs_1_ = f32[104,128]{1,0:T(8,128)S(1)} collective-permute-done((f32[104,128]{1,0:T(8,128)S(1)}, f32[104,128]{1,0:T(8,128)S(1)}, u32[]{:S(2)}, u32[]{:S(2)}) %collective-permute-start.23) | collective-permute-done | bytes 53280 | tf_op jit(solution)/shard_map/ppermute | solution.py:441
  75.4 1.4 %collective-permute-done.28.refs_3_ = f32[56,128]{1,0:T(8,128)S(1)} collective-permute-done((f32[56,128]{1,0:T(8,128)S(1)}, f32[56,128]{1,0:T(8,128)S(1)}, u32[]{:S(2)}, u32[]{:S(2)}) %collective-permute-start.28) | collective-permute-done | bytes 28704 | tf_op jit(solution)/shard_map/ppermute | solution.py:441
  77.7 3.6 %sweep.5 = (f32[64,2,128,128]{3,2,1,0:T(8,128)S(1)}, f32[2,128,128]{2,1,0:T(8,128)S(1)}, f32[8,128]{1,0:T(8,128)S(1)}, f32[128,128]{1,0:T(8,128)S(1)}, f32[128,128]{1,0:T(8,128)}) custom-call(s32[3]{0:T(128)S(1)} %pad_add_fusion.ids_ref, f32[56,128]{1,0:T(8,128)S(1)} %get-tuple-element.80.refs_0_, f32[56,128]{1,0:T(8,128)S(1)} %collective-permute-done.26.refs_1_, ...), custom_call_target="tpu_custom_call" | custom-call | tf_op jit(solution)/shard_map/sweep/pallas_call | solution.py:428
  82.0 2.7 %terms.7 = (f32[56,128]{1,0:T(8,128)S(1)}, f32[56,128]{1,0:T(8,128)S(1)}, f32[56,128]{1,0:T(8,128)S(1)}, f32[56,128]{1,0:T(8,128)S(1)}) custom-call(s32[3]{0:T(128)S(1)} %pad_add_fusion.ids_ref, f32[64,2,128,128]{3,2,1,0:T(8,128)S(1)} %get-tuple-element.84.z_ref, f32[2,128,128]{2,1,0:T(8,128)S(1)} %get-tuple-element.85.r_ref), custom_call_target="tpu_custom_call" | custom-call | tf_op jit(solution)/shard_map/terms/pallas_call | solution.py:428
  84.8 1.6 %collective-permute-start.32 = (f32[56,128]{1,0:T(8,128)S(1)}, f32[56,128]{1,0:T(8,128)S(1)}, u32[]{:S(2)}, u32[]{:S(2)}) collective-permute-start(f32[56,128]{1,0:T(8,128)S(1)} %get-tuple-element.107), channel_id=1, source_target_pairs={{0,2},{1,3},{2,0},{3,1},{4,6},{5,7},{6,4},{7,5},{8,10},{9,11},{10,... | collective-permute-start | bytes 86024 | tf_op jit(solution)/shard_map/ppermute | solution.py:441
  87.1 2.2 %collective-permute-start.33 = (f32[56,128]{1,0:T(8,128)S(1)}, f32[56,128]{1,0:T(8,128)S(1)}, u32[]{:S(2)}, u32[]{:S(2)}) collective-permute-start(f32[56,128]{1,0:T(8,128)S(1)} %get-tuple-element.99), channel_id=1, source_target_pairs={{0,3},{1,2},{2,1},{3,0},{4,7},{5,6},{6,5},{7,4},{8,11},{9,10},{10,... | collective-permute-start | bytes 86024 | tf_op jit(solution)/shard_map/ppermute | solution.py:441
  90.3 2.4 %collective-permute-done.33.refs_3_ = f32[56,128]{1,0:T(8,128)S(1)} collective-permute-done((f32[56,128]{1,0:T(8,128)S(1)}, f32[56,128]{1,0:T(8,128)S(1)}, u32[]{:S(2)}, u32[]{:S(2)}) %collective-permute-start.33) | collective-permute-done | bytes 28704 | tf_op jit(solution)/shard_map/ppermute | solution.py:441
  93.4 1.6 %collective-permute-start.37 = (f32[144,128]{1,0:T(8,128)S(1)}, f32[144,128]{1,0:T(8,128)S(1)}, u32[]{:S(2)}, u32[]{:S(2)}) collective-permute-start(f32[144,128]{1,0:T(8,128)S(1)} %get-tuple-element.94.refs_4_), channel_id=1, source_target_pairs={{0,16},{16,0},{1,17},{17,1},{2,18},{18,2},{3,19},{19,3},{4,20},{20... | collective-permute-start | bytes 221192 | tf_op jit(solution)/shard_map/ppermute | solution.py:441
  98.7 1.5 %final.1 = (f32[2,32,64]{2,1,0:T(8,128)}, f32[2,32,64]{2,1,0:T(8,128)}, f32[2,32,64]{2,1,0:T(8,128)}) custom-call(s32[3]{0:T(128)S(1)} %pad_add_fusion.ids_ref, f32[8,128]{1,0:T(8,128)S(1)} %get-tuple-element.93.refs_0_, f32[8,128]{1,0:T(8,128)S(1)} %collective-permute-done.34.refs_1_, f32[8,128]{1,0:T(8,128)S(1)} %collective-permute-done.35.refs_2_, ...), custom_call_target="tpu_custom_call" | custom-call | tf_op jit(solution)/shard_map/final/pallas_call | solution.py:428
  (65 shorter events, 26.2 us)
Async XLA Ops:
  1.6 7.0 %collective-permute-start.5 = (f32[64,128]{1,0:T(8,128)S(1)}, f32[64,128]{1,0:T(8,128)S(1)}, u32[]{:S(2)}, u32[]{:S(2)}) collective-permute-start(f32[64,128]{1,0:T(8,128)S(1)} %get-tuple-element.51.refs_0_.refs_4_), channel_id=1, source_target_pairs={{0,12},{4,8},{8,4},{12,0},{1,13},{5,9},{9,5},{13,1},{2,14},{6,10},... | collective-permute-start | bytes 98312 | tf_op jit(solution)/shard_map/ppermute | solution.py:441
  4.1 8.3 %collective-permute-start.4 = (f32[64,128]{1,0:T(8,128)S(1)}, f32[64,128]{1,0:T(8,128)S(1)}, u32[]{:S(2)}, u32[]{:S(2)}) collective-permute-start(f32[64,128]{1,0:T(8,128)S(1)} %get-tuple-element.51.refs_0_.refs_4_), channel_id=1, source_target_pairs={{0,8},{4,12},{8,0},{12,4},{1,9},{5,13},{9,1},{13,5},{2,10},{6,14},... | collective-permute-start | bytes 98312 | tf_op jit(solution)/shard_map/ppermute | solution.py:441
  4.7 7.7 %collective-permute-start.3 = (f32[64,128]{1,0:T(8,128)S(1)}, f32[64,128]{1,0:T(8,128)S(1)}, u32[]{:S(2)}, u32[]{:S(2)}) collective-permute-start(f32[64,128]{1,0:T(8,128)S(1)} %get-tuple-element.51.refs_0_.refs_4_), channel_id=1, source_target_pairs={{0,4},{4,0},{8,12},{12,8},{1,5},{5,1},{9,13},{13,9},{2,6},{6,2},{1... | collective-permute-start | bytes 98312 | tf_op jit(solution)/shard_map/ppermute | solution.py:441
  4.8 7.7 %collective-permute-start.2 = (f32[64,128]{1,0:T(8,128)S(1)}, f32[64,128]{1,0:T(8,128)S(1)}, u32[]{:S(2)}, u32[]{:S(2)}) collective-permute-start(f32[64,128]{1,0:T(8,128)S(1)} %get-tuple-element.51.refs_0_.refs_4_), channel_id=1, source_target_pairs={{0,3},{1,2},{2,1},{3,0},{4,7},{5,6},{6,5},{7,4},{8,11},{9,10},{10,... | collective-permute-start | bytes 98312 | tf_op jit(solution)/shard_map/ppermute | solution.py:441
  8.6 4.8 %collective-permute-start.1 = (f32[64,128]{1,0:T(8,128)S(1)}, f32[64,128]{1,0:T(8,128)S(1)}, u32[]{:S(2)}, u32[]{:S(2)}) collective-permute-start(f32[64,128]{1,0:T(8,128)S(1)} %get-tuple-element.51.refs_0_.refs_4_), channel_id=1, source_target_pairs={{0,2},{1,3},{2,0},{3,1},{4,6},{5,7},{6,4},{7,5},{8,10},{9,11},{10,... | collective-permute-start | bytes 98312 | tf_op jit(solution)/shard_map/ppermute | solution.py:441
  8.6 4.8 %collective-permute-start = (f32[64,128]{1,0:T(8,128)S(1)}, f32[64,128]{1,0:T(8,128)S(1)}, u32[]{:S(2)}, u32[]{:S(2)}) collective-permute-start(f32[64,128]{1,0:T(8,128)S(1)} %get-tuple-element.51.refs_0_.refs_4_), channel_id=1, source_target_pairs={{0,1},{1,0},{2,3},{3,2},{4,5},{5,4},{6,7},{7,6},{8,9},{9,8},{10,11... | collective-permute-start | bytes 98312 | tf_op jit(solution)/shard_map/ppermute | solution.py:441
  20.2 6.3 %collective-permute-start.9 = (f32[104,128]{1,0:T(8,128)S(1)}, f32[104,128]{1,0:T(8,128)S(1)}, u32[]{:S(2)}, u32[]{:S(2)}) collective-permute-start(f32[104,128]{1,0:T(8,128)S(1)} %get-tuple-element.105), channel_id=1, source_target_pairs={{0,3},{1,2},{2,1},{3,0},{4,7},{5,6},{6,5},{7,4},{8,11},{9,10},{10,... | collective-permute-start | bytes 159752 | tf_op jit(solution)/shard_map/ppermute | solution.py:441
  23.3 5.9 %collective-permute-start.7 = (f32[104,128]{1,0:T(8,128)S(1)}, f32[104,128]{1,0:T(8,128)S(1)}, u32[]{:S(2)}, u32[]{:S(2)}) collective-permute-start(f32[104,128]{1,0:T(8,128)S(1)} %get-tuple-element.105), channel_id=1, source_target_pairs={{0,1},{1,0},{2,3},{3,2},{4,5},{5,4},{6,7},{7,6},{8,9},{9,8},{10,11... | collective-permute-start | bytes 159752 | tf_op jit(solution)/shard_map/ppermute | solution.py:441
  23.3 5.9 %collective-permute-start.8 = (f32[104,128]{1,0:T(8,128)S(1)}, f32[104,128]{1,0:T(8,128)S(1)}, u32[]{:S(2)}, u32[]{:S(2)}) collective-permute-start(f32[104,128]{1,0:T(8,128)S(1)} %get-tuple-element.106.refs_0_), channel_id=1, source_target_pairs={{0,2},{1,3},{2,0},{3,1},{4,6},{5,7},{6,4},{7,5},{8,10},{9,11},{10,... | collective-permute-start | bytes 159752 | tf_op jit(solution)/shard_map/ppermute | solution.py:441
  29.9 6.2 %collective-permute-start.13 = (f32[96,128]{1,0:T(8,128)S(1)}, f32[96,128]{1,0:T(8,128)S(1)}, u32[]{:S(2)}, u32[]{:S(2)}) collective-permute-start(f32[96,128]{1,0:T(8,128)S(1)} %get-tuple-element.60.refs_4_), channel_id=1, source_target_pairs={{0,1},{1,0},{2,3},{3,2},{4,5},{5,4},{6,7},{7,6},{8,9},{9,8},{10,11... | collective-permute-start | bytes 147464 | tf_op jit(solution)/shard_map/ppermute | solution.py:441
  31.3 3.5 %collective-permute-start.12 = (f32[56,128]{1,0:T(8,128)S(1)}, f32[56,128]{1,0:T(8,128)S(1)}, u32[]{:S(2)}, u32[]{:S(2)}) collective-permute-start(f32[56,128]{1,0:T(8,128)S(1)} %get-tuple-element.59.refs_0_), channel_id=1, source_target_pairs={{0,12},{4,8},{8,4},{12,0},{1,13},{5,9},{9,5},{13,1},{2,14},{6,10},... | collective-permute-start | bytes 86024 | tf_op jit(solution)/shard_map/ppermute | solution.py:441
  31.9 4.2 %collective-permute-start.11 = (f32[56,128]{1,0:T(8,128)S(1)}, f32[56,128]{1,0:T(8,128)S(1)}, u32[]{:S(2)}, u32[]{:S(2)}) collective-permute-start(f32[56,128]{1,0:T(8,128)S(1)} %get-tuple-element.59.refs_0_), channel_id=1, source_target_pairs={{0,8},{4,12},{8,0},{12,4},{1,9},{5,13},{9,1},{13,5},{2,10},{6,14},... | collective-permute-start | bytes 86024 | tf_op jit(solution)/shard_map/ppermute | solution.py:441
  32.8 3.3 %collective-permute-start.10 = (f32[56,128]{1,0:T(8,128)S(1)}, f32[56,128]{1,0:T(8,128)S(1)}, u32[]{:S(2)}, u32[]{:S(2)}) collective-permute-start(f32[56,128]{1,0:T(8,128)S(1)} %get-tuple-element.59.refs_0_), channel_id=1, source_target_pairs={{0,4},{4,0},{8,12},{12,8},{1,5},{5,1},{9,13},{13,9},{2,6},{6,2},{1... | collective-permute-start | bytes 86024 | tf_op jit(solution)/shard_map/ppermute | solution.py:441
  42.8 6.3 %collective-permute-start.17 = (f32[104,128]{1,0:T(8,128)S(1)}, f32[104,128]{1,0:T(8,128)S(1)}, u32[]{:S(2)}, u32[]{:S(2)}) collective-permute-start(f32[104,128]{1,0:T(8,128)S(1)} %get-tuple-element.103), channel_id=1, source_target_pairs={{0,3},{1,2},{2,1},{3,0},{4,7},{5,6},{6,5},{7,4},{8,11},{9,10},{10,... | collective-permute-start | bytes 159752 | tf_op jit(solution)/shard_map/ppermute | solution.py:441
  44.6 5.7 %collective-permute-start.15 = (f32[104,128]{1,0:T(8,128)S(1)}, f32[104,128]{1,0:T(8,128)S(1)}, u32[]{:S(2)}, u32[]{:S(2)}) collective-permute-start(f32[104,128]{1,0:T(8,128)S(1)} %get-tuple-element.103), channel_id=1, source_target_pairs={{0,1},{1,0},{2,3},{3,2},{4,5},{5,4},{6,7},{7,6},{8,9},{9,8},{10,11... | collective-permute-start | bytes 159752 | tf_op jit(solution)/shard_map/ppermute | solution.py:441
  45.1 5.4 %collective-permute-start.16 = (f32[104,128]{1,0:T(8,128)S(1)}, f32[104,128]{1,0:T(8,128)S(1)}, u32[]{:S(2)}, u32[]{:S(2)}) collective-permute-start(f32[104,128]{1,0:T(8,128)S(1)} %get-tuple-element.104.refs_0_), channel_id=1, source_target_pairs={{0,2},{1,3},{2,0},{3,1},{4,6},{5,7},{6,4},{7,5},{8,10},{9,11},{10,... | collective-permute-start | bytes 159752 | tf_op jit(solution)/shard_map/ppermute | solution.py:441
  51.1 5.3 %collective-permute-start.21 = (f32[96,128]{1,0:T(8,128)S(1)}, f32[96,128]{1,0:T(8,128)S(1)}, u32[]{:S(2)}, u32[]{:S(2)}) collective-permute-start(f32[96,128]{1,0:T(8,128)S(1)} %get-tuple-element.72.refs_4_), channel_id=1, source_target_pairs={{0,1},{1,0},{2,3},{3,2},{4,5},{5,4},{6,7},{7,6},{8,9},{9,8},{10,11... | collective-permute-start | bytes 147464 | tf_op jit(solution)/shard_map/ppermute | solution.py:441
  52.4 3.3 %collective-permute-start.20 = (f32[56,128]{1,0:T(8,128)S(1)}, f32[56,128]{1,0:T(8,128)S(1)}, u32[]{:S(2)}, u32[]{:S(2)}) collective-permute-start(f32[56,128]{1,0:T(8,128)S(1)} %get-tuple-element.71.refs_0_), channel_id=1, source_target_pairs={{0,12},{4,8},{8,4},{12,0},{1,13},{5,9},{9,5},{13,1},{2,14},{6,10},... | collective-permute-start | bytes 86024 | tf_op jit(solution)/shard_map/ppermute | solution.py:441
  52.5 4.0 %collective-permute-start.19 = (f32[56,128]{1,0:T(8,128)S(1)}, f32[56,128]{1,0:T(8,128)S(1)}, u32[]{:S(2)}, u32[]{:S(2)}) collective-permute-start(f32[56,128]{1,0:T(8,128)S(1)} %get-tuple-element.71.refs_0_), channel_id=1, source_target_pairs={{0,8},{4,12},{8,0},{12,4},{1,9},{5,13},{9,1},{13,5},{2,10},{6,14},... | collective-permute-start | bytes 86024 | tf_op jit(solution)/shard_map/ppermute | solution.py:441
  60.1 3.9 %collective-permute-start.22 = (f32[8,128]{1,0:T(8,128)S(1)}, f32[8,128]{1,0:T(8,128)S(1)}, u32[]{:S(2)}, u32[]{:S(2)}) collective-permute-start(f32[8,128]{1,0:T(8,128)S(1)} %get-tuple-element.78), channel_id=1, source_target_pairs={{0,20},{4,16},{8,28},{12,24},{16,4},{20,0},{24,12},{28,8},{1,21},{... | collective-permute-start | bytes 12296 | tf_op jit(solution)/shard_map/ppermute | solution.py:441
  63.9 6.5 %collective-permute-start.25 = (f32[104,128]{1,0:T(8,128)S(1)}, f32[104,128]{1,0:T(8,128)S(1)}, u32[]{:S(2)}, u32[]{:S(2)}) collective-permute-start(f32[104,128]{1,0:T(8,128)S(1)} %get-tuple-element.101), channel_id=1, source_target_pairs={{0,3},{1,2},{2,1},{3,0},{4,7},{5,6},{6,5},{7,4},{8,11},{9,10},{10,... | collective-permute-start | bytes 159752 | tf_op jit(solution)/shard_map/ppermute | solution.py:441
  65.6 6.2 %collective-permute-start.23 = (f32[104,128]{1,0:T(8,128)S(1)}, f32[104,128]{1,0:T(8,128)S(1)}, u32[]{:S(2)}, u32[]{:S(2)}) collective-permute-start(f32[104,128]{1,0:T(8,128)S(1)} %get-tuple-element.101), channel_id=1, source_target_pairs={{0,1},{1,0},{2,3},{3,2},{4,5},{5,4},{6,7},{7,6},{8,9},{9,8},{10,11... | collective-permute-start | bytes 159752 | tf_op jit(solution)/shard_map/ppermute | solution.py:441
  66.4 6.1 %collective-permute-start.24 = (f32[104,128]{1,0:T(8,128)S(1)}, f32[104,128]{1,0:T(8,128)S(1)}, u32[]{:S(2)}, u32[]{:S(2)}) collective-permute-start(f32[104,128]{1,0:T(8,128)S(1)} %get-tuple-element.102.refs_0_), channel_id=1, source_target_pairs={{0,2},{1,3},{2,0},{3,1},{4,6},{5,7},{6,4},{7,5},{8,10},{9,11},{10,... | collective-permute-start | bytes 159752 | tf_op jit(solution)/shard_map/ppermute | solution.py:441
  73.1 4.6 %collective-permute-start.29 = (f32[96,128]{1,0:T(8,128)S(1)}, f32[96,128]{1,0:T(8,128)S(1)}, u32[]{:S(2)}, u32[]{:S(2)}) collective-permute-start(f32[96,128]{1,0:T(8,128)S(1)} %get-tuple-element.81.refs_4_), channel_id=1, source_target_pairs={{0,1},{1,0},{2,3},{3,2},{4,5},{5,4},{6,7},{7,6},{8,9},{9,8},{10,11... | collective-permute-start | bytes 147464 | tf_op jit(solution)/shard_map/ppermute | solution.py:441
  73.5 3.3 %collective-permute-start.28 = (f32[56,128]{1,0:T(8,128)S(1)}, f32[56,128]{1,0:T(8,128)S(1)}, u32[]{:S(2)}, u32[]{:S(2)}) collective-permute-start(f32[56,128]{1,0:T(8,128)S(1)} %get-tuple-element.80.refs_0_), channel_id=1, source_target_pairs={{0,12},{4,8},{8,4},{12,0},{1,13},{5,9},{9,5},{13,1},{2,14},{6,10},... | collective-permute-start | bytes 86024 | tf_op jit(solution)/shard_map/ppermute | solution.py:441
  73.6 4.1 %collective-permute-start.27 = (f32[56,128]{1,0:T(8,128)S(1)}, f32[56,128]{1,0:T(8,128)S(1)}, u32[]{:S(2)}, u32[]{:S(2)}) collective-permute-start(f32[56,128]{1,0:T(8,128)S(1)} %get-tuple-element.80.refs_0_), channel_id=1, source_target_pairs={{0,8},{4,12},{8,0},{12,4},{1,9},{5,13},{9,1},{13,5},{2,10},{6,14},... | collective-permute-start | bytes 86024 | tf_op jit(solution)/shard_map/ppermute | solution.py:441
  81.3 3.5 %collective-permute-start.30 = (f32[8,128]{1,0:T(8,128)S(1)}, f32[8,128]{1,0:T(8,128)S(1)}, u32[]{:S(2)}, u32[]{:S(2)}) collective-permute-start(f32[8,128]{1,0:T(8,128)S(1)} %get-tuple-element.87), channel_id=1, source_target_pairs={{0,20},{4,16},{8,28},{12,24},{16,4},{20,0},{24,12},{28,8},{1,21},{... | collective-permute-start | bytes 12296 | tf_op jit(solution)/shard_map/ppermute | solution.py:441
  84.8 4.9 %collective-permute-start.32 = (f32[56,128]{1,0:T(8,128)S(1)}, f32[56,128]{1,0:T(8,128)S(1)}, u32[]{:S(2)}, u32[]{:S(2)}) collective-permute-start(f32[56,128]{1,0:T(8,128)S(1)} %get-tuple-element.107), channel_id=1, source_target_pairs={{0,2},{1,3},{2,0},{3,1},{4,6},{5,7},{6,4},{7,5},{8,10},{9,11},{10,... | collective-permute-start | bytes 86024 | tf_op jit(solution)/shard_map/ppermute | solution.py:441
  86.5 3.9 %collective-permute-start.31 = (f32[56,128]{1,0:T(8,128)S(1)}, f32[56,128]{1,0:T(8,128)S(1)}, u32[]{:S(2)}, u32[]{:S(2)}) collective-permute-start(f32[56,128]{1,0:T(8,128)S(1)} %get-tuple-element.108), channel_id=1, source_target_pairs={{0,1},{1,0},{2,3},{3,2},{4,5},{5,4},{6,7},{7,6},{8,9},{9,8},{10,11... | collective-permute-start | bytes 86024 | tf_op jit(solution)/shard_map/ppermute | solution.py:441
  87.1 5.7 %collective-permute-start.33 = (f32[56,128]{1,0:T(8,128)S(1)}, f32[56,128]{1,0:T(8,128)S(1)}, u32[]{:S(2)}, u32[]{:S(2)}) collective-permute-start(f32[56,128]{1,0:T(8,128)S(1)} %get-tuple-element.99), channel_id=1, source_target_pairs={{0,3},{1,2},{2,1},{3,0},{4,7},{5,6},{6,5},{7,4},{8,11},{9,10},{10,... | collective-permute-start | bytes 86024 | tf_op jit(solution)/shard_map/ppermute | solution.py:441
  93.4 5.2 %collective-permute-start.37 = (f32[144,128]{1,0:T(8,128)S(1)}, f32[144,128]{1,0:T(8,128)S(1)}, u32[]{:S(2)}, u32[]{:S(2)}) collective-permute-start(f32[144,128]{1,0:T(8,128)S(1)} %get-tuple-element.94.refs_4_), channel_id=1, source_target_pairs={{0,16},{16,0},{1,17},{17,1},{2,18},{18,2},{3,19},{19,3},{4,20},{20... | collective-permute-start | bytes 221192 | tf_op jit(solution)/shard_map/ppermute | solution.py:441
  95.0 3.6 %collective-permute-start.35 = (f32[8,128]{1,0:T(8,128)S(1)}, f32[8,128]{1,0:T(8,128)S(1)}, u32[]{:S(2)}, u32[]{:S(2)}) collective-permute-start(f32[8,128]{1,0:T(8,128)S(1)} %get-tuple-element.93.refs_0_), channel_id=1, source_target_pairs={{0,8},{4,12},{8,0},{12,4},{1,9},{5,13},{9,1},{13,5},{2,10},{6,14},... | collective-permute-start | bytes 12296 | tf_op jit(solution)/shard_map/ppermute | solution.py:441
  (6 other events, 18.2 us)

commit v6 on v5

--- a/solution.py
+++ b/solution.py
@@ -94,7 +94,8 @@
     return copies
 
 
-def pack_kernel(brow_ref, *refs):
+def pack_kernel(*refs, alone):
+    brow_ref, refs = ([1.0], refs) if alone else (refs[0], refs[1:])
     start_ref, dual_out_ref = refs[3:5]
     gains_ref, consensus_ref, dual_ref = refs[5:8]
     for copy in fetch(refs[:3], refs[5:8], refs[8]):
@@ -234,11 +235,11 @@
     return lax.rem(lane_block(shape, span), 2) == lax.rem(j, 2)
 
 
-def terms_kernel(ids_ref, z_ref, r_ref, same_ref, other_ref, all_ref, *, span):
+def terms_kernel(z_ref, r_ref, same_ref, other_ref, all_ref, *, span):
     dirs, _, cols, rows = z_ref.shape
     half = dirs // 2
     normal_terms(z_ref, r_ref, all_ref)
-    mine = own_parity((half, rows), span, ids_ref[1])
+    mine = own_parity((half, rows), span, lax.axis_index("scol"))
     for q in range(3):
         low = all_ref[q * dirs : q * dirs + half, :]
         high = pltpu.roll(all_ref[q * dirs + half : (q + 1) * dirs, :], span, 1)
@@ -270,27 +271,27 @@
     return packed
 
 
-def last_terms_kernel(ids_ref, z_ref, r_ref, *refs, span):
+def last_terms_kernel(z_ref, r_ref, *refs, span):
     outs, all_ref = refs[:-1], refs[-1]
     dirs, _, cols, rows = z_ref.shape
     depth = dirs * span // rows
     normal_terms(z_ref, r_ref, all_ref)
     for n, out_ref in enumerate(outs):
-        block = jnp.bitwise_xor(ids_ref[1], n)
+        block = jnp.bitwise_xor(lax.axis_index("scol"), n)
         for q in range(3):
             plane = all_ref[q * dirs : (q + 1) * dirs, :]
             out_ref[q * depth : (q + 1) * depth, :] = pack_plane(plane, block, span)
         out_ref[3 * depth :, :] = jnp.zeros((8, rows), jnp.float32)
 
 
-def first_kernel(ids_ref, *refs, ns, nz, span):
-    rows_in = refs[:nz]
-    cols_in = refs[nz : nz + ns]
+def first_kernel(*refs, ns, nz, span):
+    rows_in = refs[: 2 * nz : 2]
+    cols_in = refs[1 : 2 * nz : 2]
     mt_ref, vt_ref = refs[nz + ns : nz + ns + 2]
     outs = refs[nz + ns + 2 : nz + ns + 5]
     grow_ref, gcol_ref, trow_ref, tcol_ref, ct_ref = refs[nz + ns + 5 :]
     dirs = mt_ref.shape[0]
-    i, j = ids_ref[0], ids_ref[1]
+    i, j = lax.axis_index("srow"), lax.axis_index("scol")
     depth = dirs * span // mt_ref.shape[3]
     for pieces, g_ref, t_ref, me in ((rows_in, grow_ref, trow_ref, j), (cols_in, gcol_ref, tcol_ref, i)):
         blocks = [jnp.bitwise_xor(me, n) for n in range(len(pieces))]
@@ -302,14 +303,14 @@
     residual(mt_ref, vt_ref, grow_ref, gcol_ref, *outs, ct_ref)
 
 
-def sweep_kernel(ids_ref, *refs, ns, span, scale):
+def sweep_kernel(*refs, ns, span, scale):
     pieces = refs[:ns]
     same_ref, other_ref, growin_ref, gcolin_ref, trow_ref, tcol_ref = refs[ns : ns + 6]
     rho_ref, mt_ref, vt_ref = refs[ns + 6 : ns + 9]
     outs = refs[ns + 9 : ns + 12]
     grow_ref, gcol_ref, ct_ref = refs[ns + 12 :]
     dirs = mt_ref.shape[0]
-    i = ids_ref[0]
+    i = lax.axis_index("srow")
     depth = dirs * span // mt_ref.shape[3]
     power = pieces[0][3 * depth :, :]
     for p in pieces[1:]:
@@ -322,7 +323,7 @@
             same_ref[q * half : (q + 1) * half, :],
             other_ref[q * half : (q + 1) * half, :],
             span,
-            ids_ref[1],
+            lax.axis_index("scol"),
         )
         for q in range(3)
     ]
@@ -340,7 +341,7 @@
     residual(mt_ref, vt_ref, grow_ref, gcol_ref, *outs, ct_ref)
 
 
-def combine_kernel(ids_ref, *refs, nz, span):
+def combine_kernel(*refs, nz, span):
     parts = refs[:nz]
     pair_ref, own_ref = refs[nz:]
     half = pair_ref.shape[0] // 3
@@ -351,16 +352,16 @@
     pair_ref[...] = total[: 3 * half]
     for q in range(3):
         piece = total[q * half : (q + 1) * half]
-        own_ref[q * depth : (q + 1) * depth, :] = pack_folded(piece, ids_ref[1], span)
+        own_ref[q * depth : (q + 1) * depth, :] = pack_folded(piece, lax.axis_index("scol"), span)
     own_ref[3 * depth :, :] = total[3 * half :]
 
 
-def last_combine_kernel(ids_ref, *refs, nz, span):
+def last_combine_kernel(*refs, nz, span):
     parts = refs[:nz]
     g_ref, t_ref, d_ref, power_ref, mail_ref = refs[nz:]
     dirs = g_ref.shape[0] // 2
     depth = dirs * span // g_ref.shape[1]
-    j = ids_ref[1]
+    j = lax.axis_index("scol")
     total = parts[0][...]
     for p in parts[1:]:
         total = total + p[...]
@@ -374,7 +375,7 @@
     mail_ref[7 * depth :, :] = d_ref[...]
 
 
-def final_kernel(ids_ref, *refs, ns, scale, pair, span, scal):
+def final_kernel(*refs, ns, scale, pair, span, scal):
     powers = refs[:ns]
     mails = refs[ns : ns + 1 + pair]
     rho_ref = refs[ns + 1 + pair]
@@ -392,7 +393,7 @@
     fields = list(news[0])
     if pair:
         duals = [[m[q * depth : (q + 1) * depth, :] for q in (7, 8)] for m in mails]
-        first = ids_ref[2] == 0
+        first = lax.axis_index("chan") == 0
         coeffs, new_duals = [], []
         for p in range(2):
             own, other = [news[n][p] + duals[n][p] for n in range(2)]
@@ -450,8 +451,7 @@
     span = gains.shape[3]
     rows, cols = vis.shape[2:]
     depth = dirs * span // rows
-    i, j, f = lax.axis_index("srow"), lax.axis_index("scol"), lax.axis_index("chan")
-    ids = jnp.stack([i, j, f]).astype(jnp.int32)
+    f = lax.axis_index("chan")
     pair = groups == 2 and order == 1
 
     table = basis_table(groups, order)
@@ -462,16 +462,18 @@
         dual[0].transpose(1, 2, 0),
     ]
     start, dual_packed = call(
-        pack_kernel,
+        functools.partial(pack_kernel, alone=order == 1),
         "pack",
-        [brow],
+        [] if order == 1 else [brow],
         own_in,
         [f32(4 * depth, rows), f32(2 * depth, rows)],
         [pltpu.VMEM(x.shape, jnp.float32) for x in own_in] + [pltpu.SemaphoreType.DMA((3,))],
         HBM,
     )
-    row_parts = [start] + [swap(start, "scol", n) for n in range(1, nz)]
-    col_parts = [start] + [swap(start, "srow", n) for n in range(1, ns)]
+    row_parts, col_parts = [start], [start]
+    for n in range(1, max(ns, nz)):
+        col_parts += [swap(start, "srow", n)] if n < ns else []
+        row_parts += [swap(start, "scol", n)] if n < nz else []
     field_in = [rho, cluster, flags[0], model[0], vis[0]]
     mt, vt, rho_rows, rho_packed = call(
         prepare_kernel,
@@ -496,8 +498,8 @@
     z, r, power, grow, gcol, trow, tcol = call(
         functools.partial(first_kernel, ns=ns, nz=nz, span=span),
         "first",
-        [ids],
-        row_parts + col_parts + [mt, vt],
+        [],
+        [part for parts in zip(row_parts, col_parts) for part in parts] + [mt, vt],
         fields + [plane, plane, plane, plane],
         scratch,
     )
@@ -513,7 +515,7 @@
         same, other = call(
             functools.partial(terms_kernel, span=span),
             "terms",
-            [ids],
+            [],
             [z, r],
             [f32(half + 8, rows)] * 2,
             [pltpu.VMEM((3 * dirs, rows), jnp.float32)],
@@ -523,7 +525,7 @@
         pair_sums, own = call(
             functools.partial(combine_kernel, nz=nz, span=span),
             "combine",
-            [ids],
+            [],
             [same] + [swap(same if n % 2 == 0 else other, "scol", n) for n in range(1, nz)],
             [f32(half, rows), f32(3 * depth + 8, rows)],
         )
@@ -532,7 +534,7 @@
         z, r, power, grow, gcol = call(
             functools.partial(sweep_kernel, ns=ns, span=span, scale=scale),
             "sweep",
-            [ids],
+            [],
             pieces + [pair_sums, other_sums, grow, gcol, trow, tcol, rho_rows, mt, vt],
             fields + [plane, plane],
             scratch,
@@ -541,7 +543,7 @@
     parts = call(
         functools.partial(last_terms_kernel, span=span),
         "terms",
-        [ids],
+        [],
         [z, r],
         [f32(3 * depth + 8, rows)] * nz,
         [pltpu.VMEM((3 * dirs, rows), jnp.float32)],
@@ -550,7 +552,7 @@
     power, mail = call(
         functools.partial(last_combine_kernel, nz=nz, span=span),
         "combine",
-        [ids],
+        [],
         [parts[0]] + [swap(parts[n], "scol", n) for n in range(1, nz)] + [grow, trow, dual_packed],
         [f32(8, rows), f32(9 * depth, rows)],
     )
@@ -561,7 +563,7 @@
             final_kernel, ns=ns, scale=scale, pair=int(pair), span=span, scal=pair_scalars(pair)
         ),
         "final",
-        [ids],
+        [],
         powers + mails + [rho_packed],
         [f32(2, span, dirs)] * (3 if pair else 1),
     )

time: 100 us -> 92.6 us (0.926)
  Pallas kernels: 33.4 us -> 26.3 us
  waiting for transfers between devices: 25.7 us -> 24.7 us
    pallas_call x15, Pallas kernels: 33.4 us -> 26.3 us  [call(): pl.pallas_call(kernel, in_specs=[SMEM] * len(lead) + [place] * len(args),...]
    ppermute x38, waiting for transfers between devices: 25.7 us -> 24.7 us  [swap(): return lax.ppermute(x, axis, [(m, m ^ n) for m in range(size)])]
  transfers between devices with their start and end apart: 38 -> 38, of which waited for: 21 -> 21; matrix products, arithmetic and copies ran while one was open for 0% -> 0% of each run, Pallas kernels for 14% -> 13%
where the time goes in v6:
time: 92.6 us; the launch traced here: 92.4 us
  starting transfers between devices  40.6 us (44%)
  Pallas kernels  26.3 us (28%)
  waiting for transfers between devices  24.7 us (27%)
    ppermute x38, starting transfers between devices, swap(): return lax.ppermute(x, axis, [(m, m ^ n) for m in range(size)])  40.6 us
    pallas_call x15, Pallas kernels, call(): pl.pallas_call(kernel, in_specs=[SMEM] * len(lead) + [place] * len(args),...  26.3 us
    ppermute x38, waiting for transfers between devices, swap(): return lax.ppermute(x, axis, [(m, m ^ n) for m in range(size)])  24.7 us
  transfers between devices with their start and end apart: 38, of which 21 were waited for; matrix products, arithmetic and copies ran while one was open for 0% of the time, Pallas kernels for 13%

profile of v6, /device:TPU:0, one launch (start us, length us, event | category | flops | bytes accessed | tf_op | source)
XLA Modules:
  0.0 92.4 jit_solution(6283402635087698625)
XLA Ops:
  1.6 2.5 %collective-permute-start.5 = (f32[64,128]{1,0:T(8,128)S(1)}, f32[64,128]{1,0:T(8,128)S(1)}, u32[]{:S(2)}, u32[]{:S(2)}) collective-permute-start(f32[64,128]{1,0:T(8,128)S(1)} %get-tuple-element.51.refs_0_.refs_1_), channel_id=1, source_target_pairs={{0,12},{4,8},{8,4},{12,0},{1,13},{5,9},{9,5},{13,1},{2,14},{6,10},... | collective-permute-start | bytes 98312 | tf_op jit(solution)/shard_map/ppermute | solution.py:442
  4.1 3.6 %collective-permute-start.4 = (f32[64,128]{1,0:T(8,128)S(1)}, f32[64,128]{1,0:T(8,128)S(1)}, u32[]{:S(2)}, u32[]{:S(2)}) collective-permute-start(f32[64,128]{1,0:T(8,128)S(1)} %get-tuple-element.51.refs_0_.refs_1_), channel_id=1, source_target_pairs={{0,3},{1,2},{2,1},{3,0},{4,7},{5,6},{6,5},{7,4},{8,11},{9,10},{10,... | collective-permute-start | bytes 98312 | tf_op jit(solution)/shard_map/ppermute | solution.py:442
  9.1 3.2 %prepare.1 = (bf16[64,2,128,128]{3,2,1,0:T(8,128)(2,1)S(1)}, f32[2,128,128]{2,1,0:T(8,128)S(1)}, f32[64,128]{1,0:T(8,128)S(1)}, f32[16,128]{1,0:T(8,128)S(1)}) custom-call(f32[8]{0:T(128)} %refs_0_.1, s32[64]{0:T(128)} %refs_1_.1, s32[8,8]{1,0:T(8,128)} %bitcast.24, bf16[64,2,128,128]{3,2,1,0:T(8,128)(2,1)} %bitcast.19, bf16[2,128,128]{2,1,0:T(8,128)(2,1)} %bitcast.20), custom_call_target="tpu_custom_call" | custom-call | tf_op jit(solution)/shard_map/prepare/pallas_call | solution.py:429
  13.2 3.2 %first.1 = (f32[64,2,128,128]{3,2,1,0:T(8,128)S(1)}, f32[2,128,128]{2,1,0:T(8,128)S(1)}, f32[8,128]{1,0:T(8,128)S(1)}, f32[128,128]{1,0:T(8,128)S(1)}, f32[128,1...) custom-call(f32[64,128]{1,0:T(8,128)S(1)} %get-tuple-element.51.refs_0_.refs_1_, ...), custom_call_target="tpu_custom_call" | custom-call | tf_op jit(solution)/shard_map/first/pallas_call | solution.py:429
  16.9 2.1 %terms.4 = (f32[104,128]{1,0:T(8,128)S(1)}, f32[104,128]{1,0:T(8,128)S(1)}) custom-call(f32[64,2,128,128]{3,2,1,0:T(8,128)S(1)} %get-tuple-element.54.z_ref, f32[2,128,128]{2,1,0:T(8,128)S(1)} %get-tuple-element.55.r_ref), custom_call_target="tpu_custom_call" | custom-call | tf_op jit(solution)/shard_map/terms/pallas_call | solution.py:429
  19.4 3.3 %collective-permute-start.9 = (f32[104,128]{1,0:T(8,128)S(1)}, f32[104,128]{1,0:T(8,128)S(1)}, u32[]{:S(2)}, u32[]{:S(2)}) collective-permute-start(f32[104,128]{1,0:T(8,128)S(1)} %get-tuple-element.105), channel_id=1, source_target_pairs={{0,3},{1,2},{2,1},{3,0},{4,7},{5,6},{6,5},{7,4},{8,11},{9,10},{10,... | collective-permute-start | bytes 159752 | tf_op jit(solution)/shard_map/ppermute | solution.py:442
  23.8 2.1 %collective-permute-done.9.refs_3_ = f32[104,128]{1,0:T(8,128)S(1)} collective-permute-done((f32[104,128]{1,0:T(8,128)S(1)}, f32[104,128]{1,0:T(8,128)S(1)}, u32[]{:S(2)}, u32[]{:S(2)}) %collective-permute-start.9) | collective-permute-done | bytes 53280 | tf_op jit(solution)/shard_map/ppermute | solution.py:442
  25.9 1.8 %collective-permute-done.7.refs_1_ = f32[104,128]{1,0:T(8,128)S(1)} collective-permute-done((f32[104,128]{1,0:T(8,128)S(1)}, f32[104,128]{1,0:T(8,128)S(1)}, u32[]{:S(2)}, u32[]{:S(2)}) %collective-permute-start.7) | collective-permute-done | bytes 53280 | tf_op jit(solution)/shard_map/ppermute | solution.py:442
  28.4 1.5 %collective-permute-start.13 = (f32[96,128]{1,0:T(8,128)S(1)}, f32[96,128]{1,0:T(8,128)S(1)}, u32[]{:S(2)}, u32[]{:S(2)}) collective-permute-start(f32[96,128]{1,0:T(8,128)S(1)} %get-tuple-element.60.refs_4_), channel_id=1, source_target_pairs={{0,1},{1,0},{2,3},{3,2},{4,5},{5,4},{6,7},{7,6},{8,9},{9,8},{10,11... | collective-permute-start | bytes 147464 | tf_op jit(solution)/shard_map/ppermute | solution.py:442
  30.0 1.4 %collective-permute-start.11 = (f32[56,128]{1,0:T(8,128)S(1)}, f32[56,128]{1,0:T(8,128)S(1)}, u32[]{:S(2)}, u32[]{:S(2)}) collective-permute-start(f32[56,128]{1,0:T(8,128)S(1)} %get-tuple-element.59.refs_0_), channel_id=1, source_target_pairs={{0,8},{4,12},{8,0},{12,4},{1,9},{5,13},{9,1},{13,5},{2,10},{6,14},... | collective-permute-start | bytes 86024 | tf_op jit(solution)/shard_map/ppermute | solution.py:442
  31.8 1.7 %collective-permute-done.12.refs_3_ = f32[56,128]{1,0:T(8,128)S(1)} collective-permute-done((f32[56,128]{1,0:T(8,128)S(1)}, f32[56,128]{1,0:T(8,128)S(1)}, u32[]{:S(2)}, u32[]{:S(2)}) %collective-permute-start.12) | collective-permute-done | bytes 28704 | tf_op jit(solution)/shard_map/ppermute | solution.py:442
  33.9 3.1 %sweep.3 = (f32[64,2,128,128]{3,2,1,0:T(8,128)S(1)}, f32[2,128,128]{2,1,0:T(8,128)S(1)}, f32[8,128]{1,0:T(8,128)S(1)}, f32[128,128]{1,0:T(8,128)S(1)}, f32[128,128]{1,0:T(8,128)S(1)}) custom-call(f32[56,128]{1,0:T(8,128)S(1)} %get-tuple-element.59.refs_0_, f32[56,128]{1,0:T(8,128)S(1)} %collective-permute-done.10.refs_1_, ...), custom_call_target="tpu_custom_call" | custom-call | tf_op jit(solution)/shard_map/sweep/pallas_call | solution.py:429
  37.9 2.1 %terms.5 = (f32[104,128]{1,0:T(8,128)S(1)}, f32[104,128]{1,0:T(8,128)S(1)}) custom-call(f32[64,2,128,128]{3,2,1,0:T(8,128)S(1)} %get-tuple-element.66.z_ref, f32[2,128,128]{2,1,0:T(8,128)S(1)} %get-tuple-element.67.r_ref), custom_call_target="tpu_custom_call" | custom-call | tf_op jit(solution)/shard_map/terms/pallas_call | solution.py:429
  40.1 1.6 %collective-permute-start.17 = (f32[104,128]{1,0:T(8,128)S(1)}, f32[104,128]{1,0:T(8,128)S(1)}, u32[]{:S(2)}, u32[]{:S(2)}) collective-permute-start(f32[104,128]{1,0:T(8,128)S(1)} %get-tuple-element.103), channel_id=1, source_target_pairs={{0,3},{1,2},{2,1},{3,0},{4,7},{5,6},{6,5},{7,4},{8,11},{9,10},{10,... | collective-permute-start | bytes 159752 | tf_op jit(solution)/shard_map/ppermute | solution.py:442
  42.3 2.2 %collective-permute-start.16 = (f32[104,128]{1,0:T(8,128)S(1)}, f32[104,128]{1,0:T(8,128)S(1)}, u32[]{:S(2)}, u32[]{:S(2)}) collective-permute-start(f32[104,128]{1,0:T(8,128)S(1)} %get-tuple-element.104.refs_0_), channel_id=1, source_target_pairs={{0,2},{1,3},{2,0},{3,1},{4,6},{5,7},{6,4},{7,5},{8,10},{9,11},{10,... | collective-permute-start | bytes 159752 | tf_op jit(solution)/shard_map/ppermute | solution.py:442
  44.5 2.1 %collective-permute-done.17.refs_3_ = f32[104,128]{1,0:T(8,128)S(1)} collective-permute-done((f32[104,128]{1,0:T(8,128)S(1)}, f32[104,128]{1,0:T(8,128)S(1)}, u32[]{:S(2)}, u32[]{:S(2)}) %collective-permute-start.17) | collective-permute-done | bytes 53280 | tf_op jit(solution)/shard_map/ppermute | solution.py:442
  48.9 1.4 %collective-permute-start.19 = (f32[56,128]{1,0:T(8,128)S(1)}, f32[56,128]{1,0:T(8,128)S(1)}, u32[]{:S(2)}, u32[]{:S(2)}) collective-permute-start(f32[56,128]{1,0:T(8,128)S(1)} %get-tuple-element.71.refs_0_), channel_id=1, source_target_pairs={{0,8},{4,12},{8,0},{12,4},{1,9},{5,13},{9,1},{13,5},{2,10},{6,14},... | collective-permute-start | bytes 86024 | tf_op jit(solution)/shard_map/ppermute | solution.py:442
  50.8 1.7 %collective-permute-done.20.refs_3_ = f32[56,128]{1,0:T(8,128)S(1)} collective-permute-done((f32[56,128]{1,0:T(8,128)S(1)}, f32[56,128]{1,0:T(8,128)S(1)}, u32[]{:S(2)}, u32[]{:S(2)}) %collective-permute-start.20) | collective-permute-done | bytes 28704 | tf_op jit(solution)/shard_map/ppermute | solution.py:442
  52.8 3.1 %sweep.4 = (f32[64,2,128,128]{3,2,1,0:T(8,128)S(1)}, f32[2,128,128]{2,1,0:T(8,128)S(1)}, f32[8,128]{1,0:T(8,128)S(1)}, f32[128,128]{1,0:T(8,128)S(1)}, f32[128,128]{1,0:T(8,128)S(1)}) custom-call(f32[56,128]{1,0:T(8,128)S(1)} %get-tuple-element.71.refs_0_, f32[56,128]{1,0:T(8,128)S(1)} %collective-permute-done.18.refs_1_, ...), custom_call_target="tpu_custom_call" | custom-call | tf_op jit(solution)/shard_map/sweep/pallas_call | solution.py:429
  56.9 2.1 %terms.6 = (f32[104,128]{1,0:T(8,128)S(1)}, f32[104,128]{1,0:T(8,128)S(1)}) custom-call(f32[64,2,128,128]{3,2,1,0:T(8,128)S(1)} %get-tuple-element.75.z_ref, f32[2,128,128]{2,1,0:T(8,128)S(1)} %get-tuple-element.76.r_ref), custom_call_target="tpu_custom_call" | custom-call | tf_op jit(solution)/shard_map/terms/pallas_call | solution.py:429
  59.0 2.3 %collective-permute-start.25 = (f32[104,128]{1,0:T(8,128)S(1)}, f32[104,128]{1,0:T(8,128)S(1)}, u32[]{:S(2)}, u32[]{:S(2)}) collective-permute-start(f32[104,128]{1,0:T(8,128)S(1)} %get-tuple-element.101), channel_id=1, source_target_pairs={{0,3},{1,2},{2,1},{3,0},{4,7},{5,6},{6,5},{7,4},{8,11},{9,10},{10,... | collective-permute-start | bytes 159752 | tf_op jit(solution)/shard_map/ppermute | solution.py:442
  61.9 1.6 %collective-permute-start.24 = (f32[104,128]{1,0:T(8,128)S(1)}, f32[104,128]{1,0:T(8,128)S(1)}, u32[]{:S(2)}, u32[]{:S(2)}) collective-permute-start(f32[104,128]{1,0:T(8,128)S(1)} %get-tuple-element.102.refs_0_), channel_id=1, source_target_pairs={{0,2},{1,3},{2,0},{3,1},{4,6},{5,7},{6,4},{7,5},{8,10},{9,11},{10,... | collective-permute-start | bytes 159752 | tf_op jit(solution)/shard_map/ppermute | solution.py:442
  63.5 2.0 %collective-permute-done.25.refs_3_ = f32[104,128]{1,0:T(8,128)S(1)} collective-permute-done((f32[104,128]{1,0:T(8,128)S(1)}, f32[104,128]{1,0:T(8,128)S(1)}, u32[]{:S(2)}, u32[]{:S(2)}) %collective-permute-start.25) | collective-permute-done | bytes 53280 | tf_op jit(solution)/shard_map/ppermute | solution.py:442
  65.5 1.8 %collective-permute-done.23.refs_1_ = f32[104,128]{1,0:T(8,128)S(1)} collective-permute-done((f32[104,128]{1,0:T(8,128)S(1)}, f32[104,128]{1,0:T(8,128)S(1)}, u32[]{:S(2)}, u32[]{:S(2)}) %collective-permute-start.23) | collective-permute-done | bytes 53280 | tf_op jit(solution)/shard_map/ppermute | solution.py:442
  68.6 1.4 %collective-permute-start.27 = (f32[56,128]{1,0:T(8,128)S(1)}, f32[56,128]{1,0:T(8,128)S(1)}, u32[]{:S(2)}, u32[]{:S(2)}) collective-permute-start(f32[56,128]{1,0:T(8,128)S(1)} %get-tuple-element.80.refs_0_), channel_id=1, source_target_pairs={{0,8},{4,12},{8,0},{12,4},{1,9},{5,13},{9,1},{13,5},{2,10},{6,14},... | collective-permute-start | bytes 86024 | tf_op jit(solution)/shard_map/ppermute | solution.py:442
  70.4 1.7 %collective-permute-done.28.refs_3_ = f32[56,128]{1,0:T(8,128)S(1)} collective-permute-done((f32[56,128]{1,0:T(8,128)S(1)}, f32[56,128]{1,0:T(8,128)S(1)}, u32[]{:S(2)}, u32[]{:S(2)}) %collective-permute-start.28) | collective-permute-done | bytes 28704 | tf_op jit(solution)/shard_map/ppermute | solution.py:442
  72.5 3.1 %sweep.5 = (f32[64,2,128,128]{3,2,1,0:T(8,128)S(1)}, f32[2,128,128]{2,1,0:T(8,128)S(1)}, f32[8,128]{1,0:T(8,128)S(1)}, f32[128,128]{1,0:T(8,128)S(1)}, f32[128,128]{1,0:T(8,128)}) custom-call(f32[56,128]{1,0:T(8,128)S(1)} %get-tuple-element.80.refs_0_, f32[56,128]{1,0:T(8,128)S(1)} %collective-permute-done.26.refs_1_, ...), custom_call_target="tpu_custom_call" | custom-call | tf_op jit(solution)/shard_map/sweep/pallas_call | solution.py:429
  76.5 2.2 %terms.7 = (f32[56,128]{1,0:T(8,128)S(1)}, f32[56,128]{1,0:T(8,128)S(1)}, f32[56,128]{1,0:T(8,128)S(1)}, f32[56,128]{1,0:T(8,128)S(1)}) custom-call(f32[64,2,128,128]{3,2,1,0:T(8,128)S(1)} %get-tuple-element.84.z_ref, f32[2,128,128]{2,1,0:T(8,128)S(1)} %get-tuple-element.85.r_ref), custom_call_target="tpu_custom_call" | custom-call | tf_op jit(solution)/shard_map/terms/pallas_call | solution.py:429
  78.8 2.1 %collective-permute-start.32 = (f32[56,128]{1,0:T(8,128)S(1)}, f32[56,128]{1,0:T(8,128)S(1)}, u32[]{:S(2)}, u32[]{:S(2)}) collective-permute-start(f32[56,128]{1,0:T(8,128)S(1)} %get-tuple-element.107), channel_id=1, source_target_pairs={{0,2},{1,3},{2,0},{3,1},{4,6},{5,7},{6,4},{7,5},{8,10},{9,11},{10,... | collective-permute-start | bytes 86024 | tf_op jit(solution)/shard_map/ppermute | solution.py:442
  81.0 2.2 %collective-permute-start.33 = (f32[56,128]{1,0:T(8,128)S(1)}, f32[56,128]{1,0:T(8,128)S(1)}, u32[]{:S(2)}, u32[]{:S(2)}) collective-permute-start(f32[56,128]{1,0:T(8,128)S(1)} %get-tuple-element.99), channel_id=1, source_target_pairs={{0,3},{1,2},{2,1},{3,0},{4,7},{5,6},{6,5},{7,4},{8,11},{9,10},{10,... | collective-permute-start | bytes 86024 | tf_op jit(solution)/shard_map/ppermute | solution.py:442
  84.8 1.9 %collective-permute-done.33.refs_3_ = f32[56,128]{1,0:T(8,128)S(1)} collective-permute-done((f32[56,128]{1,0:T(8,128)S(1)}, f32[56,128]{1,0:T(8,128)S(1)}, u32[]{:S(2)}, u32[]{:S(2)}) %collective-permute-start.33) | collective-permute-done | bytes 28704 | tf_op jit(solution)/shard_map/ppermute | solution.py:442
  87.8 1.3 %collective-permute-start.35 = (f32[8,128]{1,0:T(8,128)S(1)}, f32[8,128]{1,0:T(8,128)S(1)}, u32[]{:S(2)}, u32[]{:S(2)}) collective-permute-start(f32[8,128]{1,0:T(8,128)S(1)} %get-tuple-element.93.refs_0_), channel_id=1, source_target_pairs={{0,8},{4,12},{8,0},{12,4},{1,9},{5,13},{9,1},{13,5},{2,10},{6,14},... | collective-permute-start | bytes 12296 | tf_op jit(solution)/shard_map/ppermute | solution.py:442
  (64 shorter events, 22.3 us)
Async XLA Ops:
  1.6 6.7 %collective-permute-start.5 = (f32[64,128]{1,0:T(8,128)S(1)}, f32[64,128]{1,0:T(8,128)S(1)}, u32[]{:S(2)}, u32[]{:S(2)}) collective-permute-start(f32[64,128]{1,0:T(8,128)S(1)} %get-tuple-element.51.refs_0_.refs_1_), channel_id=1, source_target_pairs={{0,12},{4,8},{8,4},{12,0},{1,13},{5,9},{9,5},{13,1},{2,14},{6,10},... | collective-permute-start | bytes 98312 | tf_op jit(solution)/shard_map/ppermute | solution.py:442
  4.1 8.2 %collective-permute-start.4 = (f32[64,128]{1,0:T(8,128)S(1)}, f32[64,128]{1,0:T(8,128)S(1)}, u32[]{:S(2)}, u32[]{:S(2)}) collective-permute-start(f32[64,128]{1,0:T(8,128)S(1)} %get-tuple-element.51.refs_0_.refs_1_), channel_id=1, source_target_pairs={{0,3},{1,2},{2,1},{3,0},{4,7},{5,6},{6,5},{7,4},{8,11},{9,10},{10,... | collective-permute-start | bytes 98312 | tf_op jit(solution)/shard_map/ppermute | solution.py:442
  7.7 4.6 %collective-permute-start.3 = (f32[64,128]{1,0:T(8,128)S(1)}, f32[64,128]{1,0:T(8,128)S(1)}, u32[]{:S(2)}, u32[]{:S(2)}) collective-permute-start(f32[64,128]{1,0:T(8,128)S(1)} %get-tuple-element.51.refs_0_.refs_1_), channel_id=1, source_target_pairs={{0,8},{4,12},{8,0},{12,4},{1,9},{5,13},{9,1},{13,5},{2,10},{6,14},... | collective-permute-start | bytes 98312 | tf_op jit(solution)/shard_map/ppermute | solution.py:442
  8.3 4.8 %collective-permute-start.2 = (f32[64,128]{1,0:T(8,128)S(1)}, f32[64,128]{1,0:T(8,128)S(1)}, u32[]{:S(2)}, u32[]{:S(2)}) collective-permute-start(f32[64,128]{1,0:T(8,128)S(1)} %get-tuple-element.51.refs_0_.refs_1_), channel_id=1, source_target_pairs={{0,2},{1,3},{2,0},{3,1},{4,6},{5,7},{6,4},{7,5},{8,10},{9,11},{10,... | collective-permute-start | bytes 98312 | tf_op jit(solution)/shard_map/ppermute | solution.py:442
  8.4 4.8 %collective-permute-start.1 = (f32[64,128]{1,0:T(8,128)S(1)}, f32[64,128]{1,0:T(8,128)S(1)}, u32[]{:S(2)}, u32[]{:S(2)}) collective-permute-start(f32[64,128]{1,0:T(8,128)S(1)} %get-tuple-element.51.refs_0_.refs_1_), channel_id=1, source_target_pairs={{0,4},{4,0},{8,12},{12,8},{1,5},{5,1},{9,13},{13,9},{2,6},{6,2},{1... | collective-permute-start | bytes 98312 | tf_op jit(solution)/shard_map/ppermute | solution.py:442
  8.4 4.8 %collective-permute-start = (f32[64,128]{1,0:T(8,128)S(1)}, f32[64,128]{1,0:T(8,128)S(1)}, u32[]{:S(2)}, u32[]{:S(2)}) collective-permute-start(f32[64,128]{1,0:T(8,128)S(1)} %get-tuple-element.51.refs_0_.refs_1_), channel_id=1, source_target_pairs={{0,1},{1,0},{2,3},{3,2},{4,5},{5,4},{6,7},{7,6},{8,9},{9,8},{10,11... | collective-permute-start | bytes 98312 | tf_op jit(solution)/shard_map/ppermute | solution.py:442
  19.4 6.5 %collective-permute-start.9 = (f32[104,128]{1,0:T(8,128)S(1)}, f32[104,128]{1,0:T(8,128)S(1)}, u32[]{:S(2)}, u32[]{:S(2)}) collective-permute-start(f32[104,128]{1,0:T(8,128)S(1)} %get-tuple-element.105), channel_id=1, source_target_pairs={{0,3},{1,2},{2,1},{3,0},{4,7},{5,6},{6,5},{7,4},{8,11},{9,10},{10,... | collective-permute-start | bytes 159752 | tf_op jit(solution)/shard_map/ppermute | solution.py:442
  22.7 5.0 %collective-permute-start.7 = (f32[104,128]{1,0:T(8,128)S(1)}, f32[104,128]{1,0:T(8,128)S(1)}, u32[]{:S(2)}, u32[]{:S(2)}) collective-permute-start(f32[104,128]{1,0:T(8,128)S(1)} %get-tuple-element.105), channel_id=1, source_target_pairs={{0,1},{1,0},{2,3},{3,2},{4,5},{5,4},{6,7},{7,6},{8,9},{9,8},{10,11... | collective-permute-start | bytes 159752 | tf_op jit(solution)/shard_map/ppermute | solution.py:442
  22.7 5.6 %collective-permute-start.8 = (f32[104,128]{1,0:T(8,128)S(1)}, f32[104,128]{1,0:T(8,128)S(1)}, u32[]{:S(2)}, u32[]{:S(2)}) collective-permute-start(f32[104,128]{1,0:T(8,128)S(1)} %get-tuple-element.106.refs_0_), channel_id=1, source_target_pairs={{0,2},{1,3},{2,0},{3,1},{4,6},{5,7},{6,4},{7,5},{8,10},{9,11},{10,... | collective-permute-start | bytes 159752 | tf_op jit(solution)/shard_map/ppermute | solution.py:442
  28.4 5.4 %collective-permute-start.13 = (f32[96,128]{1,0:T(8,128)S(1)}, f32[96,128]{1,0:T(8,128)S(1)}, u32[]{:S(2)}, u32[]{:S(2)}) collective-permute-start(f32[96,128]{1,0:T(8,128)S(1)} %get-tuple-element.60.refs_4_), channel_id=1, source_target_pairs={{0,1},{1,0},{2,3},{3,2},{4,5},{5,4},{6,7},{7,6},{8,9},{9,8},{10,11... | collective-permute-start | bytes 147464 | tf_op jit(solution)/shard_map/ppermute | solution.py:442
  30.0 3.5 %collective-permute-start.12 = (f32[56,128]{1,0:T(8,128)S(1)}, f32[56,128]{1,0:T(8,128)S(1)}, u32[]{:S(2)}, u32[]{:S(2)}) collective-permute-start(f32[56,128]{1,0:T(8,128)S(1)} %get-tuple-element.59.refs_0_), channel_id=1, source_target_pairs={{0,12},{4,8},{8,4},{12,0},{1,13},{5,9},{9,5},{13,1},{2,14},{6,10},... | collective-permute-start | bytes 86024 | tf_op jit(solution)/shard_map/ppermute | solution.py:442
  30.0 3.9 %collective-permute-start.11 = (f32[56,128]{1,0:T(8,128)S(1)}, f32[56,128]{1,0:T(8,128)S(1)}, u32[]{:S(2)}, u32[]{:S(2)}) collective-permute-start(f32[56,128]{1,0:T(8,128)S(1)} %get-tuple-element.59.refs_0_), channel_id=1, source_target_pairs={{0,8},{4,12},{8,0},{12,4},{1,9},{5,13},{9,1},{13,5},{2,10},{6,14},... | collective-permute-start | bytes 86024 | tf_op jit(solution)/shard_map/ppermute | solution.py:442
  36.9 3.1 %collective-permute-start.14 = (f32[8,128]{1,0:T(8,128)S(1)}, f32[8,128]{1,0:T(8,128)S(1)}, u32[]{:S(2)}, u32[]{:S(2)}) collective-permute-start(f32[8,128]{1,0:T(8,128)S(1)} %get-tuple-element.69), channel_id=1, source_target_pairs={{0,20},{4,16},{8,28},{12,24},{16,4},{20,0},{24,12},{28,8},{1,21},{... | collective-permute-start | bytes 12296 | tf_op jit(solution)/shard_map/ppermute | solution.py:442
  40.1 6.5 %collective-permute-start.17 = (f32[104,128]{1,0:T(8,128)S(1)}, f32[104,128]{1,0:T(8,128)S(1)}, u32[]{:S(2)}, u32[]{:S(2)}) collective-permute-start(f32[104,128]{1,0:T(8,128)S(1)} %get-tuple-element.103), channel_id=1, source_target_pairs={{0,3},{1,2},{2,1},{3,0},{4,7},{5,6},{6,5},{7,4},{8,11},{9,10},{10,... | collective-permute-start | bytes 159752 | tf_op jit(solution)/shard_map/ppermute | solution.py:442
  41.7 5.7 %collective-permute-start.15 = (f32[104,128]{1,0:T(8,128)S(1)}, f32[104,128]{1,0:T(8,128)S(1)}, u32[]{:S(2)}, u32[]{:S(2)}) collective-permute-start(f32[104,128]{1,0:T(8,128)S(1)} %get-tuple-element.103), channel_id=1, source_target_pairs={{0,1},{1,0},{2,3},{3,2},{4,5},{5,4},{6,7},{7,6},{8,9},{9,8},{10,11... | collective-permute-start | bytes 159752 | tf_op jit(solution)/shard_map/ppermute | solution.py:442
  42.3 6.0 %collective-permute-start.16 = (f32[104,128]{1,0:T(8,128)S(1)}, f32[104,128]{1,0:T(8,128)S(1)}, u32[]{:S(2)}, u32[]{:S(2)}) collective-permute-start(f32[104,128]{1,0:T(8,128)S(1)} %get-tuple-element.104.refs_0_), channel_id=1, source_target_pairs={{0,2},{1,3},{2,0},{3,1},{4,6},{5,7},{6,4},{7,5},{8,10},{9,11},{10,... | collective-permute-start | bytes 159752 | tf_op jit(solution)/shard_map/ppermute | solution.py:442
  48.4 4.4 %collective-permute-start.21 = (f32[96,128]{1,0:T(8,128)S(1)}, f32[96,128]{1,0:T(8,128)S(1)}, u32[]{:S(2)}, u32[]{:S(2)}) collective-permute-start(f32[96,128]{1,0:T(8,128)S(1)} %get-tuple-element.72.refs_4_), channel_id=1, source_target_pairs={{0,1},{1,0},{2,3},{3,2},{4,5},{5,4},{6,7},{7,6},{8,9},{9,8},{10,11... | collective-permute-start | bytes 147464 | tf_op jit(solution)/shard_map/ppermute | solution.py:442
  48.9 3.6 %collective-permute-start.20 = (f32[56,128]{1,0:T(8,128)S(1)}, f32[56,128]{1,0:T(8,128)S(1)}, u32[]{:S(2)}, u32[]{:S(2)}) collective-permute-start(f32[56,128]{1,0:T(8,128)S(1)} %get-tuple-element.71.refs_0_), channel_id=1, source_target_pairs={{0,12},{4,8},{8,4},{12,0},{1,13},{5,9},{9,5},{13,1},{2,14},{6,10},... | collective-permute-start | bytes 86024 | tf_op jit(solution)/shard_map/ppermute | solution.py:442
  48.9 3.9 %collective-permute-start.19 = (f32[56,128]{1,0:T(8,128)S(1)}, f32[56,128]{1,0:T(8,128)S(1)}, u32[]{:S(2)}, u32[]{:S(2)}) collective-permute-start(f32[56,128]{1,0:T(8,128)S(1)} %get-tuple-element.71.refs_0_), channel_id=1, source_target_pairs={{0,8},{4,12},{8,0},{12,4},{1,9},{5,13},{9,1},{13,5},{2,10},{6,14},... | collective-permute-start | bytes 86024 | tf_op jit(solution)/shard_map/ppermute | solution.py:442
  55.9 3.1 %collective-permute-start.22 = (f32[8,128]{1,0:T(8,128)S(1)}, f32[8,128]{1,0:T(8,128)S(1)}, u32[]{:S(2)}, u32[]{:S(2)}) collective-permute-start(f32[8,128]{1,0:T(8,128)S(1)} %get-tuple-element.78), channel_id=1, source_target_pairs={{0,20},{4,16},{8,28},{12,24},{16,4},{20,0},{24,12},{28,8},{1,21},{... | collective-permute-start | bytes 12296 | tf_op jit(solution)/shard_map/ppermute | solution.py:442
  59.0 6.4 %collective-permute-start.25 = (f32[104,128]{1,0:T(8,128)S(1)}, f32[104,128]{1,0:T(8,128)S(1)}, u32[]{:S(2)}, u32[]{:S(2)}) collective-permute-start(f32[104,128]{1,0:T(8,128)S(1)} %get-tuple-element.101), channel_id=1, source_target_pairs={{0,3},{1,2},{2,1},{3,0},{4,7},{5,6},{6,5},{7,4},{8,11},{9,10},{10,... | collective-permute-start | bytes 159752 | tf_op jit(solution)/shard_map/ppermute | solution.py:442
  61.3 5.9 %collective-permute-start.23 = (f32[104,128]{1,0:T(8,128)S(1)}, f32[104,128]{1,0:T(8,128)S(1)}, u32[]{:S(2)}, u32[]{:S(2)}) collective-permute-start(f32[104,128]{1,0:T(8,128)S(1)} %get-tuple-element.101), channel_id=1, source_target_pairs={{0,1},{1,0},{2,3},{3,2},{4,5},{5,4},{6,7},{7,6},{8,9},{9,8},{10,11... | collective-permute-start | bytes 159752 | tf_op jit(solution)/shard_map/ppermute | solution.py:442
  61.9 5.4 %collective-permute-start.24 = (f32[104,128]{1,0:T(8,128)S(1)}, f32[104,128]{1,0:T(8,128)S(1)}, u32[]{:S(2)}, u32[]{:S(2)}) collective-permute-start(f32[104,128]{1,0:T(8,128)S(1)} %get-tuple-element.102.refs_0_), channel_id=1, source_target_pairs={{0,2},{1,3},{2,0},{3,1},{4,6},{5,7},{6,4},{7,5},{8,10},{9,11},{10,... | collective-permute-start | bytes 159752 | tf_op jit(solution)/shard_map/ppermute | solution.py:442
  67.4 5.1 %collective-permute-start.29 = (f32[96,128]{1,0:T(8,128)S(1)}, f32[96,128]{1,0:T(8,128)S(1)}, u32[]{:S(2)}, u32[]{:S(2)}) collective-permute-start(f32[96,128]{1,0:T(8,128)S(1)} %get-tuple-element.81.refs_4_), channel_id=1, source_target_pairs={{0,1},{1,0},{2,3},{3,2},{4,5},{5,4},{6,7},{7,6},{8,9},{9,8},{10,11... | collective-permute-start | bytes 147464 | tf_op jit(solution)/shard_map/ppermute | solution.py:442
  68.6 3.5 %collective-permute-start.28 = (f32[56,128]{1,0:T(8,128)S(1)}, f32[56,128]{1,0:T(8,128)S(1)}, u32[]{:S(2)}, u32[]{:S(2)}) collective-permute-start(f32[56,128]{1,0:T(8,128)S(1)} %get-tuple-element.80.refs_0_), channel_id=1, source_target_pairs={{0,12},{4,8},{8,4},{12,0},{1,13},{5,9},{9,5},{13,1},{2,14},{6,10},... | collective-permute-start | bytes 86024 | tf_op jit(solution)/shard_map/ppermute | solution.py:442
  68.6 3.9 %collective-permute-start.27 = (f32[56,128]{1,0:T(8,128)S(1)}, f32[56,128]{1,0:T(8,128)S(1)}, u32[]{:S(2)}, u32[]{:S(2)}) collective-permute-start(f32[56,128]{1,0:T(8,128)S(1)} %get-tuple-element.80.refs_0_), channel_id=1, source_target_pairs={{0,8},{4,12},{8,0},{12,4},{1,9},{5,13},{9,1},{13,5},{2,10},{6,14},... | collective-permute-start | bytes 86024 | tf_op jit(solution)/shard_map/ppermute | solution.py:442
  75.5 3.2 %collective-permute-start.30 = (f32[8,128]{1,0:T(8,128)S(1)}, f32[8,128]{1,0:T(8,128)S(1)}, u32[]{:S(2)}, u32[]{:S(2)}) collective-permute-start(f32[8,128]{1,0:T(8,128)S(1)} %get-tuple-element.87), channel_id=1, source_target_pairs={{0,20},{4,16},{8,28},{12,24},{16,4},{20,0},{24,12},{28,8},{1,21},{... | collective-permute-start | bytes 12296 | tf_op jit(solution)/shard_map/ppermute | solution.py:442
  78.8 4.8 %collective-permute-start.32 = (f32[56,128]{1,0:T(8,128)S(1)}, f32[56,128]{1,0:T(8,128)S(1)}, u32[]{:S(2)}, u32[]{:S(2)}) collective-permute-start(f32[56,128]{1,0:T(8,128)S(1)} %get-tuple-element.107), channel_id=1, source_target_pairs={{0,2},{1,3},{2,0},{3,1},{4,6},{5,7},{6,4},{7,5},{8,10},{9,11},{10,... | collective-permute-start | bytes 86024 | tf_op jit(solution)/shard_map/ppermute | solution.py:442
  80.9 3.9 %collective-permute-start.31 = (f32[56,128]{1,0:T(8,128)S(1)}, f32[56,128]{1,0:T(8,128)S(1)}, u32[]{:S(2)}, u32[]{:S(2)}) collective-permute-start(f32[56,128]{1,0:T(8,128)S(1)} %get-tuple-element.108), channel_id=1, source_target_pairs={{0,1},{1,0},{2,3},{3,2},{4,5},{5,4},{6,7},{7,6},{8,9},{9,8},{10,11... | collective-permute-start | bytes 86024 | tf_op jit(solution)/shard_map/ppermute | solution.py:442
  81.0 5.7 %collective-permute-start.33 = (f32[56,128]{1,0:T(8,128)S(1)}, f32[56,128]{1,0:T(8,128)S(1)}, u32[]{:S(2)}, u32[]{:S(2)}) collective-permute-start(f32[56,128]{1,0:T(8,128)S(1)} %get-tuple-element.99), channel_id=1, source_target_pairs={{0,3},{1,2},{2,1},{3,0},{4,7},{5,6},{6,5},{7,4},{8,11},{9,10},{10,... | collective-permute-start | bytes 86024 | tf_op jit(solution)/shard_map/ppermute | solution.py:442
  86.8 4.7 %collective-permute-start.37 = (f32[144,128]{1,0:T(8,128)S(1)}, f32[144,128]{1,0:T(8,128)S(1)}, u32[]{:S(2)}, u32[]{:S(2)}) collective-permute-start(f32[144,128]{1,0:T(8,128)S(1)} %get-tuple-element.94.refs_4_), channel_id=1, source_target_pairs={{0,16},{16,0},{1,17},{17,1},{2,18},{18,2},{3,19},{19,3},{4,20},{20... | collective-permute-start | bytes 221192 | tf_op jit(solution)/shard_map/ppermute | solution.py:442
  87.8 3.6 %collective-permute-start.35 = (f32[8,128]{1,0:T(8,128)S(1)}, f32[8,128]{1,0:T(8,128)S(1)}, u32[]{:S(2)}, u32[]{:S(2)}) collective-permute-start(f32[8,128]{1,0:T(8,128)S(1)} %get-tuple-element.93.refs_0_), channel_id=1, source_target_pairs={{0,8},{4,12},{8,0},{12,4},{1,9},{5,13},{9,1},{13,5},{2,10},{6,14},... | collective-permute-start | bytes 12296 | tf_op jit(solution)/shard_map/ppermute | solution.py:442
  (6 other events, 15.9 us)

commit v7 on v6

--- a/solution.py
+++ b/solution.py
@@ -235,7 +235,7 @@
     return lax.rem(lane_block(shape, span), 2) == lax.rem(j, 2)
 
 
-def terms_kernel(z_ref, r_ref, same_ref, other_ref, all_ref, *, span):
+def terms_kernel(z_ref, r_ref, own_ref, other_ref, same_ref, all_ref, *, span):
     dirs, _, cols, rows = z_ref.shape
     half = dirs // 2
     normal_terms(z_ref, r_ref, all_ref)
@@ -243,9 +243,11 @@
     for q in range(3):
         low = all_ref[q * dirs : q * dirs + half, :]
         high = pltpu.roll(all_ref[q * dirs + half : (q + 1) * dirs, :], span, 1)
-        same_ref[q * half : (q + 1) * half, :] = jnp.where(mine, low, high)
+        keep = jnp.where(mine, low, high)
+        own_ref[q * half : (q + 1) * half, :] = keep
+        same_ref[q * half : (q + 1) * half, :] = keep
         other_ref[q * half : (q + 1) * half, :] = jnp.where(mine, high, low)
-    for ref in (same_ref, other_ref):
+    for ref in (own_ref, same_ref, other_ref):
         ref[3 * half :, :] = jnp.zeros((8, rows), jnp.float32)
 
 
@@ -285,8 +287,8 @@
 
 
 def first_kernel(*refs, ns, nz, span):
-    rows_in = refs[: 2 * nz : 2]
-    cols_in = refs[1 : 2 * nz : 2]
+    cols_in = refs[:ns]
+    rows_in = refs[ns : ns + nz]
     mt_ref, vt_ref = refs[nz + ns : nz + ns + 2]
     outs = refs[nz + ns + 2 : nz + ns + 5]
     grow_ref, gcol_ref, trow_ref, tcol_ref, ct_ref = refs[nz + ns + 5 :]
@@ -470,10 +472,8 @@
         [pltpu.VMEM(x.shape, jnp.float32) for x in own_in] + [pltpu.SemaphoreType.DMA((3,))],
         HBM,
     )
-    row_parts, col_parts = [start], [start]
-    for n in range(1, max(ns, nz)):
-        col_parts += [swap(start, "srow", n)] if n < ns else []
-        row_parts += [swap(start, "scol", n)] if n < nz else []
+    col_parts = [start] + [swap(start, "srow", n) for n in range(1, ns)]
+    row_parts = [start] + [swap(start, "scol", n) for n in range(1, nz)]
     field_in = [rho, cluster, flags[0], model[0], vis[0]]
     mt, vt, rho_rows, rho_packed = call(
         prepare_kernel,
@@ -499,7 +499,7 @@
         functools.partial(first_kernel, ns=ns, nz=nz, span=span),
         "first",
         [],
-        [part for parts in zip(row_parts, col_parts) for part in parts] + [mt, vt],
+        col_parts + row_parts + [mt, vt],
         fields + [plane, plane, plane, plane],
         scratch,
     )
@@ -512,21 +512,22 @@
         if last:
             break
         half = 3 * dirs // 2
-        same, other = call(
+        own, other, same = call(
             functools.partial(terms_kernel, span=span),
             "terms",
             [],
             [z, r],
-            [f32(half + 8, rows)] * 2,
+            [f32(half + 8, rows)] * 3,
             [pltpu.VMEM((3 * dirs, rows), jnp.float32)],
         )
-        same = lax.dynamic_update_slice(same, power, (half, 0))
-        other = lax.dynamic_update_slice(other, power, (half, 0))
+        own, other, same = [
+            lax.dynamic_update_slice(piece, power, (half, 0)) for piece in (own, other, same)
+        ]
         pair_sums, own = call(
             functools.partial(combine_kernel, nz=nz, span=span),
             "combine",
             [],
-            [same] + [swap(same if n % 2 == 0 else other, "scol", n) for n in range(1, nz)],
+            [own] + [swap(same if n % 2 == 0 else other, "scol", n) for n in (1, 3, 2)],
             [f32(half, rows), f32(3 * depth + 8, rows)],
         )
         other_sums = swap(pair_sums, "scol", 1)
@@ -553,7 +554,7 @@
         functools.partial(last_combine_kernel, nz=nz, span=span),
         "combine",
         [],
-        [parts[0]] + [swap(parts[n], "scol", n) for n in range(1, nz)] + [grow, trow, dual_packed],
+        [parts[0]] + [swap(parts[n], "scol", n) for n in (3, 2, 1)] + [grow, trow, dual_packed],
         [f32(8, rows), f32(9 * depth, rows)],
     )
     powers = [power] + [swap(power, "srow", n) for n in range(1, ns)]

time: 92.6 us -> 93.4 us (level)
  waiting for transfers between devices: 24.7 us -> 28.9 us
  starting transfers between devices: 40.6 us -> 37.1 us
    ppermute x38, waiting for transfers between devices: 24.7 us -> 28.9 us  [swap(): return lax.ppermute(x, axis, [(m, m ^ n) for m in range(size)])]
    ppermute x38, starting transfers between devices: 40.6 us -> 37.1 us  [swap(): return lax.ppermute(x, axis, [(m, m ^ n) for m in range(size)])]
  transfers between devices with their start and end apart: 38 -> 38, of which waited for: 21 -> 20; matrix products, arithmetic and copies ran while one was open for 0% -> 0% of each run, Pallas kernels for 13% -> 12%
where the time goes in v7:
time: 93.4 us; the launch traced here: 93.2 us
  starting transfers between devices  37.1 us (40%)
  waiting for transfers between devices  28.9 us (31%)
  Pallas kernels  26.3 us (28%)
    ppermute x38, starting transfers between devices, swap(): return lax.ppermute(x, axis, [(m, m ^ n) for m in range(size)])  37.1 us
    ppermute x38, waiting for transfers between devices, swap(): return lax.ppermute(x, axis, [(m, m ^ n) for m in range(size)])  28.9 us
    pallas_call x15, Pallas kernels, call(): pl.pallas_call(kernel, in_specs=[SMEM] * len(lead) + [place] * len(args),...  26.3 us
  transfers between devices with their start and end apart: 38, of which 20 were waited for; matrix products, arithmetic and copies ran while one was open for 0% of the time, Pallas kernels for 12%

profile of v7, /device:TPU:0, one launch (start us, length us, event | category | flops | bytes accessed | tf_op | source)
XLA Modules:
  0.0 93.2 jit_solution(9372543289560941852)
XLA Ops:
  1.6 5.1 %collective-permute-start.5 = (f32[64,128]{1,0:T(8,128)S(1)}, f32[64,128]{1,0:T(8,128)S(1)}, u32[]{:S(2)}, u32[]{:S(2)}) collective-permute-start(f32[64,128]{1,0:T(8,128)S(1)} %get-tuple-element.54.refs_0_.refs_4_), channel_id=1, source_target_pairs={{0,3},{1,2},{2,1},{3,0},{4,7},{5,6},{6,5},{7,4},{8,11},{9,10},{10,... | collective-permute-start | bytes 98312 | tf_op jit(solution)/shard_map/ppermute | solution.py:444
  7.8 1.3 %collective-permute-start.1 = (f32[64,128]{1,0:T(8,128)S(1)}, f32[64,128]{1,0:T(8,128)S(1)}, u32[]{:S(2)}, u32[]{:S(2)}) collective-permute-start(f32[64,128]{1,0:T(8,128)S(1)} %get-tuple-element.54.refs_0_.refs_4_), channel_id=1, source_target_pairs={{0,8},{4,12},{8,0},{12,4},{1,9},{5,13},{9,1},{13,5},{2,10},{6,14},... | collective-permute-start | bytes 98312 | tf_op jit(solution)/shard_map/ppermute | solution.py:444
  9.3 3.2 %prepare.1 = (bf16[64,2,128,128]{3,2,1,0:T(8,128)(2,1)S(1)}, f32[2,128,128]{2,1,0:T(8,128)S(1)}, f32[64,128]{1,0:T(8,128)S(1)}, f32[16,128]{1,0:T(8,128)S(1)}) custom-call(f32[8]{0:T(128)} %refs_0_.1, s32[64]{0:T(128)} %refs_1_.1, s32[8,8]{1,0:T(8,128)} %bitcast.24, bf16[64,2,128,128]{3,2,1,0:T(8,128)(2,1)} %bitcast.19, bf16[2,128,128]{2,1,0:T(8,128)(2,1)} %bitcast.20), custom_call_target="tpu_custom_call" | custom-call | tf_op jit(solution)/shard_map/prepare/pallas_call | solution.py:431
  12.5 3.2 %first.1 = (f32[64,2,128,128]{3,2,1,0:T(8,128)S(1)}, f32[2,128,128]{2,1,0:T(8,128)S(1)}, f32[8,128]{1,0:T(8,128)S(1)}, f32[128,128]{1,0:T(8,128)S(1)}, f32[128,1...) custom-call(f32[64,128]{1,0:T(8,128)S(1)} %get-tuple-element.54.refs_0_.refs_4_, ...), custom_call_target="tpu_custom_call" | custom-call | tf_op jit(solution)/shard_map/first/pallas_call | solution.py:431
  15.7 1.5 %collective-permute-start.6 = (f32[8,128]{1,0:T(8,128)S(1)}, f32[8,128]{1,0:T(8,128)S(1)}, u32[]{:S(2)}, u32[]{:S(2)}) collective-permute-start(f32[8,128]{1,0:T(8,128)S(1)} %get-tuple-element.60), channel_id=1, source_target_pairs={{0,20},{4,16},{8,28},{12,24},{16,4},{20,0},{24,12},{28,8},{1,21},{... | collective-permute-start | bytes 12296 | tf_op jit(solution)/shard_map/ppermute | solution.py:444
  17.2 2.1 %terms.4 = (f32[104,128]{1,0:T(8,128)S(1)}, f32[104,128]{1,0:T(8,128)S(1)}, f32[104,128]{1,0:T(8,128)S(1)}) custom-call(f32[64,2,128,128]{3,2,1,0:T(8,128)S(1)} %get-tuple-element.57.z_ref, f32[2,128,128]{2,1,0:T(8,128)S(1)} %get-tuple-element.58.r_ref), custom_call_target="tpu_custom_call" | custom-call | tf_op jit(solution)/shard_map/terms/pallas_call | solution.py:431
  19.3 2.2 %collective-permute-start.9 = (f32[104,128]{1,0:T(8,128)S(1)}, f32[104,128]{1,0:T(8,128)S(1)}, u32[]{:S(2)}, u32[]{:S(2)}) collective-permute-start(f32[104,128]{1,0:T(8,128)S(1)} %get-tuple-element.113), channel_id=1, source_target_pairs={{0,2},{1,3},{2,0},{3,1},{4,6},{5,7},{6,4},{7,5},{8,10},{9,11},{10,... | collective-permute-start | bytes 159752 | tf_op jit(solution)/shard_map/ppermute | solution.py:444
  21.5 1.5 %collective-permute-start.8 = (f32[104,128]{1,0:T(8,128)S(1)}, f32[104,128]{1,0:T(8,128)S(1)}, u32[]{:S(2)}, u32[]{:S(2)}) collective-permute-start(f32[104,128]{1,0:T(8,128)S(1)} %get-tuple-element.114), channel_id=1, source_target_pairs={{0,3},{1,2},{2,1},{3,0},{4,7},{5,6},{6,5},{7,4},{8,11},{9,10},{10,... | collective-permute-start | bytes 159752 | tf_op jit(solution)/shard_map/ppermute | solution.py:444
  23.5 2.0 %collective-permute-done.9.refs_3_ = f32[104,128]{1,0:T(8,128)S(1)} collective-permute-done((f32[104,128]{1,0:T(8,128)S(1)}, f32[104,128]{1,0:T(8,128)S(1)}, u32[]{:S(2)}, u32[]{:S(2)}) %collective-permute-start.9) | collective-permute-done | bytes 53280 | tf_op jit(solution)/shard_map/ppermute | solution.py:444
  25.5 2.4 %collective-permute-done.8.refs_2_ = f32[104,128]{1,0:T(8,128)S(1)} collective-permute-done((f32[104,128]{1,0:T(8,128)S(1)}, f32[104,128]{1,0:T(8,128)S(1)}, u32[]{:S(2)}, u32[]{:S(2)}) %collective-permute-start.8) | collective-permute-done | bytes 53280 | tf_op jit(solution)/shard_map/ppermute | solution.py:444
  29.1 1.1 %collective-permute-start.11 = (f32[56,128]{1,0:T(8,128)S(1)}, f32[56,128]{1,0:T(8,128)S(1)}, u32[]{:S(2)}, u32[]{:S(2)}) collective-permute-start(f32[56,128]{1,0:T(8,128)S(1)} %get-tuple-element.63.refs_0_), channel_id=1, source_target_pairs={{0,8},{4,12},{8,0},{12,4},{1,9},{5,13},{9,1},{13,5},{2,10},{6,14},... | collective-permute-start | bytes 86024 | tf_op jit(solution)/shard_map/ppermute | solution.py:444
  30.3 1.5 %collective-permute-done.12.refs_3_ = f32[56,128]{1,0:T(8,128)S(1)} collective-permute-done((f32[56,128]{1,0:T(8,128)S(1)}, f32[56,128]{1,0:T(8,128)S(1)}, u32[]{:S(2)}, u32[]{:S(2)}) %collective-permute-start.12) | collective-permute-done | bytes 28704 | tf_op jit(solution)/shard_map/ppermute | solution.py:444
  31.9 1.2 %collective-permute-done.11.refs_2_ = f32[56,128]{1,0:T(8,128)S(1)} collective-permute-done((f32[56,128]{1,0:T(8,128)S(1)}, f32[56,128]{1,0:T(8,128)S(1)}, u32[]{:S(2)}, u32[]{:S(2)}) %collective-permute-start.11) | collective-permute-done | bytes 28704 | tf_op jit(solution)/shard_map/ppermute | solution.py:444
  33.1 3.1 %sweep.3 = (f32[64,2,128,128]{3,2,1,0:T(8,128)S(1)}, f32[2,128,128]{2,1,0:T(8,128)S(1)}, f32[8,128]{1,0:T(8,128)S(1)}, f32[128,128]{1,0:T(8,128)S(1)}, f32[128,128]{1,0:T(8,128)S(1)}) custom-call(f32[56,128]{1,0:T(8,128)S(1)} %get-tuple-element.63.refs_0_, f32[56,128]{1,0:T(8,128)S(1)} %collective-permute-done.10.refs_1_, ...), custom_call_target="tpu_custom_call" | custom-call | tf_op jit(solution)/shard_map/sweep/pallas_call | solution.py:431
  36.4 2.1 %terms.5 = (f32[104,128]{1,0:T(8,128)S(1)}, f32[104,128]{1,0:T(8,128)S(1)}, f32[104,128]{1,0:T(8,128)S(1)}) custom-call(f32[64,2,128,128]{3,2,1,0:T(8,128)S(1)} %get-tuple-element.70.z_ref, f32[2,128,128]{2,1,0:T(8,128)S(1)} %get-tuple-element.71.r_ref), custom_call_target="tpu_custom_call" | custom-call | tf_op jit(solution)/shard_map/terms/pallas_call | solution.py:431
  39.3 3.3 %collective-permute-start.17 = (f32[104,128]{1,0:T(8,128)S(1)}, f32[104,128]{1,0:T(8,128)S(1)}, u32[]{:S(2)}, u32[]{:S(2)}) collective-permute-start(f32[104,128]{1,0:T(8,128)S(1)} %get-tuple-element.110), channel_id=1, source_target_pairs={{0,2},{1,3},{2,0},{3,1},{4,6},{5,7},{6,4},{7,5},{8,10},{9,11},{10,... | collective-permute-start | bytes 159752 | tf_op jit(solution)/shard_map/ppermute | solution.py:444
  43.2 3.0 %collective-permute-done.17.refs_3_ = f32[104,128]{1,0:T(8,128)S(1)} collective-permute-done((f32[104,128]{1,0:T(8,128)S(1)}, f32[104,128]{1,0:T(8,128)S(1)}, u32[]{:S(2)}, u32[]{:S(2)}) %collective-permute-start.17) | collective-permute-done | bytes 53280 | tf_op jit(solution)/shard_map/ppermute | solution.py:444
  46.1 2.3 %collective-permute-done.16.refs_2_ = f32[104,128]{1,0:T(8,128)S(1)} collective-permute-done((f32[104,128]{1,0:T(8,128)S(1)}, f32[104,128]{1,0:T(8,128)S(1)}, u32[]{:S(2)}, u32[]{:S(2)}) %collective-permute-start.16) | collective-permute-done | bytes 53280 | tf_op jit(solution)/shard_map/ppermute | solution.py:444
  50.7 1.4 %collective-permute-done.20.refs_3_ = f32[56,128]{1,0:T(8,128)S(1)} collective-permute-done((f32[56,128]{1,0:T(8,128)S(1)}, f32[56,128]{1,0:T(8,128)S(1)}, u32[]{:S(2)}, u32[]{:S(2)}) %collective-permute-start.20) | collective-permute-done | bytes 28704 | tf_op jit(solution)/shard_map/ppermute | solution.py:444
  53.0 3.1 %sweep.4 = (f32[64,2,128,128]{3,2,1,0:T(8,128)S(1)}, f32[2,128,128]{2,1,0:T(8,128)S(1)}, f32[8,128]{1,0:T(8,128)S(1)}, f32[128,128]{1,0:T(8,128)S(1)}, f32[128,128]{1,0:T(8,128)S(1)}) custom-call(f32[56,128]{1,0:T(8,128)S(1)} %get-tuple-element.76.refs_0_, f32[56,128]{1,0:T(8,128)S(1)} %collective-permute-done.18.refs_1_, ...), custom_call_target="tpu_custom_call" | custom-call | tf_op jit(solution)/shard_map/sweep/pallas_call | solution.py:431
  57.0 2.1 %terms.6 = (f32[104,128]{1,0:T(8,128)S(1)}, f32[104,128]{1,0:T(8,128)S(1)}, f32[104,128]{1,0:T(8,128)S(1)}) custom-call(f32[64,2,128,128]{3,2,1,0:T(8,128)S(1)} %get-tuple-element.80.z_ref, f32[2,128,128]{2,1,0:T(8,128)S(1)} %get-tuple-element.81.r_ref), custom_call_target="tpu_custom_call" | custom-call | tf_op jit(solution)/shard_map/terms/pallas_call | solution.py:431
  59.2 2.7 %collective-permute-start.25 = (f32[104,128]{1,0:T(8,128)S(1)}, f32[104,128]{1,0:T(8,128)S(1)}, u32[]{:S(2)}, u32[]{:S(2)}) collective-permute-start(f32[104,128]{1,0:T(8,128)S(1)} %get-tuple-element.107), channel_id=1, source_target_pairs={{0,2},{1,3},{2,0},{3,1},{4,6},{5,7},{6,4},{7,5},{8,10},{9,11},{10,... | collective-permute-start | bytes 159752 | tf_op jit(solution)/shard_map/ppermute | solution.py:444
  61.9 1.5 %collective-permute-start.24 = (f32[104,128]{1,0:T(8,128)S(1)}, f32[104,128]{1,0:T(8,128)S(1)}, u32[]{:S(2)}, u32[]{:S(2)}) collective-permute-start(f32[104,128]{1,0:T(8,128)S(1)} %get-tuple-element.108), channel_id=1, source_target_pairs={{0,3},{1,2},{2,1},{3,0},{4,7},{5,6},{6,5},{7,4},{8,11},{9,10},{10,... | collective-permute-start | bytes 159752 | tf_op jit(solution)/shard_map/ppermute | solution.py:444
  64.3 3.9 %collective-permute-done.24.refs_2_ = f32[104,128]{1,0:T(8,128)S(1)} collective-permute-done((f32[104,128]{1,0:T(8,128)S(1)}, f32[104,128]{1,0:T(8,128)S(1)}, u32[]{:S(2)}, u32[]{:S(2)}) %collective-permute-start.24) | collective-permute-done | bytes 53280 | tf_op jit(solution)/shard_map/ppermute | solution.py:444
  68.6 1.1 %collective-permute-start.27 = (f32[56,128]{1,0:T(8,128)S(1)}, f32[56,128]{1,0:T(8,128)S(1)}, u32[]{:S(2)}, u32[]{:S(2)}) collective-permute-start(f32[56,128]{1,0:T(8,128)S(1)} %get-tuple-element.86.refs_0_), channel_id=1, source_target_pairs={{0,8},{4,12},{8,0},{12,4},{1,9},{5,13},{9,1},{13,5},{2,10},{6,14},... | collective-permute-start | bytes 86024 | tf_op jit(solution)/shard_map/ppermute | solution.py:444
  70.5 1.4 %collective-permute-done.28.refs_3_ = f32[56,128]{1,0:T(8,128)S(1)} collective-permute-done((f32[56,128]{1,0:T(8,128)S(1)}, f32[56,128]{1,0:T(8,128)S(1)}, u32[]{:S(2)}, u32[]{:S(2)}) %collective-permute-start.28) | collective-permute-done | bytes 28704 | tf_op jit(solution)/shard_map/ppermute | solution.py:444
  72.6 3.1 %sweep.5 = (f32[64,2,128,128]{3,2,1,0:T(8,128)S(1)}, f32[2,128,128]{2,1,0:T(8,128)S(1)}, f32[8,128]{1,0:T(8,128)S(1)}, f32[128,128]{1,0:T(8,128)S(1)}, f32[128,128]{1,0:T(8,128)}) custom-call(f32[56,128]{1,0:T(8,128)S(1)} %get-tuple-element.86.refs_0_, f32[56,128]{1,0:T(8,128)S(1)} %collective-permute-done.26.refs_1_, ...), custom_call_target="tpu_custom_call" | custom-call | tf_op jit(solution)/shard_map/sweep/pallas_call | solution.py:431
  76.5 2.2 %terms.7 = (f32[56,128]{1,0:T(8,128)S(1)}, f32[56,128]{1,0:T(8,128)S(1)}, f32[56,128]{1,0:T(8,128)S(1)}, f32[56,128]{1,0:T(8,128)S(1)}) custom-call(f32[64,2,128,128]{3,2,1,0:T(8,128)S(1)} %get-tuple-element.90.z_ref, f32[2,128,128]{2,1,0:T(8,128)S(1)} %get-tuple-element.91.r_ref), custom_call_target="tpu_custom_call" | custom-call | tf_op jit(solution)/shard_map/terms/pallas_call | solution.py:431
  78.8 3.0 %collective-permute-start.32 = (f32[56,128]{1,0:T(8,128)S(1)}, f32[56,128]{1,0:T(8,128)S(1)}, u32[]{:S(2)}, u32[]{:S(2)}) collective-permute-start(f32[56,128]{1,0:T(8,128)S(1)} %get-tuple-element.116), channel_id=1, source_target_pairs={{0,2},{1,3},{2,0},{3,1},{4,6},{5,7},{6,4},{7,5},{8,10},{9,11},{10,... | collective-permute-start | bytes 86024 | tf_op jit(solution)/shard_map/ppermute | solution.py:444
  81.8 1.2 %collective-permute-start.31 = (f32[56,128]{1,0:T(8,128)S(1)}, f32[56,128]{1,0:T(8,128)S(1)}, u32[]{:S(2)}, u32[]{:S(2)}) collective-permute-start(f32[56,128]{1,0:T(8,128)S(1)} %get-tuple-element.117), channel_id=1, source_target_pairs={{0,3},{1,2},{2,1},{3,0},{4,7},{5,6},{6,5},{7,4},{8,11},{9,10},{10,... | collective-permute-start | bytes 86024 | tf_op jit(solution)/shard_map/ppermute | solution.py:444
  83.7 3.8 %collective-permute-done.31.refs_1_ = f32[56,128]{1,0:T(8,128)S(1)} collective-permute-done((f32[56,128]{1,0:T(8,128)S(1)}, f32[56,128]{1,0:T(8,128)S(1)}, u32[]{:S(2)}, u32[]{:S(2)}) %collective-permute-start.31) | collective-permute-done | bytes 28704 | tf_op jit(solution)/shard_map/ppermute | solution.py:444
  90.5 1.2 %collective-permute-done.36.refs_3_ = f32[8,128]{1,0:T(8,128)S(1)} collective-permute-done((f32[8,128]{1,0:T(8,128)S(1)}, f32[8,128]{1,0:T(8,128)S(1)}, u32[]{:S(2)}, u32[]{:S(2)}) %collective-permute-start.36) | collective-permute-done | bytes 4128 | tf_op jit(solution)/shard_map/ppermute | solution.py:444
  (64 shorter events, 18.6 us)
Async XLA Ops:
  1.6 7.5 %collective-permute-start.5 = (f32[64,128]{1,0:T(8,128)S(1)}, f32[64,128]{1,0:T(8,128)S(1)}, u32[]{:S(2)}, u32[]{:S(2)}) collective-permute-start(f32[64,128]{1,0:T(8,128)S(1)} %get-tuple-element.54.refs_0_.refs_4_), channel_id=1, source_target_pairs={{0,3},{1,2},{2,1},{3,0},{4,7},{5,6},{6,5},{7,4},{8,11},{9,10},{10,... | collective-permute-start | bytes 98312 | tf_op jit(solution)/shard_map/ppermute | solution.py:444
  6.8 5.7 %collective-permute-start.4 = (f32[64,128]{1,0:T(8,128)S(1)}, f32[64,128]{1,0:T(8,128)S(1)}, u32[]{:S(2)}, u32[]{:S(2)}) collective-permute-start(f32[64,128]{1,0:T(8,128)S(1)} %get-tuple-element.54.refs_0_.refs_4_), channel_id=1, source_target_pairs={{0,2},{1,3},{2,0},{3,1},{4,6},{5,7},{6,4},{7,5},{8,10},{9,11},{10,... | collective-permute-start | bytes 98312 | tf_op jit(solution)/shard_map/ppermute | solution.py:444
  6.8 5.7 %collective-permute-start.3 = (f32[64,128]{1,0:T(8,128)S(1)}, f32[64,128]{1,0:T(8,128)S(1)}, u32[]{:S(2)}, u32[]{:S(2)}) collective-permute-start(f32[64,128]{1,0:T(8,128)S(1)} %get-tuple-element.54.refs_0_.refs_4_), channel_id=1, source_target_pairs={{0,1},{1,0},{2,3},{3,2},{4,5},{5,4},{6,7},{7,6},{8,9},{9,8},{10,11... | collective-permute-start | bytes 98312 | tf_op jit(solution)/shard_map/ppermute | solution.py:444
  7.4 5.1 %collective-permute-start.2 = (f32[64,128]{1,0:T(8,128)S(1)}, f32[64,128]{1,0:T(8,128)S(1)}, u32[]{:S(2)}, u32[]{:S(2)}) collective-permute-start(f32[64,128]{1,0:T(8,128)S(1)} %get-tuple-element.54.refs_0_.refs_4_), channel_id=1, source_target_pairs={{0,12},{4,8},{8,4},{12,0},{1,13},{5,9},{9,5},{13,1},{2,14},{6,10},... | collective-permute-start | bytes 98312 | tf_op jit(solution)/shard_map/ppermute | solution.py:444
  7.8 4.7 %collective-permute-start.1 = (f32[64,128]{1,0:T(8,128)S(1)}, f32[64,128]{1,0:T(8,128)S(1)}, u32[]{:S(2)}, u32[]{:S(2)}) collective-permute-start(f32[64,128]{1,0:T(8,128)S(1)} %get-tuple-element.54.refs_0_.refs_4_), channel_id=1, source_target_pairs={{0,8},{4,12},{8,0},{12,4},{1,9},{5,13},{9,1},{13,5},{2,10},{6,14},... | collective-permute-start | bytes 98312 | tf_op jit(solution)/shard_map/ppermute | solution.py:444
  9.1 3.4 %collective-permute-start = (f32[64,128]{1,0:T(8,128)S(1)}, f32[64,128]{1,0:T(8,128)S(1)}, u32[]{:S(2)}, u32[]{:S(2)}) collective-permute-start(f32[64,128]{1,0:T(8,128)S(1)} %get-tuple-element.54.refs_0_.refs_4_), channel_id=1, source_target_pairs={{0,4},{4,0},{8,12},{12,8},{1,5},{5,1},{9,13},{13,9},{2,6},{6,2},{1... | collective-permute-start | bytes 98312 | tf_op jit(solution)/shard_map/ppermute | solution.py:444
  15.7 3.6 %collective-permute-start.6 = (f32[8,128]{1,0:T(8,128)S(1)}, f32[8,128]{1,0:T(8,128)S(1)}, u32[]{:S(2)}, u32[]{:S(2)}) collective-permute-start(f32[8,128]{1,0:T(8,128)S(1)} %get-tuple-element.60), channel_id=1, source_target_pairs={{0,20},{4,16},{8,28},{12,24},{16,4},{20,0},{24,12},{28,8},{1,21},{... | collective-permute-start | bytes 12296 | tf_op jit(solution)/shard_map/ppermute | solution.py:444
  19.3 6.2 %collective-permute-start.9 = (f32[104,128]{1,0:T(8,128)S(1)}, f32[104,128]{1,0:T(8,128)S(1)}, u32[]{:S(2)}, u32[]{:S(2)}) collective-permute-start(f32[104,128]{1,0:T(8,128)S(1)} %get-tuple-element.113), channel_id=1, source_target_pairs={{0,2},{1,3},{2,0},{3,1},{4,6},{5,7},{6,4},{7,5},{8,10},{9,11},{10,... | collective-permute-start | bytes 159752 | tf_op jit(solution)/shard_map/ppermute | solution.py:444
  21.5 6.4 %collective-permute-start.8 = (f32[104,128]{1,0:T(8,128)S(1)}, f32[104,128]{1,0:T(8,128)S(1)}, u32[]{:S(2)}, u32[]{:S(2)}) collective-permute-start(f32[104,128]{1,0:T(8,128)S(1)} %get-tuple-element.114), channel_id=1, source_target_pairs={{0,3},{1,2},{2,1},{3,0},{4,7},{5,6},{6,5},{7,4},{8,11},{9,10},{10,... | collective-permute-start | bytes 159752 | tf_op jit(solution)/shard_map/ppermute | solution.py:444
  23.1 4.9 %collective-permute-start.7 = (f32[104,128]{1,0:T(8,128)S(1)}, f32[104,128]{1,0:T(8,128)S(1)}, u32[]{:S(2)}, u32[]{:S(2)}) collective-permute-start(f32[104,128]{1,0:T(8,128)S(1)} %get-tuple-element.114), channel_id=1, source_target_pairs={{0,1},{1,0},{2,3},{3,2},{4,5},{5,4},{6,7},{7,6},{8,9},{9,8},{10,11... | collective-permute-start | bytes 159752 | tf_op jit(solution)/shard_map/ppermute | solution.py:444
  28.1 5.0 %collective-permute-start.13 = (f32[96,128]{1,0:T(8,128)S(1)}, f32[96,128]{1,0:T(8,128)S(1)}, u32[]{:S(2)}, u32[]{:S(2)}) collective-permute-start(f32[96,128]{1,0:T(8,128)S(1)} %get-tuple-element.64.refs_4_), channel_id=1, source_target_pairs={{0,1},{1,0},{2,3},{3,2},{4,5},{5,4},{6,7},{7,6},{8,9},{9,8},{10,11... | collective-permute-start | bytes 147464 | tf_op jit(solution)/shard_map/ppermute | solution.py:444
  28.5 3.4 %collective-permute-start.12 = (f32[56,128]{1,0:T(8,128)S(1)}, f32[56,128]{1,0:T(8,128)S(1)}, u32[]{:S(2)}, u32[]{:S(2)}) collective-permute-start(f32[56,128]{1,0:T(8,128)S(1)} %get-tuple-element.63.refs_0_), channel_id=1, source_target_pairs={{0,12},{4,8},{8,4},{12,0},{1,13},{5,9},{9,5},{13,1},{2,14},{6,10},... | collective-permute-start | bytes 86024 | tf_op jit(solution)/shard_map/ppermute | solution.py:444
  29.1 4.0 %collective-permute-start.11 = (f32[56,128]{1,0:T(8,128)S(1)}, f32[56,128]{1,0:T(8,128)S(1)}, u32[]{:S(2)}, u32[]{:S(2)}) collective-permute-start(f32[56,128]{1,0:T(8,128)S(1)} %get-tuple-element.63.refs_0_), channel_id=1, source_target_pairs={{0,8},{4,12},{8,0},{12,4},{1,9},{5,13},{9,1},{13,5},{2,10},{6,14},... | collective-permute-start | bytes 86024 | tf_op jit(solution)/shard_map/ppermute | solution.py:444
  36.2 3.1 %collective-permute-start.14 = (f32[8,128]{1,0:T(8,128)S(1)}, f32[8,128]{1,0:T(8,128)S(1)}, u32[]{:S(2)}, u32[]{:S(2)}) collective-permute-start(f32[8,128]{1,0:T(8,128)S(1)} %get-tuple-element.73), channel_id=1, source_target_pairs={{0,20},{4,16},{8,28},{12,24},{16,4},{20,0},{24,12},{28,8},{1,21},{... | collective-permute-start | bytes 12296 | tf_op jit(solution)/shard_map/ppermute | solution.py:444
  39.3 6.9 %collective-permute-start.17 = (f32[104,128]{1,0:T(8,128)S(1)}, f32[104,128]{1,0:T(8,128)S(1)}, u32[]{:S(2)}, u32[]{:S(2)}) collective-permute-start(f32[104,128]{1,0:T(8,128)S(1)} %get-tuple-element.110), channel_id=1, source_target_pairs={{0,2},{1,3},{2,0},{3,1},{4,6},{5,7},{6,4},{7,5},{8,10},{9,11},{10,... | collective-permute-start | bytes 159752 | tf_op jit(solution)/shard_map/ppermute | solution.py:444
  42.5 5.9 %collective-permute-start.16 = (f32[104,128]{1,0:T(8,128)S(1)}, f32[104,128]{1,0:T(8,128)S(1)}, u32[]{:S(2)}, u32[]{:S(2)}) collective-permute-start(f32[104,128]{1,0:T(8,128)S(1)} %get-tuple-element.111), channel_id=1, source_target_pairs={{0,3},{1,2},{2,1},{3,0},{4,7},{5,6},{6,5},{7,4},{8,11},{9,10},{10,... | collective-permute-start | bytes 159752 | tf_op jit(solution)/shard_map/ppermute | solution.py:444
  43.1 5.3 %collective-permute-start.15 = (f32[104,128]{1,0:T(8,128)S(1)}, f32[104,128]{1,0:T(8,128)S(1)}, u32[]{:S(2)}, u32[]{:S(2)}) collective-permute-start(f32[104,128]{1,0:T(8,128)S(1)} %get-tuple-element.111), channel_id=1, source_target_pairs={{0,1},{1,0},{2,3},{3,2},{4,5},{5,4},{6,7},{7,6},{8,9},{9,8},{10,11... | collective-permute-start | bytes 159752 | tf_op jit(solution)/shard_map/ppermute | solution.py:444
  48.6 4.4 %collective-permute-start.21 = (f32[96,128]{1,0:T(8,128)S(1)}, f32[96,128]{1,0:T(8,128)S(1)}, u32[]{:S(2)}, u32[]{:S(2)}) collective-permute-start(f32[96,128]{1,0:T(8,128)S(1)} %get-tuple-element.77.refs_4_), channel_id=1, source_target_pairs={{0,1},{1,0},{2,3},{3,2},{4,5},{5,4},{6,7},{7,6},{8,9},{9,8},{10,11... | collective-permute-start | bytes 147464 | tf_op jit(solution)/shard_map/ppermute | solution.py:444
  48.9 3.3 %collective-permute-start.20 = (f32[56,128]{1,0:T(8,128)S(1)}, f32[56,128]{1,0:T(8,128)S(1)}, u32[]{:S(2)}, u32[]{:S(2)}) collective-permute-start(f32[56,128]{1,0:T(8,128)S(1)} %get-tuple-element.76.refs_0_), channel_id=1, source_target_pairs={{0,12},{4,8},{8,4},{12,0},{1,13},{5,9},{9,5},{13,1},{2,14},{6,10},... | collective-permute-start | bytes 86024 | tf_op jit(solution)/shard_map/ppermute | solution.py:444
  48.9 4.1 %collective-permute-start.19 = (f32[56,128]{1,0:T(8,128)S(1)}, f32[56,128]{1,0:T(8,128)S(1)}, u32[]{:S(2)}, u32[]{:S(2)}) collective-permute-start(f32[56,128]{1,0:T(8,128)S(1)} %get-tuple-element.76.refs_0_), channel_id=1, source_target_pairs={{0,8},{4,12},{8,0},{12,4},{1,9},{5,13},{9,1},{13,5},{2,10},{6,14},... | collective-permute-start | bytes 86024 | tf_op jit(solution)/shard_map/ppermute | solution.py:444
  49.7 3.3 %collective-permute-start.18 = (f32[56,128]{1,0:T(8,128)S(1)}, f32[56,128]{1,0:T(8,128)S(1)}, u32[]{:S(2)}, u32[]{:S(2)}) collective-permute-start(f32[56,128]{1,0:T(8,128)S(1)} %get-tuple-element.76.refs_0_), channel_id=1, source_target_pairs={{0,4},{4,0},{8,12},{12,8},{1,5},{5,1},{9,13},{13,9},{2,6},{6,2},{1... | collective-permute-start | bytes 86024 | tf_op jit(solution)/shard_map/ppermute | solution.py:444
  59.2 5.1 %collective-permute-start.25 = (f32[104,128]{1,0:T(8,128)S(1)}, f32[104,128]{1,0:T(8,128)S(1)}, u32[]{:S(2)}, u32[]{:S(2)}) collective-permute-start(f32[104,128]{1,0:T(8,128)S(1)} %get-tuple-element.107), channel_id=1, source_target_pairs={{0,2},{1,3},{2,0},{3,1},{4,6},{5,7},{6,4},{7,5},{8,10},{9,11},{10,... | collective-permute-start | bytes 159752 | tf_op jit(solution)/shard_map/ppermute | solution.py:444
  61.9 6.3 %collective-permute-start.24 = (f32[104,128]{1,0:T(8,128)S(1)}, f32[104,128]{1,0:T(8,128)S(1)}, u32[]{:S(2)}, u32[]{:S(2)}) collective-permute-start(f32[104,128]{1,0:T(8,128)S(1)} %get-tuple-element.108), channel_id=1, source_target_pairs={{0,3},{1,2},{2,1},{3,0},{4,7},{5,6},{6,5},{7,4},{8,11},{9,10},{10,... | collective-permute-start | bytes 159752 | tf_op jit(solution)/shard_map/ppermute | solution.py:444
  63.4 4.9 %collective-permute-start.23 = (f32[104,128]{1,0:T(8,128)S(1)}, f32[104,128]{1,0:T(8,128)S(1)}, u32[]{:S(2)}, u32[]{:S(2)}) collective-permute-start(f32[104,128]{1,0:T(8,128)S(1)} %get-tuple-element.108), channel_id=1, source_target_pairs={{0,1},{1,0},{2,3},{3,2},{4,5},{5,4},{6,7},{7,6},{8,9},{9,8},{10,11... | collective-permute-start | bytes 159752 | tf_op jit(solution)/shard_map/ppermute | solution.py:444
  68.3 4.3 %collective-permute-start.29 = (f32[96,128]{1,0:T(8,128)S(1)}, f32[96,128]{1,0:T(8,128)S(1)}, u32[]{:S(2)}, u32[]{:S(2)}) collective-permute-start(f32[96,128]{1,0:T(8,128)S(1)} %get-tuple-element.87.refs_4_), channel_id=1, source_target_pairs={{0,1},{1,0},{2,3},{3,2},{4,5},{5,4},{6,7},{7,6},{8,9},{9,8},{10,11... | collective-permute-start | bytes 147464 | tf_op jit(solution)/shard_map/ppermute | solution.py:444
  68.6 3.3 %collective-permute-start.28 = (f32[56,128]{1,0:T(8,128)S(1)}, f32[56,128]{1,0:T(8,128)S(1)}, u32[]{:S(2)}, u32[]{:S(2)}) collective-permute-start(f32[56,128]{1,0:T(8,128)S(1)} %get-tuple-element.86.refs_0_), channel_id=1, source_target_pairs={{0,12},{4,8},{8,4},{12,0},{1,13},{5,9},{9,5},{13,1},{2,14},{6,10},... | collective-permute-start | bytes 86024 | tf_op jit(solution)/shard_map/ppermute | solution.py:444
  68.6 4.0 %collective-permute-start.27 = (f32[56,128]{1,0:T(8,128)S(1)}, f32[56,128]{1,0:T(8,128)S(1)}, u32[]{:S(2)}, u32[]{:S(2)}) collective-permute-start(f32[56,128]{1,0:T(8,128)S(1)} %get-tuple-element.86.refs_0_), channel_id=1, source_target_pairs={{0,8},{4,12},{8,0},{12,4},{1,9},{5,13},{9,1},{13,5},{2,10},{6,14},... | collective-permute-start | bytes 86024 | tf_op jit(solution)/shard_map/ppermute | solution.py:444
  78.8 4.9 %collective-permute-start.32 = (f32[56,128]{1,0:T(8,128)S(1)}, f32[56,128]{1,0:T(8,128)S(1)}, u32[]{:S(2)}, u32[]{:S(2)}) collective-permute-start(f32[56,128]{1,0:T(8,128)S(1)} %get-tuple-element.116), channel_id=1, source_target_pairs={{0,2},{1,3},{2,0},{3,1},{4,6},{5,7},{6,4},{7,5},{8,10},{9,11},{10,... | collective-permute-start | bytes 86024 | tf_op jit(solution)/shard_map/ppermute | solution.py:444
  81.8 5.7 %collective-permute-start.31 = (f32[56,128]{1,0:T(8,128)S(1)}, f32[56,128]{1,0:T(8,128)S(1)}, u32[]{:S(2)}, u32[]{:S(2)}) collective-permute-start(f32[56,128]{1,0:T(8,128)S(1)} %get-tuple-element.117), channel_id=1, source_target_pairs={{0,3},{1,2},{2,1},{3,0},{4,7},{5,6},{6,5},{7,4},{8,11},{9,10},{10,... | collective-permute-start | bytes 86024 | tf_op jit(solution)/shard_map/ppermute | solution.py:444
  83.1 4.4 %collective-permute-start.33 = (f32[56,128]{1,0:T(8,128)S(1)}, f32[56,128]{1,0:T(8,128)S(1)}, u32[]{:S(2)}, u32[]{:S(2)}) collective-permute-start(f32[56,128]{1,0:T(8,128)S(1)} %get-tuple-element.105), channel_id=1, source_target_pairs={{0,1},{1,0},{2,3},{3,2},{4,5},{5,4},{6,7},{7,6},{8,9},{9,8},{10,11... | collective-permute-start | bytes 86024 | tf_op jit(solution)/shard_map/ppermute | solution.py:444
  87.6 4.6 %collective-permute-start.37 = (f32[144,128]{1,0:T(8,128)S(1)}, f32[144,128]{1,0:T(8,128)S(1)}, u32[]{:S(2)}, u32[]{:S(2)}) collective-permute-start(f32[144,128]{1,0:T(8,128)S(1)} %get-tuple-element.100.refs_4_), channel_id=1, source_target_pairs={{0,16},{16,0},{1,17},{17,1},{2,18},{18,2},{3,19},{19,3},{4,20},{20... | collective-permute-start | bytes 221192 | tf_op jit(solution)/shard_map/ppermute | solution.py:444
  88.6 3.6 %collective-permute-start.35 = (f32[8,128]{1,0:T(8,128)S(1)}, f32[8,128]{1,0:T(8,128)S(1)}, u32[]{:S(2)}, u32[]{:S(2)}) collective-permute-start(f32[8,128]{1,0:T(8,128)S(1)} %get-tuple-element.99.refs_0_), channel_id=1, source_target_pairs={{0,8},{4,12},{8,0},{12,4},{1,9},{5,13},{9,1},{13,5},{2,10},{6,14},... | collective-permute-start | bytes 12296 | tf_op jit(solution)/shard_map/ppermute | solution.py:444
  (6 other events, 17.6 us)

commit v8 on v6

--- a/solution.py
+++ b/solution.py
@@ -151,6 +151,9 @@
         bands.append(jnp.broadcast_to(band, (TILE, rows)))
     weight = jnp.concatenate(bands, axis=0)
     weight_bf16 = weight.astype(jnp.bfloat16)
+    square = (cols, cols)
+    eye = lax.broadcasted_iota(jnp.int32, square, 0) == lax.broadcasted_iota(jnp.int32, square, 1)
+    eye = eye.astype(jnp.float32).astype(jnp.bfloat16)
     for p in range(2):
         vt_ref[p] = vis_ref[p].astype(jnp.float32).T * weight
     for k in range(dirs):
@@ -163,7 +166,16 @@
             for k in range(4):
                 for p in range(2):
                     at = n * size + 4 * m + k
-                    mt_ref[at, p] = model_ref[at, p].T * weight_bf16
+                    if k == 0:
+                        turned = lax.dot_general(
+                            eye,
+                            model_ref[at, p],
+                            (((1,), (1,)), ((), ())),
+                            preferred_element_type=jnp.float32,
+                        ).astype(jnp.bfloat16)
+                    else:
+                        turned = model_ref[at, p].T
+                    mt_ref[at, p] = turned * weight_bf16
             return carry
 
         lax.fori_loop(0, size // 4, turn, 0)
@@ -285,8 +297,8 @@
 
 
 def first_kernel(*refs, ns, nz, span):
-    rows_in = refs[: 2 * nz : 2]
-    cols_in = refs[1 : 2 * nz : 2]
+    cols_in = refs[:ns]
+    rows_in = refs[ns : ns + nz]
     mt_ref, vt_ref = refs[nz + ns : nz + ns + 2]
     outs = refs[nz + ns + 2 : nz + ns + 5]
     grow_ref, gcol_ref, trow_ref, tcol_ref, ct_ref = refs[nz + ns + 5 :]
@@ -470,10 +482,8 @@
         [pltpu.VMEM(x.shape, jnp.float32) for x in own_in] + [pltpu.SemaphoreType.DMA((3,))],
         HBM,
     )
-    row_parts, col_parts = [start], [start]
-    for n in range(1, max(ns, nz)):
-        col_parts += [swap(start, "srow", n)] if n < ns else []
-        row_parts += [swap(start, "scol", n)] if n < nz else []
+    col_parts = [start] + [swap(start, "srow", n) for n in range(1, ns)]
+    row_parts = [start] + [swap(start, "scol", n) for n in range(1, nz)]
     field_in = [rho, cluster, flags[0], model[0], vis[0]]
     mt, vt, rho_rows, rho_packed = call(
         prepare_kernel,
@@ -499,7 +509,7 @@
         functools.partial(first_kernel, ns=ns, nz=nz, span=span),
         "first",
         [],
-        [part for parts in zip(row_parts, col_parts) for part in parts] + [mt, vt],
+        col_parts + row_parts + [mt, vt],
         fields + [plane, plane, plane, plane],
         scratch,
     )

time: 92.6 us -> 94.5 us (1.021)
  transfers between devices with their start and end apart: 38 -> 38, of which waited for: 21 -> 20; matrix products, arithmetic and copies ran while one was open for 0% -> 0% of each run, Pallas kernels for 13% -> 13%
where the time goes in v8:
time: 94.5 us; the launch traced here: 94.3 us
  starting transfers between devices  41.5 us (44%)
  Pallas kernels  27.2 us (29%)
  waiting for transfers between devices  24.8 us (26%)
    ppermute x38, starting transfers between devices, swap(): return lax.ppermute(x, axis, [(m, m ^ n) for m in range(size)])  41.5 us
    pallas_call x15, Pallas kernels, call(): pl.pallas_call(kernel, in_specs=[SMEM] * len(lead) + [place] * len(args),...  27.2 us
    ppermute x38, waiting for transfers between devices, swap(): return lax.ppermute(x, axis, [(m, m ^ n) for m in range(size)])  24.8 us
  transfers between devices with their start and end apart: 38, of which 20 were waited for; matrix products, arithmetic and copies ran while one was open for 0% of the time, Pallas kernels for 13%

profile of v8, /device:TPU:0, one launch (start us, length us, event | category | flops | bytes accessed | tf_op | source)
XLA Modules:
  0.0 94.3 jit_solution(8124862433312378494)
XLA Ops:
  1.6 5.1 %collective-permute-start.5 = (f32[64,128]{1,0:T(8,128)S(1)}, f32[64,128]{1,0:T(8,128)S(1)}, u32[]{:S(2)}, u32[]{:S(2)}) collective-permute-start(f32[64,128]{1,0:T(8,128)S(1)} %get-tuple-element.51.refs_0_.refs_4_), channel_id=1, source_target_pairs={{0,3},{1,2},{2,1},{3,0},{4,7},{5,6},{6,5},{7,4},{8,11},{9,10},{10,... | collective-permute-start | bytes 98312 | tf_op jit(solution)/shard_map/ppermute | solution.py:454
  9.3 4.1 %prepare.1 = (bf16[64,2,128,128]{3,2,1,0:T(8,128)(2,1)S(1)}, f32[2,128,128]{2,1,0:T(8,128)S(1)}, f32[64,128]{1,0:T(8,128)S(1)}, f32[16,128]{1,0:T(8,128)S(1)}) custom-call(f32[8]{0:T(128)} %refs_0_.1, s32[64]{0:T(128)} %refs_1_.1, s32[8,8]{1,0:T(8,128)} %bitcast.24, bf16[64,2,128,128]{3,2,1,0:T(8,128)(2,1)} %bitcast.19, bf16[2,128,128]{2,1,0:T(8,128)(2,1)} %bitcast.20), custom_call_target="tpu_custom_call" | custom-call | tf_op jit(solution)/shard_map/prepare/pallas_call | solution.py:441
  13.4 3.2 %first.1 = (f32[64,2,128,128]{3,2,1,0:T(8,128)S(1)}, f32[2,128,128]{2,1,0:T(8,128)S(1)}, f32[8,128]{1,0:T(8,128)S(1)}, f32[128,128]{1,0:T(8,128)S(1)}, f32[128,1...) custom-call(f32[64,128]{1,0:T(8,128)S(1)} %get-tuple-element.51.refs_0_.refs_4_, ...), custom_call_target="tpu_custom_call" | custom-call | tf_op jit(solution)/shard_map/first/pallas_call | solution.py:441
  16.6 1.5 %collective-permute-start.6 = (f32[8,128]{1,0:T(8,128)S(1)}, f32[8,128]{1,0:T(8,128)S(1)}, u32[]{:S(2)}, u32[]{:S(2)}) collective-permute-start(f32[8,128]{1,0:T(8,128)S(1)} %get-tuple-element.57), channel_id=1, source_target_pairs={{0,20},{4,16},{8,28},{12,24},{16,4},{20,0},{24,12},{28,8},{1,21},{... | collective-permute-start | bytes 12296 | tf_op jit(solution)/shard_map/ppermute | solution.py:454
  18.1 2.1 %terms.4 = (f32[104,128]{1,0:T(8,128)S(1)}, f32[104,128]{1,0:T(8,128)S(1)}) custom-call(f32[64,2,128,128]{3,2,1,0:T(8,128)S(1)} %get-tuple-element.54.z_ref, f32[2,128,128]{2,1,0:T(8,128)S(1)} %get-tuple-element.55.r_ref), custom_call_target="tpu_custom_call" | custom-call | tf_op jit(solution)/shard_map/terms/pallas_call | solution.py:441
  20.2 3.7 %collective-permute-start.9 = (f32[104,128]{1,0:T(8,128)S(1)}, f32[104,128]{1,0:T(8,128)S(1)}, u32[]{:S(2)}, u32[]{:S(2)}) collective-permute-start(f32[104,128]{1,0:T(8,128)S(1)} %get-tuple-element.105), channel_id=1, source_target_pairs={{0,3},{1,2},{2,1},{3,0},{4,7},{5,6},{6,5},{7,4},{8,11},{9,10},{10,... | collective-permute-start | bytes 159752 | tf_op jit(solution)/shard_map/ppermute | solution.py:454
  24.6 2.1 %collective-permute-done.9.refs_3_ = f32[104,128]{1,0:T(8,128)S(1)} collective-permute-done((f32[104,128]{1,0:T(8,128)S(1)}, f32[104,128]{1,0:T(8,128)S(1)}, u32[]{:S(2)}, u32[]{:S(2)}) %collective-permute-start.9) | collective-permute-done | bytes 53280 | tf_op jit(solution)/shard_map/ppermute | solution.py:454
  26.7 2.2 %collective-permute-done.7.refs_1_ = f32[104,128]{1,0:T(8,128)S(1)} collective-permute-done((f32[104,128]{1,0:T(8,128)S(1)}, f32[104,128]{1,0:T(8,128)S(1)}, u32[]{:S(2)}, u32[]{:S(2)}) %collective-permute-start.7) | collective-permute-done | bytes 53280 | tf_op jit(solution)/shard_map/ppermute | solution.py:454
  29.6 1.5 %collective-permute-start.13 = (f32[96,128]{1,0:T(8,128)S(1)}, f32[96,128]{1,0:T(8,128)S(1)}, u32[]{:S(2)}, u32[]{:S(2)}) collective-permute-start(f32[96,128]{1,0:T(8,128)S(1)} %get-tuple-element.60.refs_4_), channel_id=1, source_target_pairs={{0,1},{1,0},{2,3},{3,2},{4,5},{5,4},{6,7},{7,6},{8,9},{9,8},{10,11... | collective-permute-start | bytes 147464 | tf_op jit(solution)/shard_map/ppermute | solution.py:454
  31.1 1.4 %collective-permute-start.11 = (f32[56,128]{1,0:T(8,128)S(1)}, f32[56,128]{1,0:T(8,128)S(1)}, u32[]{:S(2)}, u32[]{:S(2)}) collective-permute-start(f32[56,128]{1,0:T(8,128)S(1)} %get-tuple-element.59.refs_0_), channel_id=1, source_target_pairs={{0,8},{4,12},{8,0},{12,4},{1,9},{5,13},{9,1},{13,5},{2,10},{6,14},... | collective-permute-start | bytes 86024 | tf_op jit(solution)/shard_map/ppermute | solution.py:454
  33.0 1.6 %collective-permute-done.12.refs_3_ = f32[56,128]{1,0:T(8,128)S(1)} collective-permute-done((f32[56,128]{1,0:T(8,128)S(1)}, f32[56,128]{1,0:T(8,128)S(1)}, u32[]{:S(2)}, u32[]{:S(2)}) %collective-permute-start.12) | collective-permute-done | bytes 28704 | tf_op jit(solution)/shard_map/ppermute | solution.py:454
  35.0 3.1 %sweep.3 = (f32[64,2,128,128]{3,2,1,0:T(8,128)S(1)}, f32[2,128,128]{2,1,0:T(8,128)S(1)}, f32[8,128]{1,0:T(8,128)S(1)}, f32[128,128]{1,0:T(8,128)S(1)}, f32[128,128]{1,0:T(8,128)S(1)}) custom-call(f32[56,128]{1,0:T(8,128)S(1)} %get-tuple-element.59.refs_0_, f32[56,128]{1,0:T(8,128)S(1)} %collective-permute-done.10.refs_1_, ...), custom_call_target="tpu_custom_call" | custom-call | tf_op jit(solution)/shard_map/sweep/pallas_call | solution.py:441
  39.2 2.1 %terms.5 = (f32[104,128]{1,0:T(8,128)S(1)}, f32[104,128]{1,0:T(8,128)S(1)}) custom-call(f32[64,2,128,128]{3,2,1,0:T(8,128)S(1)} %get-tuple-element.66.z_ref, f32[2,128,128]{2,1,0:T(8,128)S(1)} %get-tuple-element.67.r_ref), custom_call_target="tpu_custom_call" | custom-call | tf_op jit(solution)/shard_map/terms/pallas_call | solution.py:441
  41.3 2.2 %collective-permute-start.17 = (f32[104,128]{1,0:T(8,128)S(1)}, f32[104,128]{1,0:T(8,128)S(1)}, u32[]{:S(2)}, u32[]{:S(2)}) collective-permute-start(f32[104,128]{1,0:T(8,128)S(1)} %get-tuple-element.103), channel_id=1, source_target_pairs={{0,3},{1,2},{2,1},{3,0},{4,7},{5,6},{6,5},{7,4},{8,11},{9,10},{10,... | collective-permute-start | bytes 159752 | tf_op jit(solution)/shard_map/ppermute | solution.py:454
  43.5 2.3 %collective-permute-start.16 = (f32[104,128]{1,0:T(8,128)S(1)}, f32[104,128]{1,0:T(8,128)S(1)}, u32[]{:S(2)}, u32[]{:S(2)}) collective-permute-start(f32[104,128]{1,0:T(8,128)S(1)} %get-tuple-element.104.refs_0_), channel_id=1, source_target_pairs={{0,2},{1,3},{2,0},{3,1},{4,6},{5,7},{6,4},{7,5},{8,10},{9,11},{10,... | collective-permute-start | bytes 159752 | tf_op jit(solution)/shard_map/ppermute | solution.py:454
  45.8 1.9 %collective-permute-done.17.refs_3_ = f32[104,128]{1,0:T(8,128)S(1)} collective-permute-done((f32[104,128]{1,0:T(8,128)S(1)}, f32[104,128]{1,0:T(8,128)S(1)}, u32[]{:S(2)}, u32[]{:S(2)}) %collective-permute-start.17) | collective-permute-done | bytes 53280 | tf_op jit(solution)/shard_map/ppermute | solution.py:454
  47.7 1.6 %collective-permute-done.15.refs_1_ = f32[104,128]{1,0:T(8,128)S(1)} collective-permute-done((f32[104,128]{1,0:T(8,128)S(1)}, f32[104,128]{1,0:T(8,128)S(1)}, u32[]{:S(2)}, u32[]{:S(2)}) %collective-permute-start.15) | collective-permute-done | bytes 53280 | tf_op jit(solution)/shard_map/ppermute | solution.py:454
  49.4 1.4 %collective-permute-start.21 = (f32[96,128]{1,0:T(8,128)S(1)}, f32[96,128]{1,0:T(8,128)S(1)}, u32[]{:S(2)}, u32[]{:S(2)}) collective-permute-start(f32[96,128]{1,0:T(8,128)S(1)} %get-tuple-element.72.refs_4_), channel_id=1, source_target_pairs={{0,1},{1,0},{2,3},{3,2},{4,5},{5,4},{6,7},{7,6},{8,9},{9,8},{10,11... | collective-permute-start | bytes 147464 | tf_op jit(solution)/shard_map/ppermute | solution.py:454
  52.6 1.4 %collective-permute-done.20.refs_3_ = f32[56,128]{1,0:T(8,128)S(1)} collective-permute-done((f32[56,128]{1,0:T(8,128)S(1)}, f32[56,128]{1,0:T(8,128)S(1)}, u32[]{:S(2)}, u32[]{:S(2)}) %collective-permute-start.20) | collective-permute-done | bytes 28704 | tf_op jit(solution)/shard_map/ppermute | solution.py:454
  54.9 3.1 %sweep.4 = (f32[64,2,128,128]{3,2,1,0:T(8,128)S(1)}, f32[2,128,128]{2,1,0:T(8,128)S(1)}, f32[8,128]{1,0:T(8,128)S(1)}, f32[128,128]{1,0:T(8,128)S(1)}, f32[128,128]{1,0:T(8,128)S(1)}) custom-call(f32[56,128]{1,0:T(8,128)S(1)} %get-tuple-element.71.refs_0_, f32[56,128]{1,0:T(8,128)S(1)} %collective-permute-done.18.refs_1_, ...), custom_call_target="tpu_custom_call" | custom-call | tf_op jit(solution)/shard_map/sweep/pallas_call | solution.py:441
  58.5 2.1 %terms.6 = (f32[104,128]{1,0:T(8,128)S(1)}, f32[104,128]{1,0:T(8,128)S(1)}) custom-call(f32[64,2,128,128]{3,2,1,0:T(8,128)S(1)} %get-tuple-element.75.z_ref, f32[2,128,128]{2,1,0:T(8,128)S(1)} %get-tuple-element.76.r_ref), custom_call_target="tpu_custom_call" | custom-call | tf_op jit(solution)/shard_map/terms/pallas_call | solution.py:441
  61.1 1.5 %collective-permute-start.25 = (f32[104,128]{1,0:T(8,128)S(1)}, f32[104,128]{1,0:T(8,128)S(1)}, u32[]{:S(2)}, u32[]{:S(2)}) collective-permute-start(f32[104,128]{1,0:T(8,128)S(1)} %get-tuple-element.101), channel_id=1, source_target_pairs={{0,3},{1,2},{2,1},{3,0},{4,7},{5,6},{6,5},{7,4},{8,11},{9,10},{10,... | collective-permute-start | bytes 159752 | tf_op jit(solution)/shard_map/ppermute | solution.py:454
  63.0 2.5 %collective-permute-start.24 = (f32[104,128]{1,0:T(8,128)S(1)}, f32[104,128]{1,0:T(8,128)S(1)}, u32[]{:S(2)}, u32[]{:S(2)}) collective-permute-start(f32[104,128]{1,0:T(8,128)S(1)} %get-tuple-element.102.refs_0_), channel_id=1, source_target_pairs={{0,2},{1,3},{2,0},{3,1},{4,6},{5,7},{6,4},{7,5},{8,10},{9,11},{10,... | collective-permute-start | bytes 159752 | tf_op jit(solution)/shard_map/ppermute | solution.py:454
  65.4 2.2 %collective-permute-done.25.refs_3_ = f32[104,128]{1,0:T(8,128)S(1)} collective-permute-done((f32[104,128]{1,0:T(8,128)S(1)}, f32[104,128]{1,0:T(8,128)S(1)}, u32[]{:S(2)}, u32[]{:S(2)}) %collective-permute-start.25) | collective-permute-done | bytes 53280 | tf_op jit(solution)/shard_map/ppermute | solution.py:454
  67.9 1.4 %collective-permute-done.24.refs_2_ = f32[104,128]{1,0:T(8,128)S(1)} collective-permute-done((f32[104,128]{1,0:T(8,128)S(1)}, f32[104,128]{1,0:T(8,128)S(1)}, u32[]{:S(2)}, u32[]{:S(2)}) %collective-permute-start.24) | collective-permute-done | bytes 53280 | tf_op jit(solution)/shard_map/ppermute | solution.py:454
  69.8 1.5 %collective-permute-start.27 = (f32[56,128]{1,0:T(8,128)S(1)}, f32[56,128]{1,0:T(8,128)S(1)}, u32[]{:S(2)}, u32[]{:S(2)}) collective-permute-start(f32[56,128]{1,0:T(8,128)S(1)} %get-tuple-element.80.refs_0_), channel_id=1, source_target_pairs={{0,8},{4,12},{8,0},{12,4},{1,9},{5,13},{9,1},{13,5},{2,10},{6,14},... | collective-permute-start | bytes 86024 | tf_op jit(solution)/shard_map/ppermute | solution.py:454
  71.7 1.7 %collective-permute-done.28.refs_3_ = f32[56,128]{1,0:T(8,128)S(1)} collective-permute-done((f32[56,128]{1,0:T(8,128)S(1)}, f32[56,128]{1,0:T(8,128)S(1)}, u32[]{:S(2)}, u32[]{:S(2)}) %collective-permute-start.28) | collective-permute-done | bytes 28704 | tf_op jit(solution)/shard_map/ppermute | solution.py:454
  73.7 3.1 %sweep.5 = (f32[64,2,128,128]{3,2,1,0:T(8,128)S(1)}, f32[2,128,128]{2,1,0:T(8,128)S(1)}, f32[8,128]{1,0:T(8,128)S(1)}, f32[128,128]{1,0:T(8,128)S(1)}, f32[128,128]{1,0:T(8,128)}) custom-call(f32[56,128]{1,0:T(8,128)S(1)} %get-tuple-element.80.refs_0_, f32[56,128]{1,0:T(8,128)S(1)} %collective-permute-done.26.refs_1_, ...), custom_call_target="tpu_custom_call" | custom-call | tf_op jit(solution)/shard_map/sweep/pallas_call | solution.py:441
  77.8 2.2 %terms.7 = (f32[56,128]{1,0:T(8,128)S(1)}, f32[56,128]{1,0:T(8,128)S(1)}, f32[56,128]{1,0:T(8,128)S(1)}, f32[56,128]{1,0:T(8,128)S(1)}) custom-call(f32[64,2,128,128]{3,2,1,0:T(8,128)S(1)} %get-tuple-element.84.z_ref, f32[2,128,128]{2,1,0:T(8,128)S(1)} %get-tuple-element.85.r_ref), custom_call_target="tpu_custom_call" | custom-call | tf_op jit(solution)/shard_map/terms/pallas_call | solution.py:441
  80.0 1.8 %collective-permute-start.32 = (f32[56,128]{1,0:T(8,128)S(1)}, f32[56,128]{1,0:T(8,128)S(1)}, u32[]{:S(2)}, u32[]{:S(2)}) collective-permute-start(f32[56,128]{1,0:T(8,128)S(1)} %get-tuple-element.107), channel_id=1, source_target_pairs={{0,2},{1,3},{2,0},{3,1},{4,6},{5,7},{6,4},{7,5},{8,10},{9,11},{10,... | collective-permute-start | bytes 86024 | tf_op jit(solution)/shard_map/ppermute | solution.py:454
  82.8 1.6 %collective-permute-start.33 = (f32[56,128]{1,0:T(8,128)S(1)}, f32[56,128]{1,0:T(8,128)S(1)}, u32[]{:S(2)}, u32[]{:S(2)}) collective-permute-start(f32[56,128]{1,0:T(8,128)S(1)} %get-tuple-element.99), channel_id=1, source_target_pairs={{0,3},{1,2},{2,1},{3,0},{4,7},{5,6},{6,5},{7,4},{8,11},{9,10},{10,... | collective-permute-start | bytes 86024 | tf_op jit(solution)/shard_map/ppermute | solution.py:454
  85.7 2.8 %collective-permute-done.33.refs_3_ = f32[56,128]{1,0:T(8,128)S(1)} collective-permute-done((f32[56,128]{1,0:T(8,128)S(1)}, f32[56,128]{1,0:T(8,128)S(1)}, u32[]{:S(2)}, u32[]{:S(2)}) %collective-permute-start.33) | collective-permute-done | bytes 28704 | tf_op jit(solution)/shard_map/ppermute | solution.py:454
  (64 shorter events, 21.9 us)
Async XLA Ops:
  1.6 7.5 %collective-permute-start.5 = (f32[64,128]{1,0:T(8,128)S(1)}, f32[64,128]{1,0:T(8,128)S(1)}, u32[]{:S(2)}, u32[]{:S(2)}) collective-permute-start(f32[64,128]{1,0:T(8,128)S(1)} %get-tuple-element.51.refs_0_.refs_4_), channel_id=1, source_target_pairs={{0,3},{1,2},{2,1},{3,0},{4,7},{5,6},{6,5},{7,4},{8,11},{9,10},{10,... | collective-permute-start | bytes 98312 | tf_op jit(solution)/shard_map/ppermute | solution.py:454
  6.8 6.6 %collective-permute-start.4 = (f32[64,128]{1,0:T(8,128)S(1)}, f32[64,128]{1,0:T(8,128)S(1)}, u32[]{:S(2)}, u32[]{:S(2)}) collective-permute-start(f32[64,128]{1,0:T(8,128)S(1)} %get-tuple-element.51.refs_0_.refs_4_), channel_id=1, source_target_pairs={{0,2},{1,3},{2,0},{3,1},{4,6},{5,7},{6,4},{7,5},{8,10},{9,11},{10,... | collective-permute-start | bytes 98312 | tf_op jit(solution)/shard_map/ppermute | solution.py:454
  6.8 6.6 %collective-permute-start.3 = (f32[64,128]{1,0:T(8,128)S(1)}, f32[64,128]{1,0:T(8,128)S(1)}, u32[]{:S(2)}, u32[]{:S(2)}) collective-permute-start(f32[64,128]{1,0:T(8,128)S(1)} %get-tuple-element.51.refs_0_.refs_4_), channel_id=1, source_target_pairs={{0,1},{1,0},{2,3},{3,2},{4,5},{5,4},{6,7},{7,6},{8,9},{9,8},{10,11... | collective-permute-start | bytes 98312 | tf_op jit(solution)/shard_map/ppermute | solution.py:454
  7.4 6.0 %collective-permute-start.2 = (f32[64,128]{1,0:T(8,128)S(1)}, f32[64,128]{1,0:T(8,128)S(1)}, u32[]{:S(2)}, u32[]{:S(2)}) collective-permute-start(f32[64,128]{1,0:T(8,128)S(1)} %get-tuple-element.51.refs_0_.refs_4_), channel_id=1, source_target_pairs={{0,12},{4,8},{8,4},{12,0},{1,13},{5,9},{9,5},{13,1},{2,14},{6,10},... | collective-permute-start | bytes 98312 | tf_op jit(solution)/shard_map/ppermute | solution.py:454
  7.8 5.6 %collective-permute-start.1 = (f32[64,128]{1,0:T(8,128)S(1)}, f32[64,128]{1,0:T(8,128)S(1)}, u32[]{:S(2)}, u32[]{:S(2)}) collective-permute-start(f32[64,128]{1,0:T(8,128)S(1)} %get-tuple-element.51.refs_0_.refs_4_), channel_id=1, source_target_pairs={{0,8},{4,12},{8,0},{12,4},{1,9},{5,13},{9,1},{13,5},{2,10},{6,14},... | collective-permute-start | bytes 98312 | tf_op jit(solution)/shard_map/ppermute | solution.py:454
  9.1 4.3 %collective-permute-start = (f32[64,128]{1,0:T(8,128)S(1)}, f32[64,128]{1,0:T(8,128)S(1)}, u32[]{:S(2)}, u32[]{:S(2)}) collective-permute-start(f32[64,128]{1,0:T(8,128)S(1)} %get-tuple-element.51.refs_0_.refs_4_), channel_id=1, source_target_pairs={{0,4},{4,0},{8,12},{12,8},{1,5},{5,1},{9,13},{13,9},{2,6},{6,2},{1... | collective-permute-start | bytes 98312 | tf_op jit(solution)/shard_map/ppermute | solution.py:454
  16.6 3.6 %collective-permute-start.6 = (f32[8,128]{1,0:T(8,128)S(1)}, f32[8,128]{1,0:T(8,128)S(1)}, u32[]{:S(2)}, u32[]{:S(2)}) collective-permute-start(f32[8,128]{1,0:T(8,128)S(1)} %get-tuple-element.57), channel_id=1, source_target_pairs={{0,20},{4,16},{8,28},{12,24},{16,4},{20,0},{24,12},{28,8},{1,21},{... | collective-permute-start | bytes 12296 | tf_op jit(solution)/shard_map/ppermute | solution.py:454
  20.2 6.5 %collective-permute-start.9 = (f32[104,128]{1,0:T(8,128)S(1)}, f32[104,128]{1,0:T(8,128)S(1)}, u32[]{:S(2)}, u32[]{:S(2)}) collective-permute-start(f32[104,128]{1,0:T(8,128)S(1)} %get-tuple-element.105), channel_id=1, source_target_pairs={{0,3},{1,2},{2,1},{3,0},{4,7},{5,6},{6,5},{7,4},{8,11},{9,10},{10,... | collective-permute-start | bytes 159752 | tf_op jit(solution)/shard_map/ppermute | solution.py:454
  23.9 5.0 %collective-permute-start.7 = (f32[104,128]{1,0:T(8,128)S(1)}, f32[104,128]{1,0:T(8,128)S(1)}, u32[]{:S(2)}, u32[]{:S(2)}) collective-permute-start(f32[104,128]{1,0:T(8,128)S(1)} %get-tuple-element.105), channel_id=1, source_target_pairs={{0,1},{1,0},{2,3},{3,2},{4,5},{5,4},{6,7},{7,6},{8,9},{9,8},{10,11... | collective-permute-start | bytes 159752 | tf_op jit(solution)/shard_map/ppermute | solution.py:454
  23.9 5.6 %collective-permute-start.8 = (f32[104,128]{1,0:T(8,128)S(1)}, f32[104,128]{1,0:T(8,128)S(1)}, u32[]{:S(2)}, u32[]{:S(2)}) collective-permute-start(f32[104,128]{1,0:T(8,128)S(1)} %get-tuple-element.106.refs_0_), channel_id=1, source_target_pairs={{0,2},{1,3},{2,0},{3,1},{4,6},{5,7},{6,4},{7,5},{8,10},{9,11},{10,... | collective-permute-start | bytes 159752 | tf_op jit(solution)/shard_map/ppermute | solution.py:454
  29.6 5.4 %collective-permute-start.13 = (f32[96,128]{1,0:T(8,128)S(1)}, f32[96,128]{1,0:T(8,128)S(1)}, u32[]{:S(2)}, u32[]{:S(2)}) collective-permute-start(f32[96,128]{1,0:T(8,128)S(1)} %get-tuple-element.60.refs_4_), channel_id=1, source_target_pairs={{0,1},{1,0},{2,3},{3,2},{4,5},{5,4},{6,7},{7,6},{8,9},{9,8},{10,11... | collective-permute-start | bytes 147464 | tf_op jit(solution)/shard_map/ppermute | solution.py:454
  31.1 3.5 %collective-permute-start.12 = (f32[56,128]{1,0:T(8,128)S(1)}, f32[56,128]{1,0:T(8,128)S(1)}, u32[]{:S(2)}, u32[]{:S(2)}) collective-permute-start(f32[56,128]{1,0:T(8,128)S(1)} %get-tuple-element.59.refs_0_), channel_id=1, source_target_pairs={{0,12},{4,8},{8,4},{12,0},{1,13},{5,9},{9,5},{13,1},{2,14},{6,10},... | collective-permute-start | bytes 86024 | tf_op jit(solution)/shard_map/ppermute | solution.py:454
  31.1 3.9 %collective-permute-start.11 = (f32[56,128]{1,0:T(8,128)S(1)}, f32[56,128]{1,0:T(8,128)S(1)}, u32[]{:S(2)}, u32[]{:S(2)}) collective-permute-start(f32[56,128]{1,0:T(8,128)S(1)} %get-tuple-element.59.refs_0_), channel_id=1, source_target_pairs={{0,8},{4,12},{8,0},{12,4},{1,9},{5,13},{9,1},{13,5},{2,10},{6,14},... | collective-permute-start | bytes 86024 | tf_op jit(solution)/shard_map/ppermute | solution.py:454
  38.1 3.3 %collective-permute-start.14 = (f32[8,128]{1,0:T(8,128)S(1)}, f32[8,128]{1,0:T(8,128)S(1)}, u32[]{:S(2)}, u32[]{:S(2)}) collective-permute-start(f32[8,128]{1,0:T(8,128)S(1)} %get-tuple-element.69), channel_id=1, source_target_pairs={{0,20},{4,16},{8,28},{12,24},{16,4},{20,0},{24,12},{28,8},{1,21},{... | collective-permute-start | bytes 12296 | tf_op jit(solution)/shard_map/ppermute | solution.py:454
  41.3 6.4 %collective-permute-start.17 = (f32[104,128]{1,0:T(8,128)S(1)}, f32[104,128]{1,0:T(8,128)S(1)}, u32[]{:S(2)}, u32[]{:S(2)}) collective-permute-start(f32[104,128]{1,0:T(8,128)S(1)} %get-tuple-element.103), channel_id=1, source_target_pairs={{0,3},{1,2},{2,1},{3,0},{4,7},{5,6},{6,5},{7,4},{8,11},{9,10},{10,... | collective-permute-start | bytes 159752 | tf_op jit(solution)/shard_map/ppermute | solution.py:454
  43.5 5.8 %collective-permute-start.15 = (f32[104,128]{1,0:T(8,128)S(1)}, f32[104,128]{1,0:T(8,128)S(1)}, u32[]{:S(2)}, u32[]{:S(2)}) collective-permute-start(f32[104,128]{1,0:T(8,128)S(1)} %get-tuple-element.103), channel_id=1, source_target_pairs={{0,1},{1,0},{2,3},{3,2},{4,5},{5,4},{6,7},{7,6},{8,9},{9,8},{10,11... | collective-permute-start | bytes 159752 | tf_op jit(solution)/shard_map/ppermute | solution.py:454
  43.5 5.8 %collective-permute-start.16 = (f32[104,128]{1,0:T(8,128)S(1)}, f32[104,128]{1,0:T(8,128)S(1)}, u32[]{:S(2)}, u32[]{:S(2)}) collective-permute-start(f32[104,128]{1,0:T(8,128)S(1)} %get-tuple-element.104.refs_0_), channel_id=1, source_target_pairs={{0,2},{1,3},{2,0},{3,1},{4,6},{5,7},{6,4},{7,5},{8,10},{9,11},{10,... | collective-permute-start | bytes 159752 | tf_op jit(solution)/shard_map/ppermute | solution.py:454
  49.4 5.5 %collective-permute-start.21 = (f32[96,128]{1,0:T(8,128)S(1)}, f32[96,128]{1,0:T(8,128)S(1)}, u32[]{:S(2)}, u32[]{:S(2)}) collective-permute-start(f32[96,128]{1,0:T(8,128)S(1)} %get-tuple-element.72.refs_4_), channel_id=1, source_target_pairs={{0,1},{1,0},{2,3},{3,2},{4,5},{5,4},{6,7},{7,6},{8,9},{9,8},{10,11... | collective-permute-start | bytes 147464 | tf_op jit(solution)/shard_map/ppermute | solution.py:454
  50.8 3.3 %collective-permute-start.20 = (f32[56,128]{1,0:T(8,128)S(1)}, f32[56,128]{1,0:T(8,128)S(1)}, u32[]{:S(2)}, u32[]{:S(2)}) collective-permute-start(f32[56,128]{1,0:T(8,128)S(1)} %get-tuple-element.71.refs_0_), channel_id=1, source_target_pairs={{0,12},{4,8},{8,4},{12,0},{1,13},{5,9},{9,5},{13,1},{2,14},{6,10},... | collective-permute-start | bytes 86024 | tf_op jit(solution)/shard_map/ppermute | solution.py:454
  50.8 4.1 %collective-permute-start.19 = (f32[56,128]{1,0:T(8,128)S(1)}, f32[56,128]{1,0:T(8,128)S(1)}, u32[]{:S(2)}, u32[]{:S(2)}) collective-permute-start(f32[56,128]{1,0:T(8,128)S(1)} %get-tuple-element.71.refs_0_), channel_id=1, source_target_pairs={{0,8},{4,12},{8,0},{12,4},{1,9},{5,13},{9,1},{13,5},{2,10},{6,14},... | collective-permute-start | bytes 86024 | tf_op jit(solution)/shard_map/ppermute | solution.py:454
  51.6 3.3 %collective-permute-start.18 = (f32[56,128]{1,0:T(8,128)S(1)}, f32[56,128]{1,0:T(8,128)S(1)}, u32[]{:S(2)}, u32[]{:S(2)}) collective-permute-start(f32[56,128]{1,0:T(8,128)S(1)} %get-tuple-element.71.refs_0_), channel_id=1, source_target_pairs={{0,4},{4,0},{8,12},{12,8},{1,5},{5,1},{9,13},{13,9},{2,6},{6,2},{1... | collective-permute-start | bytes 86024 | tf_op jit(solution)/shard_map/ppermute | solution.py:454
  61.1 6.6 %collective-permute-start.25 = (f32[104,128]{1,0:T(8,128)S(1)}, f32[104,128]{1,0:T(8,128)S(1)}, u32[]{:S(2)}, u32[]{:S(2)}) collective-permute-start(f32[104,128]{1,0:T(8,128)S(1)} %get-tuple-element.101), channel_id=1, source_target_pairs={{0,3},{1,2},{2,1},{3,0},{4,7},{5,6},{6,5},{7,4},{8,11},{9,10},{10,... | collective-permute-start | bytes 159752 | tf_op jit(solution)/shard_map/ppermute | solution.py:454
  62.6 5.3 %collective-permute-start.23 = (f32[104,128]{1,0:T(8,128)S(1)}, f32[104,128]{1,0:T(8,128)S(1)}, u32[]{:S(2)}, u32[]{:S(2)}) collective-permute-start(f32[104,128]{1,0:T(8,128)S(1)} %get-tuple-element.101), channel_id=1, source_target_pairs={{0,1},{1,0},{2,3},{3,2},{4,5},{5,4},{6,7},{7,6},{8,9},{9,8},{10,11... | collective-permute-start | bytes 159752 | tf_op jit(solution)/shard_map/ppermute | solution.py:454
  63.0 6.3 %collective-permute-start.24 = (f32[104,128]{1,0:T(8,128)S(1)}, f32[104,128]{1,0:T(8,128)S(1)}, u32[]{:S(2)}, u32[]{:S(2)}) collective-permute-start(f32[104,128]{1,0:T(8,128)S(1)} %get-tuple-element.102.refs_0_), channel_id=1, source_target_pairs={{0,2},{1,3},{2,0},{3,1},{4,6},{5,7},{6,4},{7,5},{8,10},{9,11},{10,... | collective-permute-start | bytes 159752 | tf_op jit(solution)/shard_map/ppermute | solution.py:454
  69.4 4.3 %collective-permute-start.29 = (f32[96,128]{1,0:T(8,128)S(1)}, f32[96,128]{1,0:T(8,128)S(1)}, u32[]{:S(2)}, u32[]{:S(2)}) collective-permute-start(f32[96,128]{1,0:T(8,128)S(1)} %get-tuple-element.81.refs_4_), channel_id=1, source_target_pairs={{0,1},{1,0},{2,3},{3,2},{4,5},{5,4},{6,7},{7,6},{8,9},{9,8},{10,11... | collective-permute-start | bytes 147464 | tf_op jit(solution)/shard_map/ppermute | solution.py:454
  69.8 3.6 %collective-permute-start.28 = (f32[56,128]{1,0:T(8,128)S(1)}, f32[56,128]{1,0:T(8,128)S(1)}, u32[]{:S(2)}, u32[]{:S(2)}) collective-permute-start(f32[56,128]{1,0:T(8,128)S(1)} %get-tuple-element.80.refs_0_), channel_id=1, source_target_pairs={{0,12},{4,8},{8,4},{12,0},{1,13},{5,9},{9,5},{13,1},{2,14},{6,10},... | collective-permute-start | bytes 86024 | tf_op jit(solution)/shard_map/ppermute | solution.py:454
  69.8 3.9 %collective-permute-start.27 = (f32[56,128]{1,0:T(8,128)S(1)}, f32[56,128]{1,0:T(8,128)S(1)}, u32[]{:S(2)}, u32[]{:S(2)}) collective-permute-start(f32[56,128]{1,0:T(8,128)S(1)} %get-tuple-element.80.refs_0_), channel_id=1, source_target_pairs={{0,8},{4,12},{8,0},{12,4},{1,9},{5,13},{9,1},{13,5},{2,10},{6,14},... | collective-permute-start | bytes 86024 | tf_op jit(solution)/shard_map/ppermute | solution.py:454
  80.0 4.9 %collective-permute-start.32 = (f32[56,128]{1,0:T(8,128)S(1)}, f32[56,128]{1,0:T(8,128)S(1)}, u32[]{:S(2)}, u32[]{:S(2)}) collective-permute-start(f32[56,128]{1,0:T(8,128)S(1)} %get-tuple-element.107), channel_id=1, source_target_pairs={{0,2},{1,3},{2,0},{3,1},{4,6},{5,7},{6,4},{7,5},{8,10},{9,11},{10,... | collective-permute-start | bytes 86024 | tf_op jit(solution)/shard_map/ppermute | solution.py:454
  81.8 3.9 %collective-permute-start.31 = (f32[56,128]{1,0:T(8,128)S(1)}, f32[56,128]{1,0:T(8,128)S(1)}, u32[]{:S(2)}, u32[]{:S(2)}) collective-permute-start(f32[56,128]{1,0:T(8,128)S(1)} %get-tuple-element.108), channel_id=1, source_target_pairs={{0,1},{1,0},{2,3},{3,2},{4,5},{5,4},{6,7},{7,6},{8,9},{9,8},{10,11... | collective-permute-start | bytes 86024 | tf_op jit(solution)/shard_map/ppermute | solution.py:454
  82.8 5.7 %collective-permute-start.33 = (f32[56,128]{1,0:T(8,128)S(1)}, f32[56,128]{1,0:T(8,128)S(1)}, u32[]{:S(2)}, u32[]{:S(2)}) collective-permute-start(f32[56,128]{1,0:T(8,128)S(1)} %get-tuple-element.99), channel_id=1, source_target_pairs={{0,3},{1,2},{2,1},{3,0},{4,7},{5,6},{6,5},{7,4},{8,11},{9,10},{10,... | collective-permute-start | bytes 86024 | tf_op jit(solution)/shard_map/ppermute | solution.py:454
  88.6 4.8 %collective-permute-start.37 = (f32[144,128]{1,0:T(8,128)S(1)}, f32[144,128]{1,0:T(8,128)S(1)}, u32[]{:S(2)}, u32[]{:S(2)}) collective-permute-start(f32[144,128]{1,0:T(8,128)S(1)} %get-tuple-element.94.refs_4_), channel_id=1, source_target_pairs={{0,16},{16,0},{1,17},{17,1},{2,18},{18,2},{3,19},{19,3},{4,20},{20... | collective-permute-start | bytes 221192 | tf_op jit(solution)/shard_map/ppermute | solution.py:454
  89.8 3.6 %collective-permute-start.35 = (f32[8,128]{1,0:T(8,128)S(1)}, f32[8,128]{1,0:T(8,128)S(1)}, u32[]{:S(2)}, u32[]{:S(2)}) collective-permute-start(f32[8,128]{1,0:T(8,128)S(1)} %get-tuple-element.93.refs_0_), channel_id=1, source_target_pairs={{0,8},{4,12},{8,0},{12,4},{1,9},{5,13},{9,1},{13,5},{2,10},{6,14},... | collective-permute-start | bytes 12296 | tf_op jit(solution)/shard_map/ppermute | solution.py:454
  (6 other events, 17.2 us)

commit v9 on v6

--- a/solution.py
+++ b/solution.py
@@ -285,8 +285,8 @@
 
 
 def first_kernel(*refs, ns, nz, span):
-    rows_in = refs[: 2 * nz : 2]
-    cols_in = refs[1 : 2 * nz : 2]
+    cols_in = refs[:ns]
+    rows_in = refs[ns : ns + nz]
     mt_ref, vt_ref = refs[nz + ns : nz + ns + 2]
     outs = refs[nz + ns + 2 : nz + ns + 5]
     grow_ref, gcol_ref, trow_ref, tcol_ref, ct_ref = refs[nz + ns + 5 :]
@@ -339,6 +339,10 @@
         a, cr, ci, gcolin_ref[re, :], gcolin_ref[im, :], tcol_ref[re, :], tcol_ref[im, :], rho_eff
     )
     residual(mt_ref, vt_ref, grow_ref, gcol_ref, *outs, ct_ref)
+
+
+def add_kernel(a_ref, b_ref, out_ref):
+    out_ref[...] = a_ref[...] + b_ref[...]
 
 
 def combine_kernel(*refs, nz, span):
@@ -470,10 +474,8 @@
         [pltpu.VMEM(x.shape, jnp.float32) for x in own_in] + [pltpu.SemaphoreType.DMA((3,))],
         HBM,
     )
-    row_parts, col_parts = [start], [start]
-    for n in range(1, max(ns, nz)):
-        col_parts += [swap(start, "srow", n)] if n < ns else []
-        row_parts += [swap(start, "scol", n)] if n < nz else []
+    col_parts = [start] + [swap(start, "srow", n) for n in range(1, ns)]
+    row_parts = [start] + [swap(start, "scol", n) for n in range(1, nz)]
     field_in = [rho, cluster, flags[0], model[0], vis[0]]
     mt, vt, rho_rows, rho_packed = call(
         prepare_kernel,
@@ -499,7 +501,7 @@
         functools.partial(first_kernel, ns=ns, nz=nz, span=span),
         "first",
         [],
-        [part for parts in zip(row_parts, col_parts) for part in parts] + [mt, vt],
+        col_parts + row_parts + [mt, vt],
         fields + [plane, plane, plane, plane],
         scratch,
     )
@@ -522,11 +524,12 @@
         )
         same = lax.dynamic_update_slice(same, power, (half, 0))
         other = lax.dynamic_update_slice(other, power, (half, 0))
+        sums = call(add_kernel, "add", [], [same, swap(other, "scol", 1)], [f32(half + 8, rows)])[0]
         pair_sums, own = call(
-            functools.partial(combine_kernel, nz=nz, span=span),
+            functools.partial(combine_kernel, nz=2, span=span),
             "combine",
             [],
-            [same] + [swap(same if n % 2 == 0 else other, "scol", n) for n in range(1, nz)],
+            [sums, swap(sums, "scol", 2)],
             [f32(half, rows), f32(3 * depth + 8, rows)],
         )
         other_sums = swap(pair_sums, "scol", 1)

time: 92.6 us -> 97.4 us (1.052)
  waiting for transfers between devices: 24.7 us -> 29 us
    ppermute x38 -> x35, waiting for transfers between devices: 24.7 us -> 29 us  [swap(): return lax.ppermute(x, axis, [(m, m ^ n) for m in range(size)])]
    ppermute x38 -> x35, starting transfers between devices: 40.6 us -> 41 us  [swap(): return lax.ppermute(x, axis, [(m, m ^ n) for m in range(size)])]
    pallas_call x15 -> x18, Pallas kernels: 26.3 us -> 26.3 us  [call(): pl.pallas_call(kernel, in_specs=[SMEM] * len(lead) + [place] * len(args),...]
  transfers between devices with their start and end apart: 38 -> 35, of which waited for: 21 -> 18; matrix products, arithmetic and copies ran while one was open for 0% -> 0% of each run, Pallas kernels for 13% -> 12%
where the time goes in v9:
time: 97.4 us; the launch traced here: 97.2 us
  starting transfers between devices  41 us (42%)
  waiting for transfers between devices  29 us (30%)
  Pallas kernels  26.3 us (27%)
    ppermute x35, starting transfers between devices, swap(): return lax.ppermute(x, axis, [(m, m ^ n) for m in range(size)])  41 us
    ppermute x35, waiting for transfers between devices, swap(): return lax.ppermute(x, axis, [(m, m ^ n) for m in range(size)])  29 us
    pallas_call x18, Pallas kernels, call(): pl.pallas_call(kernel, in_specs=[SMEM] * len(lead) + [place] * len(args),...  26.3 us
  transfers between devices with their start and end apart: 35, of which 18 were waited for; matrix products, arithmetic and copies ran while one was open for 0% of the time, Pallas kernels for 12%

profile of v9, /device:TPU:0, one launch (start us, length us, event | category | flops | bytes accessed | tf_op | source)
XLA Modules:
  0.0 97.2 jit_solution(295538079991891791)
XLA Ops:
  1.6 5.1 %collective-permute-start.5 = (f32[64,128]{1,0:T(8,128)S(1)}, f32[64,128]{1,0:T(8,128)S(1)}, u32[]{:S(2)}, u32[]{:S(2)}) collective-permute-start(f32[64,128]{1,0:T(8,128)S(1)} %get-tuple-element.51.refs_0_.refs_4_), channel_id=1, source_target_pairs={{0,3},{1,2},{2,1},{3,0},{4,7},{5,6},{6,5},{7,4},{8,11},{9,10},{10,... | collective-permute-start | bytes 98312 | tf_op jit(solution)/shard_map/ppermute | solution.py:446
  9.3 3.2 %prepare.1 = (bf16[64,2,128,128]{3,2,1,0:T(8,128)(2,1)S(1)}, f32[2,128,128]{2,1,0:T(8,128)S(1)}, f32[64,128]{1,0:T(8,128)S(1)}, f32[16,128]{1,0:T(8,128)S(1)}) custom-call(f32[8]{0:T(128)} %refs_0_.1, s32[64]{0:T(128)} %refs_1_.1, s32[8,8]{1,0:T(8,128)} %bitcast.24, bf16[64,2,128,128]{3,2,1,0:T(8,128)(2,1)} %bitcast.19, bf16[2,128,128]{2,1,0:T(8,128)(2,1)} %bitcast.20), custom_call_target="tpu_custom_call" | custom-call | tf_op jit(solution)/shard_map/prepare/pallas_call | solution.py:433
  12.5 3.2 %first.1 = (f32[64,2,128,128]{3,2,1,0:T(8,128)S(1)}, f32[2,128,128]{2,1,0:T(8,128)S(1)}, f32[8,128]{1,0:T(8,128)S(1)}, f32[128,128]{1,0:T(8,128)S(1)}, f32[128,1...) custom-call(f32[64,128]{1,0:T(8,128)S(1)} %get-tuple-element.51.refs_0_.refs_4_, ...), custom_call_target="tpu_custom_call" | custom-call | tf_op jit(solution)/shard_map/first/pallas_call | solution.py:433
  15.7 1.5 %collective-permute-start.6 = (f32[8,128]{1,0:T(8,128)S(1)}, f32[8,128]{1,0:T(8,128)S(1)}, u32[]{:S(2)}, u32[]{:S(2)}) collective-permute-start(f32[8,128]{1,0:T(8,128)S(1)} %get-tuple-element.57), channel_id=1, source_target_pairs={{0,20},{4,16},{8,28},{12,24},{16,4},{20,0},{24,12},{28,8},{1,21},{... | collective-permute-start | bytes 12296 | tf_op jit(solution)/shard_map/ppermute | solution.py:446
  17.2 2.1 %terms.4 = (f32[104,128]{1,0:T(8,128)S(1)}, f32[104,128]{1,0:T(8,128)S(1)}) custom-call(f32[64,2,128,128]{3,2,1,0:T(8,128)S(1)} %get-tuple-element.54.z_ref, f32[2,128,128]{2,1,0:T(8,128)S(1)} %get-tuple-element.55.r_ref), custom_call_target="tpu_custom_call" | custom-call | tf_op jit(solution)/shard_map/terms/pallas_call | solution.py:433
  20.6 2.9 %collective-permute-done.7.b_ref = f32[104,128]{1,0:T(8,128)S(1)} collective-permute-done((f32[104,128]{1,0:T(8,128)S(1)}, f32[104,128]{1,0:T(8,128)S(1)}, u32[]{:S(2)}, u32[]{:S(2)}) %collective-permute-start.7) | collective-permute-done | bytes 53280 | tf_op jit(solution)/shard_map/ppermute | solution.py:446
  23.5 2.4 %collective-permute-start.8 = (f32[104,128]{1,0:T(8,128)S(1)}, f32[104,128]{1,0:T(8,128)S(1)}, u32[]{:S(2)}, u32[]{:S(2)}) collective-permute-start(f32[104,128]{1,0:T(8,128)S(1)} %add.26.refs_0_), channel_id=1, source_target_pairs={{0,2},{1,3},{2,0},{3,1},{4,6},{5,7},{6,4},{7,5},{8,10},{9,11},{10,... | collective-permute-start | bytes 159752 | tf_op jit(solution)/shard_map/ppermute | solution.py:446
  25.9 2.7 %collective-permute-done.8.refs_1_ = f32[104,128]{1,0:T(8,128)S(1)} collective-permute-done((f32[104,128]{1,0:T(8,128)S(1)}, f32[104,128]{1,0:T(8,128)S(1)}, u32[]{:S(2)}, u32[]{:S(2)}) %collective-permute-start.8) | collective-permute-done | bytes 53280 | tf_op jit(solution)/shard_map/ppermute | solution.py:446
  30.0 1.5 %collective-permute-start.10 = (f32[56,128]{1,0:T(8,128)S(1)}, f32[56,128]{1,0:T(8,128)S(1)}, u32[]{:S(2)}, u32[]{:S(2)}) collective-permute-start(f32[56,128]{1,0:T(8,128)S(1)} %get-tuple-element.59.refs_0_), channel_id=1, source_target_pairs={{0,8},{4,12},{8,0},{12,4},{1,9},{5,13},{9,1},{13,5},{2,10},{6,14},... | collective-permute-start | bytes 86024 | tf_op jit(solution)/shard_map/ppermute | solution.py:446
  31.9 1.7 %collective-permute-done.11.refs_3_ = f32[56,128]{1,0:T(8,128)S(1)} collective-permute-done((f32[56,128]{1,0:T(8,128)S(1)}, f32[56,128]{1,0:T(8,128)S(1)}, u32[]{:S(2)}, u32[]{:S(2)}) %collective-permute-start.11) | collective-permute-done | bytes 28704 | tf_op jit(solution)/shard_map/ppermute | solution.py:446
  33.9 3.1 %sweep.3 = (f32[64,2,128,128]{3,2,1,0:T(8,128)S(1)}, f32[2,128,128]{2,1,0:T(8,128)S(1)}, f32[8,128]{1,0:T(8,128)S(1)}, f32[128,128]{1,0:T(8,128)S(1)}, f32[128,128]{1,0:T(8,128)S(1)}) custom-call(f32[56,128]{1,0:T(8,128)S(1)} %get-tuple-element.59.refs_0_, f32[56,128]{1,0:T(8,128)S(1)} %collective-permute-done.9.refs_1_, ...), custom_call_target="tpu_custom_call" | custom-call | tf_op jit(solution)/shard_map/sweep/pallas_call | solution.py:433
  38.2 2.1 %terms.5 = (f32[104,128]{1,0:T(8,128)S(1)}, f32[104,128]{1,0:T(8,128)S(1)}) custom-call(f32[64,2,128,128]{3,2,1,0:T(8,128)S(1)} %get-tuple-element.66.z_ref, f32[2,128,128]{2,1,0:T(8,128)S(1)} %get-tuple-element.67.r_ref), custom_call_target="tpu_custom_call" | custom-call | tf_op jit(solution)/shard_map/terms/pallas_call | solution.py:433
  41.4 3.1 %collective-permute-done.14.b_ref = f32[104,128]{1,0:T(8,128)S(1)} collective-permute-done((f32[104,128]{1,0:T(8,128)S(1)}, f32[104,128]{1,0:T(8,128)S(1)}, u32[]{:S(2)}, u32[]{:S(2)}) %collective-permute-start.14) | collective-permute-done | bytes 53280 | tf_op jit(solution)/shard_map/ppermute | solution.py:446
  44.5 3.6 %collective-permute-start.15 = (f32[104,128]{1,0:T(8,128)S(1)}, f32[104,128]{1,0:T(8,128)S(1)}, u32[]{:S(2)}, u32[]{:S(2)}) collective-permute-start(f32[104,128]{1,0:T(8,128)S(1)} %add.27.refs_0_), channel_id=1, source_target_pairs={{0,2},{1,3},{2,0},{3,1},{4,6},{5,7},{6,4},{7,5},{8,10},{9,11},{10,... | collective-permute-start | bytes 159752 | tf_op jit(solution)/shard_map/ppermute | solution.py:446
  48.0 2.7 %collective-permute-done.15.refs_1_ = f32[104,128]{1,0:T(8,128)S(1)} collective-permute-done((f32[104,128]{1,0:T(8,128)S(1)}, f32[104,128]{1,0:T(8,128)S(1)}, u32[]{:S(2)}, u32[]{:S(2)}) %collective-permute-start.15) | collective-permute-done | bytes 53280 | tf_op jit(solution)/shard_map/ppermute | solution.py:446
  51.2 1.4 %collective-permute-start.17 = (f32[56,128]{1,0:T(8,128)S(1)}, f32[56,128]{1,0:T(8,128)S(1)}, u32[]{:S(2)}, u32[]{:S(2)}) collective-permute-start(f32[56,128]{1,0:T(8,128)S(1)} %get-tuple-element.71.refs_0_), channel_id=1, source_target_pairs={{0,8},{4,12},{8,0},{12,4},{1,9},{5,13},{9,1},{13,5},{2,10},{6,14},... | collective-permute-start | bytes 86024 | tf_op jit(solution)/shard_map/ppermute | solution.py:446
  53.1 1.7 %collective-permute-done.18.refs_3_ = f32[56,128]{1,0:T(8,128)S(1)} collective-permute-done((f32[56,128]{1,0:T(8,128)S(1)}, f32[56,128]{1,0:T(8,128)S(1)}, u32[]{:S(2)}, u32[]{:S(2)}) %collective-permute-start.18) | collective-permute-done | bytes 28704 | tf_op jit(solution)/shard_map/ppermute | solution.py:446
  55.1 3.1 %sweep.4 = (f32[64,2,128,128]{3,2,1,0:T(8,128)S(1)}, f32[2,128,128]{2,1,0:T(8,128)S(1)}, f32[8,128]{1,0:T(8,128)S(1)}, f32[128,128]{1,0:T(8,128)S(1)}, f32[128,128]{1,0:T(8,128)S(1)}) custom-call(f32[56,128]{1,0:T(8,128)S(1)} %get-tuple-element.71.refs_0_, f32[56,128]{1,0:T(8,128)S(1)} %collective-permute-done.16.refs_1_, ...), custom_call_target="tpu_custom_call" | custom-call | tf_op jit(solution)/shard_map/sweep/pallas_call | solution.py:433
  59.2 2.1 %terms.6 = (f32[104,128]{1,0:T(8,128)S(1)}, f32[104,128]{1,0:T(8,128)S(1)}) custom-call(f32[64,2,128,128]{3,2,1,0:T(8,128)S(1)} %get-tuple-element.75.z_ref, f32[2,128,128]{2,1,0:T(8,128)S(1)} %get-tuple-element.76.r_ref), custom_call_target="tpu_custom_call" | custom-call | tf_op jit(solution)/shard_map/terms/pallas_call | solution.py:433
  61.3 1.7 %collective-permute-start.21 = (f32[104,128]{1,0:T(8,128)S(1)}, f32[104,128]{1,0:T(8,128)S(1)}, u32[]{:S(2)}, u32[]{:S(2)}) collective-permute-start(f32[104,128]{1,0:T(8,128)S(1)} %get-tuple-element.101), channel_id=1, source_target_pairs={{0,1},{1,0},{2,3},{3,2},{4,5},{5,4},{6,7},{7,6},{8,9},{9,8},{10,11... | collective-permute-start | bytes 159752 | tf_op jit(solution)/shard_map/ppermute | solution.py:446
  63.0 2.5 %collective-permute-done.21.b_ref = f32[104,128]{1,0:T(8,128)S(1)} collective-permute-done((f32[104,128]{1,0:T(8,128)S(1)}, f32[104,128]{1,0:T(8,128)S(1)}, u32[]{:S(2)}, u32[]{:S(2)}) %collective-permute-start.21) | collective-permute-done | bytes 53280 | tf_op jit(solution)/shard_map/ppermute | solution.py:446
  65.6 2.7 %collective-permute-start.22 = (f32[104,128]{1,0:T(8,128)S(1)}, f32[104,128]{1,0:T(8,128)S(1)}, u32[]{:S(2)}, u32[]{:S(2)}) collective-permute-start(f32[104,128]{1,0:T(8,128)S(1)} %add.28.refs_0_), channel_id=1, source_target_pairs={{0,2},{1,3},{2,0},{3,1},{4,6},{5,7},{6,4},{7,5},{8,10},{9,11},{10,... | collective-permute-start | bytes 159752 | tf_op jit(solution)/shard_map/ppermute | solution.py:446
  68.2 2.5 %collective-permute-done.22.refs_1_ = f32[104,128]{1,0:T(8,128)S(1)} collective-permute-done((f32[104,128]{1,0:T(8,128)S(1)}, f32[104,128]{1,0:T(8,128)S(1)}, u32[]{:S(2)}, u32[]{:S(2)}) %collective-permute-start.22) | collective-permute-done | bytes 53280 | tf_op jit(solution)/shard_map/ppermute | solution.py:446
  70.8 1.6 %collective-permute-start.26 = (f32[96,128]{1,0:T(8,128)S(1)}, f32[96,128]{1,0:T(8,128)S(1)}, u32[]{:S(2)}, u32[]{:S(2)}) collective-permute-start(f32[96,128]{1,0:T(8,128)S(1)} %get-tuple-element.81.refs_4_), channel_id=1, source_target_pairs={{0,1},{1,0},{2,3},{3,2},{4,5},{5,4},{6,7},{7,6},{8,9},{9,8},{10,11... | collective-permute-start | bytes 147464 | tf_op jit(solution)/shard_map/ppermute | solution.py:446
  74.3 1.4 %collective-permute-done.25.refs_3_ = f32[56,128]{1,0:T(8,128)S(1)} collective-permute-done((f32[56,128]{1,0:T(8,128)S(1)}, f32[56,128]{1,0:T(8,128)S(1)}, u32[]{:S(2)}, u32[]{:S(2)}) %collective-permute-start.25) | collective-permute-done | bytes 28704 | tf_op jit(solution)/shard_map/ppermute | solution.py:446
  76.6 3.1 %sweep.5 = (f32[64,2,128,128]{3,2,1,0:T(8,128)S(1)}, f32[2,128,128]{2,1,0:T(8,128)S(1)}, f32[8,128]{1,0:T(8,128)S(1)}, f32[128,128]{1,0:T(8,128)S(1)}, f32[128,128]{1,0:T(8,128)}) custom-call(f32[56,128]{1,0:T(8,128)S(1)} %get-tuple-element.80.refs_0_, f32[56,128]{1,0:T(8,128)S(1)} %collective-permute-done.23.refs_1_, ...), custom_call_target="tpu_custom_call" | custom-call | tf_op jit(solution)/shard_map/sweep/pallas_call | solution.py:433
  80.4 2.2 %terms.7 = (f32[56,128]{1,0:T(8,128)S(1)}, f32[56,128]{1,0:T(8,128)S(1)}, f32[56,128]{1,0:T(8,128)S(1)}, f32[56,128]{1,0:T(8,128)S(1)}) custom-call(f32[64,2,128,128]{3,2,1,0:T(8,128)S(1)} %get-tuple-element.84.z_ref, f32[2,128,128]{2,1,0:T(8,128)S(1)} %get-tuple-element.85.r_ref), custom_call_target="tpu_custom_call" | custom-call | tf_op jit(solution)/shard_map/terms/pallas_call | solution.py:433
  82.8 2.8 %collective-permute-start.29 = (f32[56,128]{1,0:T(8,128)S(1)}, f32[56,128]{1,0:T(8,128)S(1)}, u32[]{:S(2)}, u32[]{:S(2)}) collective-permute-start(f32[56,128]{1,0:T(8,128)S(1)} %get-tuple-element.107), channel_id=1, source_target_pairs={{0,2},{1,3},{2,0},{3,1},{4,6},{5,7},{6,4},{7,5},{8,10},{9,11},{10,... | collective-permute-start | bytes 86024 | tf_op jit(solution)/shard_map/ppermute | solution.py:446
  85.7 1.4 %collective-permute-start.30 = (f32[56,128]{1,0:T(8,128)S(1)}, f32[56,128]{1,0:T(8,128)S(1)}, u32[]{:S(2)}, u32[]{:S(2)}) collective-permute-start(f32[56,128]{1,0:T(8,128)S(1)} %get-tuple-element.99), channel_id=1, source_target_pairs={{0,3},{1,2},{2,1},{3,0},{4,7},{5,6},{6,5},{7,4},{8,11},{9,10},{10,... | collective-permute-start | bytes 86024 | tf_op jit(solution)/shard_map/ppermute | solution.py:446
  87.5 1.9 %collective-permute-done.28.refs_1_ = f32[56,128]{1,0:T(8,128)S(1)} collective-permute-done((f32[56,128]{1,0:T(8,128)S(1)}, f32[56,128]{1,0:T(8,128)S(1)}, u32[]{:S(2)}, u32[]{:S(2)}) %collective-permute-start.28) | collective-permute-done | bytes 28704 | tf_op jit(solution)/shard_map/ppermute | solution.py:446
  89.4 2.0 %collective-permute-done.30.refs_3_ = f32[56,128]{1,0:T(8,128)S(1)} collective-permute-done((f32[56,128]{1,0:T(8,128)S(1)}, f32[56,128]{1,0:T(8,128)S(1)}, u32[]{:S(2)}, u32[]{:S(2)}) %collective-permute-start.30) | collective-permute-done | bytes 28704 | tf_op jit(solution)/shard_map/ppermute | solution.py:446
  92.6 1.4 %collective-permute-start.32 = (f32[8,128]{1,0:T(8,128)S(1)}, f32[8,128]{1,0:T(8,128)S(1)}, u32[]{:S(2)}, u32[]{:S(2)}) collective-permute-start(f32[8,128]{1,0:T(8,128)S(1)} %get-tuple-element.93.refs_0_), channel_id=1, source_target_pairs={{0,8},{4,12},{8,0},{12,4},{1,9},{5,13},{9,1},{13,5},{2,10},{6,14},... | collective-permute-start | bytes 12296 | tf_op jit(solution)/shard_map/ppermute | solution.py:446
  (61 shorter events, 20.2 us)
Async XLA Ops:
  1.6 7.5 %collective-permute-start.5 = (f32[64,128]{1,0:T(8,128)S(1)}, f32[64,128]{1,0:T(8,128)S(1)}, u32[]{:S(2)}, u32[]{:S(2)}) collective-permute-start(f32[64,128]{1,0:T(8,128)S(1)} %get-tuple-element.51.refs_0_.refs_4_), channel_id=1, source_target_pairs={{0,3},{1,2},{2,1},{3,0},{4,7},{5,6},{6,5},{7,4},{8,11},{9,10},{10,... | collective-permute-start | bytes 98312 | tf_op jit(solution)/shard_map/ppermute | solution.py:446
  6.8 5.7 %collective-permute-start.4 = (f32[64,128]{1,0:T(8,128)S(1)}, f32[64,128]{1,0:T(8,128)S(1)}, u32[]{:S(2)}, u32[]{:S(2)}) collective-permute-start(f32[64,128]{1,0:T(8,128)S(1)} %get-tuple-element.51.refs_0_.refs_4_), channel_id=1, source_target_pairs={{0,2},{1,3},{2,0},{3,1},{4,6},{5,7},{6,4},{7,5},{8,10},{9,11},{10,... | collective-permute-start | bytes 98312 | tf_op jit(solution)/shard_map/ppermute | solution.py:446
  6.8 5.7 %collective-permute-start.3 = (f32[64,128]{1,0:T(8,128)S(1)}, f32[64,128]{1,0:T(8,128)S(1)}, u32[]{:S(2)}, u32[]{:S(2)}) collective-permute-start(f32[64,128]{1,0:T(8,128)S(1)} %get-tuple-element.51.refs_0_.refs_4_), channel_id=1, source_target_pairs={{0,1},{1,0},{2,3},{3,2},{4,5},{5,4},{6,7},{7,6},{8,9},{9,8},{10,11... | collective-permute-start | bytes 98312 | tf_op jit(solution)/shard_map/ppermute | solution.py:446
  7.4 5.1 %collective-permute-start.2 = (f32[64,128]{1,0:T(8,128)S(1)}, f32[64,128]{1,0:T(8,128)S(1)}, u32[]{:S(2)}, u32[]{:S(2)}) collective-permute-start(f32[64,128]{1,0:T(8,128)S(1)} %get-tuple-element.51.refs_0_.refs_4_), channel_id=1, source_target_pairs={{0,12},{4,8},{8,4},{12,0},{1,13},{5,9},{9,5},{13,1},{2,14},{6,10},... | collective-permute-start | bytes 98312 | tf_op jit(solution)/shard_map/ppermute | solution.py:446
  7.8 4.7 %collective-permute-start.1 = (f32[64,128]{1,0:T(8,128)S(1)}, f32[64,128]{1,0:T(8,128)S(1)}, u32[]{:S(2)}, u32[]{:S(2)}) collective-permute-start(f32[64,128]{1,0:T(8,128)S(1)} %get-tuple-element.51.refs_0_.refs_4_), channel_id=1, source_target_pairs={{0,8},{4,12},{8,0},{12,4},{1,9},{5,13},{9,1},{13,5},{2,10},{6,14},... | collective-permute-start | bytes 98312 | tf_op jit(solution)/shard_map/ppermute | solution.py:446
  9.1 3.4 %collective-permute-start = (f32[64,128]{1,0:T(8,128)S(1)}, f32[64,128]{1,0:T(8,128)S(1)}, u32[]{:S(2)}, u32[]{:S(2)}) collective-permute-start(f32[64,128]{1,0:T(8,128)S(1)} %get-tuple-element.51.refs_0_.refs_4_), channel_id=1, source_target_pairs={{0,4},{4,0},{8,12},{12,8},{1,5},{5,1},{9,13},{13,9},{2,6},{6,2},{1... | collective-permute-start | bytes 98312 | tf_op jit(solution)/shard_map/ppermute | solution.py:446
  15.7 3.6 %collective-permute-start.6 = (f32[8,128]{1,0:T(8,128)S(1)}, f32[8,128]{1,0:T(8,128)S(1)}, u32[]{:S(2)}, u32[]{:S(2)}) collective-permute-start(f32[8,128]{1,0:T(8,128)S(1)} %get-tuple-element.57), channel_id=1, source_target_pairs={{0,20},{4,16},{8,28},{12,24},{16,4},{20,0},{24,12},{28,8},{1,21},{... | collective-permute-start | bytes 12296 | tf_op jit(solution)/shard_map/ppermute | solution.py:446
  19.3 4.2 %collective-permute-start.7 = (f32[104,128]{1,0:T(8,128)S(1)}, f32[104,128]{1,0:T(8,128)S(1)}, u32[]{:S(2)}, u32[]{:S(2)}) collective-permute-start(f32[104,128]{1,0:T(8,128)S(1)} %get-tuple-element.105), channel_id=1, source_target_pairs={{0,1},{1,0},{2,3},{3,2},{4,5},{5,4},{6,7},{7,6},{8,9},{9,8},{10,11... | collective-permute-start | bytes 159752 | tf_op jit(solution)/shard_map/ppermute | solution.py:446
  23.5 5.1 %collective-permute-start.8 = (f32[104,128]{1,0:T(8,128)S(1)}, f32[104,128]{1,0:T(8,128)S(1)}, u32[]{:S(2)}, u32[]{:S(2)}) collective-permute-start(f32[104,128]{1,0:T(8,128)S(1)} %add.26.refs_0_), channel_id=1, source_target_pairs={{0,2},{1,3},{2,0},{3,1},{4,6},{5,7},{6,4},{7,5},{8,10},{9,11},{10,... | collective-permute-start | bytes 159752 | tf_op jit(solution)/shard_map/ppermute | solution.py:446
  28.7 5.2 %collective-permute-start.12 = (f32[96,128]{1,0:T(8,128)S(1)}, f32[96,128]{1,0:T(8,128)S(1)}, u32[]{:S(2)}, u32[]{:S(2)}) collective-permute-start(f32[96,128]{1,0:T(8,128)S(1)} %get-tuple-element.60.refs_4_), channel_id=1, source_target_pairs={{0,1},{1,0},{2,3},{3,2},{4,5},{5,4},{6,7},{7,6},{8,9},{9,8},{10,11... | collective-permute-start | bytes 147464 | tf_op jit(solution)/shard_map/ppermute | solution.py:446
  30.0 3.6 %collective-permute-start.11 = (f32[56,128]{1,0:T(8,128)S(1)}, f32[56,128]{1,0:T(8,128)S(1)}, u32[]{:S(2)}, u32[]{:S(2)}) collective-permute-start(f32[56,128]{1,0:T(8,128)S(1)} %get-tuple-element.59.refs_0_), channel_id=1, source_target_pairs={{0,12},{4,8},{8,4},{12,0},{1,13},{5,9},{9,5},{13,1},{2,14},{6,10},... | collective-permute-start | bytes 86024 | tf_op jit(solution)/shard_map/ppermute | solution.py:446
  30.0 3.9 %collective-permute-start.10 = (f32[56,128]{1,0:T(8,128)S(1)}, f32[56,128]{1,0:T(8,128)S(1)}, u32[]{:S(2)}, u32[]{:S(2)}) collective-permute-start(f32[56,128]{1,0:T(8,128)S(1)} %get-tuple-element.59.refs_0_), channel_id=1, source_target_pairs={{0,8},{4,12},{8,0},{12,4},{1,9},{5,13},{9,1},{13,5},{2,10},{6,14},... | collective-permute-start | bytes 86024 | tf_op jit(solution)/shard_map/ppermute | solution.py:446
  37.0 3.3 %collective-permute-start.13 = (f32[8,128]{1,0:T(8,128)S(1)}, f32[8,128]{1,0:T(8,128)S(1)}, u32[]{:S(2)}, u32[]{:S(2)}) collective-permute-start(f32[8,128]{1,0:T(8,128)S(1)} %get-tuple-element.69), channel_id=1, source_target_pairs={{0,20},{4,16},{8,28},{12,24},{16,4},{20,0},{24,12},{28,8},{1,21},{... | collective-permute-start | bytes 12296 | tf_op jit(solution)/shard_map/ppermute | solution.py:446
  40.3 4.2 %collective-permute-start.14 = (f32[104,128]{1,0:T(8,128)S(1)}, f32[104,128]{1,0:T(8,128)S(1)}, u32[]{:S(2)}, u32[]{:S(2)}) collective-permute-start(f32[104,128]{1,0:T(8,128)S(1)} %get-tuple-element.103), channel_id=1, source_target_pairs={{0,1},{1,0},{2,3},{3,2},{4,5},{5,4},{6,7},{7,6},{8,9},{9,8},{10,11... | collective-permute-start | bytes 159752 | tf_op jit(solution)/shard_map/ppermute | solution.py:446
  44.5 6.2 %collective-permute-start.15 = (f32[104,128]{1,0:T(8,128)S(1)}, f32[104,128]{1,0:T(8,128)S(1)}, u32[]{:S(2)}, u32[]{:S(2)}) collective-permute-start(f32[104,128]{1,0:T(8,128)S(1)} %add.27.refs_0_), channel_id=1, source_target_pairs={{0,2},{1,3},{2,0},{3,1},{4,6},{5,7},{6,4},{7,5},{8,10},{9,11},{10,... | collective-permute-start | bytes 159752 | tf_op jit(solution)/shard_map/ppermute | solution.py:446
  50.8 4.3 %collective-permute-start.19 = (f32[96,128]{1,0:T(8,128)S(1)}, f32[96,128]{1,0:T(8,128)S(1)}, u32[]{:S(2)}, u32[]{:S(2)}) collective-permute-start(f32[96,128]{1,0:T(8,128)S(1)} %get-tuple-element.72.refs_4_), channel_id=1, source_target_pairs={{0,1},{1,0},{2,3},{3,2},{4,5},{5,4},{6,7},{7,6},{8,9},{9,8},{10,11... | collective-permute-start | bytes 147464 | tf_op jit(solution)/shard_map/ppermute | solution.py:446
  51.2 3.5 %collective-permute-start.18 = (f32[56,128]{1,0:T(8,128)S(1)}, f32[56,128]{1,0:T(8,128)S(1)}, u32[]{:S(2)}, u32[]{:S(2)}) collective-permute-start(f32[56,128]{1,0:T(8,128)S(1)} %get-tuple-element.71.refs_0_), channel_id=1, source_target_pairs={{0,12},{4,8},{8,4},{12,0},{1,13},{5,9},{9,5},{13,1},{2,14},{6,10},... | collective-permute-start | bytes 86024 | tf_op jit(solution)/shard_map/ppermute | solution.py:446
  51.2 3.9 %collective-permute-start.17 = (f32[56,128]{1,0:T(8,128)S(1)}, f32[56,128]{1,0:T(8,128)S(1)}, u32[]{:S(2)}, u32[]{:S(2)}) collective-permute-start(f32[56,128]{1,0:T(8,128)S(1)} %get-tuple-element.71.refs_0_), channel_id=1, source_target_pairs={{0,8},{4,12},{8,0},{12,4},{1,9},{5,13},{9,1},{13,5},{2,10},{6,14},... | collective-permute-start | bytes 86024 | tf_op jit(solution)/shard_map/ppermute | solution.py:446
  58.2 3.1 %collective-permute-start.20 = (f32[8,128]{1,0:T(8,128)S(1)}, f32[8,128]{1,0:T(8,128)S(1)}, u32[]{:S(2)}, u32[]{:S(2)}) collective-permute-start(f32[8,128]{1,0:T(8,128)S(1)} %get-tuple-element.78), channel_id=1, source_target_pairs={{0,20},{4,16},{8,28},{12,24},{16,4},{20,0},{24,12},{28,8},{1,21},{... | collective-permute-start | bytes 12296 | tf_op jit(solution)/shard_map/ppermute | solution.py:446
  61.3 4.2 %collective-permute-start.21 = (f32[104,128]{1,0:T(8,128)S(1)}, f32[104,128]{1,0:T(8,128)S(1)}, u32[]{:S(2)}, u32[]{:S(2)}) collective-permute-start(f32[104,128]{1,0:T(8,128)S(1)} %get-tuple-element.101), channel_id=1, source_target_pairs={{0,1},{1,0},{2,3},{3,2},{4,5},{5,4},{6,7},{7,6},{8,9},{9,8},{10,11... | collective-permute-start | bytes 159752 | tf_op jit(solution)/shard_map/ppermute | solution.py:446
  65.6 5.1 %collective-permute-start.22 = (f32[104,128]{1,0:T(8,128)S(1)}, f32[104,128]{1,0:T(8,128)S(1)}, u32[]{:S(2)}, u32[]{:S(2)}) collective-permute-start(f32[104,128]{1,0:T(8,128)S(1)} %add.28.refs_0_), channel_id=1, source_target_pairs={{0,2},{1,3},{2,0},{3,1},{4,6},{5,7},{6,4},{7,5},{8,10},{9,11},{10,... | collective-permute-start | bytes 159752 | tf_op jit(solution)/shard_map/ppermute | solution.py:446
  70.8 5.8 %collective-permute-start.26 = (f32[96,128]{1,0:T(8,128)S(1)}, f32[96,128]{1,0:T(8,128)S(1)}, u32[]{:S(2)}, u32[]{:S(2)}) collective-permute-start(f32[96,128]{1,0:T(8,128)S(1)} %get-tuple-element.81.refs_4_), channel_id=1, source_target_pairs={{0,1},{1,0},{2,3},{3,2},{4,5},{5,4},{6,7},{7,6},{8,9},{9,8},{10,11... | collective-permute-start | bytes 147464 | tf_op jit(solution)/shard_map/ppermute | solution.py:446
  72.4 3.3 %collective-permute-start.25 = (f32[56,128]{1,0:T(8,128)S(1)}, f32[56,128]{1,0:T(8,128)S(1)}, u32[]{:S(2)}, u32[]{:S(2)}) collective-permute-start(f32[56,128]{1,0:T(8,128)S(1)} %get-tuple-element.80.refs_0_), channel_id=1, source_target_pairs={{0,12},{4,8},{8,4},{12,0},{1,13},{5,9},{9,5},{13,1},{2,14},{6,10},... | collective-permute-start | bytes 86024 | tf_op jit(solution)/shard_map/ppermute | solution.py:446
  72.4 4.2 %collective-permute-start.24 = (f32[56,128]{1,0:T(8,128)S(1)}, f32[56,128]{1,0:T(8,128)S(1)}, u32[]{:S(2)}, u32[]{:S(2)}) collective-permute-start(f32[56,128]{1,0:T(8,128)S(1)} %get-tuple-element.80.refs_0_), channel_id=1, source_target_pairs={{0,8},{4,12},{8,0},{12,4},{1,9},{5,13},{9,1},{13,5},{2,10},{6,14},... | collective-permute-start | bytes 86024 | tf_op jit(solution)/shard_map/ppermute | solution.py:446
  73.4 3.2 %collective-permute-start.23 = (f32[56,128]{1,0:T(8,128)S(1)}, f32[56,128]{1,0:T(8,128)S(1)}, u32[]{:S(2)}, u32[]{:S(2)}) collective-permute-start(f32[56,128]{1,0:T(8,128)S(1)} %get-tuple-element.80.refs_0_), channel_id=1, source_target_pairs={{0,4},{4,0},{8,12},{12,8},{1,5},{5,1},{9,13},{13,9},{2,6},{6,2},{1... | collective-permute-start | bytes 86024 | tf_op jit(solution)/shard_map/ppermute | solution.py:446
  79.6 3.1 %collective-permute-start.27 = (f32[8,128]{1,0:T(8,128)S(1)}, f32[8,128]{1,0:T(8,128)S(1)}, u32[]{:S(2)}, u32[]{:S(2)}) collective-permute-start(f32[8,128]{1,0:T(8,128)S(1)} %get-tuple-element.87), channel_id=1, source_target_pairs={{0,20},{4,16},{8,28},{12,24},{16,4},{20,0},{24,12},{28,8},{1,21},{... | collective-permute-start | bytes 12296 | tf_op jit(solution)/shard_map/ppermute | solution.py:446
  82.8 4.8 %collective-permute-start.29 = (f32[56,128]{1,0:T(8,128)S(1)}, f32[56,128]{1,0:T(8,128)S(1)}, u32[]{:S(2)}, u32[]{:S(2)}) collective-permute-start(f32[56,128]{1,0:T(8,128)S(1)} %get-tuple-element.107), channel_id=1, source_target_pairs={{0,2},{1,3},{2,0},{3,1},{4,6},{5,7},{6,4},{7,5},{8,10},{9,11},{10,... | collective-permute-start | bytes 86024 | tf_op jit(solution)/shard_map/ppermute | solution.py:446
  85.6 3.9 %collective-permute-start.28 = (f32[56,128]{1,0:T(8,128)S(1)}, f32[56,128]{1,0:T(8,128)S(1)}, u32[]{:S(2)}, u32[]{:S(2)}) collective-permute-start(f32[56,128]{1,0:T(8,128)S(1)} %get-tuple-element.108), channel_id=1, source_target_pairs={{0,1},{1,0},{2,3},{3,2},{4,5},{5,4},{6,7},{7,6},{8,9},{9,8},{10,11... | collective-permute-start | bytes 86024 | tf_op jit(solution)/shard_map/ppermute | solution.py:446
  85.7 5.7 %collective-permute-start.30 = (f32[56,128]{1,0:T(8,128)S(1)}, f32[56,128]{1,0:T(8,128)S(1)}, u32[]{:S(2)}, u32[]{:S(2)}) collective-permute-start(f32[56,128]{1,0:T(8,128)S(1)} %get-tuple-element.99), channel_id=1, source_target_pairs={{0,3},{1,2},{2,1},{3,0},{4,7},{5,6},{6,5},{7,4},{8,11},{9,10},{10,... | collective-permute-start | bytes 86024 | tf_op jit(solution)/shard_map/ppermute | solution.py:446
  91.5 4.7 %collective-permute-start.34 = (f32[144,128]{1,0:T(8,128)S(1)}, f32[144,128]{1,0:T(8,128)S(1)}, u32[]{:S(2)}, u32[]{:S(2)}) collective-permute-start(f32[144,128]{1,0:T(8,128)S(1)} %get-tuple-element.94.refs_4_), channel_id=1, source_target_pairs={{0,16},{16,0},{1,17},{17,1},{2,18},{18,2},{3,19},{19,3},{4,20},{20... | collective-permute-start | bytes 221192 | tf_op jit(solution)/shard_map/ppermute | solution.py:446
  92.6 3.0 %collective-permute-start.33 = (f32[8,128]{1,0:T(8,128)S(1)}, f32[8,128]{1,0:T(8,128)S(1)}, u32[]{:S(2)}, u32[]{:S(2)}) collective-permute-start(f32[8,128]{1,0:T(8,128)S(1)} %get-tuple-element.93.refs_0_), channel_id=1, source_target_pairs={{0,12},{4,8},{8,4},{12,0},{1,13},{5,9},{9,5},{13,1},{2,14},{6,10},... | collective-permute-start | bytes 12296 | tf_op jit(solution)/shard_map/ppermute | solution.py:446
  92.6 3.6 %collective-permute-start.32 = (f32[8,128]{1,0:T(8,128)S(1)}, f32[8,128]{1,0:T(8,128)S(1)}, u32[]{:S(2)}, u32[]{:S(2)}) collective-permute-start(f32[8,128]{1,0:T(8,128)S(1)} %get-tuple-element.93.refs_0_), channel_id=1, source_target_pairs={{0,8},{4,12},{8,0},{12,4},{1,9},{5,13},{9,1},{13,5},{2,10},{6,14},... | collective-permute-start | bytes 12296 | tf_op jit(solution)/shard_map/ppermute | solution.py:446
  (3 other events, 7.1 us)

commit v10 on v9

--- a/solution.py
+++ b/solution.py
@@ -339,10 +339,6 @@
         a, cr, ci, gcolin_ref[re, :], gcolin_ref[im, :], tcol_ref[re, :], tcol_ref[im, :], rho_eff
     )
     residual(mt_ref, vt_ref, grow_ref, gcol_ref, *outs, ct_ref)
-
-
-def add_kernel(a_ref, b_ref, out_ref):
-    out_ref[...] = a_ref[...] + b_ref[...]
 
 
 def combine_kernel(*refs, nz, span):
@@ -524,12 +520,11 @@
         )
         same = lax.dynamic_update_slice(same, power, (half, 0))
         other = lax.dynamic_update_slice(other, power, (half, 0))
-        sums = call(add_kernel, "add", [], [same, swap(other, "scol", 1)], [f32(half + 8, rows)])[0]
         pair_sums, own = call(
-            functools.partial(combine_kernel, nz=2, span=span),
+            functools.partial(combine_kernel, nz=nz, span=span),
             "combine",
             [],
-            [sums, swap(sums, "scol", 2)],
+            [same] + [swap(same if n % 2 == 0 else other, "scol", n) for n in range(1, nz)],
             [f32(half, rows), f32(3 * depth + 8, rows)],
         )
         other_sums = swap(pair_sums, "scol", 1)

time: 97.4 us -> 93.6 us (0.961)
  waiting for transfers between devices: 29 us -> 24.8 us
    ppermute x35 -> x38, waiting for transfers between devices: 29 us -> 24.8 us  [swap(): return lax.ppermute(x, axis, [(m, m ^ n) for m in range(size)])]
    ppermute x35 -> x38, starting transfers between devices: 41 us -> 41.5 us  [swap(): return lax.ppermute(x, axis, [(m, m ^ n) for m in range(size)])]
    pallas_call x18 -> x15, Pallas kernels: 26.3 us -> 26.3 us  [call(): pl.pallas_call(kernel, in_specs=[SMEM] * len(lead) + [place] * len(args),...]
  transfers between devices with their start and end apart: 35 -> 38, of which waited for: 18 -> 20; matrix products, arithmetic and copies ran while one was open for 0% -> 0% of each run, Pallas kernels for 12% -> 12%
where the time goes in v10:
time: 93.6 us; the launch traced here: 93.5 us
  starting transfers between devices  41.5 us (44%)
  Pallas kernels  26.3 us (28%)
  waiting for transfers between devices  24.8 us (26%)
    ppermute x38, starting transfers between devices, swap(): return lax.ppermute(x, axis, [(m, m ^ n) for m in range(size)])  41.5 us
    pallas_call x15, Pallas kernels, call(): pl.pallas_call(kernel, in_specs=[SMEM] * len(lead) + [place] * len(args),...  26.3 us
    ppermute x38, waiting for transfers between devices, swap(): return lax.ppermute(x, axis, [(m, m ^ n) for m in range(size)])  24.8 us
  transfers between devices with their start and end apart: 38, of which 20 were waited for; matrix products, arithmetic and copies ran while one was open for 0% of the time, Pallas kernels for 12%

profile of v10, /device:TPU:0, one launch (start us, length us, event | category | flops | bytes accessed | tf_op | source)
XLA Modules:
  0.0 93.5 jit_solution(16542217812196896301)
XLA Ops:
  1.6 5.1 %collective-permute-start.5 = (f32[64,128]{1,0:T(8,128)S(1)}, f32[64,128]{1,0:T(8,128)S(1)}, u32[]{:S(2)}, u32[]{:S(2)}) collective-permute-start(f32[64,128]{1,0:T(8,128)S(1)} %get-tuple-element.51.refs_0_.refs_4_), channel_id=1, source_target_pairs={{0,3},{1,2},{2,1},{3,0},{4,7},{5,6},{6,5},{7,4},{8,11},{9,10},{10,... | collective-permute-start | bytes 98312 | tf_op jit(solution)/shard_map/ppermute | solution.py:442
  9.3 3.2 %prepare.1 = (bf16[64,2,128,128]{3,2,1,0:T(8,128)(2,1)S(1)}, f32[2,128,128]{2,1,0:T(8,128)S(1)}, f32[64,128]{1,0:T(8,128)S(1)}, f32[16,128]{1,0:T(8,128)S(1)}) custom-call(f32[8]{0:T(128)} %refs_0_.1, s32[64]{0:T(128)} %refs_1_.1, s32[8,8]{1,0:T(8,128)} %bitcast.24, bf16[64,2,128,128]{3,2,1,0:T(8,128)(2,1)} %bitcast.19, bf16[2,128,128]{2,1,0:T(8,128)(2,1)} %bitcast.20), custom_call_target="tpu_custom_call" | custom-call | tf_op jit(solution)/shard_map/prepare/pallas_call | solution.py:429
  12.5 3.2 %first.1 = (f32[64,2,128,128]{3,2,1,0:T(8,128)S(1)}, f32[2,128,128]{2,1,0:T(8,128)S(1)}, f32[8,128]{1,0:T(8,128)S(1)}, f32[128,128]{1,0:T(8,128)S(1)}, f32[128,1...) custom-call(f32[64,128]{1,0:T(8,128)S(1)} %get-tuple-element.51.refs_0_.refs_4_, ...), custom_call_target="tpu_custom_call" | custom-call | tf_op jit(solution)/shard_map/first/pallas_call | solution.py:429
  15.7 1.5 %collective-permute-start.6 = (f32[8,128]{1,0:T(8,128)S(1)}, f32[8,128]{1,0:T(8,128)S(1)}, u32[]{:S(2)}, u32[]{:S(2)}) collective-permute-start(f32[8,128]{1,0:T(8,128)S(1)} %get-tuple-element.57), channel_id=1, source_target_pairs={{0,20},{4,16},{8,28},{12,24},{16,4},{20,0},{24,12},{28,8},{1,21},{... | collective-permute-start | bytes 12296 | tf_op jit(solution)/shard_map/ppermute | solution.py:442
  17.2 2.1 %terms.4 = (f32[104,128]{1,0:T(8,128)S(1)}, f32[104,128]{1,0:T(8,128)S(1)}) custom-call(f32[64,2,128,128]{3,2,1,0:T(8,128)S(1)} %get-tuple-element.54.z_ref, f32[2,128,128]{2,1,0:T(8,128)S(1)} %get-tuple-element.55.r_ref), custom_call_target="tpu_custom_call" | custom-call | tf_op jit(solution)/shard_map/terms/pallas_call | solution.py:429
  19.3 3.7 %collective-permute-start.9 = (f32[104,128]{1,0:T(8,128)S(1)}, f32[104,128]{1,0:T(8,128)S(1)}, u32[]{:S(2)}, u32[]{:S(2)}) collective-permute-start(f32[104,128]{1,0:T(8,128)S(1)} %get-tuple-element.105), channel_id=1, source_target_pairs={{0,3},{1,2},{2,1},{3,0},{4,7},{5,6},{6,5},{7,4},{8,11},{9,10},{10,... | collective-permute-start | bytes 159752 | tf_op jit(solution)/shard_map/ppermute | solution.py:442
  23.8 2.0 %collective-permute-done.9.refs_3_ = f32[104,128]{1,0:T(8,128)S(1)} collective-permute-done((f32[104,128]{1,0:T(8,128)S(1)}, f32[104,128]{1,0:T(8,128)S(1)}, u32[]{:S(2)}, u32[]{:S(2)}) %collective-permute-start.9) | collective-permute-done | bytes 53280 | tf_op jit(solution)/shard_map/ppermute | solution.py:442
  25.8 2.2 %collective-permute-done.7.refs_1_ = f32[104,128]{1,0:T(8,128)S(1)} collective-permute-done((f32[104,128]{1,0:T(8,128)S(1)}, f32[104,128]{1,0:T(8,128)S(1)}, u32[]{:S(2)}, u32[]{:S(2)}) %collective-permute-start.7) | collective-permute-done | bytes 53280 | tf_op jit(solution)/shard_map/ppermute | solution.py:442
  28.7 1.5 %collective-permute-start.13 = (f32[96,128]{1,0:T(8,128)S(1)}, f32[96,128]{1,0:T(8,128)S(1)}, u32[]{:S(2)}, u32[]{:S(2)}) collective-permute-start(f32[96,128]{1,0:T(8,128)S(1)} %get-tuple-element.60.refs_4_), channel_id=1, source_target_pairs={{0,1},{1,0},{2,3},{3,2},{4,5},{5,4},{6,7},{7,6},{8,9},{9,8},{10,11... | collective-permute-start | bytes 147464 | tf_op jit(solution)/shard_map/ppermute | solution.py:442
  30.2 1.4 %collective-permute-start.11 = (f32[56,128]{1,0:T(8,128)S(1)}, f32[56,128]{1,0:T(8,128)S(1)}, u32[]{:S(2)}, u32[]{:S(2)}) collective-permute-start(f32[56,128]{1,0:T(8,128)S(1)} %get-tuple-element.59.refs_0_), channel_id=1, source_target_pairs={{0,8},{4,12},{8,0},{12,4},{1,9},{5,13},{9,1},{13,5},{2,10},{6,14},... | collective-permute-start | bytes 86024 | tf_op jit(solution)/shard_map/ppermute | solution.py:442
  32.1 1.6 %collective-permute-done.12.refs_3_ = f32[56,128]{1,0:T(8,128)S(1)} collective-permute-done((f32[56,128]{1,0:T(8,128)S(1)}, f32[56,128]{1,0:T(8,128)S(1)}, u32[]{:S(2)}, u32[]{:S(2)}) %collective-permute-start.12) | collective-permute-done | bytes 28704 | tf_op jit(solution)/shard_map/ppermute | solution.py:442
  34.1 3.1 %sweep.3 = (f32[64,2,128,128]{3,2,1,0:T(8,128)S(1)}, f32[2,128,128]{2,1,0:T(8,128)S(1)}, f32[8,128]{1,0:T(8,128)S(1)}, f32[128,128]{1,0:T(8,128)S(1)}, f32[128,128]{1,0:T(8,128)S(1)}) custom-call(f32[56,128]{1,0:T(8,128)S(1)} %get-tuple-element.59.refs_0_, f32[56,128]{1,0:T(8,128)S(1)} %collective-permute-done.10.refs_1_, ...), custom_call_target="tpu_custom_call" | custom-call | tf_op jit(solution)/shard_map/sweep/pallas_call | solution.py:429
  38.3 2.1 %terms.5 = (f32[104,128]{1,0:T(8,128)S(1)}, f32[104,128]{1,0:T(8,128)S(1)}) custom-call(f32[64,2,128,128]{3,2,1,0:T(8,128)S(1)} %get-tuple-element.66.z_ref, f32[2,128,128]{2,1,0:T(8,128)S(1)} %get-tuple-element.67.r_ref), custom_call_target="tpu_custom_call" | custom-call | tf_op jit(solution)/shard_map/terms/pallas_call | solution.py:429
  40.5 2.2 %collective-permute-start.17 = (f32[104,128]{1,0:T(8,128)S(1)}, f32[104,128]{1,0:T(8,128)S(1)}, u32[]{:S(2)}, u32[]{:S(2)}) collective-permute-start(f32[104,128]{1,0:T(8,128)S(1)} %get-tuple-element.103), channel_id=1, source_target_pairs={{0,3},{1,2},{2,1},{3,0},{4,7},{5,6},{6,5},{7,4},{8,11},{9,10},{10,... | collective-permute-start | bytes 159752 | tf_op jit(solution)/shard_map/ppermute | solution.py:442
  42.7 2.3 %collective-permute-start.16 = (f32[104,128]{1,0:T(8,128)S(1)}, f32[104,128]{1,0:T(8,128)S(1)}, u32[]{:S(2)}, u32[]{:S(2)}) collective-permute-start(f32[104,128]{1,0:T(8,128)S(1)} %get-tuple-element.104.refs_0_), channel_id=1, source_target_pairs={{0,2},{1,3},{2,0},{3,1},{4,6},{5,7},{6,4},{7,5},{8,10},{9,11},{10,... | collective-permute-start | bytes 159752 | tf_op jit(solution)/shard_map/ppermute | solution.py:442
  44.9 1.9 %collective-permute-done.17.refs_3_ = f32[104,128]{1,0:T(8,128)S(1)} collective-permute-done((f32[104,128]{1,0:T(8,128)S(1)}, f32[104,128]{1,0:T(8,128)S(1)}, u32[]{:S(2)}, u32[]{:S(2)}) %collective-permute-start.17) | collective-permute-done | bytes 53280 | tf_op jit(solution)/shard_map/ppermute | solution.py:442
  46.8 1.6 %collective-permute-done.15.refs_1_ = f32[104,128]{1,0:T(8,128)S(1)} collective-permute-done((f32[104,128]{1,0:T(8,128)S(1)}, f32[104,128]{1,0:T(8,128)S(1)}, u32[]{:S(2)}, u32[]{:S(2)}) %collective-permute-start.15) | collective-permute-done | bytes 53280 | tf_op jit(solution)/shard_map/ppermute | solution.py:442
  48.5 1.4 %collective-permute-start.21 = (f32[96,128]{1,0:T(8,128)S(1)}, f32[96,128]{1,0:T(8,128)S(1)}, u32[]{:S(2)}, u32[]{:S(2)}) collective-permute-start(f32[96,128]{1,0:T(8,128)S(1)} %get-tuple-element.72.refs_4_), channel_id=1, source_target_pairs={{0,1},{1,0},{2,3},{3,2},{4,5},{5,4},{6,7},{7,6},{8,9},{9,8},{10,11... | collective-permute-start | bytes 147464 | tf_op jit(solution)/shard_map/ppermute | solution.py:442
  51.7 1.4 %collective-permute-done.20.refs_3_ = f32[56,128]{1,0:T(8,128)S(1)} collective-permute-done((f32[56,128]{1,0:T(8,128)S(1)}, f32[56,128]{1,0:T(8,128)S(1)}, u32[]{:S(2)}, u32[]{:S(2)}) %collective-permute-start.20) | collective-permute-done | bytes 28704 | tf_op jit(solution)/shard_map/ppermute | solution.py:442
  54.0 3.1 %sweep.4 = (f32[64,2,128,128]{3,2,1,0:T(8,128)S(1)}, f32[2,128,128]{2,1,0:T(8,128)S(1)}, f32[8,128]{1,0:T(8,128)S(1)}, f32[128,128]{1,0:T(8,128)S(1)}, f32[128,128]{1,0:T(8,128)S(1)}) custom-call(f32[56,128]{1,0:T(8,128)S(1)} %get-tuple-element.71.refs_0_, f32[56,128]{1,0:T(8,128)S(1)} %collective-permute-done.18.refs_1_, ...), custom_call_target="tpu_custom_call" | custom-call | tf_op jit(solution)/shard_map/sweep/pallas_call | solution.py:429
  57.7 2.1 %terms.6 = (f32[104,128]{1,0:T(8,128)S(1)}, f32[104,128]{1,0:T(8,128)S(1)}) custom-call(f32[64,2,128,128]{3,2,1,0:T(8,128)S(1)} %get-tuple-element.75.z_ref, f32[2,128,128]{2,1,0:T(8,128)S(1)} %get-tuple-element.76.r_ref), custom_call_target="tpu_custom_call" | custom-call | tf_op jit(solution)/shard_map/terms/pallas_call | solution.py:429
  60.2 1.5 %collective-permute-start.25 = (f32[104,128]{1,0:T(8,128)S(1)}, f32[104,128]{1,0:T(8,128)S(1)}, u32[]{:S(2)}, u32[]{:S(2)}) collective-permute-start(f32[104,128]{1,0:T(8,128)S(1)} %get-tuple-element.101), channel_id=1, source_target_pairs={{0,3},{1,2},{2,1},{3,0},{4,7},{5,6},{6,5},{7,4},{8,11},{9,10},{10,... | collective-permute-start | bytes 159752 | tf_op jit(solution)/shard_map/ppermute | solution.py:442
  62.1 2.5 %collective-permute-start.24 = (f32[104,128]{1,0:T(8,128)S(1)}, f32[104,128]{1,0:T(8,128)S(1)}, u32[]{:S(2)}, u32[]{:S(2)}) collective-permute-start(f32[104,128]{1,0:T(8,128)S(1)} %get-tuple-element.102.refs_0_), channel_id=1, source_target_pairs={{0,2},{1,3},{2,0},{3,1},{4,6},{5,7},{6,4},{7,5},{8,10},{9,11},{10,... | collective-permute-start | bytes 159752 | tf_op jit(solution)/shard_map/ppermute | solution.py:442
  64.6 2.2 %collective-permute-done.25.refs_3_ = f32[104,128]{1,0:T(8,128)S(1)} collective-permute-done((f32[104,128]{1,0:T(8,128)S(1)}, f32[104,128]{1,0:T(8,128)S(1)}, u32[]{:S(2)}, u32[]{:S(2)}) %collective-permute-start.25) | collective-permute-done | bytes 53280 | tf_op jit(solution)/shard_map/ppermute | solution.py:442
  67.0 1.4 %collective-permute-done.24.refs_2_ = f32[104,128]{1,0:T(8,128)S(1)} collective-permute-done((f32[104,128]{1,0:T(8,128)S(1)}, f32[104,128]{1,0:T(8,128)S(1)}, u32[]{:S(2)}, u32[]{:S(2)}) %collective-permute-start.24) | collective-permute-done | bytes 53280 | tf_op jit(solution)/shard_map/ppermute | solution.py:442
  68.9 1.5 %collective-permute-start.27 = (f32[56,128]{1,0:T(8,128)S(1)}, f32[56,128]{1,0:T(8,128)S(1)}, u32[]{:S(2)}, u32[]{:S(2)}) collective-permute-start(f32[56,128]{1,0:T(8,128)S(1)} %get-tuple-element.80.refs_0_), channel_id=1, source_target_pairs={{0,8},{4,12},{8,0},{12,4},{1,9},{5,13},{9,1},{13,5},{2,10},{6,14},... | collective-permute-start | bytes 86024 | tf_op jit(solution)/shard_map/ppermute | solution.py:442
  70.8 1.7 %collective-permute-done.28.refs_3_ = f32[56,128]{1,0:T(8,128)S(1)} collective-permute-done((f32[56,128]{1,0:T(8,128)S(1)}, f32[56,128]{1,0:T(8,128)S(1)}, u32[]{:S(2)}, u32[]{:S(2)}) %collective-permute-start.28) | collective-permute-done | bytes 28704 | tf_op jit(solution)/shard_map/ppermute | solution.py:442
  72.8 3.1 %sweep.5 = (f32[64,2,128,128]{3,2,1,0:T(8,128)S(1)}, f32[2,128,128]{2,1,0:T(8,128)S(1)}, f32[8,128]{1,0:T(8,128)S(1)}, f32[128,128]{1,0:T(8,128)S(1)}, f32[128,128]{1,0:T(8,128)}) custom-call(f32[56,128]{1,0:T(8,128)S(1)} %get-tuple-element.80.refs_0_, f32[56,128]{1,0:T(8,128)S(1)} %collective-permute-done.26.refs_1_, ...), custom_call_target="tpu_custom_call" | custom-call | tf_op jit(solution)/shard_map/sweep/pallas_call | solution.py:429
  76.9 2.2 %terms.7 = (f32[56,128]{1,0:T(8,128)S(1)}, f32[56,128]{1,0:T(8,128)S(1)}, f32[56,128]{1,0:T(8,128)S(1)}, f32[56,128]{1,0:T(8,128)S(1)}) custom-call(f32[64,2,128,128]{3,2,1,0:T(8,128)S(1)} %get-tuple-element.84.z_ref, f32[2,128,128]{2,1,0:T(8,128)S(1)} %get-tuple-element.85.r_ref), custom_call_target="tpu_custom_call" | custom-call | tf_op jit(solution)/shard_map/terms/pallas_call | solution.py:429
  79.1 1.8 %collective-permute-start.32 = (f32[56,128]{1,0:T(8,128)S(1)}, f32[56,128]{1,0:T(8,128)S(1)}, u32[]{:S(2)}, u32[]{:S(2)}) collective-permute-start(f32[56,128]{1,0:T(8,128)S(1)} %get-tuple-element.107), channel_id=1, source_target_pairs={{0,2},{1,3},{2,0},{3,1},{4,6},{5,7},{6,4},{7,5},{8,10},{9,11},{10,... | collective-permute-start | bytes 86024 | tf_op jit(solution)/shard_map/ppermute | solution.py:442
  81.9 1.6 %collective-permute-start.33 = (f32[56,128]{1,0:T(8,128)S(1)}, f32[56,128]{1,0:T(8,128)S(1)}, u32[]{:S(2)}, u32[]{:S(2)}) collective-permute-start(f32[56,128]{1,0:T(8,128)S(1)} %get-tuple-element.99), channel_id=1, source_target_pairs={{0,3},{1,2},{2,1},{3,0},{4,7},{5,6},{6,5},{7,4},{8,11},{9,10},{10,... | collective-permute-start | bytes 86024 | tf_op jit(solution)/shard_map/ppermute | solution.py:442
  84.8 2.8 %collective-permute-done.33.refs_3_ = f32[56,128]{1,0:T(8,128)S(1)} collective-permute-done((f32[56,128]{1,0:T(8,128)S(1)}, f32[56,128]{1,0:T(8,128)S(1)}, u32[]{:S(2)}, u32[]{:S(2)}) %collective-permute-start.33) | collective-permute-done | bytes 28704 | tf_op jit(solution)/shard_map/ppermute | solution.py:442
  (64 shorter events, 21.9 us)
Async XLA Ops:
  1.6 7.5 %collective-permute-start.5 = (f32[64,128]{1,0:T(8,128)S(1)}, f32[64,128]{1,0:T(8,128)S(1)}, u32[]{:S(2)}, u32[]{:S(2)}) collective-permute-start(f32[64,128]{1,0:T(8,128)S(1)} %get-tuple-element.51.refs_0_.refs_4_), channel_id=1, source_target_pairs={{0,3},{1,2},{2,1},{3,0},{4,7},{5,6},{6,5},{7,4},{8,11},{9,10},{10,... | collective-permute-start | bytes 98312 | tf_op jit(solution)/shard_map/ppermute | solution.py:442
  6.8 5.7 %collective-permute-start.4 = (f32[64,128]{1,0:T(8,128)S(1)}, f32[64,128]{1,0:T(8,128)S(1)}, u32[]{:S(2)}, u32[]{:S(2)}) collective-permute-start(f32[64,128]{1,0:T(8,128)S(1)} %get-tuple-element.51.refs_0_.refs_4_), channel_id=1, source_target_pairs={{0,2},{1,3},{2,0},{3,1},{4,6},{5,7},{6,4},{7,5},{8,10},{9,11},{10,... | collective-permute-start | bytes 98312 | tf_op jit(solution)/shard_map/ppermute | solution.py:442
  6.8 5.7 %collective-permute-start.3 = (f32[64,128]{1,0:T(8,128)S(1)}, f32[64,128]{1,0:T(8,128)S(1)}, u32[]{:S(2)}, u32[]{:S(2)}) collective-permute-start(f32[64,128]{1,0:T(8,128)S(1)} %get-tuple-element.51.refs_0_.refs_4_), channel_id=1, source_target_pairs={{0,1},{1,0},{2,3},{3,2},{4,5},{5,4},{6,7},{7,6},{8,9},{9,8},{10,11... | collective-permute-start | bytes 98312 | tf_op jit(solution)/shard_map/ppermute | solution.py:442
  7.4 5.1 %collective-permute-start.2 = (f32[64,128]{1,0:T(8,128)S(1)}, f32[64,128]{1,0:T(8,128)S(1)}, u32[]{:S(2)}, u32[]{:S(2)}) collective-permute-start(f32[64,128]{1,0:T(8,128)S(1)} %get-tuple-element.51.refs_0_.refs_4_), channel_id=1, source_target_pairs={{0,12},{4,8},{8,4},{12,0},{1,13},{5,9},{9,5},{13,1},{2,14},{6,10},... | collective-permute-start | bytes 98312 | tf_op jit(solution)/shard_map/ppermute | solution.py:442
  7.8 4.7 %collective-permute-start.1 = (f32[64,128]{1,0:T(8,128)S(1)}, f32[64,128]{1,0:T(8,128)S(1)}, u32[]{:S(2)}, u32[]{:S(2)}) collective-permute-start(f32[64,128]{1,0:T(8,128)S(1)} %get-tuple-element.51.refs_0_.refs_4_), channel_id=1, source_target_pairs={{0,8},{4,12},{8,0},{12,4},{1,9},{5,13},{9,1},{13,5},{2,10},{6,14},... | collective-permute-start | bytes 98312 | tf_op jit(solution)/shard_map/ppermute | solution.py:442
  9.1 3.4 %collective-permute-start = (f32[64,128]{1,0:T(8,128)S(1)}, f32[64,128]{1,0:T(8,128)S(1)}, u32[]{:S(2)}, u32[]{:S(2)}) collective-permute-start(f32[64,128]{1,0:T(8,128)S(1)} %get-tuple-element.51.refs_0_.refs_4_), channel_id=1, source_target_pairs={{0,4},{4,0},{8,12},{12,8},{1,5},{5,1},{9,13},{13,9},{2,6},{6,2},{1... | collective-permute-start | bytes 98312 | tf_op jit(solution)/shard_map/ppermute | solution.py:442
  15.7 3.6 %collective-permute-start.6 = (f32[8,128]{1,0:T(8,128)S(1)}, f32[8,128]{1,0:T(8,128)S(1)}, u32[]{:S(2)}, u32[]{:S(2)}) collective-permute-start(f32[8,128]{1,0:T(8,128)S(1)} %get-tuple-element.57), channel_id=1, source_target_pairs={{0,20},{4,16},{8,28},{12,24},{16,4},{20,0},{24,12},{28,8},{1,21},{... | collective-permute-start | bytes 12296 | tf_op jit(solution)/shard_map/ppermute | solution.py:442
  19.3 6.5 %collective-permute-start.9 = (f32[104,128]{1,0:T(8,128)S(1)}, f32[104,128]{1,0:T(8,128)S(1)}, u32[]{:S(2)}, u32[]{:S(2)}) collective-permute-start(f32[104,128]{1,0:T(8,128)S(1)} %get-tuple-element.105), channel_id=1, source_target_pairs={{0,3},{1,2},{2,1},{3,0},{4,7},{5,6},{6,5},{7,4},{8,11},{9,10},{10,... | collective-permute-start | bytes 159752 | tf_op jit(solution)/shard_map/ppermute | solution.py:442
  23.0 5.0 %collective-permute-start.7 = (f32[104,128]{1,0:T(8,128)S(1)}, f32[104,128]{1,0:T(8,128)S(1)}, u32[]{:S(2)}, u32[]{:S(2)}) collective-permute-start(f32[104,128]{1,0:T(8,128)S(1)} %get-tuple-element.105), channel_id=1, source_target_pairs={{0,1},{1,0},{2,3},{3,2},{4,5},{5,4},{6,7},{7,6},{8,9},{9,8},{10,11... | collective-permute-start | bytes 159752 | tf_op jit(solution)/shard_map/ppermute | solution.py:442
  23.0 5.6 %collective-permute-start.8 = (f32[104,128]{1,0:T(8,128)S(1)}, f32[104,128]{1,0:T(8,128)S(1)}, u32[]{:S(2)}, u32[]{:S(2)}) collective-permute-start(f32[104,128]{1,0:T(8,128)S(1)} %get-tuple-element.106.refs_0_), channel_id=1, source_target_pairs={{0,2},{1,3},{2,0},{3,1},{4,6},{5,7},{6,4},{7,5},{8,10},{9,11},{10,... | collective-permute-start | bytes 159752 | tf_op jit(solution)/shard_map/ppermute | solution.py:442
  28.7 5.4 %collective-permute-start.13 = (f32[96,128]{1,0:T(8,128)S(1)}, f32[96,128]{1,0:T(8,128)S(1)}, u32[]{:S(2)}, u32[]{:S(2)}) collective-permute-start(f32[96,128]{1,0:T(8,128)S(1)} %get-tuple-element.60.refs_4_), channel_id=1, source_target_pairs={{0,1},{1,0},{2,3},{3,2},{4,5},{5,4},{6,7},{7,6},{8,9},{9,8},{10,11... | collective-permute-start | bytes 147464 | tf_op jit(solution)/shard_map/ppermute | solution.py:442
  30.2 3.5 %collective-permute-start.12 = (f32[56,128]{1,0:T(8,128)S(1)}, f32[56,128]{1,0:T(8,128)S(1)}, u32[]{:S(2)}, u32[]{:S(2)}) collective-permute-start(f32[56,128]{1,0:T(8,128)S(1)} %get-tuple-element.59.refs_0_), channel_id=1, source_target_pairs={{0,12},{4,8},{8,4},{12,0},{1,13},{5,9},{9,5},{13,1},{2,14},{6,10},... | collective-permute-start | bytes 86024 | tf_op jit(solution)/shard_map/ppermute | solution.py:442
  30.2 3.9 %collective-permute-start.11 = (f32[56,128]{1,0:T(8,128)S(1)}, f32[56,128]{1,0:T(8,128)S(1)}, u32[]{:S(2)}, u32[]{:S(2)}) collective-permute-start(f32[56,128]{1,0:T(8,128)S(1)} %get-tuple-element.59.refs_0_), channel_id=1, source_target_pairs={{0,8},{4,12},{8,0},{12,4},{1,9},{5,13},{9,1},{13,5},{2,10},{6,14},... | collective-permute-start | bytes 86024 | tf_op jit(solution)/shard_map/ppermute | solution.py:442
  37.2 3.3 %collective-permute-start.14 = (f32[8,128]{1,0:T(8,128)S(1)}, f32[8,128]{1,0:T(8,128)S(1)}, u32[]{:S(2)}, u32[]{:S(2)}) collective-permute-start(f32[8,128]{1,0:T(8,128)S(1)} %get-tuple-element.69), channel_id=1, source_target_pairs={{0,20},{4,16},{8,28},{12,24},{16,4},{20,0},{24,12},{28,8},{1,21},{... | collective-permute-start | bytes 12296 | tf_op jit(solution)/shard_map/ppermute | solution.py:442
  40.5 6.4 %collective-permute-start.17 = (f32[104,128]{1,0:T(8,128)S(1)}, f32[104,128]{1,0:T(8,128)S(1)}, u32[]{:S(2)}, u32[]{:S(2)}) collective-permute-start(f32[104,128]{1,0:T(8,128)S(1)} %get-tuple-element.103), channel_id=1, source_target_pairs={{0,3},{1,2},{2,1},{3,0},{4,7},{5,6},{6,5},{7,4},{8,11},{9,10},{10,... | collective-permute-start | bytes 159752 | tf_op jit(solution)/shard_map/ppermute | solution.py:442
  42.6 5.8 %collective-permute-start.15 = (f32[104,128]{1,0:T(8,128)S(1)}, f32[104,128]{1,0:T(8,128)S(1)}, u32[]{:S(2)}, u32[]{:S(2)}) collective-permute-start(f32[104,128]{1,0:T(8,128)S(1)} %get-tuple-element.103), channel_id=1, source_target_pairs={{0,1},{1,0},{2,3},{3,2},{4,5},{5,4},{6,7},{7,6},{8,9},{9,8},{10,11... | collective-permute-start | bytes 159752 | tf_op jit(solution)/shard_map/ppermute | solution.py:442
  42.7 5.8 %collective-permute-start.16 = (f32[104,128]{1,0:T(8,128)S(1)}, f32[104,128]{1,0:T(8,128)S(1)}, u32[]{:S(2)}, u32[]{:S(2)}) collective-permute-start(f32[104,128]{1,0:T(8,128)S(1)} %get-tuple-element.104.refs_0_), channel_id=1, source_target_pairs={{0,2},{1,3},{2,0},{3,1},{4,6},{5,7},{6,4},{7,5},{8,10},{9,11},{10,... | collective-permute-start | bytes 159752 | tf_op jit(solution)/shard_map/ppermute | solution.py:442
  48.5 5.5 %collective-permute-start.21 = (f32[96,128]{1,0:T(8,128)S(1)}, f32[96,128]{1,0:T(8,128)S(1)}, u32[]{:S(2)}, u32[]{:S(2)}) collective-permute-start(f32[96,128]{1,0:T(8,128)S(1)} %get-tuple-element.72.refs_4_), channel_id=1, source_target_pairs={{0,1},{1,0},{2,3},{3,2},{4,5},{5,4},{6,7},{7,6},{8,9},{9,8},{10,11... | collective-permute-start | bytes 147464 | tf_op jit(solution)/shard_map/ppermute | solution.py:442
  49.9 3.3 %collective-permute-start.20 = (f32[56,128]{1,0:T(8,128)S(1)}, f32[56,128]{1,0:T(8,128)S(1)}, u32[]{:S(2)}, u32[]{:S(2)}) collective-permute-start(f32[56,128]{1,0:T(8,128)S(1)} %get-tuple-element.71.refs_0_), channel_id=1, source_target_pairs={{0,12},{4,8},{8,4},{12,0},{1,13},{5,9},{9,5},{13,1},{2,14},{6,10},... | collective-permute-start | bytes 86024 | tf_op jit(solution)/shard_map/ppermute | solution.py:442
  49.9 4.1 %collective-permute-start.19 = (f32[56,128]{1,0:T(8,128)S(1)}, f32[56,128]{1,0:T(8,128)S(1)}, u32[]{:S(2)}, u32[]{:S(2)}) collective-permute-start(f32[56,128]{1,0:T(8,128)S(1)} %get-tuple-element.71.refs_0_), channel_id=1, source_target_pairs={{0,8},{4,12},{8,0},{12,4},{1,9},{5,13},{9,1},{13,5},{2,10},{6,14},... | collective-permute-start | bytes 86024 | tf_op jit(solution)/shard_map/ppermute | solution.py:442
  50.7 3.3 %collective-permute-start.18 = (f32[56,128]{1,0:T(8,128)S(1)}, f32[56,128]{1,0:T(8,128)S(1)}, u32[]{:S(2)}, u32[]{:S(2)}) collective-permute-start(f32[56,128]{1,0:T(8,128)S(1)} %get-tuple-element.71.refs_0_), channel_id=1, source_target_pairs={{0,4},{4,0},{8,12},{12,8},{1,5},{5,1},{9,13},{13,9},{2,6},{6,2},{1... | collective-permute-start | bytes 86024 | tf_op jit(solution)/shard_map/ppermute | solution.py:442
  60.2 6.6 %collective-permute-start.25 = (f32[104,128]{1,0:T(8,128)S(1)}, f32[104,128]{1,0:T(8,128)S(1)}, u32[]{:S(2)}, u32[]{:S(2)}) collective-permute-start(f32[104,128]{1,0:T(8,128)S(1)} %get-tuple-element.101), channel_id=1, source_target_pairs={{0,3},{1,2},{2,1},{3,0},{4,7},{5,6},{6,5},{7,4},{8,11},{9,10},{10,... | collective-permute-start | bytes 159752 | tf_op jit(solution)/shard_map/ppermute | solution.py:442
  61.7 5.3 %collective-permute-start.23 = (f32[104,128]{1,0:T(8,128)S(1)}, f32[104,128]{1,0:T(8,128)S(1)}, u32[]{:S(2)}, u32[]{:S(2)}) collective-permute-start(f32[104,128]{1,0:T(8,128)S(1)} %get-tuple-element.101), channel_id=1, source_target_pairs={{0,1},{1,0},{2,3},{3,2},{4,5},{5,4},{6,7},{7,6},{8,9},{9,8},{10,11... | collective-permute-start | bytes 159752 | tf_op jit(solution)/shard_map/ppermute | solution.py:442
  62.1 6.3 %collective-permute-start.24 = (f32[104,128]{1,0:T(8,128)S(1)}, f32[104,128]{1,0:T(8,128)S(1)}, u32[]{:S(2)}, u32[]{:S(2)}) collective-permute-start(f32[104,128]{1,0:T(8,128)S(1)} %get-tuple-element.102.refs_0_), channel_id=1, source_target_pairs={{0,2},{1,3},{2,0},{3,1},{4,6},{5,7},{6,4},{7,5},{8,10},{9,11},{10,... | collective-permute-start | bytes 159752 | tf_op jit(solution)/shard_map/ppermute | solution.py:442
  68.5 4.3 %collective-permute-start.29 = (f32[96,128]{1,0:T(8,128)S(1)}, f32[96,128]{1,0:T(8,128)S(1)}, u32[]{:S(2)}, u32[]{:S(2)}) collective-permute-start(f32[96,128]{1,0:T(8,128)S(1)} %get-tuple-element.81.refs_4_), channel_id=1, source_target_pairs={{0,1},{1,0},{2,3},{3,2},{4,5},{5,4},{6,7},{7,6},{8,9},{9,8},{10,11... | collective-permute-start | bytes 147464 | tf_op jit(solution)/shard_map/ppermute | solution.py:442
  68.9 3.6 %collective-permute-start.28 = (f32[56,128]{1,0:T(8,128)S(1)}, f32[56,128]{1,0:T(8,128)S(1)}, u32[]{:S(2)}, u32[]{:S(2)}) collective-permute-start(f32[56,128]{1,0:T(8,128)S(1)} %get-tuple-element.80.refs_0_), channel_id=1, source_target_pairs={{0,12},{4,8},{8,4},{12,0},{1,13},{5,9},{9,5},{13,1},{2,14},{6,10},... | collective-permute-start | bytes 86024 | tf_op jit(solution)/shard_map/ppermute | solution.py:442
  68.9 3.9 %collective-permute-start.27 = (f32[56,128]{1,0:T(8,128)S(1)}, f32[56,128]{1,0:T(8,128)S(1)}, u32[]{:S(2)}, u32[]{:S(2)}) collective-permute-start(f32[56,128]{1,0:T(8,128)S(1)} %get-tuple-element.80.refs_0_), channel_id=1, source_target_pairs={{0,8},{4,12},{8,0},{12,4},{1,9},{5,13},{9,1},{13,5},{2,10},{6,14},... | collective-permute-start | bytes 86024 | tf_op jit(solution)/shard_map/ppermute | solution.py:442
  79.1 4.9 %collective-permute-start.32 = (f32[56,128]{1,0:T(8,128)S(1)}, f32[56,128]{1,0:T(8,128)S(1)}, u32[]{:S(2)}, u32[]{:S(2)}) collective-permute-start(f32[56,128]{1,0:T(8,128)S(1)} %get-tuple-element.107), channel_id=1, source_target_pairs={{0,2},{1,3},{2,0},{3,1},{4,6},{5,7},{6,4},{7,5},{8,10},{9,11},{10,... | collective-permute-start | bytes 86024 | tf_op jit(solution)/shard_map/ppermute | solution.py:442
  80.9 3.9 %collective-permute-start.31 = (f32[56,128]{1,0:T(8,128)S(1)}, f32[56,128]{1,0:T(8,128)S(1)}, u32[]{:S(2)}, u32[]{:S(2)}) collective-permute-start(f32[56,128]{1,0:T(8,128)S(1)} %get-tuple-element.108), channel_id=1, source_target_pairs={{0,1},{1,0},{2,3},{3,2},{4,5},{5,4},{6,7},{7,6},{8,9},{9,8},{10,11... | collective-permute-start | bytes 86024 | tf_op jit(solution)/shard_map/ppermute | solution.py:442
  81.9 5.7 %collective-permute-start.33 = (f32[56,128]{1,0:T(8,128)S(1)}, f32[56,128]{1,0:T(8,128)S(1)}, u32[]{:S(2)}, u32[]{:S(2)}) collective-permute-start(f32[56,128]{1,0:T(8,128)S(1)} %get-tuple-element.99), channel_id=1, source_target_pairs={{0,3},{1,2},{2,1},{3,0},{4,7},{5,6},{6,5},{7,4},{8,11},{9,10},{10,... | collective-permute-start | bytes 86024 | tf_op jit(solution)/shard_map/ppermute | solution.py:442
  87.7 4.8 %collective-permute-start.37 = (f32[144,128]{1,0:T(8,128)S(1)}, f32[144,128]{1,0:T(8,128)S(1)}, u32[]{:S(2)}, u32[]{:S(2)}) collective-permute-start(f32[144,128]{1,0:T(8,128)S(1)} %get-tuple-element.94.refs_4_), channel_id=1, source_target_pairs={{0,16},{16,0},{1,17},{17,1},{2,18},{18,2},{3,19},{19,3},{4,20},{20... | collective-permute-start | bytes 221192 | tf_op jit(solution)/shard_map/ppermute | solution.py:442
  88.9 3.6 %collective-permute-start.35 = (f32[8,128]{1,0:T(8,128)S(1)}, f32[8,128]{1,0:T(8,128)S(1)}, u32[]{:S(2)}, u32[]{:S(2)}) collective-permute-start(f32[8,128]{1,0:T(8,128)S(1)} %get-tuple-element.93.refs_0_), channel_id=1, source_target_pairs={{0,8},{4,12},{8,0},{12,4},{1,9},{5,13},{9,1},{13,5},{2,10},{6,14},... | collective-permute-start | bytes 12296 | tf_op jit(solution)/shard_map/ppermute | solution.py:442
  (6 other events, 17.2 us)

commit v11 on v6

--- a/solution.py
+++ b/solution.py
@@ -304,8 +304,9 @@
 
 
 def sweep_kernel(*refs, ns, span, scale):
-    pieces = refs[:ns]
-    same_ref, other_ref, growin_ref, gcolin_ref, trow_ref, tcol_ref = refs[ns : ns + 6]
+    pieces = refs[:2] + refs[3 : ns + 1]
+    other_ref = refs[2]
+    same_ref, growin_ref, gcolin_ref, trow_ref, tcol_ref = refs[ns + 1 : ns + 6]
     rho_ref, mt_ref, vt_ref = refs[ns + 6 : ns + 9]
     outs = refs[ns + 9 : ns + 12]
     grow_ref, gcol_ref, ct_ref = refs[ns + 12 :]
@@ -343,7 +344,7 @@
 
 def combine_kernel(*refs, nz, span):
     parts = refs[:nz]
-    pair_ref, own_ref = refs[nz:]
+    pair_ref, own_ref, *copies = refs[nz:]
     half = pair_ref.shape[0] // 3
     depth = 2 * half * span // pair_ref.shape[1]
     total = parts[0][...]
@@ -354,6 +355,8 @@
         piece = total[q * half : (q + 1) * half]
         own_ref[q * depth : (q + 1) * depth, :] = pack_folded(piece, lax.axis_index("scol"), span)
     own_ref[3 * depth :, :] = total[3 * half :]
+    for ref in copies:
+        ref[...] = own_ref[...]
 
 
 def last_combine_kernel(*refs, nz, span):
@@ -522,20 +525,21 @@
         )
         same = lax.dynamic_update_slice(same, power, (half, 0))
         other = lax.dynamic_update_slice(other, power, (half, 0))
-        pair_sums, own = call(
+        pair_sums, own, *copies = call(
             functools.partial(combine_kernel, nz=nz, span=span),
             "combine",
             [],
             [same] + [swap(same if n % 2 == 0 else other, "scol", n) for n in range(1, nz)],
-            [f32(half, rows), f32(3 * depth + 8, rows)],
+            [f32(half, rows)] + [f32(3 * depth + 8, rows)] * (ns - 1),
         )
         other_sums = swap(pair_sums, "scol", 1)
-        pieces = [own] + [swap(own, "srow", n) for n in range(1, ns)]
+        pieces = [own, swap(own, "srow", 1)]
+        pieces += [swap(copy, "srow", n + 2) for n, copy in enumerate(copies)]
         z, r, power, grow, gcol = call(
             functools.partial(sweep_kernel, ns=ns, span=span, scale=scale),
             "sweep",
             [],
-            pieces + [pair_sums, other_sums, grow, gcol, trow, tcol, rho_rows, mt, vt],
+            pieces[:2] + [other_sums] + pieces[2:] + [pair_sums, grow, gcol, trow, tcol, rho_rows, mt, vt],
             fields + [plane, plane],
             scratch,
         )

time: 92.6 us -> 94.2 us (1.017)
  waiting for transfers between devices: 24.7 us -> 27.1 us
    ppermute x38, waiting for transfers between devices: 24.7 us -> 27.1 us  [swap(): return lax.ppermute(x, axis, [(m, m ^ n) for m in range(size)])]
  transfers between devices with their start and end apart: 38 -> 38, of which waited for: 21 -> 24; matrix products, arithmetic and copies ran while one was open for 0% -> 0% of each run, Pallas kernels for 13% -> 12%
where the time goes in v11:
time: 94.2 us; the launch traced here: 94.1 us
  starting transfers between devices  39.8 us (42%)
  waiting for transfers between devices  27.1 us (29%)
  Pallas kernels  26.3 us (28%)
    ppermute x38, starting transfers between devices, swap(): return lax.ppermute(x, axis, [(m, m ^ n) for m in range(size)])  39.8 us
    ppermute x38, waiting for transfers between devices, swap(): return lax.ppermute(x, axis, [(m, m ^ n) for m in range(size)])  27.1 us
    pallas_call x15, Pallas kernels, call(): pl.pallas_call(kernel, in_specs=[SMEM] * len(lead) + [place] * len(args),...  26.3 us
  transfers between devices with their start and end apart: 38, of which 24 were waited for; matrix products, arithmetic and copies ran while one was open for 0% of the time, Pallas kernels for 12%

profile of v11, /device:TPU:0, one launch (start us, length us, event | category | flops | bytes accessed | tf_op | source)
XLA Modules:
  0.0 94.1 jit_solution(902212963492941385)
XLA Ops:
  1.6 2.5 %collective-permute-start.5 = (f32[64,128]{1,0:T(8,128)S(1)}, f32[64,128]{1,0:T(8,128)S(1)}, u32[]{:S(2)}, u32[]{:S(2)}) collective-permute-start(f32[64,128]{1,0:T(8,128)S(1)} %get-tuple-element.57.refs_0_.refs_1_), channel_id=1, source_target_pairs={{0,12},{4,8},{8,4},{12,0},{1,13},{5,9},{9,5},{13,1},{2,14},{6,10},... | collective-permute-start | bytes 98312 | tf_op jit(solution)/shard_map/ppermute | solution.py:445
  4.1 3.6 %collective-permute-start.4 = (f32[64,128]{1,0:T(8,128)S(1)}, f32[64,128]{1,0:T(8,128)S(1)}, u32[]{:S(2)}, u32[]{:S(2)}) collective-permute-start(f32[64,128]{1,0:T(8,128)S(1)} %get-tuple-element.57.refs_0_.refs_1_), channel_id=1, source_target_pairs={{0,3},{1,2},{2,1},{3,0},{4,7},{5,6},{6,5},{7,4},{8,11},{9,10},{10,... | collective-permute-start | bytes 98312 | tf_op jit(solution)/shard_map/ppermute | solution.py:445
  9.1 3.2 %prepare.1 = (bf16[64,2,128,128]{3,2,1,0:T(8,128)(2,1)S(1)}, f32[2,128,128]{2,1,0:T(8,128)S(1)}, f32[64,128]{1,0:T(8,128)S(1)}, f32[16,128]{1,0:T(8,128)S(1)}) custom-call(f32[8]{0:T(128)} %refs_0_.1, s32[64]{0:T(128)} %refs_1_.1, s32[8,8]{1,0:T(8,128)} %bitcast.24, bf16[64,2,128,128]{3,2,1,0:T(8,128)(2,1)} %bitcast.19, bf16[2,128,128]{2,1,0:T(8,128)(2,1)} %bitcast.20), custom_call_target="tpu_custom_call" | custom-call | tf_op jit(solution)/shard_map/prepare/pallas_call | solution.py:432
  13.2 3.2 %first.1 = (f32[64,2,128,128]{3,2,1,0:T(8,128)S(1)}, f32[2,128,128]{2,1,0:T(8,128)S(1)}, f32[8,128]{1,0:T(8,128)S(1)}, f32[128,128]{1,0:T(8,128)S(1)}, f32[128,1...) custom-call(f32[64,128]{1,0:T(8,128)S(1)} %get-tuple-element.57.refs_0_.refs_1_, ...), custom_call_target="tpu_custom_call" | custom-call | tf_op jit(solution)/shard_map/first/pallas_call | solution.py:432
  16.9 2.1 %terms.4 = (f32[104,128]{1,0:T(8,128)S(1)}, f32[104,128]{1,0:T(8,128)S(1)}) custom-call(f32[64,2,128,128]{3,2,1,0:T(8,128)S(1)} %get-tuple-element.60.z_ref, f32[2,128,128]{2,1,0:T(8,128)S(1)} %get-tuple-element.61.r_ref), custom_call_target="tpu_custom_call" | custom-call | tf_op jit(solution)/shard_map/terms/pallas_call | solution.py:432
  19.4 3.3 %collective-permute-start.9 = (f32[104,128]{1,0:T(8,128)S(1)}, f32[104,128]{1,0:T(8,128)S(1)}, u32[]{:S(2)}, u32[]{:S(2)}) collective-permute-start(f32[104,128]{1,0:T(8,128)S(1)} %get-tuple-element.117), channel_id=1, source_target_pairs={{0,3},{1,2},{2,1},{3,0},{4,7},{5,6},{6,5},{7,4},{8,11},{9,10},{10,... | collective-permute-start | bytes 159752 | tf_op jit(solution)/shard_map/ppermute | solution.py:445
  23.8 2.1 %collective-permute-done.9.refs_3_ = f32[104,128]{1,0:T(8,128)S(1)} collective-permute-done((f32[104,128]{1,0:T(8,128)S(1)}, f32[104,128]{1,0:T(8,128)S(1)}, u32[]{:S(2)}, u32[]{:S(2)}) %collective-permute-start.9) | collective-permute-done | bytes 53280 | tf_op jit(solution)/shard_map/ppermute | solution.py:445
  25.9 1.8 %collective-permute-done.7.refs_1_ = f32[104,128]{1,0:T(8,128)S(1)} collective-permute-done((f32[104,128]{1,0:T(8,128)S(1)}, f32[104,128]{1,0:T(8,128)S(1)}, u32[]{:S(2)}, u32[]{:S(2)}) %collective-permute-start.7) | collective-permute-done | bytes 53280 | tf_op jit(solution)/shard_map/ppermute | solution.py:445
  28.5 1.5 %collective-permute-start.11 = (f32[96,128]{1,0:T(8,128)S(1)}, f32[96,128]{1,0:T(8,128)S(1)}, u32[]{:S(2)}, u32[]{:S(2)}) collective-permute-start(f32[96,128]{1,0:T(8,128)S(1)} %get-tuple-element.66.refs_5_), channel_id=1, source_target_pairs={{0,1},{1,0},{2,3},{3,2},{4,5},{5,4},{6,7},{7,6},{8,9},{9,8},{10,11... | collective-permute-start | bytes 147464 | tf_op jit(solution)/shard_map/ppermute | solution.py:445
  30.0 1.4 %collective-permute-start.12 = (f32[56,128]{1,0:T(8,128)S(1)}, f32[56,128]{1,0:T(8,128)S(1)}, u32[]{:S(2)}, u32[]{:S(2)}) collective-permute-start(f32[56,128]{1,0:T(8,128)S(1)} %get-tuple-element.67), channel_id=1, source_target_pairs={{0,8},{4,12},{8,0},{12,4},{1,9},{5,13},{9,1},{13,5},{2,10},{6,14},... | collective-permute-start | bytes 86024 | tf_op jit(solution)/shard_map/ppermute | solution.py:445
  32.1 1.7 %collective-permute-done.12.refs_3_ = f32[56,128]{1,0:T(8,128)S(1)} collective-permute-done((f32[56,128]{1,0:T(8,128)S(1)}, f32[56,128]{1,0:T(8,128)S(1)}, u32[]{:S(2)}, u32[]{:S(2)}) %collective-permute-start.12) | collective-permute-done | bytes 28704 | tf_op jit(solution)/shard_map/ppermute | solution.py:445
  34.7 3.1 %sweep.3 = (f32[64,2,128,128]{3,2,1,0:T(8,128)S(1)}, f32[2,128,128]{2,1,0:T(8,128)S(1)}, f32[8,128]{1,0:T(8,128)S(1)}, f32[128,128]{1,0:T(8,128)S(1)}, f32[128,128]{1,0:T(8,128)S(1)}) custom-call(f32[56,128]{1,0:T(8,128)S(1)} %get-tuple-element.65.refs_0_, f32[56,128]{1,0:T(8,128)S(1)} %collective-permute-done.10.refs_1_, ...), custom_call_target="tpu_custom_call" | custom-call | tf_op jit(solution)/shard_map/sweep/pallas_call | solution.py:432
  37.8 2.1 %terms.5 = (f32[104,128]{1,0:T(8,128)S(1)}, f32[104,128]{1,0:T(8,128)S(1)}) custom-call(f32[64,2,128,128]{3,2,1,0:T(8,128)S(1)} %get-tuple-element.74.z_ref, f32[2,128,128]{2,1,0:T(8,128)S(1)} %get-tuple-element.75.r_ref), custom_call_target="tpu_custom_call" | custom-call | tf_op jit(solution)/shard_map/terms/pallas_call | solution.py:432
  40.8 1.6 %collective-permute-start.17 = (f32[104,128]{1,0:T(8,128)S(1)}, f32[104,128]{1,0:T(8,128)S(1)}, u32[]{:S(2)}, u32[]{:S(2)}) collective-permute-start(f32[104,128]{1,0:T(8,128)S(1)} %get-tuple-element.115), channel_id=1, source_target_pairs={{0,3},{1,2},{2,1},{3,0},{4,7},{5,6},{6,5},{7,4},{8,11},{9,10},{10,... | collective-permute-start | bytes 159752 | tf_op jit(solution)/shard_map/ppermute | solution.py:445
  43.0 2.2 %collective-permute-start.16 = (f32[104,128]{1,0:T(8,128)S(1)}, f32[104,128]{1,0:T(8,128)S(1)}, u32[]{:S(2)}, u32[]{:S(2)}) collective-permute-start(f32[104,128]{1,0:T(8,128)S(1)} %get-tuple-element.116.refs_0_), channel_id=1, source_target_pairs={{0,2},{1,3},{2,0},{3,1},{4,6},{5,7},{6,4},{7,5},{8,10},{9,11},{10,... | collective-permute-start | bytes 159752 | tf_op jit(solution)/shard_map/ppermute | solution.py:445
  45.2 2.1 %collective-permute-done.17.refs_3_ = f32[104,128]{1,0:T(8,128)S(1)} collective-permute-done((f32[104,128]{1,0:T(8,128)S(1)}, f32[104,128]{1,0:T(8,128)S(1)}, u32[]{:S(2)}, u32[]{:S(2)}) %collective-permute-start.17) | collective-permute-done | bytes 53280 | tf_op jit(solution)/shard_map/ppermute | solution.py:445
  50.6 1.2 %collective-permute-start.18 = (f32[56,128]{1,0:T(8,128)S(1)}, f32[56,128]{1,0:T(8,128)S(1)}, u32[]{:S(2)}, u32[]{:S(2)}) collective-permute-start(f32[56,128]{1,0:T(8,128)S(1)} %get-tuple-element.79.refs_0_), channel_id=1, source_target_pairs={{0,4},{4,0},{8,12},{12,8},{1,5},{5,1},{9,13},{13,9},{2,6},{6,2},{1... | collective-permute-start | bytes 86024 | tf_op jit(solution)/shard_map/ppermute | solution.py:445
  51.8 1.7 %collective-permute-done.20.refs_3_ = f32[56,128]{1,0:T(8,128)S(1)} collective-permute-done((f32[56,128]{1,0:T(8,128)S(1)}, f32[56,128]{1,0:T(8,128)S(1)}, u32[]{:S(2)}, u32[]{:S(2)}) %collective-permute-start.20) | collective-permute-done | bytes 28704 | tf_op jit(solution)/shard_map/ppermute | solution.py:445
  54.1 3.1 %sweep.4 = (f32[64,2,128,128]{3,2,1,0:T(8,128)S(1)}, f32[2,128,128]{2,1,0:T(8,128)S(1)}, f32[8,128]{1,0:T(8,128)S(1)}, f32[128,128]{1,0:T(8,128)S(1)}, f32[128,128]{1,0:T(8,128)S(1)}) custom-call(f32[56,128]{1,0:T(8,128)S(1)} %get-tuple-element.79.refs_0_, f32[56,128]{1,0:T(8,128)S(1)} %collective-permute-done.18.refs_1_, ...), custom_call_target="tpu_custom_call" | custom-call | tf_op jit(solution)/shard_map/sweep/pallas_call | solution.py:432
  58.0 2.1 %terms.6 = (f32[104,128]{1,0:T(8,128)S(1)}, f32[104,128]{1,0:T(8,128)S(1)}) custom-call(f32[64,2,128,128]{3,2,1,0:T(8,128)S(1)} %get-tuple-element.85.z_ref, f32[2,128,128]{2,1,0:T(8,128)S(1)} %get-tuple-element.86.r_ref), custom_call_target="tpu_custom_call" | custom-call | tf_op jit(solution)/shard_map/terms/pallas_call | solution.py:432
  60.3 2.2 %collective-permute-start.25 = (f32[104,128]{1,0:T(8,128)S(1)}, f32[104,128]{1,0:T(8,128)S(1)}, u32[]{:S(2)}, u32[]{:S(2)}) collective-permute-start(f32[104,128]{1,0:T(8,128)S(1)} %get-tuple-element.113), channel_id=1, source_target_pairs={{0,3},{1,2},{2,1},{3,0},{4,7},{5,6},{6,5},{7,4},{8,11},{9,10},{10,... | collective-permute-start | bytes 159752 | tf_op jit(solution)/shard_map/ppermute | solution.py:445
  62.5 2.2 %collective-permute-start.24 = (f32[104,128]{1,0:T(8,128)S(1)}, f32[104,128]{1,0:T(8,128)S(1)}, u32[]{:S(2)}, u32[]{:S(2)}) collective-permute-start(f32[104,128]{1,0:T(8,128)S(1)} %get-tuple-element.114.refs_0_), channel_id=1, source_target_pairs={{0,2},{1,3},{2,0},{3,1},{4,6},{5,7},{6,4},{7,5},{8,10},{9,11},{10,... | collective-permute-start | bytes 159752 | tf_op jit(solution)/shard_map/ppermute | solution.py:445
  64.7 2.0 %collective-permute-done.25.refs_3_ = f32[104,128]{1,0:T(8,128)S(1)} collective-permute-done((f32[104,128]{1,0:T(8,128)S(1)}, f32[104,128]{1,0:T(8,128)S(1)}, u32[]{:S(2)}, u32[]{:S(2)}) %collective-permute-start.25) | collective-permute-done | bytes 53280 | tf_op jit(solution)/shard_map/ppermute | solution.py:445
  66.7 1.8 %collective-permute-done.23.refs_1_ = f32[104,128]{1,0:T(8,128)S(1)} collective-permute-done((f32[104,128]{1,0:T(8,128)S(1)}, f32[104,128]{1,0:T(8,128)S(1)}, u32[]{:S(2)}, u32[]{:S(2)}) %collective-permute-start.23) | collective-permute-done | bytes 53280 | tf_op jit(solution)/shard_map/ppermute | solution.py:445
  70.7 1.2 %collective-permute-start.26 = (f32[56,128]{1,0:T(8,128)S(1)}, f32[56,128]{1,0:T(8,128)S(1)}, u32[]{:S(2)}, u32[]{:S(2)}) collective-permute-start(f32[56,128]{1,0:T(8,128)S(1)} %get-tuple-element.90.refs_0_), channel_id=1, source_target_pairs={{0,4},{4,0},{8,12},{12,8},{1,5},{5,1},{9,13},{13,9},{2,6},{6,2},{1... | collective-permute-start | bytes 86024 | tf_op jit(solution)/shard_map/ppermute | solution.py:445
  71.9 1.7 %collective-permute-done.28.refs_3_ = f32[56,128]{1,0:T(8,128)S(1)} collective-permute-done((f32[56,128]{1,0:T(8,128)S(1)}, f32[56,128]{1,0:T(8,128)S(1)}, u32[]{:S(2)}, u32[]{:S(2)}) %collective-permute-start.28) | collective-permute-done | bytes 28704 | tf_op jit(solution)/shard_map/ppermute | solution.py:445
  74.2 3.1 %sweep.5 = (f32[64,2,128,128]{3,2,1,0:T(8,128)S(1)}, f32[2,128,128]{2,1,0:T(8,128)S(1)}, f32[8,128]{1,0:T(8,128)S(1)}, f32[128,128]{1,0:T(8,128)S(1)}, f32[128,128]{1,0:T(8,128)}) custom-call(f32[56,128]{1,0:T(8,128)S(1)} %get-tuple-element.90.refs_0_, f32[56,128]{1,0:T(8,128)S(1)} %collective-permute-done.26.refs_1_, ...), custom_call_target="tpu_custom_call" | custom-call | tf_op jit(solution)/shard_map/sweep/pallas_call | solution.py:432
  78.1 2.2 %terms.7 = (f32[56,128]{1,0:T(8,128)S(1)}, f32[56,128]{1,0:T(8,128)S(1)}, f32[56,128]{1,0:T(8,128)S(1)}, f32[56,128]{1,0:T(8,128)S(1)}) custom-call(f32[64,2,128,128]{3,2,1,0:T(8,128)S(1)} %get-tuple-element.96.z_ref, f32[2,128,128]{2,1,0:T(8,128)S(1)} %get-tuple-element.97.r_ref), custom_call_target="tpu_custom_call" | custom-call | tf_op jit(solution)/shard_map/terms/pallas_call | solution.py:432
  80.4 1.8 %collective-permute-start.32 = (f32[56,128]{1,0:T(8,128)S(1)}, f32[56,128]{1,0:T(8,128)S(1)}, u32[]{:S(2)}, u32[]{:S(2)}) collective-permute-start(f32[56,128]{1,0:T(8,128)S(1)} %get-tuple-element.119), channel_id=1, source_target_pairs={{0,2},{1,3},{2,0},{3,1},{4,6},{5,7},{6,4},{7,5},{8,10},{9,11},{10,... | collective-permute-start | bytes 86024 | tf_op jit(solution)/shard_map/ppermute | solution.py:445
  82.6 2.2 %collective-permute-start.33 = (f32[56,128]{1,0:T(8,128)S(1)}, f32[56,128]{1,0:T(8,128)S(1)}, u32[]{:S(2)}, u32[]{:S(2)}) collective-permute-start(f32[56,128]{1,0:T(8,128)S(1)} %get-tuple-element.111), channel_id=1, source_target_pairs={{0,3},{1,2},{2,1},{3,0},{4,7},{5,6},{6,5},{7,4},{8,11},{9,10},{10,... | collective-permute-start | bytes 86024 | tf_op jit(solution)/shard_map/ppermute | solution.py:445
  86.1 2.2 %collective-permute-done.33.refs_3_ = f32[56,128]{1,0:T(8,128)S(1)} collective-permute-done((f32[56,128]{1,0:T(8,128)S(1)}, f32[56,128]{1,0:T(8,128)S(1)}, u32[]{:S(2)}, u32[]{:S(2)}) %collective-permute-start.33) | collective-permute-done | bytes 28704 | tf_op jit(solution)/shard_map/ppermute | solution.py:445
  91.3 1.2 %collective-permute-done.36.refs_3_ = f32[8,128]{1,0:T(8,128)S(1)} collective-permute-done((f32[8,128]{1,0:T(8,128)S(1)}, f32[8,128]{1,0:T(8,128)S(1)}, u32[]{:S(2)}, u32[]{:S(2)}) %collective-permute-start.36) | collective-permute-done | bytes 4128 | tf_op jit(solution)/shard_map/ppermute | solution.py:445
  (64 shorter events, 24.1 us)
Async XLA Ops:
  1.6 6.7 %collective-permute-start.5 = (f32[64,128]{1,0:T(8,128)S(1)}, f32[64,128]{1,0:T(8,128)S(1)}, u32[]{:S(2)}, u32[]{:S(2)}) collective-permute-start(f32[64,128]{1,0:T(8,128)S(1)} %get-tuple-element.57.refs_0_.refs_1_), channel_id=1, source_target_pairs={{0,12},{4,8},{8,4},{12,0},{1,13},{5,9},{9,5},{13,1},{2,14},{6,10},... | collective-permute-start | bytes 98312 | tf_op jit(solution)/shard_map/ppermute | solution.py:445
  4.1 8.2 %collective-permute-start.4 = (f32[64,128]{1,0:T(8,128)S(1)}, f32[64,128]{1,0:T(8,128)S(1)}, u32[]{:S(2)}, u32[]{:S(2)}) collective-permute-start(f32[64,128]{1,0:T(8,128)S(1)} %get-tuple-element.57.refs_0_.refs_1_), channel_id=1, source_target_pairs={{0,3},{1,2},{2,1},{3,0},{4,7},{5,6},{6,5},{7,4},{8,11},{9,10},{10,... | collective-permute-start | bytes 98312 | tf_op jit(solution)/shard_map/ppermute | solution.py:445
  7.7 4.6 %collective-permute-start.3 = (f32[64,128]{1,0:T(8,128)S(1)}, f32[64,128]{1,0:T(8,128)S(1)}, u32[]{:S(2)}, u32[]{:S(2)}) collective-permute-start(f32[64,128]{1,0:T(8,128)S(1)} %get-tuple-element.57.refs_0_.refs_1_), channel_id=1, source_target_pairs={{0,8},{4,12},{8,0},{12,4},{1,9},{5,13},{9,1},{13,5},{2,10},{6,14},... | collective-permute-start | bytes 98312 | tf_op jit(solution)/shard_map/ppermute | solution.py:445
  8.3 4.8 %collective-permute-start.2 = (f32[64,128]{1,0:T(8,128)S(1)}, f32[64,128]{1,0:T(8,128)S(1)}, u32[]{:S(2)}, u32[]{:S(2)}) collective-permute-start(f32[64,128]{1,0:T(8,128)S(1)} %get-tuple-element.57.refs_0_.refs_1_), channel_id=1, source_target_pairs={{0,2},{1,3},{2,0},{3,1},{4,6},{5,7},{6,4},{7,5},{8,10},{9,11},{10,... | collective-permute-start | bytes 98312 | tf_op jit(solution)/shard_map/ppermute | solution.py:445
  8.4 4.8 %collective-permute-start.1 = (f32[64,128]{1,0:T(8,128)S(1)}, f32[64,128]{1,0:T(8,128)S(1)}, u32[]{:S(2)}, u32[]{:S(2)}) collective-permute-start(f32[64,128]{1,0:T(8,128)S(1)} %get-tuple-element.57.refs_0_.refs_1_), channel_id=1, source_target_pairs={{0,4},{4,0},{8,12},{12,8},{1,5},{5,1},{9,13},{13,9},{2,6},{6,2},{1... | collective-permute-start | bytes 98312 | tf_op jit(solution)/shard_map/ppermute | solution.py:445
  8.4 4.8 %collective-permute-start = (f32[64,128]{1,0:T(8,128)S(1)}, f32[64,128]{1,0:T(8,128)S(1)}, u32[]{:S(2)}, u32[]{:S(2)}) collective-permute-start(f32[64,128]{1,0:T(8,128)S(1)} %get-tuple-element.57.refs_0_.refs_1_), channel_id=1, source_target_pairs={{0,1},{1,0},{2,3},{3,2},{4,5},{5,4},{6,7},{7,6},{8,9},{9,8},{10,11... | collective-permute-start | bytes 98312 | tf_op jit(solution)/shard_map/ppermute | solution.py:445
  19.4 6.5 %collective-permute-start.9 = (f32[104,128]{1,0:T(8,128)S(1)}, f32[104,128]{1,0:T(8,128)S(1)}, u32[]{:S(2)}, u32[]{:S(2)}) collective-permute-start(f32[104,128]{1,0:T(8,128)S(1)} %get-tuple-element.117), channel_id=1, source_target_pairs={{0,3},{1,2},{2,1},{3,0},{4,7},{5,6},{6,5},{7,4},{8,11},{9,10},{10,... | collective-permute-start | bytes 159752 | tf_op jit(solution)/shard_map/ppermute | solution.py:445
  22.7 5.0 %collective-permute-start.7 = (f32[104,128]{1,0:T(8,128)S(1)}, f32[104,128]{1,0:T(8,128)S(1)}, u32[]{:S(2)}, u32[]{:S(2)}) collective-permute-start(f32[104,128]{1,0:T(8,128)S(1)} %get-tuple-element.117), channel_id=1, source_target_pairs={{0,1},{1,0},{2,3},{3,2},{4,5},{5,4},{6,7},{7,6},{8,9},{9,8},{10,11... | collective-permute-start | bytes 159752 | tf_op jit(solution)/shard_map/ppermute | solution.py:445
  22.7 5.6 %collective-permute-start.8 = (f32[104,128]{1,0:T(8,128)S(1)}, f32[104,128]{1,0:T(8,128)S(1)}, u32[]{:S(2)}, u32[]{:S(2)}) collective-permute-start(f32[104,128]{1,0:T(8,128)S(1)} %get-tuple-element.118.refs_0_), channel_id=1, source_target_pairs={{0,2},{1,3},{2,0},{3,1},{4,6},{5,7},{6,4},{7,5},{8,10},{9,11},{10,... | collective-permute-start | bytes 159752 | tf_op jit(solution)/shard_map/ppermute | solution.py:445
  28.5 6.2 %collective-permute-start.11 = (f32[96,128]{1,0:T(8,128)S(1)}, f32[96,128]{1,0:T(8,128)S(1)}, u32[]{:S(2)}, u32[]{:S(2)}) collective-permute-start(f32[96,128]{1,0:T(8,128)S(1)} %get-tuple-element.66.refs_5_), channel_id=1, source_target_pairs={{0,1},{1,0},{2,3},{3,2},{4,5},{5,4},{6,7},{7,6},{8,9},{9,8},{10,11... | collective-permute-start | bytes 147464 | tf_op jit(solution)/shard_map/ppermute | solution.py:445
  30.0 3.9 %collective-permute-start.12 = (f32[56,128]{1,0:T(8,128)S(1)}, f32[56,128]{1,0:T(8,128)S(1)}, u32[]{:S(2)}, u32[]{:S(2)}) collective-permute-start(f32[56,128]{1,0:T(8,128)S(1)} %get-tuple-element.67), channel_id=1, source_target_pairs={{0,8},{4,12},{8,0},{12,4},{1,9},{5,13},{9,1},{13,5},{2,10},{6,14},... | collective-permute-start | bytes 86024 | tf_op jit(solution)/shard_map/ppermute | solution.py:445
  31.4 3.3 %collective-permute-start.13 = (f32[56,128]{1,0:T(8,128)S(1)}, f32[56,128]{1,0:T(8,128)S(1)}, u32[]{:S(2)}, u32[]{:S(2)}) collective-permute-start(f32[56,128]{1,0:T(8,128)S(1)} %get-tuple-element.68), channel_id=1, source_target_pairs={{0,12},{4,8},{8,4},{12,0},{1,13},{5,9},{9,5},{13,1},{2,14},{6,10},... | collective-permute-start | bytes 86024 | tf_op jit(solution)/shard_map/ppermute | solution.py:445
  31.4 3.3 %collective-permute-start.10 = (f32[56,128]{1,0:T(8,128)S(1)}, f32[56,128]{1,0:T(8,128)S(1)}, u32[]{:S(2)}, u32[]{:S(2)}) collective-permute-start(f32[56,128]{1,0:T(8,128)S(1)} %get-tuple-element.65.refs_0_), channel_id=1, source_target_pairs={{0,4},{4,0},{8,12},{12,8},{1,5},{5,1},{9,13},{13,9},{2,6},{6,2},{1... | collective-permute-start | bytes 86024 | tf_op jit(solution)/shard_map/ppermute | solution.py:445
  40.8 6.5 %collective-permute-start.17 = (f32[104,128]{1,0:T(8,128)S(1)}, f32[104,128]{1,0:T(8,128)S(1)}, u32[]{:S(2)}, u32[]{:S(2)}) collective-permute-start(f32[104,128]{1,0:T(8,128)S(1)} %get-tuple-element.115), channel_id=1, source_target_pairs={{0,3},{1,2},{2,1},{3,0},{4,7},{5,6},{6,5},{7,4},{8,11},{9,10},{10,... | collective-permute-start | bytes 159752 | tf_op jit(solution)/shard_map/ppermute | solution.py:445
  42.4 5.7 %collective-permute-start.15 = (f32[104,128]{1,0:T(8,128)S(1)}, f32[104,128]{1,0:T(8,128)S(1)}, u32[]{:S(2)}, u32[]{:S(2)}) collective-permute-start(f32[104,128]{1,0:T(8,128)S(1)} %get-tuple-element.115), channel_id=1, source_target_pairs={{0,1},{1,0},{2,3},{3,2},{4,5},{5,4},{6,7},{7,6},{8,9},{9,8},{10,11... | collective-permute-start | bytes 159752 | tf_op jit(solution)/shard_map/ppermute | solution.py:445
  43.0 6.0 %collective-permute-start.16 = (f32[104,128]{1,0:T(8,128)S(1)}, f32[104,128]{1,0:T(8,128)S(1)}, u32[]{:S(2)}, u32[]{:S(2)}) collective-permute-start(f32[104,128]{1,0:T(8,128)S(1)} %get-tuple-element.116.refs_0_), channel_id=1, source_target_pairs={{0,2},{1,3},{2,0},{3,1},{4,6},{5,7},{6,4},{7,5},{8,10},{9,11},{10,... | collective-permute-start | bytes 159752 | tf_op jit(solution)/shard_map/ppermute | solution.py:445
  49.1 5.0 %collective-permute-start.19 = (f32[96,128]{1,0:T(8,128)S(1)}, f32[96,128]{1,0:T(8,128)S(1)}, u32[]{:S(2)}, u32[]{:S(2)}) collective-permute-start(f32[96,128]{1,0:T(8,128)S(1)} %get-tuple-element.80.refs_5_), channel_id=1, source_target_pairs={{0,1},{1,0},{2,3},{3,2},{4,5},{5,4},{6,7},{7,6},{8,9},{9,8},{10,11... | collective-permute-start | bytes 147464 | tf_op jit(solution)/shard_map/ppermute | solution.py:445
  49.7 3.9 %collective-permute-start.20 = (f32[56,128]{1,0:T(8,128)S(1)}, f32[56,128]{1,0:T(8,128)S(1)}, u32[]{:S(2)}, u32[]{:S(2)}) collective-permute-start(f32[56,128]{1,0:T(8,128)S(1)} %get-tuple-element.81), channel_id=1, source_target_pairs={{0,8},{4,12},{8,0},{12,4},{1,9},{5,13},{9,1},{13,5},{2,10},{6,14},... | collective-permute-start | bytes 86024 | tf_op jit(solution)/shard_map/ppermute | solution.py:445
  50.6 3.5 %collective-permute-start.21 = (f32[56,128]{1,0:T(8,128)S(1)}, f32[56,128]{1,0:T(8,128)S(1)}, u32[]{:S(2)}, u32[]{:S(2)}) collective-permute-start(f32[56,128]{1,0:T(8,128)S(1)} %get-tuple-element.82), channel_id=1, source_target_pairs={{0,12},{4,8},{8,4},{12,0},{1,13},{5,9},{9,5},{13,1},{2,14},{6,10},... | collective-permute-start | bytes 86024 | tf_op jit(solution)/shard_map/ppermute | solution.py:445
  50.6 3.5 %collective-permute-start.18 = (f32[56,128]{1,0:T(8,128)S(1)}, f32[56,128]{1,0:T(8,128)S(1)}, u32[]{:S(2)}, u32[]{:S(2)}) collective-permute-start(f32[56,128]{1,0:T(8,128)S(1)} %get-tuple-element.79.refs_0_), channel_id=1, source_target_pairs={{0,4},{4,0},{8,12},{12,8},{1,5},{5,1},{9,13},{13,9},{2,6},{6,2},{1... | collective-permute-start | bytes 86024 | tf_op jit(solution)/shard_map/ppermute | solution.py:445
  60.3 6.4 %collective-permute-start.25 = (f32[104,128]{1,0:T(8,128)S(1)}, f32[104,128]{1,0:T(8,128)S(1)}, u32[]{:S(2)}, u32[]{:S(2)}) collective-permute-start(f32[104,128]{1,0:T(8,128)S(1)} %get-tuple-element.113), channel_id=1, source_target_pairs={{0,3},{1,2},{2,1},{3,0},{4,7},{5,6},{6,5},{7,4},{8,11},{9,10},{10,... | collective-permute-start | bytes 159752 | tf_op jit(solution)/shard_map/ppermute | solution.py:445
  62.5 6.0 %collective-permute-start.23 = (f32[104,128]{1,0:T(8,128)S(1)}, f32[104,128]{1,0:T(8,128)S(1)}, u32[]{:S(2)}, u32[]{:S(2)}) collective-permute-start(f32[104,128]{1,0:T(8,128)S(1)} %get-tuple-element.113), channel_id=1, source_target_pairs={{0,1},{1,0},{2,3},{3,2},{4,5},{5,4},{6,7},{7,6},{8,9},{9,8},{10,11... | collective-permute-start | bytes 159752 | tf_op jit(solution)/shard_map/ppermute | solution.py:445
  62.5 6.0 %collective-permute-start.24 = (f32[104,128]{1,0:T(8,128)S(1)}, f32[104,128]{1,0:T(8,128)S(1)}, u32[]{:S(2)}, u32[]{:S(2)}) collective-permute-start(f32[104,128]{1,0:T(8,128)S(1)} %get-tuple-element.114.refs_0_), channel_id=1, source_target_pairs={{0,2},{1,3},{2,0},{3,1},{4,6},{5,7},{6,4},{7,5},{8,10},{9,11},{10,... | collective-permute-start | bytes 159752 | tf_op jit(solution)/shard_map/ppermute | solution.py:445
  68.6 5.6 %collective-permute-start.27 = (f32[96,128]{1,0:T(8,128)S(1)}, f32[96,128]{1,0:T(8,128)S(1)}, u32[]{:S(2)}, u32[]{:S(2)}) collective-permute-start(f32[96,128]{1,0:T(8,128)S(1)} %get-tuple-element.91.refs_5_), channel_id=1, source_target_pairs={{0,1},{1,0},{2,3},{3,2},{4,5},{5,4},{6,7},{7,6},{8,9},{9,8},{10,11... | collective-permute-start | bytes 147464 | tf_op jit(solution)/shard_map/ppermute | solution.py:445
  69.7 3.9 %collective-permute-start.28 = (f32[56,128]{1,0:T(8,128)S(1)}, f32[56,128]{1,0:T(8,128)S(1)}, u32[]{:S(2)}, u32[]{:S(2)}) collective-permute-start(f32[56,128]{1,0:T(8,128)S(1)} %get-tuple-element.92), channel_id=1, source_target_pairs={{0,8},{4,12},{8,0},{12,4},{1,9},{5,13},{9,1},{13,5},{2,10},{6,14},... | collective-permute-start | bytes 86024 | tf_op jit(solution)/shard_map/ppermute | solution.py:445
  70.7 3.5 %collective-permute-start.29 = (f32[56,128]{1,0:T(8,128)S(1)}, f32[56,128]{1,0:T(8,128)S(1)}, u32[]{:S(2)}, u32[]{:S(2)}) collective-permute-start(f32[56,128]{1,0:T(8,128)S(1)} %get-tuple-element.93), channel_id=1, source_target_pairs={{0,12},{4,8},{8,4},{12,0},{1,13},{5,9},{9,5},{13,1},{2,14},{6,10},... | collective-permute-start | bytes 86024 | tf_op jit(solution)/shard_map/ppermute | solution.py:445
  70.7 3.5 %collective-permute-start.26 = (f32[56,128]{1,0:T(8,128)S(1)}, f32[56,128]{1,0:T(8,128)S(1)}, u32[]{:S(2)}, u32[]{:S(2)}) collective-permute-start(f32[56,128]{1,0:T(8,128)S(1)} %get-tuple-element.90.refs_0_), channel_id=1, source_target_pairs={{0,4},{4,0},{8,12},{12,8},{1,5},{5,1},{9,13},{13,9},{2,6},{6,2},{1... | collective-permute-start | bytes 86024 | tf_op jit(solution)/shard_map/ppermute | solution.py:445
  80.4 5.1 %collective-permute-start.32 = (f32[56,128]{1,0:T(8,128)S(1)}, f32[56,128]{1,0:T(8,128)S(1)}, u32[]{:S(2)}, u32[]{:S(2)}) collective-permute-start(f32[56,128]{1,0:T(8,128)S(1)} %get-tuple-element.119), channel_id=1, source_target_pairs={{0,2},{1,3},{2,0},{3,1},{4,6},{5,7},{6,4},{7,5},{8,10},{9,11},{10,... | collective-permute-start | bytes 86024 | tf_op jit(solution)/shard_map/ppermute | solution.py:445
  82.2 3.9 %collective-permute-start.31 = (f32[56,128]{1,0:T(8,128)S(1)}, f32[56,128]{1,0:T(8,128)S(1)}, u32[]{:S(2)}, u32[]{:S(2)}) collective-permute-start(f32[56,128]{1,0:T(8,128)S(1)} %get-tuple-element.120), channel_id=1, source_target_pairs={{0,1},{1,0},{2,3},{3,2},{4,5},{5,4},{6,7},{7,6},{8,9},{9,8},{10,11... | collective-permute-start | bytes 86024 | tf_op jit(solution)/shard_map/ppermute | solution.py:445
  82.6 5.7 %collective-permute-start.33 = (f32[56,128]{1,0:T(8,128)S(1)}, f32[56,128]{1,0:T(8,128)S(1)}, u32[]{:S(2)}, u32[]{:S(2)}) collective-permute-start(f32[56,128]{1,0:T(8,128)S(1)} %get-tuple-element.111), channel_id=1, source_target_pairs={{0,3},{1,2},{2,1},{3,0},{4,7},{5,6},{6,5},{7,4},{8,11},{9,10},{10,... | collective-permute-start | bytes 86024 | tf_op jit(solution)/shard_map/ppermute | solution.py:445
  88.4 4.7 %collective-permute-start.37 = (f32[144,128]{1,0:T(8,128)S(1)}, f32[144,128]{1,0:T(8,128)S(1)}, u32[]{:S(2)}, u32[]{:S(2)}) collective-permute-start(f32[144,128]{1,0:T(8,128)S(1)} %get-tuple-element.106.refs_4_), channel_id=1, source_target_pairs={{0,16},{16,0},{1,17},{17,1},{2,18},{18,2},{3,19},{19,3},{4,20},{20... | collective-permute-start | bytes 221192 | tf_op jit(solution)/shard_map/ppermute | solution.py:445
  89.5 3.6 %collective-permute-start.35 = (f32[8,128]{1,0:T(8,128)S(1)}, f32[8,128]{1,0:T(8,128)S(1)}, u32[]{:S(2)}, u32[]{:S(2)}) collective-permute-start(f32[8,128]{1,0:T(8,128)S(1)} %get-tuple-element.105.refs_0_), channel_id=1, source_target_pairs={{0,8},{4,12},{8,0},{12,4},{1,9},{5,13},{9,1},{13,5},{2,10},{6,14},... | collective-permute-start | bytes 12296 | tf_op jit(solution)/shard_map/ppermute | solution.py:445
  (6 other events, 18.1 us)
